TPU v7x, 32 devices: a whole 2x2x4 slice. The times are simulated.
32 devices in a mesh: groups: 2 (over y), seq: 4 (over z), tensor: 4 (over x, core).
Axes of the slice: x: 2, y: 2, z: 4, core: 2. Of those that a mesh axis runs over, the one named last changes fastest.
Arguments:
- residual_in: float32 [1024, 4096], P(('groups', 'seq'), 'tensor'), parts along dimension 0, may hold values from -48 to 48
- norm_gain: float32 [4096], replicated, may hold values from 0.1 to 1.9
- in_weight: bfloat16 [3, 4096, 2048], P(None, 'seq', 'tensor'), may hold values from -0.09375 to 0.09375
- short_taps: float32 [3, 3, 2048], P(None, None, 'tensor'), may hold values from -3 to 3
- long_filter: float32 [2048, 512], P(('tensor', 'seq')), may hold values from -0.25 to 0.25
- out_weight: bfloat16 [4096, 2048], P('seq', 'tensor'), may hold values from -0.125 to 0.125
Outputs:
- block_out: float32 [1024, 4096], P(('groups', 'seq'), 'tensor'), parts along dimension 0
There are 2 independent parts, one for each index of `groups`. A program takes and returns all parts, laid end to end along the dimension named above; an argument that names none is the same for every part. Nothing has to cross between parts.
All inputs are finite; a program needn't handle non-finite values.
Results may differ from a plain program's by a relative error of at most 0.015.
Values may be sent and summed in bfloat16 or wider, within the bound.
No kernel may reach another device: no remote copies, remote signals or barrier semaphores. Data moves between devices by JAX's collectives and lax.ppermute only.
A program may use at most 64 MiB of HBM per device.

v0:
```python
import functools

import jax
import jax.numpy as jnp
import numpy as np
from jax import lax
from jax.experimental import pallas as pl
from jax.experimental.pallas import tpu as pltpu
from jax.sharding import PartitionSpec as P


EPSILON = 1e-05
BLOCK = 512


def pick(stacked, index):
    return lax.dynamic_index_in_dim(stacked, index, 0, keepdims=False)


def hop(value, axis, mask):
    count = lax.axis_size(axis)
    return lax.ppermute(value, axis, [(a, a ^ mask) for a in range(count)])


def exchange(blocks, axis):
    me = lax.axis_index(axis)
    count = lax.axis_size(axis)
    got = [pick(blocks, me)]
    got += [hop(pick(blocks, me ^ mask), axis, mask) for mask in range(1, count)]
    got = jnp.stack(got)
    return jnp.stack([pick(got, me ^ source) for source in range(count)])


def spread(value, axis):
    parts = {0: value}
    mask = lax.axis_size(axis) // 2
    while mask:
        parts.update({slot ^ mask: hop(part, axis, mask) for slot, part in parts.items()})
        mask //= 2
    return parts


def fold(parts, axis, masks):
    parts = dict(parts)
    for mask in masks:
        for slot in sorted(parts, reverse=True):
            if slot & mask:
                came = hop(parts.pop(slot).astype(jnp.bfloat16), axis, mask)
                parts[slot ^ mask] = parts[slot ^ mask] + came.astype(jnp.float32)
    return parts


def sum_over_seq(rows, weight_of):
    count = lax.axis_size("seq")
    narrow = weight_of(0).shape[2] % 128 != 0

    def product(mask):
        form = "rd,sdc->scr" if narrow else "rd,sdc->src"
        return jnp.einsum(form, rows, weight_of(mask), preferred_element_type=jnp.float32)

    sent = {mask: product(mask).astype(jnp.bfloat16) for mask in range(1, count)}
    came = [hop(sent[mask], "seq", mask) for mask in sent]
    if narrow:
        return [term.transpose(0, 2, 1) for term in [product(0)] + came]
    return [product(0)] + came


def tables(block):
    odd = 2 * np.arange(block)[:, None] + 1
    theta = (odd * np.arange(2 * block)[None, :] % (4 * block)) * (np.pi / (2 * block))
    return np.concatenate([np.cos(theta), np.sin(theta)]).astype(np.float32)


def causal_convolution(signal, taps):
    length, channels = signal.shape
    block = min(length, BLOCK)
    count = length // block
    table = jnp.asarray(tables(block))
    forward = table[:, :block]
    taps_all = jnp.einsum("ft,ckt->kfc", forward, taps.reshape(channels, count, block), precision=lax.Precision.HIGH)
    taps_cos, taps_sin = taps_all[:, :block], taps_all[:, block:]
    both = jnp.stack(
        [
            jnp.einsum("ft,tc->fc", forward, signal[one * block : (one + 1) * block], precision=lax.Precision.HIGH)
            for one in range(count)
        ]
    )
    cos, sin = both[:, :block], both[:, block:]
    outputs = []
    spill = None
    for last in range(count):
        real = imag = 0.0
        for one in range(last + 1):
            other = last - one
            real = real + cos[one] * taps_cos[other] - sin[one] * taps_sin[other]
            imag = imag + cos[one] * taps_sin[other] + sin[one] * taps_cos[other]
        both = jnp.concatenate([real, imag])
        reach = block if last == count - 1 else 2 * block
        back = jnp.einsum("ft,fc->tc", table[:, :reach], both, precision=lax.Precision.HIGH) / block
        here = back[:block]
        outputs.append(here if spill is None else here + spill)
        spill = back[block:]
    return outputs[0] if count == 1 else jnp.concatenate(outputs)


def halves(value):
    high = value.astype(jnp.bfloat16)
    return high, (value - high.astype(jnp.float32)).astype(jnp.bfloat16)


def split_tables(block):
    table = tables(block)[:, :block]
    out = []
    for part in (table, table.T / np.float32(block)):
        high = part.astype(jnp.bfloat16)
        out += [high, (part - high.astype(np.float32)).astype(jnp.bfloat16)]
    return out


def wide_dot(high, low, value, dims):
    dot = functools.partial(lax.dot_general, dimension_numbers=(dims, ((), ())), preferred_element_type=jnp.float32)
    upper, lower = halves(value)
    free = 1 - dims[1][0]
    width = value.shape[free]
    both = dot(high, jnp.concatenate([upper, lower], axis=free))
    return both[:, :width] + both[:, width:] + dot(low, upper)


def filter_kernel(high_ref, low_ref, taps_ref, out_ref):
    out_ref[...] = wide_dot(high_ref[...], low_ref[...], taps_ref[...], ((1,), (1,)))


def local_kernel(groups, seq, sub, t_ref, taps_ref, *refs):
    count = seq * len(groups)
    moved = count + 5
    sources, outs = refs[:moved], refs[moved : moved + 2]
    proj, gated, sems = refs[moved + 2 : moved + 5]
    held = refs[moved + 5 :]
    copies = [pltpu.make_async_copy(sources[i], held[i], sems.at[i]) for i in range(moved)]
    for copy in copies:
        copy.start()
    terms = held[:count]
    fore_high, fore_low, spectrum_ref, back_high, back_low = held[count:]
    t = t_ref[0]
    length = gated.shape[0]
    shard = length // seq
    tensor = shard // sub

    def place(slot, source, lead):
        return pl.ds(pl.multiple_of(lead + source * shard + (t ^ slot) * sub, 8), sub)

    proj[:, :8] = jnp.zeros((proj.shape[0], 8, proj.shape[2]), jnp.float32)
    for group, slots in enumerate(groups):
        mine = terms[group * seq : (group + 1) * seq]
        for copy in copies[group * seq : (group + 1) * seq]:
            copy.wait()
        for position, slot in enumerate(slots):
            for source in range(seq):
                rows = pl.ds((position * seq + source) * sub, sub)
                total = mine[0][:, rows]
                for term in mine[1:]:
                    total = total + term[:, rows].astype(jnp.float32)
                proj[:, place(slot, source, 8)] = total

    def mixed(stream):
        total = taps_ref[stream, 0:1] * proj[stream, pl.ds(8, length)]
        for offset in range(1, taps_ref.shape[1]):
            total = total + taps_ref[stream, offset : offset + 1] * proj[stream, pl.ds(8 - offset, length)]
        return total

    signal = mixed(1) * mixed(2)
    for copy in copies[count : count + 3]:
        copy.wait()
    both = wide_dot(fore_high[...], fore_low[...], signal, ((1,), (0,)))
    cos, sin = both[:length], both[length:]
    taps_cos, taps_sin = spectrum_ref[:length], spectrum_ref[length:]
    both = jnp.concatenate([cos * taps_cos - sin * taps_sin, cos * taps_sin + sin * taps_cos])
    for copy in copies[count + 3 :]:
        copy.wait()
    gated[...] = mixed(0) * wide_dot(back_high[...], back_low[...], both, ((1,), (0,)))
    for slot in range(tensor):
        out = outs[slot // (tensor // 2)]
        for source in range(seq):
            row = ((slot % (tensor // 2)) * seq + source) * sub
            out[row : row + sub] = gated[place(slot, source, 0)].astype(jnp.bfloat16)


def local_stage(groups, terms, taps, long_filter, t, seq, sub):
    own, length = long_filter.shape
    wide = split_tables(length)
    vmem = pl.BlockSpec(memory_space=pltpu.VMEM)
    make_spectrum = pl.pallas_call(
        filter_kernel,
        out_shape=jax.ShapeDtypeStruct((2 * length, own), jnp.float32),
        in_specs=[vmem] * 3,
        out_specs=vmem,
        name="filter_spectrum",
        cost_estimate=pl.CostEstimate(flops=12 * length * length * own, bytes_accessed=4 * length * length, transcendentals=0),
    )
    spectrum = make_spectrum(*wide[:2], long_filter)
    flat = [term for group in terms for term in group]
    lines = length // 2
    moved = [*flat, *wide[:2], spectrum, *wide[2:]]
    return pl.pallas_call(
        functools.partial(local_kernel, groups, seq, sub),
        out_shape=[jax.ShapeDtypeStruct((lines, own), jnp.bfloat16)] * 2,
        in_specs=[pl.BlockSpec(memory_space=pltpu.SMEM), vmem] + [pl.BlockSpec(memory_space=pl.ANY)] * len(moved),
        out_specs=[vmem] * 2,
        scratch_shapes=[
            pltpu.VMEM((3, length + 8, own), jnp.float32),
            pltpu.VMEM((length, own), jnp.float32),
            pltpu.SemaphoreType.DMA((len(moved),)),
            *(pltpu.VMEM(part.shape, part.dtype) for part in moved),
        ],
        name="filters",
        cost_estimate=pl.CostEstimate(flops=24 * length * length * own, bytes_accessed=8 * length * length, transcendentals=0),
    )(t.reshape(1).astype(jnp.int32), taps, *moved)


def plain_stage(terms, taps, long_filter, t, seq, sub):
    streams, _, own = terms[0][0].shape
    length = long_filter.shape[1]
    tensor = length // (seq * sub)
    sums = []
    for group in terms:
        total = group[0]
        for term in group[1:]:
            total = total + term.astype(jnp.float32)
        sums.append(total)
    slots = range(tensor)
    projected = jnp.concatenate(sums, axis=1).reshape(streams, tensor, seq, sub, own)
    projected = jnp.stack([lax.dynamic_index_in_dim(projected, t ^ slot, 1, keepdims=False) for slot in slots], axis=2)
    projected = projected.reshape(streams, length, own)
    reach = taps.shape[1] - 1
    padded = jnp.pad(projected, ((0, 0), (reach, 0), (0, 0)))
    mixed = 0.0
    for offset in range(reach + 1):
        mixed = mixed + taps[:, offset, None] * padded[:, reach - offset : reach - offset + length]
    query, key, value = mixed
    conv = causal_convolution(key * value, long_filter)
    gated = (query * conv).astype(jnp.bfloat16).reshape(seq, tensor, sub, own)
    gated = [lax.dynamic_index_in_dim(gated, t ^ slot, 1, keepdims=False) for slot in slots]
    return [rows.reshape(seq * sub, own) for rows in gated]


def shards(residual_in, norm_gain, in_weight, short_taps, long_filter, out_weight):
    seq, tensor = lax.axis_size("seq"), lax.axis_size("tensor")
    z, t = lax.axis_index("seq"), lax.axis_index("tensor")
    rows, width = residual_in.shape
    _, depth, channels = in_weight.shape
    model = width * tensor
    sub = rows // tensor
    own = channels // seq
    length = rows * seq
    slots = range(tensor)

    whole = exchange(residual_in.astype(jnp.bfloat16).reshape(tensor, sub, width), "tensor")

    def in_part(mask):
        return lax.dynamic_slice_in_dim(in_weight, (z ^ mask) * own, own, 2)

    out_parts = [lax.dynamic_slice_in_dim(out_weight, (z ^ mask) * own, own, 1) for mask in range(seq)]
    out_turned = jnp.concatenate(out_parts, axis=1)
    taps = lax.dynamic_slice_in_dim(short_taps, z * own, own, 2)
    whole = whole.transpose(1, 0, 2).reshape(sub, model).astype(jnp.float32)
    mean_sq = jnp.mean(whole * whole, axis=1, keepdims=True)
    normed = (whole * lax.rsqrt(mean_sq + EPSILON) * norm_gain).astype(jnp.bfloat16)
    normed = exchange(normed.reshape(sub, seq, depth).transpose(1, 0, 2), "seq")
    parts = spread(normed.reshape(seq * sub, depth), "tensor")
    groups = (tuple(slots[:1]), tuple(slots[1:]))
    terms = []
    for group in groups:
        terms.append(sum_over_seq(jnp.concatenate([parts[slot] for slot in group]), in_part))
    half = tensor // 2
    if own % 128 == 0 and length <= BLOCK and sub % 16 == 0:
        lower_gated, upper_gated = local_stage(groups, terms, taps, long_filter, t, seq, sub)
    else:
        gated = plain_stage(terms, taps, long_filter, t, seq, sub)
        lower_gated = jnp.concatenate(gated[:half])
        upper_gated = jnp.concatenate(gated[half:])

    lower = [1 << bit for bit in range(half.bit_length() - 1)]
    held = None
    for chosen, piece in ((slots[half:], upper_gated), (slots[:half], lower_gated)):
        got = [piece] + [hop(piece, "seq", mask) for mask in range(1, seq)]
        got = jnp.concatenate(got, axis=1)
        terms = {}
        for place, slot in enumerate(chosen):
            terms[slot] = jnp.einsum(
                "rc,nc->rn",
                got[place * seq * sub : (place + 1) * seq * sub],
                out_turned,
                preferred_element_type=jnp.float32,
            )
        terms = fold(terms, "tensor", lower)
        if held is None:
            held = hop(terms[half].astype(jnp.bfloat16), "tensor", half)
        else:
            held = (terms[0] + held.astype(jnp.float32)).astype(jnp.bfloat16)
    back = exchange(held.reshape(seq, sub, depth), "seq")
    back = back.transpose(1, 0, 2).reshape(sub, tensor, width).transpose(1, 0, 2)
    summed = exchange(back, "tensor").reshape(rows, width)
    return residual_in + summed.astype(jnp.float32)


def solution(mesh):
    return jax.shard_map(
        shards,
        mesh=mesh,
        in_specs=(
            P(("groups", "seq"), "tensor"),
            P(),
            P(None, "seq", "tensor"),
            P(None, None, "tensor"),
            P(("tensor", "seq"), None),
            P("seq", "tensor"),
        ),
        out_specs=P(("groups", "seq"), "tensor"),
        check_vma=False,
    )
```

profile of v0, /device:TPU:0, one launch (start us, length us, event | category | flops | bytes accessed | tf_op | source)
XLA Modules:
  0.0 118.4 jit_solution(516585960585692316)
XLA Ops:
  0.0 1.2 %convert_element_type.77 = bf16[128,1024]{1,0:T(8,128)(2,1)S(1)} convert(f32[128,1024]{1,0:T(8,128)} %param.10) | non-fusion elementwise | flops 131072 | bytes 786432 | tf_op jit(solution)/shard_map/convert_element_type | solution.py:257
  1.3 0.7 constant_dynamic-slice_fusion.23
  1.9 0.5 collective-permute-start
  2.4 2.5 %collective-permute-start.1 = (bf16[32,1024]{1,0:T(8,128)(2,1)}, bf16[32,1024]{1,0:T(8,128)(2,1)S(1)}, u32[]{:S(2)}, u32[]{:S(2)}) collective-permute-start(bf16[32,1024]{1,0:T(8,128)(2,1)} %get-tuple-element.43), channel_id=1, source_target_pairs={{0,2},{1,3},{2,0},{3,1},{4,6},{5,7},{6,4},{7,5},{8,10},{9,11},{10,... | collective-permute-start | bytes 196616 | tf_op jit(solution)/shard_map/ppermute | solution.py:22
  4.9 0.1 collective-permute-start.2
  5.0 2.2 %constant_dynamic-slice_fusion.13 = (bf16[1024,128]{1,0:T(8,128)(2,1)}, bf16[1024,128]{1,0:T(8,128)(2,1)}, bf16[1024,128]{1,0:T(8,128)(2,1)}, bf16[1024,128]{1,0:T(8,128)(2,1)}) fusion(bf16[1024,512]{1,0:T(8,128)(2,1)} %param.15, s32[]{:T(128)S(6)} %select_n.70, s32[]{:T(128)S(6)} %select_n.79, s32[]{:T(128)S(6)} %select_n.81, s32[]{:T(128)S(6)} %select_n.80), kind=kLoop, calls=%fused_computation.86 | loop fusion | bytes 2097168 | tf_op jit(solution)/shard_map/dynamic_slice | solution.py:262
  7.3 0.6 collective-permute-done.1
  7.9 1.0 collective-permute-done.2
  9.0 0.2 fusion.17
  9.2 0.1 fusion.19
  9.3 3.1 %collective-permute-start.4 = (bf16[32,1024]{1,0:T(8,128)(2,1)S(1)}, bf16[32,1024]{1,0:T(8,128)(2,1)S(1)}, u32[]{:S(2)}, u32[]{:S(2)}) collective-permute-start(bf16[32,1024]{1,0:T(8,128)(2,1)S(1)} %get-tuple-element.35), channel_id=1, source_target_pairs={{0,8},{4,12},{8,0},{12,4},{1,9},{5,13},{9,1},{13,5},{2,10},{6,14},... | collective-permute-start | bytes 196616 | tf_op jit(solution)/shard_map/ppermute | solution.py:22
  12.4 1.3 %collective-permute-start.5 = (bf16[32,1024]{1,0:T(8,128)(2,1)S(1)}, bf16[32,1024]{1,0:T(8,128)(2,1)S(1)}, u32[]{:S(2)}, u32[]{:S(2)}) collective-permute-start(bf16[32,1024]{1,0:T(8,128)(2,1)S(1)} %get-tuple-element.34), channel_id=1, source_target_pairs={{0,12},{4,8},{8,4},{12,0},{1,13},{5,9},{9,5},{13,1},{2,14},{6,10},... | collective-permute-start | bytes 196616 | tf_op jit(solution)/shard_map/ppermute | solution.py:22
  13.8 0.2 collective-permute-start.3
  14.0 1.3 %constant_dynamic-slice_fusion.24.taps_ref = f32[3,3,128]{2,1,0:T(4,128)} fusion(f32[3,3,512]{2,1,0:T(4,128)} %param.13, s32[]{:T(128)S(6)} %select_n.70), kind=kLoop, calls=%fused_computation.101 | loop fusion | bytes 9220 | tf_op jit(solution)/shard_map/dynamic_slice | solution.py:264
  15.3 1.1 collective-permute-done.4
  16.4 2.4 %collective-permute-done.5 = bf16[32,1024]{1,0:T(8,128)(2,1)S(1)} collective-permute-done((bf16[32,1024]{1,0:T(8,128)(2,1)S(1)}, bf16[32,1024]{1,0:T(8,128)(2,1)S(1)}, u32[]{:S(2)}, u32[]{:S(2)}) %collective-permute-start.5) | collective-permute-done | bytes 65568 | tf_op jit(solution)/shard_map/ppermute | solution.py:22
  18.7 0.2 collective-permute-done.3
  19.0 1.6 %collective-permute-start.10 = (bf16[128,1024]{1,0:T(8,128)(2,1)S(1)}, bf16[128,1024]{1,0:T(8,128)(2,1)}, u32[]{:S(2)}, u32[]{:S(2)}) collective-permute-start(bf16[128,1024]{1,0:T(8,128)(2,1)S(1)} %bitcast.71), channel_id=1, source_target_pairs={{0,2},{1,3},{2,0},{3,1},{4,6},{5,7},{6,4},{7,5},{8,10},{9,11},{10,... | collective-permute-start | bytes 786440 | tf_op jit(solution)/shard_map/ppermute | solution.py:22
  20.6 3.1 %filter_spectrum.1.refs_10_ = f32[1024,128]{1,0:T(8,128)} custom-call(bf16[1024,512]{1,0:T(8,128)(2,1)} %constant.101.clone.high_ref.refs_8_, bf16[1024,512]{1,0:T(8,128)(2,1)} %constant.102.clone.low_ref.refs_9_, f32[128,512]{1,0:T(8,128)} %taps_ref.1), custom_call_target="tpu_custom_call" | custom-call | flops 402653184 | bytes 1048576 | tf_op jit(solution)/shard_map/filter_spectrum/pallas_call | solution.py:200
  23.8 0.3 fusion.6
  24.1 2.2 %collective-permute-done.10 = bf16[128,1024]{1,0:T(8,128)(2,1)} collective-permute-done((bf16[128,1024]{1,0:T(8,128)(2,1)S(1)}, bf16[128,1024]{1,0:T(8,128)(2,1)}, u32[]{:S(2)}, u32[]{:S(2)}) %collective-permute-start.10) | collective-permute-done | bytes 262176 | tf_op jit(solution)/shard_map/ppermute | solution.py:22
  26.3 0.3 fusion.7
  26.6 2.0 %collective-permute-start.6 = (bf16[3,128,128]{2,1,0:T(8,128)(2,1)S(1)}, bf16[3,128,128]{2,1,0:T(8,128)(2,1)S(1)}, u32[]{:S(2)}, u32[]{:S(2)}) collective-permute-start(bf16[3,128,128]{2,1,0:T(8,128)(2,1)S(1)} %fusion.6), channel_id=1, source_target_pairs={{0,4},{4,0},{8,12},{12,8},{1,5},{5,1},{9,13},{13,9},{2,6},{6,2},{1... | collective-permute-start | bytes 294920 | tf_op jit(solution)/shard_map/ppermute | solution.py:22
  28.6 1.0 convolution_bitcast_fusion.1.refs_0_
  29.6 1.5 %fusion.5 = bf16[3,384,128]{2,1,0:T(8,128)(2,1)S(1)} fusion(bf16[3,1024,512]{2,1,0:T(8,128)(2,1)S(1)} %copy-done, s32[]{:T(128)S(6)} %select_n.81, bf16[128,1024]{1,0:T(8,128)(2,1)S(1)} %collective-permute-done.11, bf16[128,1024]{1,0:T(8,128)(2,1)} %collective-permute-done.10, bf16[128,1024]{1,0:T(8,128)(2,1)S(1)} %collective-permute-done.9), kind=kOutput, calls=%fused_computation.13 | convolution fusion | flops 304496640 | bytes 1867780 | tf_op jit(solution)/shard_map/rd,sdc->src/dot_general | solution.py:59
  31.1 3.4 %collective-permute-start.14 = (bf16[3,384,128]{2,1,0:T(8,128)(2,1)S(1)}, bf16[3,384,128]{2,1,0:T(8,128)(2,1)}, u32[]{:S(2)}, u32[]{:S(2)}) collective-permute-start(bf16[3,384,128]{2,1,0:T(8,128)(2,1)S(1)} %fusion.5), channel_id=1, source_target_pairs={{0,12},{4,8},{8,4},{12,0},{1,13},{5,9},{9,5},{13,1},{2,14},{6,10},... | collective-permute-start | bytes 884744 | tf_op jit(solution)/shard_map/ppermute | solution.py:22
  34.6 1.5 %fusion.4 = bf16[3,384,128]{2,1,0:T(8,128)(2,1)S(1)} fusion(bf16[3,1024,512]{2,1,0:T(8,128)(2,1)S(1)} %copy-done, s32[]{:T(128)S(6)} %select_n.80, bf16[128,1024]{1,0:T(8,128)(2,1)S(1)} %collective-permute-done.11, bf16[128,1024]{1,0:T(8,128)(2,1)} %collective-permute-done.10, bf16[128,1024]{1,0:T(8,128)(2,1)S(1)} %collective-permute-done.9), kind=kOutput, calls=%fused_computation.12 | convolution fusion | flops 304496640 | bytes 1867780 | tf_op jit(solution)/shard_map/rd,sdc->src/dot_general | solution.py:59
  36.1 0.1 collective-permute-start.13
  36.2 1.6 %fusion.3 = bf16[3,384,128]{2,1,0:T(8,128)(2,1)S(1)} fusion(bf16[3,1024,512]{2,1,0:T(8,128)(2,1)S(1)} %copy-done, s32[]{:T(128)S(6)} %select_n.79, bf16[128,1024]{1,0:T(8,128)(2,1)S(1)} %collective-permute-done.11, bf16[128,1024]{1,0:T(8,128)(2,1)} %collective-permute-done.10, bf16[128,1024]{1,0:T(8,128)(2,1)S(1)} %collective-permute-done.9), kind=kOutput, calls=%fused_computation.11 | convolution fusion | flops 304496640 | bytes 1867780 | tf_op jit(solution)/shard_map/rd,sdc->src/dot_general | solution.py:59
  37.7 1.1 collective-permute-start.12
  38.8 0.3 fusion.8
  39.1 2.0 %collective-permute-start.7 = (bf16[3,128,128]{2,1,0:T(8,128)(2,1)S(1)}, bf16[3,128,128]{2,1,0:T(8,128)(2,1)S(1)}, u32[]{:S(2)}, u32[]{:S(2)}) collective-permute-start(bf16[3,128,128]{2,1,0:T(8,128)(2,1)S(1)} %fusion.7), channel_id=1, source_target_pairs={{0,8},{4,12},{8,0},{12,4},{1,9},{5,13},{9,1},{13,5},{2,10},{6,14},... | collective-permute-start | bytes 294920 | tf_op jit(solution)/shard_map/ppermute | solution.py:22
  41.1 1.5 %collective-permute-start.8 = (bf16[3,128,128]{2,1,0:T(8,128)(2,1)S(1)}, bf16[3,128,128]{2,1,0:T(8,128)(2,1)S(1)}, u32[]{:S(2)}, u32[]{:S(2)}) collective-permute-start(bf16[3,128,128]{2,1,0:T(8,128)(2,1)S(1)} %fusion.8), channel_id=1, source_target_pairs={{0,12},{4,8},{8,4},{12,0},{1,13},{5,9},{9,5},{13,1},{2,14},{6,10},... | collective-permute-start | bytes 294920 | tf_op jit(solution)/shard_map/ppermute | solution.py:22
  42.6 2.3 %convolution_bitcast_fusion.refs_4_ = f32[3,384,128]{2,1,0:T(8,128)} fusion(bf16[3,1024,512]{2,1,0:T(8,128)(2,1)S(1)} %copy-done, s32[]{:T(128)S(6)} %select_n.70, bf16[128,1024]{1,0:T(8,128)(2,1)S(1)} %collective-permute-done.11, bf16[128,1024]{1,0:T(8,128)(2,1)} %collective-permute-done.10, bf16[128,1024]{1,0:T(8,128)(2,1)S(1)} %collective-permute-done.9), kind=kOutput, calls=%fused_computation | convolution fusion | flops 304349184 | bytes 2162692 | tf_op jit(solution)/shard_map/rd,sdc->src/dot_general | solution.py:59
  45.0 22.2 %collective-permute-done.7.refs_2_ = bf16[3,128,128]{2,1,0:T(8,128)(2,1)S(1)} collective-permute-done((bf16[3,128,128]{2,1,0:T(8,128)(2,1)S(1)}, bf16[3,128,128]{2,1,0:T(8,128)(2,1)S(1)}, u32[]{:S(2)}, u32[]{:S(2)}) %collective-permute-start.7) | collective-permute-done | bytes 98336 | tf_op jit(solution)/shard_map/ppermute | solution.py:22
  67.2 0.6 copy-done.7
  67.9 5.3 %filters.1 = (bf16[256,128]{1,0:T(8,128)(2,1)}, bf16[256,128]{1,0:T(8,128)(2,1)}) custom-call(s32[1]{0:T(128)} %bitcast.t_ref, f32[3,3,128]{2,1,0:T(4,128)} %constant_dynamic-slice_fusion.24.taps_ref, f32[3,128,128]{2,1,0:T(8,128)} %convolution_bitcast_fusion.1.refs_0_, bf16[3,128,128]{2,1,0:T(8,128)(2,1)} %copy-done.6, bf16[3,128,128]{2,1,0:T(8,128)(2,1)} %copy-done.7, ...), custom_call_target="tpu_custom_call" | custom-call | flops 805306368 | bytes 2097152 | tf_op jit(solution)/shard_map/filters/pallas_call | solution.py:204
  73.2 2.2 %collective-permute-start.15 = (bf16[256,128]{1,0:T(8,128)(2,1)}, bf16[256,128]{1,0:T(8,128)(2,1)S(1)}, u32[]{:S(2)}, u32[]{:S(2)}) collective-permute-start(bf16[256,128]{1,0:T(8,128)(2,1)} %get-tuple-element.7), channel_id=1, source_target_pairs={{0,4},{4,0},{8,12},{12,8},{1,5},{5,1},{9,13},{13,9},{2,6},{6,2},{1... | collective-permute-start | bytes 196616 | tf_op jit(solution)/shard_map/ppermute | solution.py:22
  75.4 1.3 %collective-permute-start.16 = (bf16[256,128]{1,0:T(8,128)(2,1)}, bf16[256,128]{1,0:T(8,128)(2,1)S(1)}, u32[]{:S(2)}, u32[]{:S(2)}) collective-permute-start(bf16[256,128]{1,0:T(8,128)(2,1)} %get-tuple-element.7), channel_id=1, source_target_pairs={{0,8},{4,12},{8,0},{12,4},{1,9},{5,13},{9,1},{13,5},{2,10},{6,14},... | collective-permute-start | bytes 196616 | tf_op jit(solution)/shard_map/ppermute | solution.py:22
  76.7 1.3 %collective-permute-start.17 = (bf16[256,128]{1,0:T(8,128)(2,1)}, bf16[256,128]{1,0:T(8,128)(2,1)S(1)}, u32[]{:S(2)}, u32[]{:S(2)}) collective-permute-start(bf16[256,128]{1,0:T(8,128)(2,1)} %get-tuple-element.7), channel_id=1, source_target_pairs={{0,12},{4,8},{8,4},{12,0},{1,13},{5,9},{9,5},{13,1},{2,14},{6,10},... | collective-permute-start | bytes 196616 | tf_op jit(solution)/shard_map/ppermute | solution.py:22
  78.1 0.8 collective-permute-start.19
  78.9 2.2 %collective-permute-start.20 = (bf16[256,128]{1,0:T(8,128)(2,1)}, bf16[256,128]{1,0:T(8,128)(2,1)S(1)}, u32[]{:S(2)}, u32[]{:S(2)}) collective-permute-start(bf16[256,128]{1,0:T(8,128)(2,1)} %get-tuple-element.8), channel_id=1, source_target_pairs={{0,8},{4,12},{8,0},{12,4},{1,9},{5,13},{9,1},{13,5},{2,10},{6,14},... | collective-permute-start | bytes 196616 | tf_op jit(solution)/shard_map/ppermute | solution.py:22
  81.1 0.9 constant_dynamic-update-slice_fusion.3
  82.0 1.6 %collective-permute-done.19 = bf16[256,128]{1,0:T(8,128)(2,1)S(1)} collective-permute-done((bf16[256,128]{1,0:T(8,128)(2,1)}, bf16[256,128]{1,0:T(8,128)(2,1)S(1)}, u32[]{:S(2)}, u32[]{:S(2)}) %collective-permute-start.19) | collective-permute-done | bytes 65568 | tf_op jit(solution)/shard_map/ppermute | solution.py:22
  83.6 2.0 %collective-permute-start.21 = (bf16[256,128]{1,0:T(8,128)(2,1)}, bf16[256,128]{1,0:T(8,128)(2,1)S(1)}, u32[]{:S(2)}, u32[]{:S(2)}) collective-permute-start(bf16[256,128]{1,0:T(8,128)(2,1)} %get-tuple-element.8), channel_id=1, source_target_pairs={{0,12},{4,8},{8,4},{12,0},{1,13},{5,9},{9,5},{13,1},{2,14},{6,10},... | collective-permute-start | bytes 196616 | tf_op jit(solution)/shard_map/ppermute | solution.py:22
  85.6 2.7 %collective-permute-done.20 = bf16[256,128]{1,0:T(8,128)(2,1)S(1)} collective-permute-done((bf16[256,128]{1,0:T(8,128)(2,1)}, bf16[256,128]{1,0:T(8,128)(2,1)S(1)}, u32[]{:S(2)}, u32[]{:S(2)}) %collective-permute-start.20) | collective-permute-done | bytes 65568 | tf_op jit(solution)/shard_map/ppermute | solution.py:22
  88.4 1.5 %collective-permute-done.21 = bf16[256,128]{1,0:T(8,128)(2,1)S(1)} collective-permute-done((bf16[256,128]{1,0:T(8,128)(2,1)}, bf16[256,128]{1,0:T(8,128)(2,1)S(1)}, u32[]{:S(2)}, u32[]{:S(2)}) %collective-permute-start.21) | collective-permute-done | bytes 65568 | tf_op jit(solution)/shard_map/ppermute | solution.py:22
  90.0 1.6 %convolution_convert_fusion.3 = bf16[128,1024]{1,0:T(8,128)(2,1)S(1)} fusion(bf16[256,512]{1,0:T(8,128)(2,1)S(1)} %constant_dynamic-update-slice_fusion.4, bf16[1024,128]{1,0:T(8,128)(2,1)} %get-tuple-element.11, bf16[1024,128]{1,0:T(8,128)(2,1)} %get-tuple-element.12, bf16[1024,128]{1,0:T(8,128)(2,1)} %get-tuple-element.10, bf16[1024,128]{1,0:T(8,128)(2,1)S(1)} %copy-done.2), kind=kOutput, calls=%fused_computation.9 | convolution fusion | flops 138543104 | bytes 1441792 | tf_op jit(solution)/shard_map/rc,nc->rn/dot_general | solution.py:289
  91.8 0.5 convolution_convert_fusion.4
  92.3 0.6 collective-permute-start.18
  92.9 0.3 collective-permute-done.22
  93.2 0.5 fusion.2
  93.7 1.7 %collective-permute-start.23 = (bf16[128,1024]{1,0:T(8,128)(2,1)S(1)}, bf16[128,1024]{1,0:T(8,128)(2,1)S(1)}, u32[]{:S(2)}, u32[]{:S(2)}) collective-permute-start(bf16[128,1024]{1,0:T(8,128)(2,1)S(1)} %fusion.2), channel_id=1, source_target_pairs={{0,2},{1,3},{2,0},{3,1},{4,6},{5,7},{6,4},{7,5},{8,10},{9,11},{10,... | collective-permute-start | bytes 786440 | tf_op jit(solution)/shard_map/ppermute | solution.py:22
  95.4 6.7 %collective-permute-done.23 = bf16[128,1024]{1,0:T(8,128)(2,1)S(1)} collective-permute-done((bf16[128,1024]{1,0:T(8,128)(2,1)S(1)}, bf16[128,1024]{1,0:T(8,128)(2,1)S(1)}, u32[]{:S(2)}, u32[]{:S(2)}) %collective-permute-start.23) | collective-permute-done | bytes 262176 | tf_op jit(solution)/shard_map/ppermute | solution.py:22
  102.1 0.5 fusion.1
  102.7 2.5 %collective-permute-start.25 = (bf16[32,1024]{1,0:T(8,128)(2,1)S(1)}, bf16[32,1024]{1,0:T(8,128)(2,1)S(1)}, u32[]{:S(2)}, u32[]{:S(2)}) collective-permute-start(bf16[32,1024]{1,0:T(8,128)(2,1)S(1)} %get-tuple-element.27), channel_id=1, source_target_pairs={{0,8},{4,12},{8,0},{12,4},{1,9},{5,13},{9,1},{13,5},{2,10},{6,14},... | collective-permute-start | bytes 196616 | tf_op jit(solution)/shard_map/ppermute | solution.py:22
  105.3 1.8 %collective-permute-start.26 = (bf16[32,1024]{1,0:T(8,128)(2,1)S(1)}, bf16[32,1024]{1,0:T(8,128)(2,1)S(1)}, u32[]{:S(2)}, u32[]{:S(2)}) collective-permute-start(bf16[32,1024]{1,0:T(8,128)(2,1)S(1)} %get-tuple-element.26), channel_id=1, source_target_pairs={{0,12},{4,8},{8,4},{12,0},{1,13},{5,9},{9,5},{13,1},{2,14},{6,10},... | collective-permute-start | bytes 196616 | tf_op jit(solution)/shard_map/ppermute | solution.py:22
  107.1 1.4 %collective-permute-done.25 = bf16[32,1024]{1,0:T(8,128)(2,1)S(1)} collective-permute-done((bf16[32,1024]{1,0:T(8,128)(2,1)S(1)}, bf16[32,1024]{1,0:T(8,128)(2,1)S(1)}, u32[]{:S(2)}, u32[]{:S(2)}) %collective-permute-start.25) | collective-permute-done | bytes 65568 | tf_op jit(solution)/shard_map/ppermute | solution.py:22
  108.5 2.8 %collective-permute-done.26 = bf16[32,1024]{1,0:T(8,128)(2,1)S(1)} collective-permute-done((bf16[32,1024]{1,0:T(8,128)(2,1)S(1)}, bf16[32,1024]{1,0:T(8,128)(2,1)S(1)}, u32[]{:S(2)}, u32[]{:S(2)}) %collective-permute-start.26) | collective-permute-done | bytes 65568 | tf_op jit(solution)/shard_map/ppermute | solution.py:22
  111.6 1.7 %collective-permute-start.28 = (bf16[32,1024]{1,0:T(8,128)(2,1)S(1)}, bf16[32,1024]{1,0:T(8,128)(2,1)S(1)}, u32[]{:S(2)}, u32[]{:S(2)}) collective-permute-start(bf16[32,1024]{1,0:T(8,128)(2,1)S(1)} %get-tuple-element.19), channel_id=1, source_target_pairs={{0,2},{1,3},{2,0},{3,1},{4,6},{5,7},{6,4},{7,5},{8,10},{9,11},{10,... | collective-permute-start | bytes 196616 | tf_op jit(solution)/shard_map/ppermute | solution.py:22
  113.3 0.1 collective-permute-start.29
  113.4 2.6 %collective-permute-done.28 = bf16[32,1024]{1,0:T(8,128)(2,1)S(1)} collective-permute-done((bf16[32,1024]{1,0:T(8,128)(2,1)S(1)}, bf16[32,1024]{1,0:T(8,128)(2,1)S(1)}, u32[]{:S(2)}, u32[]{:S(2)}) %collective-permute-start.28) | collective-permute-done | bytes 65568 | tf_op jit(solution)/shard_map/ppermute | solution.py:22
  116.1 1.3 %collective-permute-done.29 = bf16[32,1024]{1,0:T(8,128)(2,1)S(1)} collective-permute-done((bf16[32,1024]{1,0:T(8,128)(2,1)S(1)}, bf16[32,1024]{1,0:T(8,128)(2,1)S(1)}, u32[]{:S(2)}, u32[]{:S(2)}) %collective-permute-start.29) | collective-permute-done | bytes 65568 | tf_op jit(solution)/shard_map/ppermute | solution.py:22
  117.5 0.9 convert_add_fusion
  (60 shorter events, 0.9 us)
Async XLA Ops:
  0.0 23.8 %copy-start = (bf16[3,1024,512]{2,1,0:T(8,128)(2,1)S(1)}, bf16[3,1024,512]{2,1,0:T(8,128)(2,1)}, u32[]{:S(2)}) copy-start(bf16[3,1024,512]{2,1,0:T(8,128)(2,1)} %param.12) | copy-start | bytes 9437188
  0.0 7.3 %copy-start.9 = (f32[4096]{0:T(1024)S(1)}, f32[4096]{0:T(1024)}, u32[]{:S(2)}) copy-start(f32[4096]{0:T(1024)} %param.11) | copy-start | bytes 49156
  1.9 5.3 %collective-permute-start = (bf16[32,1024]{1,0:T(8,128)(2,1)}, bf16[32,1024]{1,0:T(8,128)(2,1)S(1)}, u32[]{:S(2)}, u32[]{:S(2)}) collective-permute-start(bf16[32,1024]{1,0:T(8,128)(2,1)} %get-tuple-element.44), channel_id=1, source_target_pairs={{0,1},{1,0},{2,3},{3,2},{4,5},{5,4},{6,7},{7,6},{8,9},{9,8},{10,11... | collective-permute-start | bytes 196616 | tf_op jit(solution)/shard_map/ppermute | solution.py:22
  2.4 5.4 %collective-permute-start.1 = (bf16[32,1024]{1,0:T(8,128)(2,1)}, bf16[32,1024]{1,0:T(8,128)(2,1)S(1)}, u32[]{:S(2)}, u32[]{:S(2)}) collective-permute-start(bf16[32,1024]{1,0:T(8,128)(2,1)} %get-tuple-element.43), channel_id=1, source_target_pairs={{0,2},{1,3},{2,0},{3,1},{4,6},{5,7},{6,4},{7,5},{8,10},{9,11},{10,... | collective-permute-start | bytes 196616 | tf_op jit(solution)/shard_map/ppermute | solution.py:22
  4.9 4.0 %collective-permute-start.2 = (bf16[32,1024]{1,0:T(8,128)(2,1)S(1)}, bf16[32,1024]{1,0:T(8,128)(2,1)S(1)}, u32[]{:S(2)}, u32[]{:S(2)}) collective-permute-start(bf16[32,1024]{1,0:T(8,128)(2,1)S(1)} %get-tuple-element.42), channel_id=1, source_target_pairs={{0,3},{1,2},{2,1},{3,0},{4,7},{5,6},{6,5},{7,4},{8,11},{9,10},{10,... | collective-permute-start | bytes 196616 | tf_op jit(solution)/shard_map/ppermute | solution.py:22
  9.3 7.0 %collective-permute-start.4 = (bf16[32,1024]{1,0:T(8,128)(2,1)S(1)}, bf16[32,1024]{1,0:T(8,128)(2,1)S(1)}, u32[]{:S(2)}, u32[]{:S(2)}) collective-permute-start(bf16[32,1024]{1,0:T(8,128)(2,1)S(1)} %get-tuple-element.35), channel_id=1, source_target_pairs={{0,8},{4,12},{8,0},{12,4},{1,9},{5,13},{9,1},{13,5},{2,10},{6,14},... | collective-permute-start | bytes 196616 | tf_op jit(solution)/shard_map/ppermute | solution.py:22
  12.4 6.3 %collective-permute-start.5 = (bf16[32,1024]{1,0:T(8,128)(2,1)S(1)}, bf16[32,1024]{1,0:T(8,128)(2,1)S(1)}, u32[]{:S(2)}, u32[]{:S(2)}) collective-permute-start(bf16[32,1024]{1,0:T(8,128)(2,1)S(1)} %get-tuple-element.34), channel_id=1, source_target_pairs={{0,12},{4,8},{8,4},{12,0},{1,13},{5,9},{9,5},{13,1},{2,14},{6,10},... | collective-permute-start | bytes 196616 | tf_op jit(solution)/shard_map/ppermute | solution.py:22
  13.8 5.2 %collective-permute-start.3 = (bf16[32,1024]{1,0:T(8,128)(2,1)S(1)}, bf16[32,1024]{1,0:T(8,128)(2,1)S(1)}, u32[]{:S(2)}, u32[]{:S(2)}) collective-permute-start(bf16[32,1024]{1,0:T(8,128)(2,1)S(1)} %get-tuple-element.36), channel_id=1, source_target_pairs={{0,4},{4,0},{8,12},{12,8},{1,5},{5,1},{9,13},{13,9},{2,6},{6,2},{1... | collective-permute-start | bytes 196616 | tf_op jit(solution)/shard_map/ppermute | solution.py:22
  19.0 7.3 %collective-permute-start.10 = (bf16[128,1024]{1,0:T(8,128)(2,1)S(1)}, bf16[128,1024]{1,0:T(8,128)(2,1)}, u32[]{:S(2)}, u32[]{:S(2)}) collective-permute-start(bf16[128,1024]{1,0:T(8,128)(2,1)S(1)} %bitcast.71), channel_id=1, source_target_pairs={{0,2},{1,3},{2,0},{3,1},{4,6},{5,7},{6,4},{7,5},{8,10},{9,11},{10,... | collective-permute-start | bytes 786440 | tf_op jit(solution)/shard_map/ppermute | solution.py:22
  23.8 5.8 %collective-permute-start.9 = (bf16[128,1024]{1,0:T(8,128)(2,1)S(1)}, bf16[128,1024]{1,0:T(8,128)(2,1)S(1)}, u32[]{:S(2)}, u32[]{:S(2)}) collective-permute-start(bf16[128,1024]{1,0:T(8,128)(2,1)S(1)} %bitcast.72), channel_id=1, source_target_pairs={{0,1},{1,0},{2,3},{3,2},{4,5},{5,4},{6,7},{7,6},{8,9},{9,8},{10,11... | collective-permute-start | bytes 786440 | tf_op jit(solution)/shard_map/ppermute | solution.py:22
  26.3 3.3 %collective-permute-start.11 = (bf16[128,1024]{1,0:T(8,128)(2,1)}, bf16[128,1024]{1,0:T(8,128)(2,1)S(1)}, u32[]{:S(2)}, u32[]{:S(2)}) collective-permute-start(bf16[128,1024]{1,0:T(8,128)(2,1)} %collective-permute-done.10), channel_id=1, source_target_pairs={{0,1},{1,0},{2,3},{3,2},{4,5},{5,4},{6,7},{7,6},{8,9},{9,8},{10,11... | collective-permute-start | bytes 786440 | tf_op jit(solution)/shard_map/ppermute | solution.py:22
  26.6 14.5 %collective-permute-start.6 = (bf16[3,128,128]{2,1,0:T(8,128)(2,1)S(1)}, bf16[3,128,128]{2,1,0:T(8,128)(2,1)S(1)}, u32[]{:S(2)}, u32[]{:S(2)}) collective-permute-start(bf16[3,128,128]{2,1,0:T(8,128)(2,1)S(1)} %fusion.6), channel_id=1, source_target_pairs={{0,4},{4,0},{8,12},{12,8},{1,5},{5,1},{9,13},{13,9},{2,6},{6,2},{1... | collective-permute-start | bytes 294920 | tf_op jit(solution)/shard_map/ppermute | solution.py:22
  31.1 36.1 %collective-permute-start.14 = (bf16[3,384,128]{2,1,0:T(8,128)(2,1)S(1)}, bf16[3,384,128]{2,1,0:T(8,128)(2,1)}, u32[]{:S(2)}, u32[]{:S(2)}) collective-permute-start(bf16[3,384,128]{2,1,0:T(8,128)(2,1)S(1)} %fusion.5), channel_id=1, source_target_pairs={{0,12},{4,8},{8,4},{12,0},{1,13},{5,9},{9,5},{13,1},{2,14},{6,10},... | collective-permute-start | bytes 884744 | tf_op jit(solution)/shard_map/ppermute | solution.py:22
  36.1 31.1 %collective-permute-start.13 = (bf16[3,384,128]{2,1,0:T(8,128)(2,1)S(1)}, bf16[3,384,128]{2,1,0:T(8,128)(2,1)}, u32[]{:S(2)}, u32[]{:S(2)}) collective-permute-start(bf16[3,384,128]{2,1,0:T(8,128)(2,1)S(1)} %fusion.4), channel_id=1, source_target_pairs={{0,8},{4,12},{8,0},{12,4},{1,9},{5,13},{9,1},{13,5},{2,10},{6,14},... | collective-permute-start | bytes 884744 | tf_op jit(solution)/shard_map/ppermute | solution.py:22
  37.7 29.5 %collective-permute-start.12 = (bf16[3,384,128]{2,1,0:T(8,128)(2,1)S(1)}, bf16[3,384,128]{2,1,0:T(8,128)(2,1)}, u32[]{:S(2)}, u32[]{:S(2)}) collective-permute-start(bf16[3,384,128]{2,1,0:T(8,128)(2,1)S(1)} %fusion.3), channel_id=1, source_target_pairs={{0,4},{4,0},{8,12},{12,8},{1,5},{5,1},{9,13},{13,9},{2,6},{6,2},{1... | collective-permute-start | bytes 884744 | tf_op jit(solution)/shard_map/ppermute | solution.py:22
  39.1 28.1 %collective-permute-start.7 = (bf16[3,128,128]{2,1,0:T(8,128)(2,1)S(1)}, bf16[3,128,128]{2,1,0:T(8,128)(2,1)S(1)}, u32[]{:S(2)}, u32[]{:S(2)}) collective-permute-start(bf16[3,128,128]{2,1,0:T(8,128)(2,1)S(1)} %fusion.7), channel_id=1, source_target_pairs={{0,8},{4,12},{8,0},{12,4},{1,9},{5,13},{9,1},{13,5},{2,10},{6,14},... | collective-permute-start | bytes 294920 | tf_op jit(solution)/shard_map/ppermute | solution.py:22
  41.1 26.7 %copy-start.6 = (bf16[3,128,128]{2,1,0:T(8,128)(2,1)}, bf16[3,128,128]{2,1,0:T(8,128)(2,1)S(1)}, u32[]{:S(2)}) copy-start(bf16[3,128,128]{2,1,0:T(8,128)(2,1)S(1)} %collective-permute-done.6.refs_1_) | copy-start | bytes 294916
  41.1 26.1 %collective-permute-start.8 = (bf16[3,128,128]{2,1,0:T(8,128)(2,1)S(1)}, bf16[3,128,128]{2,1,0:T(8,128)(2,1)S(1)}, u32[]{:S(2)}, u32[]{:S(2)}) collective-permute-start(bf16[3,128,128]{2,1,0:T(8,128)(2,1)S(1)} %fusion.8), channel_id=1, source_target_pairs={{0,12},{4,8},{8,4},{12,0},{1,13},{5,9},{9,5},{13,1},{2,14},{6,10},... | collective-permute-start | bytes 294920 | tf_op jit(solution)/shard_map/ppermute | solution.py:22
  67.2 0.6 copy-start.7
  67.2 0.7 copy-start.8
  67.9 22.1 %copy-start.2 = (bf16[1024,128]{1,0:T(8,128)(2,1)S(1)}, bf16[1024,128]{1,0:T(8,128)(2,1)}, u32[]{:S(2)}) copy-start(bf16[1024,128]{1,0:T(8,128)(2,1)} %get-tuple-element.9) | copy-start | bytes 786436
  73.2 18.5 %collective-permute-start.15 = (bf16[256,128]{1,0:T(8,128)(2,1)}, bf16[256,128]{1,0:T(8,128)(2,1)S(1)}, u32[]{:S(2)}, u32[]{:S(2)}) collective-permute-start(bf16[256,128]{1,0:T(8,128)(2,1)} %get-tuple-element.7), channel_id=1, source_target_pairs={{0,4},{4,0},{8,12},{12,8},{1,5},{5,1},{9,13},{13,9},{2,6},{6,2},{1... | collective-permute-start | bytes 196616 | tf_op jit(solution)/shard_map/ppermute | solution.py:22
  75.4 16.3 %collective-permute-start.16 = (bf16[256,128]{1,0:T(8,128)(2,1)}, bf16[256,128]{1,0:T(8,128)(2,1)S(1)}, u32[]{:S(2)}, u32[]{:S(2)}) collective-permute-start(bf16[256,128]{1,0:T(8,128)(2,1)} %get-tuple-element.7), channel_id=1, source_target_pairs={{0,8},{4,12},{8,0},{12,4},{1,9},{5,13},{9,1},{13,5},{2,10},{6,14},... | collective-permute-start | bytes 196616 | tf_op jit(solution)/shard_map/ppermute | solution.py:22
  76.7 15.0 %collective-permute-start.17 = (bf16[256,128]{1,0:T(8,128)(2,1)}, bf16[256,128]{1,0:T(8,128)(2,1)S(1)}, u32[]{:S(2)}, u32[]{:S(2)}) collective-permute-start(bf16[256,128]{1,0:T(8,128)(2,1)} %get-tuple-element.7), channel_id=1, source_target_pairs={{0,12},{4,8},{8,4},{12,0},{1,13},{5,9},{9,5},{13,1},{2,14},{6,10},... | collective-permute-start | bytes 196616 | tf_op jit(solution)/shard_map/ppermute | solution.py:22
  78.1 5.6 %collective-permute-start.19 = (bf16[256,128]{1,0:T(8,128)(2,1)}, bf16[256,128]{1,0:T(8,128)(2,1)S(1)}, u32[]{:S(2)}, u32[]{:S(2)}) collective-permute-start(bf16[256,128]{1,0:T(8,128)(2,1)} %get-tuple-element.8), channel_id=1, source_target_pairs={{0,4},{4,0},{8,12},{12,8},{1,5},{5,1},{9,13},{13,9},{2,6},{6,2},{1... | collective-permute-start | bytes 196616 | tf_op jit(solution)/shard_map/ppermute | solution.py:22
  78.9 9.4 %collective-permute-start.20 = (bf16[256,128]{1,0:T(8,128)(2,1)}, bf16[256,128]{1,0:T(8,128)(2,1)S(1)}, u32[]{:S(2)}, u32[]{:S(2)}) collective-permute-start(bf16[256,128]{1,0:T(8,128)(2,1)} %get-tuple-element.8), channel_id=1, source_target_pairs={{0,8},{4,12},{8,0},{12,4},{1,9},{5,13},{9,1},{13,5},{2,10},{6,14},... | collective-permute-start | bytes 196616 | tf_op jit(solution)/shard_map/ppermute | solution.py:22
  83.6 6.3 %collective-permute-start.21 = (bf16[256,128]{1,0:T(8,128)(2,1)}, bf16[256,128]{1,0:T(8,128)(2,1)S(1)}, u32[]{:S(2)}, u32[]{:S(2)}) collective-permute-start(bf16[256,128]{1,0:T(8,128)(2,1)} %get-tuple-element.8), channel_id=1, source_target_pairs={{0,12},{4,8},{8,4},{12,0},{1,13},{5,9},{9,5},{13,1},{2,14},{6,10},... | collective-permute-start | bytes 196616 | tf_op jit(solution)/shard_map/ppermute | solution.py:22
  89.9 1.9 %copy-start.3 = (bf16[1024,128]{1,0:T(8,128)(2,1)S(1)}, bf16[1024,128]{1,0:T(8,128)(2,1)}, u32[]{:S(2)}) copy-start(bf16[1024,128]{1,0:T(8,128)(2,1)} %get-tuple-element.10) | copy-start | bytes 786436
  89.9 1.9 %copy-start.4 = (bf16[1024,128]{1,0:T(8,128)(2,1)S(1)}, bf16[1024,128]{1,0:T(8,128)(2,1)}, u32[]{:S(2)}) copy-start(bf16[1024,128]{1,0:T(8,128)(2,1)} %get-tuple-element.11) | copy-start | bytes 786436
  90.0 1.9 %copy-start.5 = (bf16[1024,128]{1,0:T(8,128)(2,1)S(1)}, bf16[1024,128]{1,0:T(8,128)(2,1)}, u32[]{:S(2)}) copy-start(bf16[1024,128]{1,0:T(8,128)(2,1)} %get-tuple-element.12) | copy-start | bytes 786436
  91.6 1.6 %collective-permute-start.22 = (bf16[128,1024]{1,0:T(8,128)(2,1)S(1)}, bf16[128,1024]{1,0:T(8,128)(2,1)S(1)}, u32[]{:S(2)}, u32[]{:S(2)}) collective-permute-start(bf16[128,1024]{1,0:T(8,128)(2,1)S(1)} %convolution_convert_fusion.3), channel_id=1, source_target_pairs={{0,1},{1,0},{2,3},{3,2},{4,5},{5,4},{6,7},{7,6},{8,9},{9,8},{10,11... | collective-permute-start | bytes 786440 | tf_op jit(solution)/shard_map/ppermute | solution.py:22
  92.3 3.1 %collective-permute-start.18 = (bf16[128,1024]{1,0:T(8,128)(2,1)S(1)}, bf16[128,1024]{1,0:T(8,128)(2,1)S(1)}, u32[]{:S(2)}, u32[]{:S(2)}) collective-permute-start(bf16[128,1024]{1,0:T(8,128)(2,1)S(1)} %convolution_convert_fusion.4), channel_id=1, source_target_pairs={{0,1},{1,0},{2,3},{3,2},{4,5},{5,4},{6,7},{7,6},{8,9},{9,8},{10,11... | collective-permute-start | bytes 786440 | tf_op jit(solution)/shard_map/ppermute | solution.py:22
  93.7 8.4 %collective-permute-start.23 = (bf16[128,1024]{1,0:T(8,128)(2,1)S(1)}, bf16[128,1024]{1,0:T(8,128)(2,1)S(1)}, u32[]{:S(2)}, u32[]{:S(2)}) collective-permute-start(bf16[128,1024]{1,0:T(8,128)(2,1)S(1)} %fusion.2), channel_id=1, source_target_pairs={{0,2},{1,3},{2,0},{3,1},{4,6},{5,7},{6,4},{7,5},{8,10},{9,11},{10,... | collective-permute-start | bytes 786440 | tf_op jit(solution)/shard_map/ppermute | solution.py:22
  102.6 14.9 %copy-start.1 = (f32[128,1024]{1,0:T(8,128)S(1)}, f32[128,1024]{1,0:T(8,128)}, u32[]{:S(2)}) copy-start(f32[128,1024]{1,0:T(8,128)} %param.10) | copy-start | bytes 1572868
  102.7 4.5 %collective-permute-start.24 = (bf16[32,1024]{1,0:T(8,128)(2,1)S(1)}, bf16[32,1024]{1,0:T(8,128)(2,1)S(1)}, u32[]{:S(2)}, u32[]{:S(2)}) collective-permute-start(bf16[32,1024]{1,0:T(8,128)(2,1)S(1)} %get-tuple-element.28), channel_id=1, source_target_pairs={{0,4},{4,0},{8,12},{12,8},{1,5},{5,1},{9,13},{13,9},{2,6},{6,2},{1... | collective-permute-start | bytes 196616 | tf_op jit(solution)/shard_map/ppermute | solution.py:22
  102.7 5.8 %collective-permute-start.25 = (bf16[32,1024]{1,0:T(8,128)(2,1)S(1)}, bf16[32,1024]{1,0:T(8,128)(2,1)S(1)}, u32[]{:S(2)}, u32[]{:S(2)}) collective-permute-start(bf16[32,1024]{1,0:T(8,128)(2,1)S(1)} %get-tuple-element.27), channel_id=1, source_target_pairs={{0,8},{4,12},{8,0},{12,4},{1,9},{5,13},{9,1},{13,5},{2,10},{6,14},... | collective-permute-start | bytes 196616 | tf_op jit(solution)/shard_map/ppermute | solution.py:22
  105.3 6.1 %collective-permute-start.26 = (bf16[32,1024]{1,0:T(8,128)(2,1)S(1)}, bf16[32,1024]{1,0:T(8,128)(2,1)S(1)}, u32[]{:S(2)}, u32[]{:S(2)}) collective-permute-start(bf16[32,1024]{1,0:T(8,128)(2,1)S(1)} %get-tuple-element.26), channel_id=1, source_target_pairs={{0,12},{4,8},{8,4},{12,0},{1,13},{5,9},{9,5},{13,1},{2,14},{6,10},... | collective-permute-start | bytes 196616 | tf_op jit(solution)/shard_map/ppermute | solution.py:22
  111.5 1.9 %collective-permute-start.27 = (bf16[32,1024]{1,0:T(8,128)(2,1)S(1)}, bf16[32,1024]{1,0:T(8,128)(2,1)S(1)}, u32[]{:S(2)}, u32[]{:S(2)}) collective-permute-start(bf16[32,1024]{1,0:T(8,128)(2,1)S(1)} %get-tuple-element.20), channel_id=1, source_target_pairs={{0,1},{1,0},{2,3},{3,2},{4,5},{5,4},{6,7},{7,6},{8,9},{9,8},{10,11... | collective-permute-start | bytes 196616 | tf_op jit(solution)/shard_map/ppermute | solution.py:22
  111.6 4.5 %collective-permute-start.28 = (bf16[32,1024]{1,0:T(8,128)(2,1)S(1)}, bf16[32,1024]{1,0:T(8,128)(2,1)S(1)}, u32[]{:S(2)}, u32[]{:S(2)}) collective-permute-start(bf16[32,1024]{1,0:T(8,128)(2,1)S(1)} %get-tuple-element.19), channel_id=1, source_target_pairs={{0,2},{1,3},{2,0},{3,1},{4,6},{5,7},{6,4},{7,5},{8,10},{9,11},{10,... | collective-permute-start | bytes 196616 | tf_op jit(solution)/shard_map/ppermute | solution.py:22
  113.3 4.1 %collective-permute-start.29 = (bf16[32,1024]{1,0:T(8,128)(2,1)S(1)}, bf16[32,1024]{1,0:T(8,128)(2,1)S(1)}, u32[]{:S(2)}, u32[]{:S(2)}) collective-permute-start(bf16[32,1024]{1,0:T(8,128)(2,1)S(1)} %get-tuple-element.18), channel_id=1, source_target_pairs={{0,3},{1,2},{2,1},{3,0},{4,7},{5,6},{6,5},{7,4},{8,11},{9,10},{10,... | collective-permute-start | bytes 196616 | tf_op jit(solution)/shard_map/ppermute | solution.py:22
where the time goes:
time: 119 us; the launch traced here: 118 us
  waiting for transfers between devices  50.8 us (43%)
  starting transfers between devices  38 us (32%)
  matrix products  11.9 us (10%)
  Pallas kernels  8.42 us (7%)
  local copies, waits for them, and re-layouts  6.09 us (5%)
  other arithmetic  2.68 us (2%)
    ppermute x30, waiting for transfers between devices, hop(): return lax.ppermute(value, axis, [(a, a ^ mask) for a in range(count)])  50.8 us
    ppermute x30, starting transfers between devices, hop(): return lax.ppermute(value, axis, [(a, a ^ mask) for a in range(count)])  38 us
    dot_general x8, matrix products, product(): jnp.einsum(form, rows, weight_of(mask), preferred_element_type=jnp.float32)  8.83 us
    pallas_call x1, Pallas kernels, local_stage(): pl.pallas_call(functools.partial(local_kernel, groups, seq, sub), out_sha...  5.32 us
    pallas_call x1, Pallas kernels, local_stage(): spectrum = make_spectrum(*wide[:2], long_filter)  3.11 us
    dot_general x4, matrix products, shards(): jnp.einsum('rc,nc->rn', got[place * seq * sub:(place + 1) * seq * sub], o...  3.08 us
  transfers between devices with their start and end apart: 30, of which 16 were waited for; matrix products, arithmetic and copies ran while one was open for 13% of the time, Pallas kernels for 3%

commit v1 on v0

--- a/solution.py
+++ b/solution.py
@@ -58,8 +58,20 @@
         form = "rd,sdc->scr" if narrow else "rd,sdc->src"
         return jnp.einsum(form, rows, weight_of(mask), preferred_element_type=jnp.float32)
 
-    sent = {mask: product(mask).astype(jnp.bfloat16) for mask in range(1, count)}
-    came = [hop(sent[mask], "seq", mask) for mask in sent]
+    low = jnp.bfloat16
+    if count != 4:
+        sent = {mask: product(mask).astype(low) for mask in range(1, count)}
+        came = [hop(sent[mask], "seq", mask) for mask in sent]
+    else:
+        crossing = product(3).astype(low)
+        relayed = lax.ppermute(crossing, "seq", [(0, 1), (3, 2)])
+        middle = lax.ppermute(crossing, "seq", [(1, 2), (2, 1)])
+        skipped = lax.ppermute(product(2).astype(low), "seq", [(0, 2), (3, 1)])
+        near = hop(product(1).astype(low), "seq", 1)
+        rows, relayed = lax.optimization_barrier((rows, relayed))
+        merged = (product(2) + relayed.astype(jnp.float32)).astype(low)
+        merged = lax.ppermute(merged, "seq", [(1, 3), (2, 0)])
+        came = [near, middle, skipped, merged]
     if narrow:
         return [term.transpose(0, 2, 1) for term in [product(0)] + came]
     return [product(0)] + came
@@ -130,8 +142,8 @@
     out_ref[...] = wide_dot(high_ref[...], low_ref[...], taps_ref[...], ((1,), (1,)))
 
 
-def local_kernel(groups, seq, sub, t_ref, taps_ref, *refs):
-    count = seq * len(groups)
+def local_kernel(groups, each, seq, sub, t_ref, taps_ref, *refs):
+    count = each * len(groups)
     moved = count + 5
     sources, outs = refs[:moved], refs[moved : moved + 2]
     proj, gated, sems = refs[moved + 2 : moved + 5]
@@ -151,8 +163,8 @@
 
     proj[:, :8] = jnp.zeros((proj.shape[0], 8, proj.shape[2]), jnp.float32)
     for group, slots in enumerate(groups):
-        mine = terms[group * seq : (group + 1) * seq]
-        for copy in copies[group * seq : (group + 1) * seq]:
+        mine = terms[group * each : (group + 1) * each]
+        for copy in copies[group * each : (group + 1) * each]:
             copy.wait()
         for position, slot in enumerate(slots):
             for source in range(seq):
@@ -202,7 +214,7 @@
     lines = length // 2
     moved = [*flat, *wide[:2], spectrum, *wide[2:]]
     return pl.pallas_call(
-        functools.partial(local_kernel, groups, seq, sub),
+        functools.partial(local_kernel, groups, len(terms[0]), seq, sub),
         out_shape=[jax.ShapeDtypeStruct((lines, own), jnp.bfloat16)] * 2,
         in_specs=[pl.BlockSpec(memory_space=pltpu.SMEM), vmem] + [pl.BlockSpec(memory_space=pl.ANY)] * len(moved),
         out_specs=[vmem] * 2,

time: 119 us -> 120 us (level)
  starting transfers between devices: 38 us -> 48.5 us
  waiting for transfers between devices: 50.8 us -> 42.1 us
  matrix products: 11.9 us -> 9.16 us
    ppermute x30 -> x26, waiting for transfers between devices: 50.8 us -> 22.9 us  [hop(): return lax.ppermute(value, axis, [(a, a ^ mask) for a in range(count)])]
    ppermute x0 -> x8, waiting for transfers between devices: none -> 19.2 us  [the longest x2 14.3 us: sum_over_seq(): merged = lax.ppermute(merged, 'seq', [(1, 3), (2, 0)])]
    ppermute x0 -> x8, starting transfers between devices: none -> 14.5 us  [the longest x2 6.52 us: sum_over_seq(): skipped = lax.ppermute(product(2).astype(low), 'seq', [(0, 2), (3, 1)])]
    ppermute x30 -> x26, starting transfers between devices: 38 us -> 34 us  [hop(): return lax.ppermute(value, axis, [(a, a ^ mask) for a in range(count)])]
    dot_general x8 -> x10, matrix products: 8.83 us -> 5.98 us  [product(): jnp.einsum(form, rows, weight_of(mask), preferred_element_type=jnp.float32)]
    unnamed x25 -> x37, local copies, waits for them, and re-layouts: 1.65 us -> 2.61 us
  transfers between devices with their start and end apart: 30 -> 34, of which waited for: 16 -> 17; matrix products, arithmetic and copies ran while one was open for 13% -> 11% of each run, Pallas kernels for 3% -> 3%
where the time goes in v1:
time: 120 us
  starting transfers between devices  48.5 us (40%)
  waiting for transfers between devices  42.1 us (35%)
  matrix products  9.16 us (8%)
  Pallas kernels  8.53 us (7%)
  local copies, waits for them, and re-layouts  7.1 us (6%)
  other arithmetic  3.52 us (3%)
    ppermute x26, starting transfers between devices, hop(): return lax.ppermute(value, axis, [(a, a ^ mask) for a in range(count)])  34 us
    ppermute x26, waiting for transfers between devices, hop(): return lax.ppermute(value, axis, [(a, a ^ mask) for a in range(count)])  22.9 us
    ppermute x2, waiting for transfers between devices, sum_over_seq(): merged = lax.ppermute(merged, 'seq', [(1, 3), (2, 0)])  14.3 us
    ppermute x2, starting transfers between devices, sum_over_seq(): skipped = lax.ppermute(product(2).astype(low), 'seq', [(0, 2), (3, 1)])  6.52 us
    dot_general x10, matrix products, product(): jnp.einsum(form, rows, weight_of(mask), preferred_element_type=jnp.float32)  5.98 us
    pallas_call x1, Pallas kernels, local_stage(): pl.pallas_call(functools.partial(local_kernel, groups, len(terms[0]), seq...  5.42 us
    ppermute x2, waiting for transfers between devices, sum_over_seq(): relayed = lax.ppermute(crossing, 'seq', [(0, 1), (3, 2)])  4.93 us
    ppermute x2, starting transfers between devices, sum_over_seq(): relayed = lax.ppermute(crossing, 'seq', [(0, 1), (3, 2)])  4.1 us
  transfers between devices with their start and end apart: 34, of which 17 were waited for; matrix products, arithmetic and copies ran while one was open for 11% of the time, Pallas kernels for 3%

profile of v1, /device:TPU:0, one launch (start us, length us, event | category | flops | bytes accessed | tf_op | source)
XLA Modules:
  0.0 119.6 jit_solution(8847108930278621199)
XLA Ops:
  0.0 1.2 %convert_element_type.89 = bf16[128,1024]{1,0:T(8,128)(2,1)S(1)} convert(f32[128,1024]{1,0:T(8,128)} %param.10) | non-fusion elementwise | flops 131072 | bytes 786432 | tf_op jit(solution)/shard_map/convert_element_type | solution.py:269
  1.3 0.7 constant_dynamic-slice_fusion.23
  2.0 0.5 collective-permute-start
  2.4 2.5 %collective-permute-start.1 = (bf16[32,1024]{1,0:T(8,128)(2,1)}, bf16[32,1024]{1,0:T(8,128)(2,1)S(1)}, u32[]{:S(2)}, u32[]{:S(2)}) collective-permute-start(bf16[32,1024]{1,0:T(8,128)(2,1)} %get-tuple-element.51), channel_id=1, source_target_pairs={{0,2},{1,3},{2,0},{3,1},{4,6},{5,7},{6,4},{7,5},{8,10},{9,11},{10,... | collective-permute-start | bytes 196616 | tf_op jit(solution)/shard_map/ppermute | solution.py:22
  5.0 2.2 %constant_dynamic-slice_fusion.13 = (bf16[1024,128]{1,0:T(8,128)(2,1)}, bf16[1024,128]{1,0:T(8,128)(2,1)}, bf16[1024,128]{1,0:T(8,128)(2,1)}, bf16[1024,128]{1,0:T(8,128)(2,1)}) fusion(bf16[1024,512]{1,0:T(8,128)(2,1)} %param.15, s32[]{:T(128)S(6)} %select_n.72, s32[]{:T(128)S(6)} %select_n.82, s32[]{:T(128)S(6)} %select_n.81, s32[]{:T(128)S(6)} %select_n.83), kind=kLoop, calls=%fused_computation.105 | loop fusion | bytes 2097168 | tf_op jit(solution)/shard_map/dynamic_slice | solution.py:274
  7.3 0.6 collective-permute-done.1
  7.9 1.0 collective-permute-done.2
  9.3 3.1 %collective-permute-start.4 = (bf16[32,1024]{1,0:T(8,128)(2,1)S(1)}, bf16[32,1024]{1,0:T(8,128)(2,1)S(1)}, u32[]{:S(2)}, u32[]{:S(2)}) collective-permute-start(bf16[32,1024]{1,0:T(8,128)(2,1)S(1)} %get-tuple-element.43), channel_id=1, source_target_pairs={{0,8},{4,12},{8,0},{12,4},{1,9},{5,13},{9,1},{13,5},{2,10},{6,14},... | collective-permute-start | bytes 196616 | tf_op jit(solution)/shard_map/ppermute | solution.py:22
  12.4 1.3 %collective-permute-start.5 = (bf16[32,1024]{1,0:T(8,128)(2,1)S(1)}, bf16[32,1024]{1,0:T(8,128)(2,1)S(1)}, u32[]{:S(2)}, u32[]{:S(2)}) collective-permute-start(bf16[32,1024]{1,0:T(8,128)(2,1)S(1)} %get-tuple-element.42), channel_id=1, source_target_pairs={{0,12},{4,8},{8,4},{12,0},{1,13},{5,9},{9,5},{13,1},{2,14},{6,10},... | collective-permute-start | bytes 196616 | tf_op jit(solution)/shard_map/ppermute | solution.py:22
  14.0 1.3 %constant_dynamic-slice_fusion.24.taps_ref = f32[3,3,128]{2,1,0:T(4,128)} fusion(f32[3,3,512]{2,1,0:T(4,128)} %param.13, s32[]{:T(128)S(6)} %select_n.72), kind=kLoop, calls=%fused_computation.120 | loop fusion | bytes 9220 | tf_op jit(solution)/shard_map/dynamic_slice | solution.py:276
  15.3 3.1 %filter_spectrum.1.refs_12_ = f32[1024,128]{1,0:T(8,128)} custom-call(bf16[1024,512]{1,0:T(8,128)(2,1)} %constant.101.clone.high_ref.refs_10_, bf16[1024,512]{1,0:T(8,128)(2,1)} %constant.102.clone.low_ref.refs_11_, f32[128,512]{1,0:T(8,128)} %taps_ref.1), custom_call_target="tpu_custom_call" | custom-call | flops 402653184 | bytes 1048576 | tf_op jit(solution)/shard_map/filter_spectrum/pallas_call | solution.py:212
  18.4 0.4 collective-permute-done.5
  19.0 0.9 pad_maximum_fusion.3
  20.1 1.6 %collective-permute-start.12 = (bf16[128,1024]{1,0:T(8,128)(2,1)S(1)}, bf16[128,1024]{1,0:T(8,128)(2,1)S(1)}, u32[]{:S(2)}, u32[]{:S(2)}) collective-permute-start(bf16[128,1024]{1,0:T(8,128)(2,1)S(1)} %bitcast.94), channel_id=1, source_target_pairs={{0,2},{1,3},{2,0},{3,1},{4,6},{5,7},{6,4},{7,5},{8,10},{9,11},{10,... | collective-permute-start | bytes 786440 | tf_op jit(solution)/shard_map/ppermute | solution.py:22
  22.0 0.3 fusion.11
  22.3 2.8 %collective-permute-start.6 = (bf16[3,128,128]{2,1,0:T(8,128)(2,1)S(1)}, bf16[3,128,128]{2,1,0:T(8,128)(2,1)S(1)}, u32[]{:S(2)}, u32[]{:S(2)}) collective-permute-start(bf16[3,128,128]{2,1,0:T(8,128)(2,1)S(1)} %fusion.10), channel_id=1, source_target_pairs={{0,4},{12,8},{1,5},{13,9},{2,6},{14,10},{3,7},{15,11},{16,20},{28,... | collective-permute-start | bytes 294920 | tf_op jit(solution)/shard_map/ppermute | solution.py:67
  25.1 0.3 fusion.12
  25.4 0.7 collective-permute-start.8
  26.1 2.9 %collective-permute-start.7 = (bf16[3,128,128]{2,1,0:T(8,128)(2,1)S(1)}, bf16[3,128,128]{2,1,0:T(8,128)(2,1)S(1)}, u32[]{:S(2)}, u32[]{:S(2)}) collective-permute-start(bf16[3,128,128]{2,1,0:T(8,128)(2,1)S(1)} %fusion.11), channel_id=1, source_target_pairs={{0,4},{4,0},{8,12},{12,8},{1,5},{5,1},{9,13},{13,9},{2,6},{6,2},{1... | collective-permute-start | bytes 294920 | tf_op jit(solution)/shard_map/ppermute | solution.py:22
  29.0 4.9 %collective-permute-start.9 = (bf16[3,128,128]{2,1,0:T(8,128)(2,1)S(1)}, bf16[3,128,128]{2,1,0:T(8,128)(2,1)S(1)}, u32[]{:S(2)}, u32[]{:S(2)}) collective-permute-start(bf16[3,128,128]{2,1,0:T(8,128)(2,1)S(1)} %fusion.12), channel_id=1, source_target_pairs={{0,8},{12,4},{1,9},{13,5},{2,10},{14,6},{3,11},{15,7},{16,24},{28,... | collective-permute-start | bytes 294920 | tf_op jit(solution)/shard_map/ppermute | solution.py:69
  34.0 1.0 convolution_bitcast_fusion.3.refs_0_
  35.0 0.5 collective-permute-done.13
  35.5 0.6 fusion.5
  36.1 1.3 %collective-permute-start.14 = (bf16[3,384,128]{2,1,0:T(8,128)(2,1)S(1)}, bf16[3,384,128]{2,1,0:T(8,128)(2,1)S(1)}, u32[]{:S(2)}, u32[]{:S(2)}) collective-permute-start(bf16[3,384,128]{2,1,0:T(8,128)(2,1)S(1)} %fusion.5), channel_id=1, source_target_pairs={{0,4},{12,8},{1,5},{13,9},{2,6},{14,10},{3,7},{15,11},{16,20},{28,... | collective-permute-start | bytes 884744 | tf_op jit(solution)/shard_map/ppermute | solution.py:67
  37.4 0.6 fusion.6
  38.0 0.7 collective-permute-start.16
  38.7 0.6 fusion.7
  39.3 4.9 %collective-permute-done.14 = bf16[3,384,128]{2,1,0:T(8,128)(2,1)S(1)} collective-permute-done((bf16[3,384,128]{2,1,0:T(8,128)(2,1)S(1)}, bf16[3,384,128]{2,1,0:T(8,128)(2,1)S(1)}, u32[]{:S(2)}, u32[]{:S(2)}) %collective-permute-start.14) | collective-permute-done | bytes 294944 | tf_op jit(solution)/shard_map/ppermute | solution.py:67
  44.2 2.5 %collective-permute-start.15 = (bf16[3,384,128]{2,1,0:T(8,128)(2,1)S(1)}, bf16[3,384,128]{2,1,0:T(8,128)(2,1)S(1)}, u32[]{:S(2)}, u32[]{:S(2)}) collective-permute-start(bf16[3,384,128]{2,1,0:T(8,128)(2,1)S(1)} %fusion.6), channel_id=1, source_target_pairs={{0,4},{4,0},{8,12},{12,8},{1,5},{5,1},{9,13},{13,9},{2,6},{6,2},{1... | collective-permute-start | bytes 884744 | tf_op jit(solution)/shard_map/ppermute | solution.py:22
  46.7 0.6 fusion.2
  47.3 1.6 %collective-permute-start.17 = (bf16[3,384,128]{2,1,0:T(8,128)(2,1)S(1)}, bf16[3,384,128]{2,1,0:T(8,128)(2,1)S(1)}, u32[]{:S(2)}, u32[]{:S(2)}) collective-permute-start(bf16[3,384,128]{2,1,0:T(8,128)(2,1)S(1)} %fusion.7), channel_id=1, source_target_pairs={{0,8},{12,4},{1,9},{13,5},{2,10},{14,6},{3,11},{15,7},{16,24},{28,... | collective-permute-start | bytes 884744 | tf_op jit(solution)/shard_map/ppermute | solution.py:69
  49.0 1.3 %collective-permute-start.18 = (bf16[3,384,128]{2,1,0:T(8,128)(2,1)S(1)}, bf16[3,384,128]{2,1,0:T(8,128)(2,1)S(1)}, u32[]{:S(2)}, u32[]{:S(2)}) collective-permute-start(bf16[3,384,128]{2,1,0:T(8,128)(2,1)S(1)} %fusion.2), channel_id=1, source_target_pairs={{4,12},{8,0},{5,13},{9,1},{6,14},{10,2},{7,15},{11,3},{20,28},{24,... | collective-permute-start | bytes 884744 | tf_op jit(solution)/shard_map/ppermute | solution.py:73
  50.3 0.3 fusion.9
  50.6 1.3 %collective-permute-start.10 = (bf16[3,128,128]{2,1,0:T(8,128)(2,1)S(1)}, bf16[3,128,128]{2,1,0:T(8,128)(2,1)S(1)}, u32[]{:S(2)}, u32[]{:S(2)}) collective-permute-start(bf16[3,128,128]{2,1,0:T(8,128)(2,1)S(1)} %fusion.9), channel_id=1, source_target_pairs={{4,12},{8,0},{5,13},{9,1},{6,14},{10,2},{7,15},{11,3},{20,28},{24,... | collective-permute-start | bytes 294920 | tf_op jit(solution)/shard_map/ppermute | solution.py:73
  51.9 1.4 %convolution_bitcast_fusion.1.refs_5_ = f32[3,384,128]{2,1,0:T(8,128)} fusion(bf16[384,1024]{1,0:T(8,128)(2,1)S(1)} %constant_dynamic-update-slice_fusion, bf16[3,1024,512]{2,1,0:T(8,128)(2,1)S(1)} %copy-done, s32[]{:T(128)S(6)} %select_n.72), kind=kOutput, calls=%fused_computation.2 | convolution fusion | flops 301989888 | bytes 2162692 | tf_op jit(solution)/shard_map/rd,sdc->src/dot_general | solution.py:59
  53.4 14.3 %collective-permute-done.10.refs_4_ = bf16[3,128,128]{2,1,0:T(8,128)(2,1)S(1)} collective-permute-done((bf16[3,128,128]{2,1,0:T(8,128)(2,1)S(1)}, bf16[3,128,128]{2,1,0:T(8,128)(2,1)S(1)}, u32[]{:S(2)}, u32[]{:S(2)}) %collective-permute-start.10) | collective-permute-done | bytes 98336 | tf_op jit(solution)/shard_map/ppermute | solution.py:73
  67.7 0.7 copy-done.3
  68.5 0.7 copy-done.5
  69.3 5.4 %filters.1 = (bf16[256,128]{1,0:T(8,128)(2,1)}, bf16[256,128]{1,0:T(8,128)(2,1)}) custom-call(s32[1]{0:T(128)} %bitcast.t_ref, f32[3,3,128]{2,1,0:T(4,128)} %constant_dynamic-slice_fusion.24.taps_ref, f32[3,128,128]{2,1,0:T(8,128)} %convolution_bitcast_fusion.3.refs_0_, bf16[3,128,128]{2,1,0:T(8,128)(2,1)} %copy-done.11, bf16[3,128,128]{2,1,0:T(8,128)(2,1)} %copy-done.10, ...), custom_call_target="tpu_custom_call" | custom-call | flops 805306368 | bytes 2097152 | tf_op jit(solution)/shard_map/filters/pallas_call | solution.py:216
  75.0 3.4 %collective-permute-start.20 = (bf16[256,128]{1,0:T(8,128)(2,1)}, bf16[256,128]{1,0:T(8,128)(2,1)S(1)}, u32[]{:S(2)}, u32[]{:S(2)}) collective-permute-start(bf16[256,128]{1,0:T(8,128)(2,1)} %get-tuple-element.15), channel_id=1, source_target_pairs={{0,8},{4,12},{8,0},{12,4},{1,9},{5,13},{9,1},{13,5},{2,10},{6,14},... | collective-permute-start | bytes 196616 | tf_op jit(solution)/shard_map/ppermute | solution.py:22
  78.4 0.8 collective-permute-start.21
  79.1 3.6 %collective-permute-start.24 = (bf16[256,128]{1,0:T(8,128)(2,1)}, bf16[256,128]{1,0:T(8,128)(2,1)S(1)}, u32[]{:S(2)}, u32[]{:S(2)}) collective-permute-start(bf16[256,128]{1,0:T(8,128)(2,1)} %get-tuple-element.16), channel_id=1, source_target_pairs={{0,8},{4,12},{8,0},{12,4},{1,9},{5,13},{9,1},{13,5},{2,10},{6,14},... | collective-permute-start | bytes 196616 | tf_op jit(solution)/shard_map/ppermute | solution.py:22
  82.8 0.9 constant_dynamic-update-slice_fusion.6
  83.7 3.4 %collective-permute-start.25 = (bf16[256,128]{1,0:T(8,128)(2,1)}, bf16[256,128]{1,0:T(8,128)(2,1)S(1)}, u32[]{:S(2)}, u32[]{:S(2)}) collective-permute-start(bf16[256,128]{1,0:T(8,128)(2,1)} %get-tuple-element.16), channel_id=1, source_target_pairs={{0,12},{4,8},{8,4},{12,0},{1,13},{5,9},{9,5},{13,1},{2,14},{6,10},... | collective-permute-start | bytes 196616 | tf_op jit(solution)/shard_map/ppermute | solution.py:22
  87.2 1.1 collective-permute-done.24
  88.3 1.7 %collective-permute-done.25 = bf16[256,128]{1,0:T(8,128)(2,1)S(1)} collective-permute-done((bf16[256,128]{1,0:T(8,128)(2,1)}, bf16[256,128]{1,0:T(8,128)(2,1)S(1)}, u32[]{:S(2)}, u32[]{:S(2)}) %collective-permute-start.25) | collective-permute-done | bytes 65568 | tf_op jit(solution)/shard_map/ppermute | solution.py:22
  90.1 1.7 %convolution_convert_fusion.3 = bf16[128,1024]{1,0:T(8,128)(2,1)S(1)} fusion(bf16[256,512]{1,0:T(8,128)(2,1)S(1)} %constant_dynamic-update-slice_fusion.7, bf16[1024,128]{1,0:T(8,128)(2,1)} %get-tuple-element.19, bf16[1024,128]{1,0:T(8,128)(2,1)} %get-tuple-element.20, bf16[1024,128]{1,0:T(8,128)(2,1)} %get-tuple-element.18, ...), kind=kOutput, calls=%fused_computation.12 | convolution fusion | flops 138543104 | bytes 1441792 | tf_op jit(solution)/shard_map/rc,nc->rn/dot_general | solution.py:301
  92.1 0.5 convolution_convert_fusion.4
  92.5 0.6 collective-permute-start.22
  93.1 0.3 collective-permute-done.26
  93.4 0.5 fusion.4
  93.9 0.7 collective-permute-start.27
  94.6 7.7 %collective-permute-done.27 = bf16[128,1024]{1,0:T(8,128)(2,1)S(1)} collective-permute-done((bf16[128,1024]{1,0:T(8,128)(2,1)S(1)}, bf16[128,1024]{1,0:T(8,128)(2,1)S(1)}, u32[]{:S(2)}, u32[]{:S(2)}) %collective-permute-start.27) | collective-permute-done | bytes 262176 | tf_op jit(solution)/shard_map/ppermute | solution.py:22
  102.3 0.5 fusion.3
  102.9 3.9 %collective-permute-start.29 = (bf16[32,1024]{1,0:T(8,128)(2,1)S(1)}, bf16[32,1024]{1,0:T(8,128)(2,1)S(1)}, u32[]{:S(2)}, u32[]{:S(2)}) collective-permute-start(bf16[32,1024]{1,0:T(8,128)(2,1)S(1)} %get-tuple-element.35), channel_id=1, source_target_pairs={{0,8},{4,12},{8,0},{12,4},{1,9},{5,13},{9,1},{13,5},{2,10},{6,14},... | collective-permute-start | bytes 196616 | tf_op jit(solution)/shard_map/ppermute | solution.py:22
  106.9 0.4 collective-permute-start.30
  107.3 0.4 collective-permute-done.28
  107.7 3.2 %collective-permute-done.29 = bf16[32,1024]{1,0:T(8,128)(2,1)S(1)} collective-permute-done((bf16[32,1024]{1,0:T(8,128)(2,1)S(1)}, bf16[32,1024]{1,0:T(8,128)(2,1)S(1)}, u32[]{:S(2)}, u32[]{:S(2)}) %collective-permute-start.29) | collective-permute-done | bytes 65568 | tf_op jit(solution)/shard_map/ppermute | solution.py:22
  110.9 2.0 %collective-permute-done.30 = bf16[32,1024]{1,0:T(8,128)(2,1)S(1)} collective-permute-done((bf16[32,1024]{1,0:T(8,128)(2,1)S(1)}, bf16[32,1024]{1,0:T(8,128)(2,1)S(1)}, u32[]{:S(2)}, u32[]{:S(2)}) %collective-permute-start.30) | collective-permute-done | bytes 65568 | tf_op jit(solution)/shard_map/ppermute | solution.py:22
  113.2 0.7 collective-permute-start.32
  113.8 1.2 collective-permute-start.33
  115.0 3.2 %collective-permute-done.32 = bf16[32,1024]{1,0:T(8,128)(2,1)S(1)} collective-permute-done((bf16[32,1024]{1,0:T(8,128)(2,1)S(1)}, bf16[32,1024]{1,0:T(8,128)(2,1)S(1)}, u32[]{:S(2)}, u32[]{:S(2)}) %collective-permute-start.32) | collective-permute-done | bytes 65568 | tf_op jit(solution)/shard_map/ppermute | solution.py:22
  118.2 0.3 collective-permute-done.33
  118.7 0.9 convert_add_fusion
  (83 shorter events, 2.8 us)
Async XLA Ops:
  0.0 21.7 %copy-start = (bf16[3,1024,512]{2,1,0:T(8,128)(2,1)S(1)}, bf16[3,1024,512]{2,1,0:T(8,128)(2,1)}, u32[]{:S(2)}) copy-start(bf16[3,1024,512]{2,1,0:T(8,128)(2,1)} %param.12) | copy-start | bytes 9437188
  0.0 7.3 %copy-start.14 = (f32[4096]{0:T(1024)S(1)}, f32[4096]{0:T(1024)}, u32[]{:S(2)}) copy-start(f32[4096]{0:T(1024)} %param.11) | copy-start | bytes 49156
  2.0 5.4 %collective-permute-start = (bf16[32,1024]{1,0:T(8,128)(2,1)}, bf16[32,1024]{1,0:T(8,128)(2,1)S(1)}, u32[]{:S(2)}, u32[]{:S(2)}) collective-permute-start(bf16[32,1024]{1,0:T(8,128)(2,1)} %get-tuple-element.52), channel_id=1, source_target_pairs={{0,1},{1,0},{2,3},{3,2},{4,5},{5,4},{6,7},{7,6},{8,9},{9,8},{10,11... | collective-permute-start | bytes 196616 | tf_op jit(solution)/shard_map/ppermute | solution.py:22
  2.4 5.4 %collective-permute-start.1 = (bf16[32,1024]{1,0:T(8,128)(2,1)}, bf16[32,1024]{1,0:T(8,128)(2,1)S(1)}, u32[]{:S(2)}, u32[]{:S(2)}) collective-permute-start(bf16[32,1024]{1,0:T(8,128)(2,1)} %get-tuple-element.51), channel_id=1, source_target_pairs={{0,2},{1,3},{2,0},{3,1},{4,6},{5,7},{6,4},{7,5},{8,10},{9,11},{10,... | collective-permute-start | bytes 196616 | tf_op jit(solution)/shard_map/ppermute | solution.py:22
  4.9 4.0 %collective-permute-start.2 = (bf16[32,1024]{1,0:T(8,128)(2,1)S(1)}, bf16[32,1024]{1,0:T(8,128)(2,1)S(1)}, u32[]{:S(2)}, u32[]{:S(2)}) collective-permute-start(bf16[32,1024]{1,0:T(8,128)(2,1)S(1)} %get-tuple-element.50), channel_id=1, source_target_pairs={{0,3},{1,2},{2,1},{3,0},{4,7},{5,6},{6,5},{7,4},{8,11},{9,10},{10,... | collective-permute-start | bytes 196616 | tf_op jit(solution)/shard_map/ppermute | solution.py:22
  9.3 9.0 %collective-permute-start.4 = (bf16[32,1024]{1,0:T(8,128)(2,1)S(1)}, bf16[32,1024]{1,0:T(8,128)(2,1)S(1)}, u32[]{:S(2)}, u32[]{:S(2)}) collective-permute-start(bf16[32,1024]{1,0:T(8,128)(2,1)S(1)} %get-tuple-element.43), channel_id=1, source_target_pairs={{0,8},{4,12},{8,0},{12,4},{1,9},{5,13},{9,1},{13,5},{2,10},{6,14},... | collective-permute-start | bytes 196616 | tf_op jit(solution)/shard_map/ppermute | solution.py:22
  12.4 6.3 %collective-permute-start.5 = (bf16[32,1024]{1,0:T(8,128)(2,1)S(1)}, bf16[32,1024]{1,0:T(8,128)(2,1)S(1)}, u32[]{:S(2)}, u32[]{:S(2)}) collective-permute-start(bf16[32,1024]{1,0:T(8,128)(2,1)S(1)} %get-tuple-element.42), channel_id=1, source_target_pairs={{0,12},{4,8},{8,4},{12,0},{1,13},{5,9},{9,5},{13,1},{2,14},{6,10},... | collective-permute-start | bytes 196616 | tf_op jit(solution)/shard_map/ppermute | solution.py:22
  13.8 5.3 %collective-permute-start.3 = (bf16[32,1024]{1,0:T(8,128)(2,1)S(1)}, bf16[32,1024]{1,0:T(8,128)(2,1)}, u32[]{:S(2)}, u32[]{:S(2)}) collective-permute-start(bf16[32,1024]{1,0:T(8,128)(2,1)S(1)} %get-tuple-element.44), channel_id=1, source_target_pairs={{0,4},{4,0},{8,12},{12,8},{1,5},{5,1},{9,13},{13,9},{2,6},{6,2},{1... | collective-permute-start | bytes 196616 | tf_op jit(solution)/shard_map/ppermute | solution.py:22
  20.0 15.0 %collective-permute-start.11 = (bf16[128,1024]{1,0:T(8,128)(2,1)S(1)}, bf16[128,1024]{1,0:T(8,128)(2,1)S(1)}, u32[]{:S(2)}, u32[]{:S(2)}) collective-permute-start(bf16[128,1024]{1,0:T(8,128)(2,1)S(1)} %bitcast.93), channel_id=1, source_target_pairs={{0,1},{1,0},{2,3},{3,2},{4,5},{5,4},{6,7},{7,6},{8,9},{9,8},{10,11... | collective-permute-start | bytes 786440 | tf_op jit(solution)/shard_map/ppermute | solution.py:22
  20.1 13.8 %collective-permute-start.12 = (bf16[128,1024]{1,0:T(8,128)(2,1)S(1)}, bf16[128,1024]{1,0:T(8,128)(2,1)S(1)}, u32[]{:S(2)}, u32[]{:S(2)}) collective-permute-start(bf16[128,1024]{1,0:T(8,128)(2,1)S(1)} %bitcast.94), channel_id=1, source_target_pairs={{0,2},{1,3},{2,0},{3,1},{4,6},{5,7},{6,4},{7,5},{8,10},{9,11},{10,... | collective-permute-start | bytes 786440 | tf_op jit(solution)/shard_map/ppermute | solution.py:22
  22.3 6.7 %collective-permute-start.6 = (bf16[3,128,128]{2,1,0:T(8,128)(2,1)S(1)}, bf16[3,128,128]{2,1,0:T(8,128)(2,1)S(1)}, u32[]{:S(2)}, u32[]{:S(2)}) collective-permute-start(bf16[3,128,128]{2,1,0:T(8,128)(2,1)S(1)} %fusion.10), channel_id=1, source_target_pairs={{0,4},{12,8},{1,5},{13,9},{2,6},{14,10},{3,7},{15,11},{16,20},{28,... | collective-permute-start | bytes 294920 | tf_op jit(solution)/shard_map/ppermute | solution.py:67
  25.4 25.2 %collective-permute-start.8 = (bf16[3,128,128]{2,1,0:T(8,128)(2,1)S(1)}, bf16[3,128,128]{2,1,0:T(8,128)(2,1)S(1)}, u32[]{:S(2)}, u32[]{:S(2)}) collective-permute-start(bf16[3,128,128]{2,1,0:T(8,128)(2,1)S(1)} %fusion.10), channel_id=1, source_target_pairs={{4,8},{8,4},{5,9},{9,5},{6,10},{10,6},{7,11},{11,7},{20,24},{24,20... | collective-permute-start | bytes 294920 | tf_op jit(solution)/shard_map/ppermute | solution.py:68
  26.1 21.2 %collective-permute-start.7 = (bf16[3,128,128]{2,1,0:T(8,128)(2,1)S(1)}, bf16[3,128,128]{2,1,0:T(8,128)(2,1)S(1)}, u32[]{:S(2)}, u32[]{:S(2)}) collective-permute-start(bf16[3,128,128]{2,1,0:T(8,128)(2,1)S(1)} %fusion.11), channel_id=1, source_target_pairs={{0,4},{4,0},{8,12},{12,8},{1,5},{5,1},{9,13},{13,9},{2,6},{6,2},{1... | collective-permute-start | bytes 294920 | tf_op jit(solution)/shard_map/ppermute | solution.py:22
  29.0 20.0 %collective-permute-start.9 = (bf16[3,128,128]{2,1,0:T(8,128)(2,1)S(1)}, bf16[3,128,128]{2,1,0:T(8,128)(2,1)S(1)}, u32[]{:S(2)}, u32[]{:S(2)}) collective-permute-start(bf16[3,128,128]{2,1,0:T(8,128)(2,1)S(1)} %fusion.12), channel_id=1, source_target_pairs={{0,8},{12,4},{1,9},{13,5},{2,10},{14,6},{3,11},{15,7},{16,24},{28,... | collective-permute-start | bytes 294920 | tf_op jit(solution)/shard_map/ppermute | solution.py:69
  33.9 1.6 %collective-permute-start.13 = (bf16[128,1024]{1,0:T(8,128)(2,1)S(1)}, bf16[128,1024]{1,0:T(8,128)(2,1)S(1)}, u32[]{:S(2)}, u32[]{:S(2)}) collective-permute-start(bf16[128,1024]{1,0:T(8,128)(2,1)S(1)} %collective-permute-done.12), channel_id=1, source_target_pairs={{0,1},{1,0},{2,3},{3,2},{4,5},{5,4},{6,7},{7,6},{8,9},{9,8},{10,11... | collective-permute-start | bytes 786440 | tf_op jit(solution)/shard_map/ppermute | solution.py:22
  36.1 8.1 %collective-permute-start.14 = (bf16[3,384,128]{2,1,0:T(8,128)(2,1)S(1)}, bf16[3,384,128]{2,1,0:T(8,128)(2,1)S(1)}, u32[]{:S(2)}, u32[]{:S(2)}) collective-permute-start(bf16[3,384,128]{2,1,0:T(8,128)(2,1)S(1)} %fusion.5), channel_id=1, source_target_pairs={{0,4},{12,8},{1,5},{13,9},{2,6},{14,10},{3,7},{15,11},{16,20},{28,... | collective-permute-start | bytes 884744 | tf_op jit(solution)/shard_map/ppermute | solution.py:67
  38.0 29.6 %collective-permute-start.16 = (bf16[3,384,128]{2,1,0:T(8,128)(2,1)S(1)}, bf16[3,384,128]{2,1,0:T(8,128)(2,1)S(1)}, u32[]{:S(2)}, u32[]{:S(2)}) collective-permute-start(bf16[3,384,128]{2,1,0:T(8,128)(2,1)S(1)} %fusion.5), channel_id=1, source_target_pairs={{4,8},{8,4},{5,9},{9,5},{6,10},{10,6},{7,11},{11,7},{20,24},{24,20... | collective-permute-start | bytes 884744 | tf_op jit(solution)/shard_map/ppermute | solution.py:68
  44.2 23.4 %collective-permute-start.15 = (bf16[3,384,128]{2,1,0:T(8,128)(2,1)S(1)}, bf16[3,384,128]{2,1,0:T(8,128)(2,1)S(1)}, u32[]{:S(2)}, u32[]{:S(2)}) collective-permute-start(bf16[3,384,128]{2,1,0:T(8,128)(2,1)S(1)} %fusion.6), channel_id=1, source_target_pairs={{0,4},{4,0},{8,12},{12,8},{1,5},{5,1},{9,13},{13,9},{2,6},{6,2},{1... | collective-permute-start | bytes 884744 | tf_op jit(solution)/shard_map/ppermute | solution.py:22
  47.3 21.1 %copy-start.11 = (bf16[3,128,128]{2,1,0:T(8,128)(2,1)}, bf16[3,128,128]{2,1,0:T(8,128)(2,1)S(1)}, u32[]{:S(2)}) copy-start(bf16[3,128,128]{2,1,0:T(8,128)(2,1)S(1)} %collective-permute-done.7.refs_1_) | copy-start | bytes 294916
  47.3 20.3 %collective-permute-start.17 = (bf16[3,384,128]{2,1,0:T(8,128)(2,1)S(1)}, bf16[3,384,128]{2,1,0:T(8,128)(2,1)S(1)}, u32[]{:S(2)}, u32[]{:S(2)}) collective-permute-start(bf16[3,384,128]{2,1,0:T(8,128)(2,1)S(1)} %fusion.7), channel_id=1, source_target_pairs={{0,8},{12,4},{1,9},{13,5},{2,10},{14,6},{3,11},{15,7},{16,24},{28,... | collective-permute-start | bytes 884744 | tf_op jit(solution)/shard_map/ppermute | solution.py:69
  49.0 19.4 %copy-start.12 = (bf16[3,128,128]{2,1,0:T(8,128)(2,1)}, bf16[3,128,128]{2,1,0:T(8,128)(2,1)S(1)}, u32[]{:S(2)}) copy-start(bf16[3,128,128]{2,1,0:T(8,128)(2,1)S(1)} %collective-permute-done.9.refs_3_) | copy-start | bytes 294916
  49.0 19.4 %collective-permute-start.18 = (bf16[3,384,128]{2,1,0:T(8,128)(2,1)S(1)}, bf16[3,384,128]{2,1,0:T(8,128)(2,1)S(1)}, u32[]{:S(2)}, u32[]{:S(2)}) collective-permute-start(bf16[3,384,128]{2,1,0:T(8,128)(2,1)S(1)} %fusion.2), channel_id=1, source_target_pairs={{4,12},{8,0},{5,13},{9,1},{6,14},{10,2},{7,15},{11,3},{20,28},{24,... | collective-permute-start | bytes 884744 | tf_op jit(solution)/shard_map/ppermute | solution.py:73
  50.6 18.6 %copy-start.10 = (bf16[3,128,128]{2,1,0:T(8,128)(2,1)}, bf16[3,128,128]{2,1,0:T(8,128)(2,1)S(1)}, u32[]{:S(2)}) copy-start(bf16[3,128,128]{2,1,0:T(8,128)(2,1)S(1)} %collective-permute-done.8.refs_2_) | copy-start | bytes 294916
  50.6 17.0 %collective-permute-start.10 = (bf16[3,128,128]{2,1,0:T(8,128)(2,1)S(1)}, bf16[3,128,128]{2,1,0:T(8,128)(2,1)S(1)}, u32[]{:S(2)}, u32[]{:S(2)}) collective-permute-start(bf16[3,128,128]{2,1,0:T(8,128)(2,1)S(1)} %fusion.9), channel_id=1, source_target_pairs={{4,12},{8,0},{5,13},{9,1},{6,14},{10,2},{7,15},{11,3},{20,28},{24,... | collective-permute-start | bytes 294920 | tf_op jit(solution)/shard_map/ppermute | solution.py:73
  67.6 0.8 copy-start.13
  67.6 0.7 copy-start.3
  67.7 0.9 copy-start.4
  68.4 0.9 copy-start.2
  68.5 0.7 copy-start.5
  74.7 17.2 %collective-permute-start.19 = (bf16[256,128]{1,0:T(8,128)(2,1)}, bf16[256,128]{1,0:T(8,128)(2,1)S(1)}, u32[]{:S(2)}, u32[]{:S(2)}) collective-permute-start(bf16[256,128]{1,0:T(8,128)(2,1)} %get-tuple-element.15), channel_id=1, source_target_pairs={{0,4},{4,0},{8,12},{12,8},{1,5},{5,1},{9,13},{13,9},{2,6},{6,2},{1... | collective-permute-start | bytes 196616 | tf_op jit(solution)/shard_map/ppermute | solution.py:22
  75.0 17.0 %collective-permute-start.20 = (bf16[256,128]{1,0:T(8,128)(2,1)}, bf16[256,128]{1,0:T(8,128)(2,1)S(1)}, u32[]{:S(2)}, u32[]{:S(2)}) collective-permute-start(bf16[256,128]{1,0:T(8,128)(2,1)} %get-tuple-element.15), channel_id=1, source_target_pairs={{0,8},{4,12},{8,0},{12,4},{1,9},{5,13},{9,1},{13,5},{2,10},{6,14},... | collective-permute-start | bytes 196616 | tf_op jit(solution)/shard_map/ppermute | solution.py:22
  78.4 13.6 %collective-permute-start.21 = (bf16[256,128]{1,0:T(8,128)(2,1)}, bf16[256,128]{1,0:T(8,128)(2,1)S(1)}, u32[]{:S(2)}, u32[]{:S(2)}) collective-permute-start(bf16[256,128]{1,0:T(8,128)(2,1)} %get-tuple-element.15), channel_id=1, source_target_pairs={{0,12},{4,8},{8,4},{12,0},{1,13},{5,9},{9,5},{13,1},{2,14},{6,10},... | collective-permute-start | bytes 196616 | tf_op jit(solution)/shard_map/ppermute | solution.py:22
  79.1 4.6 %collective-permute-start.23 = (bf16[256,128]{1,0:T(8,128)(2,1)}, bf16[256,128]{1,0:T(8,128)(2,1)S(1)}, u32[]{:S(2)}, u32[]{:S(2)}) collective-permute-start(bf16[256,128]{1,0:T(8,128)(2,1)} %get-tuple-element.16), channel_id=1, source_target_pairs={{0,4},{4,0},{8,12},{12,8},{1,5},{5,1},{9,13},{13,9},{2,6},{6,2},{1... | collective-permute-start | bytes 196616 | tf_op jit(solution)/shard_map/ppermute | solution.py:22
  79.1 9.1 %collective-permute-start.24 = (bf16[256,128]{1,0:T(8,128)(2,1)}, bf16[256,128]{1,0:T(8,128)(2,1)S(1)}, u32[]{:S(2)}, u32[]{:S(2)}) collective-permute-start(bf16[256,128]{1,0:T(8,128)(2,1)} %get-tuple-element.16), channel_id=1, source_target_pairs={{0,8},{4,12},{8,0},{12,4},{1,9},{5,13},{9,1},{13,5},{2,10},{6,14},... | collective-permute-start | bytes 196616 | tf_op jit(solution)/shard_map/ppermute | solution.py:22
  83.7 6.3 %collective-permute-start.25 = (bf16[256,128]{1,0:T(8,128)(2,1)}, bf16[256,128]{1,0:T(8,128)(2,1)S(1)}, u32[]{:S(2)}, u32[]{:S(2)}) collective-permute-start(bf16[256,128]{1,0:T(8,128)(2,1)} %get-tuple-element.16), channel_id=1, source_target_pairs={{0,12},{4,8},{8,4},{12,0},{1,13},{5,9},{9,5},{13,1},{2,14},{6,10},... | collective-permute-start | bytes 196616 | tf_op jit(solution)/shard_map/ppermute | solution.py:22
  90.0 2.0 %copy-start.6 = (bf16[1024,128]{1,0:T(8,128)(2,1)S(1)}, bf16[1024,128]{1,0:T(8,128)(2,1)}, u32[]{:S(2)}) copy-start(bf16[1024,128]{1,0:T(8,128)(2,1)} %get-tuple-element.17) | copy-start | bytes 786436
  90.1 2.0 %copy-start.7 = (bf16[1024,128]{1,0:T(8,128)(2,1)S(1)}, bf16[1024,128]{1,0:T(8,128)(2,1)}, u32[]{:S(2)}) copy-start(bf16[1024,128]{1,0:T(8,128)(2,1)} %get-tuple-element.18) | copy-start | bytes 786436
  90.1 2.0 %copy-start.8 = (bf16[1024,128]{1,0:T(8,128)(2,1)S(1)}, bf16[1024,128]{1,0:T(8,128)(2,1)}, u32[]{:S(2)}) copy-start(bf16[1024,128]{1,0:T(8,128)(2,1)} %get-tuple-element.19) | copy-start | bytes 786436
  90.1 2.0 %copy-start.9 = (bf16[1024,128]{1,0:T(8,128)(2,1)S(1)}, bf16[1024,128]{1,0:T(8,128)(2,1)}, u32[]{:S(2)}) copy-start(bf16[1024,128]{1,0:T(8,128)(2,1)} %get-tuple-element.20) | copy-start | bytes 786436
  91.8 1.6 %collective-permute-start.26 = (bf16[128,1024]{1,0:T(8,128)(2,1)S(1)}, bf16[128,1024]{1,0:T(8,128)(2,1)S(1)}, u32[]{:S(2)}, u32[]{:S(2)}) collective-permute-start(bf16[128,1024]{1,0:T(8,128)(2,1)S(1)} %convolution_convert_fusion.3), channel_id=1, source_target_pairs={{0,1},{1,0},{2,3},{3,2},{4,5},{5,4},{6,7},{7,6},{8,9},{9,8},{10,11... | collective-permute-start | bytes 786440 | tf_op jit(solution)/shard_map/ppermute | solution.py:22
  92.5 2.0 %collective-permute-start.22 = (bf16[128,1024]{1,0:T(8,128)(2,1)S(1)}, bf16[128,1024]{1,0:T(8,128)(2,1)S(1)}, u32[]{:S(2)}, u32[]{:S(2)}) collective-permute-start(bf16[128,1024]{1,0:T(8,128)(2,1)S(1)} %convolution_convert_fusion.4), channel_id=1, source_target_pairs={{0,1},{1,0},{2,3},{3,2},{4,5},{5,4},{6,7},{7,6},{8,9},{9,8},{10,11... | collective-permute-start | bytes 786440 | tf_op jit(solution)/shard_map/ppermute | solution.py:22
  93.9 8.4 %collective-permute-start.27 = (bf16[128,1024]{1,0:T(8,128)(2,1)S(1)}, bf16[128,1024]{1,0:T(8,128)(2,1)S(1)}, u32[]{:S(2)}, u32[]{:S(2)}) collective-permute-start(bf16[128,1024]{1,0:T(8,128)(2,1)S(1)} %fusion.4), channel_id=1, source_target_pairs={{0,2},{1,3},{2,0},{3,1},{4,6},{5,7},{6,4},{7,5},{8,10},{9,11},{10,... | collective-permute-start | bytes 786440 | tf_op jit(solution)/shard_map/ppermute | solution.py:22
  102.8 15.8 %copy-start.1 = (f32[128,1024]{1,0:T(8,128)S(1)}, f32[128,1024]{1,0:T(8,128)}, u32[]{:S(2)}) copy-start(f32[128,1024]{1,0:T(8,128)} %param.10) | copy-start | bytes 1572868
  102.9 4.9 %collective-permute-start.28 = (bf16[32,1024]{1,0:T(8,128)(2,1)S(1)}, bf16[32,1024]{1,0:T(8,128)(2,1)S(1)}, u32[]{:S(2)}, u32[]{:S(2)}) collective-permute-start(bf16[32,1024]{1,0:T(8,128)(2,1)S(1)} %get-tuple-element.36), channel_id=1, source_target_pairs={{0,4},{4,0},{8,12},{12,8},{1,5},{5,1},{9,13},{13,9},{2,6},{6,2},{1... | collective-permute-start | bytes 196616 | tf_op jit(solution)/shard_map/ppermute | solution.py:22
  102.9 8.0 %collective-permute-start.29 = (bf16[32,1024]{1,0:T(8,128)(2,1)S(1)}, bf16[32,1024]{1,0:T(8,128)(2,1)S(1)}, u32[]{:S(2)}, u32[]{:S(2)}) collective-permute-start(bf16[32,1024]{1,0:T(8,128)(2,1)S(1)} %get-tuple-element.35), channel_id=1, source_target_pairs={{0,8},{4,12},{8,0},{12,4},{1,9},{5,13},{9,1},{13,5},{2,10},{6,14},... | collective-permute-start | bytes 196616 | tf_op jit(solution)/shard_map/ppermute | solution.py:22
  106.9 6.1 %collective-permute-start.30 = (bf16[32,1024]{1,0:T(8,128)(2,1)S(1)}, bf16[32,1024]{1,0:T(8,128)(2,1)S(1)}, u32[]{:S(2)}, u32[]{:S(2)}) collective-permute-start(bf16[32,1024]{1,0:T(8,128)(2,1)S(1)} %get-tuple-element.34), channel_id=1, source_target_pairs={{0,12},{4,8},{8,4},{12,0},{1,13},{5,9},{9,5},{13,1},{2,14},{6,10},... | collective-permute-start | bytes 196616 | tf_op jit(solution)/shard_map/ppermute | solution.py:22
  113.1 1.9 %collective-permute-start.31 = (bf16[32,1024]{1,0:T(8,128)(2,1)S(1)}, bf16[32,1024]{1,0:T(8,128)(2,1)S(1)}, u32[]{:S(2)}, u32[]{:S(2)}) collective-permute-start(bf16[32,1024]{1,0:T(8,128)(2,1)S(1)} %get-tuple-element.28), channel_id=1, source_target_pairs={{0,1},{1,0},{2,3},{3,2},{4,5},{5,4},{6,7},{7,6},{8,9},{9,8},{10,11... | collective-permute-start | bytes 196616 | tf_op jit(solution)/shard_map/ppermute | solution.py:22
  113.2 5.0 %collective-permute-start.32 = (bf16[32,1024]{1,0:T(8,128)(2,1)S(1)}, bf16[32,1024]{1,0:T(8,128)(2,1)S(1)}, u32[]{:S(2)}, u32[]{:S(2)}) collective-permute-start(bf16[32,1024]{1,0:T(8,128)(2,1)S(1)} %get-tuple-element.27), channel_id=1, source_target_pairs={{0,2},{1,3},{2,0},{3,1},{4,6},{5,7},{6,4},{7,5},{8,10},{9,11},{10,... | collective-permute-start | bytes 196616 | tf_op jit(solution)/shard_map/ppermute | solution.py:22
  113.8 4.7 %collective-permute-start.33 = (bf16[32,1024]{1,0:T(8,128)(2,1)S(1)}, bf16[32,1024]{1,0:T(8,128)(2,1)S(1)}, u32[]{:S(2)}, u32[]{:S(2)}) collective-permute-start(bf16[32,1024]{1,0:T(8,128)(2,1)S(1)} %get-tuple-element.26), channel_id=1, source_target_pairs={{0,3},{1,2},{2,1},{3,0},{4,7},{5,6},{6,5},{7,4},{8,11},{9,10},{10,... | collective-permute-start | bytes 196616 | tf_op jit(solution)/shard_map/ppermute | solution.py:22

commit v2 on v1

--- a/solution.py
+++ b/solution.py
@@ -35,7 +35,8 @@
     parts = {0: value}
     mask = lax.axis_size(axis) // 2
     while mask:
-        parts.update({slot ^ mask: hop(part, axis, mask) for slot, part in parts.items()})
+        for slot, part in list(parts.items()):
+            parts[slot ^ mask] = hop(part, axis, mask)
         mask //= 2
     return parts
 
@@ -63,15 +64,18 @@
         sent = {mask: product(mask).astype(low) for mask in range(1, count)}
         came = [hop(sent[mask], "seq", mask) for mask in sent]
     else:
-        crossing = product(3).astype(low)
-        relayed = lax.ppermute(crossing, "seq", [(0, 1), (3, 2)])
-        middle = lax.ppermute(crossing, "seq", [(1, 2), (2, 1)])
-        skipped = lax.ppermute(product(2).astype(low), "seq", [(0, 2), (3, 1)])
-        near = hop(product(1).astype(low), "seq", 1)
-        rows, relayed = lax.optimization_barrier((rows, relayed))
-        merged = (product(2) + relayed.astype(jnp.float32)).astype(low)
-        merged = lax.ppermute(merged, "seq", [(1, 3), (2, 0)])
-        came = [near, middle, skipped, merged]
+        z = lax.axis_index("seq")
+        end = (z == 0) | (z == 3)
+        first = hop(product(jnp.where(end, 3, 1)).astype(low), "seq", 1)
+        second = product(jnp.where(end, 1, 3)).astype(low)
+        middle = lax.ppermute(second, "seq", [(1, 2), (2, 1)])
+        near = lax.ppermute(second, "seq", [(0, 1), (3, 2)])
+        rows, first = lax.optimization_barrier((rows, first))
+        relayed = jnp.where(end, 0.0, first.astype(jnp.float32))
+        last = hop((product(2) + relayed).astype(low), "seq", 2)
+        total = product(0) + jnp.where(end, first.astype(jnp.float32), 0.0)
+        total = total + middle.astype(jnp.float32) + near.astype(jnp.float32)
+        return [total, last]
     if narrow:
         return [term.transpose(0, 2, 1) for term in [product(0)] + came]
     return [product(0)] + came
@@ -279,7 +283,7 @@
     normed = (whole * lax.rsqrt(mean_sq + EPSILON) * norm_gain).astype(jnp.bfloat16)
     normed = exchange(normed.reshape(sub, seq, depth).transpose(1, 0, 2), "seq")
     parts = spread(normed.reshape(seq * sub, depth), "tensor")
-    groups = (tuple(slots[:1]), tuple(slots[1:]))
+    groups = (tuple(slots[:2]), tuple(slots[2:]))
     terms = []
     for group in groups:
         terms.append(sum_over_seq(jnp.concatenate([parts[slot] for slot in group]), in_part))

time: 120 us -> 112 us (0.933)
  starting transfers between devices: 48.5 us -> 40.2 us
    ppermute x8 -> x4, waiting for transfers between devices: 19.2 us -> 0.57 us  [the longest x2 0.56 us: sum_over_seq(): near = lax.ppermute(second, 'seq', [(0, 1), (3, 2)])]
    ppermute x26 -> x28, waiting for transfers between devices: 22.9 us -> 40.5 us  [hop(): return lax.ppermute(value, axis, [(a, a ^ mask) for a in range(count)])]
    ppermute x8 -> x4, starting transfers between devices: 14.5 us -> 8.36 us  [the longest x2 7.02 us: sum_over_seq(): near = lax.ppermute(second, 'seq', [(0, 1), (3, 2)])]
    ppermute x26 -> x28, starting transfers between devices: 34 us -> 31.8 us  [hop(): return lax.ppermute(value, axis, [(a, a ^ mask) for a in range(count)])]
    dot_general x10 -> x8, matrix products: 5.98 us -> 6.95 us  [product(): jnp.einsum(form, rows, weight_of(mask), preferred_element_type=jnp.float32)]
    unnamed x37 -> x24, local copies, waits for them, and re-layouts: 2.61 us -> 2.65 us
  transfers between devices with their start and end apart: 34 -> 32, of which waited for: 17 -> 16; matrix products, arithmetic and copies ran while one was open for 11% -> 14% of each run, Pallas kernels for 3% -> 3%
where the time goes in v2:
time: 112 us; the launch traced here: 111 us
  waiting for transfers between devices  41 us (37%)
  starting transfers between devices  40.2 us (36%)
  matrix products  10 us (9%)
  Pallas kernels  8.08 us (7%)
  local copies, waits for them, and re-layouts  6.69 us (6%)
  other arithmetic  4.49 us (4%)
    ppermute x28, waiting for transfers between devices, hop(): return lax.ppermute(value, axis, [(a, a ^ mask) for a in range(count)])  40.5 us
    ppermute x28, starting transfers between devices, hop(): return lax.ppermute(value, axis, [(a, a ^ mask) for a in range(count)])  31.8 us
    ppermute x2, starting transfers between devices, sum_over_seq(): near = lax.ppermute(second, 'seq', [(0, 1), (3, 2)])  7.02 us
    dot_general x8, matrix products, product(): jnp.einsum(form, rows, weight_of(mask), preferred_element_type=jnp.float32)  6.95 us
    pallas_call x1, Pallas kernels, local_stage(): pl.pallas_call(functools.partial(local_kernel, groups, len(terms[0]), seq...  4.98 us
    pallas_call x1, Pallas kernels, local_stage(): spectrum = make_spectrum(*wide[:2], long_filter)  3.11 us
    dot_general x4, matrix products, shards(): jnp.einsum('rc,nc->rn', got[place * seq * sub:(place + 1) * seq * sub], o...  3.08 us
    unnamed x24, local copies, waits for them, and re-layouts  2.65 us
  transfers between devices with their start and end apart: 32, of which 16 were waited for; matrix products, arithmetic and copies ran while one was open for 14% of the time, Pallas kernels for 3%

profile of v2, /device:TPU:0, one launch (start us, length us, event | category | flops | bytes accessed | tf_op | source)
XLA Modules:
  0.0 111.0 jit_solution(495343047786601213)
XLA Ops:
  0.0 1.2 %convert_element_type.91 = bf16[128,1024]{1,0:T(8,128)(2,1)S(1)} convert(f32[128,1024]{1,0:T(8,128)} %param.10) | non-fusion elementwise | flops 131072 | bytes 786432 | tf_op jit(solution)/shard_map/convert_element_type | solution.py:273
  1.2 0.7 constant_dynamic-slice_fusion.23
  1.9 2.4 %collective-permute-start.2 = (bf16[32,1024]{1,0:T(8,128)(2,1)}, bf16[32,1024]{1,0:T(8,128)(2,1)S(1)}, u32[]{:S(2)}, u32[]{:S(2)}) collective-permute-start(bf16[32,1024]{1,0:T(8,128)(2,1)} %get-tuple-element.50), channel_id=1, source_target_pairs={{0,3},{1,2},{2,1},{3,0},{4,7},{5,6},{6,5},{7,4},{8,11},{9,10},{10,... | collective-permute-start | bytes 196616 | tf_op jit(solution)/shard_map/ppermute | solution.py:22
  4.3 0.6 collective-permute-start.1
  5.0 0.7 mul.56
  5.7 1.4 %collective-permute-done.2 = bf16[32,1024]{1,0:T(8,128)(2,1)S(1)} collective-permute-done((bf16[32,1024]{1,0:T(8,128)(2,1)}, bf16[32,1024]{1,0:T(8,128)(2,1)S(1)}, u32[]{:S(2)}, u32[]{:S(2)}) %collective-permute-start.2) | collective-permute-done | bytes 65568 | tf_op jit(solution)/shard_map/ppermute | solution.py:22
  7.1 2.1 %collective-permute-done.1 = bf16[32,1024]{1,0:T(8,128)(2,1)S(1)} collective-permute-done((bf16[32,1024]{1,0:T(8,128)(2,1)}, bf16[32,1024]{1,0:T(8,128)(2,1)S(1)}, u32[]{:S(2)}, u32[]{:S(2)}) %collective-permute-start.1) | collective-permute-done | bytes 65568 | tf_op jit(solution)/shard_map/ppermute | solution.py:22
  9.3 0.2 fusion.25
  9.5 0.1 fusion.27
  9.7 3.9 %collective-permute-start.5 = (bf16[32,1024]{1,0:T(8,128)(2,1)S(1)}, bf16[32,1024]{1,0:T(8,128)(2,1)S(1)}, u32[]{:S(2)}, u32[]{:S(2)}) collective-permute-start(bf16[32,1024]{1,0:T(8,128)(2,1)S(1)} %get-tuple-element.42), channel_id=1, source_target_pairs={{0,12},{4,8},{8,4},{12,0},{1,13},{5,9},{9,5},{13,1},{2,14},{6,10},... | collective-permute-start | bytes 196616 | tf_op jit(solution)/shard_map/ppermute | solution.py:22
  13.5 0.6 collective-permute-start.3
  14.2 1.9 %collective-permute-done.5 = bf16[32,1024]{1,0:T(8,128)(2,1)S(1)} collective-permute-done((bf16[32,1024]{1,0:T(8,128)(2,1)S(1)}, bf16[32,1024]{1,0:T(8,128)(2,1)S(1)}, u32[]{:S(2)}, u32[]{:S(2)}) %collective-permute-start.5) | collective-permute-done | bytes 65568 | tf_op jit(solution)/shard_map/ppermute | solution.py:22
  16.0 3.3 %collective-permute-done.4 = bf16[32,1024]{1,0:T(8,128)(2,1)S(1)} collective-permute-done((bf16[32,1024]{1,0:T(8,128)(2,1)S(1)}, bf16[32,1024]{1,0:T(8,128)(2,1)S(1)}, u32[]{:S(2)}, u32[]{:S(2)}) %collective-permute-start.4) | collective-permute-done | bytes 65568 | tf_op jit(solution)/shard_map/ppermute | solution.py:22
  19.3 0.9 pad_maximum_fusion.4
  20.3 1.3 %constant_dynamic-slice_fusion.24.taps_ref = f32[3,3,128]{2,1,0:T(4,128)} fusion(f32[3,3,512]{2,1,0:T(4,128)} %param.13, s32[]{:T(128)S(6)} %select_n.105), kind=kLoop, calls=%fused_computation.123 | loop fusion | bytes 9220 | tf_op jit(solution)/shard_map/dynamic_slice | solution.py:280
  21.6 1.1 constant_dynamic-slice_fusion.13
  22.7 1.6 %collective-permute-start.11 = (bf16[128,1024]{1,0:T(8,128)(2,1)S(1)}, bf16[128,1024]{1,0:T(8,128)(2,1)}, u32[]{:S(2)}, u32[]{:S(2)}) collective-permute-start(bf16[128,1024]{1,0:T(8,128)(2,1)S(1)} %bitcast.101), channel_id=1, source_target_pairs={{0,2},{1,3},{2,0},{3,1},{4,6},{5,7},{6,4},{7,5},{8,10},{9,11},{10,... | collective-permute-start | bytes 786440 | tf_op jit(solution)/shard_map/ppermute | solution.py:22
  24.3 3.1 %filter_spectrum.1.refs_6_ = f32[1024,128]{1,0:T(8,128)} custom-call(bf16[1024,512]{1,0:T(8,128)(2,1)} %constant.101.clone.high_ref.refs_4_, bf16[1024,512]{1,0:T(8,128)(2,1)} %constant.102.clone.low_ref.refs_5_, f32[128,512]{1,0:T(8,128)} %taps_ref.1), custom_call_target="tpu_custom_call" | custom-call | flops 402653184 | bytes 1048576 | tf_op jit(solution)/shard_map/filter_spectrum/pallas_call | solution.py:216
  27.4 1.4 %fusion.14 = bf16[3,256,128]{2,1,0:T(8,128)(2,1)S(1)} fusion(bf16[3,1024,512]{2,1,0:T(8,128)(2,1)S(1)} %copy-done, s32[]{:T(128)S(6)} %select_n.119, bf16[128,1024]{1,0:T(8,128)(2,1)} %collective-permute-done.6, bf16[128,1024]{1,0:T(8,128)(2,1)S(1)} %bitcast.102), kind=kOutput, calls=%fused_computation.26 | convolution fusion | flops 202473472 | bytes 1507332 | tf_op jit(solution)/shard_map/rd,sdc->src/dot_general | solution.py:60
  28.8 3.1 %collective-permute-start.9 = (bf16[3,256,128]{2,1,0:T(8,128)(2,1)S(1)}, bf16[3,256,128]{2,1,0:T(8,128)(2,1)S(1)}, u32[]{:S(2)}, u32[]{:S(2)}) collective-permute-start(bf16[3,256,128]{2,1,0:T(8,128)(2,1)S(1)} %fusion.14), channel_id=1, source_target_pairs={{0,4},{12,8},{1,5},{13,9},{2,6},{14,10},{3,7},{15,11},{16,20},{28,... | collective-permute-start | bytes 589832 | tf_op jit(solution)/shard_map/ppermute | solution.py:72
  31.9 0.7 collective-permute-start.8
  32.6 1.4 %fusion.13 = bf16[3,256,128]{2,1,0:T(8,128)(2,1)S(1)} fusion(bf16[3,1024,512]{2,1,0:T(8,128)(2,1)S(1)} %copy-done, s32[]{:T(128)S(6)} %select_n.115, bf16[128,1024]{1,0:T(8,128)(2,1)} %collective-permute-done.6, bf16[128,1024]{1,0:T(8,128)(2,1)S(1)} %bitcast.103), kind=kOutput, calls=%fused_computation.25 | convolution fusion | flops 202473472 | bytes 1507332 | tf_op jit(solution)/shard_map/rd,sdc->src/dot_general | solution.py:60
  34.0 1.5 %collective-permute-start.7 = (bf16[3,256,128]{2,1,0:T(8,128)(2,1)S(1)}, bf16[3,256,128]{2,1,0:T(8,128)(2,1)S(1)}, u32[]{:S(2)}, u32[]{:S(2)}) collective-permute-start(bf16[3,256,128]{2,1,0:T(8,128)(2,1)S(1)} %fusion.13), channel_id=1, source_target_pairs={{0,4},{4,0},{8,12},{12,8},{1,5},{5,1},{9,13},{13,9},{2,6},{6,2},{1... | collective-permute-start | bytes 589832 | tf_op jit(solution)/shard_map/ppermute | solution.py:22
  35.5 1.0 constant_dynamic-update-slice_fusion.1
  36.5 1.0 pad_maximum_fusion.1
  37.5 3.3 %collective-permute-done.7 = bf16[3,256,128]{2,1,0:T(8,128)(2,1)S(1)} collective-permute-done((bf16[3,256,128]{2,1,0:T(8,128)(2,1)S(1)}, bf16[3,256,128]{2,1,0:T(8,128)(2,1)S(1)}, u32[]{:S(2)}, u32[]{:S(2)}) %collective-permute-start.7) | collective-permute-done | bytes 196640 | tf_op jit(solution)/shard_map/ppermute | solution.py:22
  40.8 0.4 fusion.11
  41.2 2.6 %collective-permute-start.10 = (bf16[3,256,128]{2,1,0:T(8,128)(2,1)S(1)}, bf16[3,256,128]{2,1,0:T(8,128)(2,1)S(1)}, u32[]{:S(2)}, u32[]{:S(2)}) collective-permute-start(bf16[3,256,128]{2,1,0:T(8,128)(2,1)S(1)} %fusion.11), channel_id=1, source_target_pairs={{0,8},{4,12},{8,0},{12,4},{1,9},{5,13},{9,1},{13,5},{2,10},{6,14},... | collective-permute-start | bytes 589832 | tf_op jit(solution)/shard_map/ppermute | solution.py:22
  43.9 1.2 %fusion.8.refs_0_ = f32[3,256,128]{2,1,0:T(8,128)} fusion(bf16[3,1024,512]{2,1,0:T(8,128)(2,1)S(1)} %copy-done, s32[]{:T(128)S(6)} %select_n.105, bf16[256,1024]{1,0:T(8,128)(2,1)S(1)} %pad_maximum_fusion.1, bf16[3,256,128]{2,1,0:T(8,128)(2,1)S(1)} %collective-permute-done.7, bf16[3,256,128]{2,1,0:T(8,128)(2,1)S(1)} %collective-permute-done.9, ...), kind=kOutput, calls=%fused_computation.16 | convolution fusion | flops 202014720 | bytes 2293765 | tf_op jit(solution)/shard_map/rd,sdc->src/dot_general | solution.py:60
  45.1 0.4 fusion.15
  45.6 0.4 fusion.16
  46.1 3.9 %collective-permute-start.15 = (bf16[3,256,128]{2,1,0:T(8,128)(2,1)S(1)}, bf16[3,256,128]{2,1,0:T(8,128)(2,1)S(1)}, u32[]{:S(2)}, u32[]{:S(2)}) collective-permute-start(bf16[3,256,128]{2,1,0:T(8,128)(2,1)S(1)} %fusion.16), channel_id=1, source_target_pairs={{0,4},{12,8},{1,5},{13,9},{2,6},{14,10},{3,7},{15,11},{16,20},{28,... | collective-permute-start | bytes 589832 | tf_op jit(solution)/shard_map/ppermute | solution.py:72
  50.0 0.7 collective-permute-start.14
  50.7 3.5 %collective-permute-done.13 = bf16[3,256,128]{2,1,0:T(8,128)(2,1)S(1)} collective-permute-done((bf16[3,256,128]{2,1,0:T(8,128)(2,1)S(1)}, bf16[3,256,128]{2,1,0:T(8,128)(2,1)S(1)}, u32[]{:S(2)}, u32[]{:S(2)}) %collective-permute-start.13) | collective-permute-done | bytes 196640 | tf_op jit(solution)/shard_map/ppermute | solution.py:22
  54.2 0.4 fusion.12
  54.6 2.4 %collective-permute-start.16 = (bf16[3,256,128]{2,1,0:T(8,128)(2,1)S(1)}, bf16[3,256,128]{2,1,0:T(8,128)(2,1)S(1)}, u32[]{:S(2)}, u32[]{:S(2)}) collective-permute-start(bf16[3,256,128]{2,1,0:T(8,128)(2,1)S(1)} %fusion.12), channel_id=1, source_target_pairs={{0,8},{4,12},{8,0},{12,4},{1,9},{5,13},{9,1},{13,5},{2,10},{6,14},... | collective-permute-start | bytes 589832 | tf_op jit(solution)/shard_map/ppermute | solution.py:22
  57.0 0.6 collective-permute-done.15
  57.6 1.2 %fusion.10.refs_2_ = f32[3,256,128]{2,1,0:T(8,128)} fusion(bf16[3,1024,512]{2,1,0:T(8,128)(2,1)S(1)} %copy-done, s32[]{:T(128)S(6)} %select_n.105, bf16[256,1024]{1,0:T(8,128)(2,1)S(1)} %constant_dynamic-update-slice_fusion, bf16[3,256,128]{2,1,0:T(8,128)(2,1)S(1)} %collective-permute-done.13, bf16[3,256,128]{2,1,0:T(8,128)(2,1)S(1)} %collective-permute-done.15, ...), kind=kOutput, calls=%fused_computation.18 | convolution fusion | flops 202014720 | bytes 2293765 | tf_op jit(solution)/shard_map/rd,sdc->src/dot_general | solution.py:60
  58.8 6.5 %collective-permute-done.16.refs_3_ = bf16[3,256,128]{2,1,0:T(8,128)(2,1)S(1)} collective-permute-done((bf16[3,256,128]{2,1,0:T(8,128)(2,1)S(1)}, bf16[3,256,128]{2,1,0:T(8,128)(2,1)S(1)}, u32[]{:S(2)}, u32[]{:S(2)}) %collective-permute-start.16) | collective-permute-done | bytes 196640 | tf_op jit(solution)/shard_map/ppermute | solution.py:22
  65.4 0.7 copy-done.8
  66.0 5.0 %filters.1 = (bf16[256,128]{1,0:T(8,128)(2,1)}, bf16[256,128]{1,0:T(8,128)(2,1)}) custom-call(s32[1]{0:T(128)} %bitcast.t_ref, f32[3,3,128]{2,1,0:T(4,128)} %constant_dynamic-slice_fusion.24.taps_ref, f32[3,256,128]{2,1,0:T(8,128)} %fusion.8.refs_0_, bf16[3,256,128]{2,1,0:T(8,128)(2,1)} %copy-done.7, f32[3,256,128]{2,1,0:T(8,128)} %fusion.10.refs_2_, ...), custom_call_target="tpu_custom_call" | custom-call | flops 805306368 | bytes 2097152 | tf_op jit(solution)/shard_map/filters/pallas_call | solution.py:220
  71.1 2.5 %collective-permute-start.22 = (bf16[256,128]{1,0:T(8,128)(2,1)}, bf16[256,128]{1,0:T(8,128)(2,1)S(1)}, u32[]{:S(2)}, u32[]{:S(2)}) collective-permute-start(bf16[256,128]{1,0:T(8,128)(2,1)} %get-tuple-element.16), channel_id=1, source_target_pairs={{0,8},{4,12},{8,0},{12,4},{1,9},{5,13},{9,1},{13,5},{2,10},{6,14},... | collective-permute-start | bytes 196616 | tf_op jit(solution)/shard_map/ppermute | solution.py:22
  73.6 1.9 %collective-permute-start.23 = (bf16[256,128]{1,0:T(8,128)(2,1)}, bf16[256,128]{1,0:T(8,128)(2,1)S(1)}, u32[]{:S(2)}, u32[]{:S(2)}) collective-permute-start(bf16[256,128]{1,0:T(8,128)(2,1)} %get-tuple-element.16), channel_id=1, source_target_pairs={{0,12},{4,8},{8,4},{12,0},{1,13},{5,9},{9,5},{13,1},{2,14},{6,10},... | collective-permute-start | bytes 196616 | tf_op jit(solution)/shard_map/ppermute | solution.py:22
  75.5 2.5 %collective-permute-start.18 = (bf16[256,128]{1,0:T(8,128)(2,1)}, bf16[256,128]{1,0:T(8,128)(2,1)S(1)}, u32[]{:S(2)}, u32[]{:S(2)}) collective-permute-start(bf16[256,128]{1,0:T(8,128)(2,1)} %get-tuple-element.15), channel_id=1, source_target_pairs={{0,8},{4,12},{8,0},{12,4},{1,9},{5,13},{9,1},{13,5},{2,10},{6,14},... | collective-permute-start | bytes 196616 | tf_op jit(solution)/shard_map/ppermute | solution.py:22
  78.0 0.9 constant_dynamic-update-slice_fusion.5
  78.9 2.0 %collective-permute-start.19 = (bf16[256,128]{1,0:T(8,128)(2,1)}, bf16[256,128]{1,0:T(8,128)(2,1)S(1)}, u32[]{:S(2)}, u32[]{:S(2)}) collective-permute-start(bf16[256,128]{1,0:T(8,128)(2,1)} %get-tuple-element.15), channel_id=1, source_target_pairs={{0,12},{4,8},{8,4},{12,0},{1,13},{5,9},{9,5},{13,1},{2,14},{6,10},... | collective-permute-start | bytes 196616 | tf_op jit(solution)/shard_map/ppermute | solution.py:22
  81.0 1.6 %convolution_convert_fusion = bf16[128,1024]{1,0:T(8,128)(2,1)S(1)} fusion(bf16[256,512]{1,0:T(8,128)(2,1)S(1)} %constant_dynamic-update-slice_fusion.6, bf16[1024,128]{1,0:T(8,128)(2,1)} %get-tuple-element.19, bf16[1024,128]{1,0:T(8,128)(2,1)} %get-tuple-element.20, bf16[1024,128]{1,0:T(8,128)(2,1)} %get-tuple-element.18, bf16[1024,128]{1,0:T(8,128)(2,1)S(1)} %copy-done.3), kind=kOutput, calls=%fused_computation.13 | convolution fusion | flops 138543104 | bytes 1441792 | tf_op jit(solution)/shard_map/rc,nc->rn/dot_general | solution.py:305
  82.8 1.1 collective-permute-done.18
  83.8 1.4 %collective-permute-done.19 = bf16[256,128]{1,0:T(8,128)(2,1)S(1)} collective-permute-done((bf16[256,128]{1,0:T(8,128)(2,1)}, bf16[256,128]{1,0:T(8,128)(2,1)S(1)}, u32[]{:S(2)}, u32[]{:S(2)}) %collective-permute-start.19) | collective-permute-done | bytes 65568 | tf_op jit(solution)/shard_map/ppermute | solution.py:22
  85.3 0.5 convolution_convert_fusion.1
  85.8 0.5 fusion.2
  86.3 0.6 collective-permute-start.25
  86.9 0.5 collective-permute-done.20
  87.4 7.7 %collective-permute-done.25 = bf16[128,1024]{1,0:T(8,128)(2,1)S(1)} collective-permute-done((bf16[128,1024]{1,0:T(8,128)(2,1)S(1)}, bf16[128,1024]{1,0:T(8,128)(2,1)S(1)}, u32[]{:S(2)}, u32[]{:S(2)}) %collective-permute-start.25) | collective-permute-done | bytes 262176 | tf_op jit(solution)/shard_map/ppermute | solution.py:22
  95.1 0.5 fusion.1
  95.6 2.0 %collective-permute-start.28 = (bf16[32,1024]{1,0:T(8,128)(2,1)S(1)}, bf16[32,1024]{1,0:T(8,128)(2,1)S(1)}, u32[]{:S(2)}, u32[]{:S(2)}) collective-permute-start(bf16[32,1024]{1,0:T(8,128)(2,1)S(1)} %get-tuple-element.34), channel_id=1, source_target_pairs={{0,12},{4,8},{8,4},{12,0},{1,13},{5,9},{9,5},{13,1},{2,14},{6,10},... | collective-permute-start | bytes 196616 | tf_op jit(solution)/shard_map/ppermute | solution.py:22
  97.6 2.5 %collective-permute-start.26 = (bf16[32,1024]{1,0:T(8,128)(2,1)S(1)}, bf16[32,1024]{1,0:T(8,128)(2,1)S(1)}, u32[]{:S(2)}, u32[]{:S(2)}) collective-permute-start(bf16[32,1024]{1,0:T(8,128)(2,1)S(1)} %get-tuple-element.36), channel_id=1, source_target_pairs={{0,4},{4,0},{8,12},{12,8},{1,5},{5,1},{9,13},{13,9},{2,6},{6,2},{1... | collective-permute-start | bytes 196616 | tf_op jit(solution)/shard_map/ppermute | solution.py:22
  100.1 1.9 %collective-permute-done.28 = bf16[32,1024]{1,0:T(8,128)(2,1)S(1)} collective-permute-done((bf16[32,1024]{1,0:T(8,128)(2,1)S(1)}, bf16[32,1024]{1,0:T(8,128)(2,1)S(1)}, u32[]{:S(2)}, u32[]{:S(2)}) %collective-permute-start.28) | collective-permute-done | bytes 65568 | tf_op jit(solution)/shard_map/ppermute | solution.py:22
  102.0 1.9 %collective-permute-done.27 = bf16[32,1024]{1,0:T(8,128)(2,1)S(1)} collective-permute-done((bf16[32,1024]{1,0:T(8,128)(2,1)S(1)}, bf16[32,1024]{1,0:T(8,128)(2,1)S(1)}, u32[]{:S(2)}, u32[]{:S(2)}) %collective-permute-start.27) | collective-permute-done | bytes 65568 | tf_op jit(solution)/shard_map/ppermute | solution.py:22
  104.2 1.5 %collective-permute-start.30 = (bf16[32,1024]{1,0:T(8,128)(2,1)S(1)}, bf16[32,1024]{1,0:T(8,128)(2,1)S(1)}, u32[]{:S(2)}, u32[]{:S(2)}) collective-permute-start(bf16[32,1024]{1,0:T(8,128)(2,1)S(1)} %get-tuple-element.27), channel_id=1, source_target_pairs={{0,2},{1,3},{2,0},{3,1},{4,6},{5,7},{6,4},{7,5},{8,10},{9,11},{10,... | collective-permute-start | bytes 196616 | tf_op jit(solution)/shard_map/ppermute | solution.py:22
  105.7 0.3 collective-permute-start.29
  106.0 2.4 %collective-permute-done.31 = bf16[32,1024]{1,0:T(8,128)(2,1)S(1)} collective-permute-done((bf16[32,1024]{1,0:T(8,128)(2,1)S(1)}, bf16[32,1024]{1,0:T(8,128)(2,1)S(1)}, u32[]{:S(2)}, u32[]{:S(2)}) %collective-permute-start.31) | collective-permute-done | bytes 65568 | tf_op jit(solution)/shard_map/ppermute | solution.py:22
  108.5 1.5 %collective-permute-done.30 = bf16[32,1024]{1,0:T(8,128)(2,1)S(1)} collective-permute-done((bf16[32,1024]{1,0:T(8,128)(2,1)S(1)}, bf16[32,1024]{1,0:T(8,128)(2,1)S(1)}, u32[]{:S(2)}, u32[]{:S(2)}) %collective-permute-start.30) | collective-permute-done | bytes 65568 | tf_op jit(solution)/shard_map/ppermute | solution.py:22
  110.1 0.9 convert_add_fusion
  (65 shorter events, 1.2 us)
Async XLA Ops:
  0.0 27.4 %copy-start = (bf16[3,1024,512]{2,1,0:T(8,128)(2,1)S(1)}, bf16[3,1024,512]{2,1,0:T(8,128)(2,1)}, u32[]{:S(2)}) copy-start(bf16[3,1024,512]{2,1,0:T(8,128)(2,1)} %param.12) | copy-start | bytes 9437188
  1.9 5.2 %collective-permute-start.2 = (bf16[32,1024]{1,0:T(8,128)(2,1)}, bf16[32,1024]{1,0:T(8,128)(2,1)S(1)}, u32[]{:S(2)}, u32[]{:S(2)}) collective-permute-start(bf16[32,1024]{1,0:T(8,128)(2,1)} %get-tuple-element.50), channel_id=1, source_target_pairs={{0,3},{1,2},{2,1},{3,0},{4,7},{5,6},{6,5},{7,4},{8,11},{9,10},{10,... | collective-permute-start | bytes 196616 | tf_op jit(solution)/shard_map/ppermute | solution.py:22
  4.3 4.9 %collective-permute-start.1 = (bf16[32,1024]{1,0:T(8,128)(2,1)}, bf16[32,1024]{1,0:T(8,128)(2,1)S(1)}, u32[]{:S(2)}, u32[]{:S(2)}) collective-permute-start(bf16[32,1024]{1,0:T(8,128)(2,1)} %get-tuple-element.51), channel_id=1, source_target_pairs={{0,2},{1,3},{2,0},{3,1},{4,6},{5,7},{6,4},{7,5},{8,10},{9,11},{10,... | collective-permute-start | bytes 196616 | tf_op jit(solution)/shard_map/ppermute | solution.py:22
  4.9 4.3 %collective-permute-start = (bf16[32,1024]{1,0:T(8,128)(2,1)S(1)}, bf16[32,1024]{1,0:T(8,128)(2,1)S(1)}, u32[]{:S(2)}, u32[]{:S(2)}) collective-permute-start(bf16[32,1024]{1,0:T(8,128)(2,1)S(1)} %get-tuple-element.52), channel_id=1, source_target_pairs={{0,1},{1,0},{2,3},{3,2},{4,5},{5,4},{6,7},{7,6},{8,9},{9,8},{10,11... | collective-permute-start | bytes 196616 | tf_op jit(solution)/shard_map/ppermute | solution.py:22
  9.7 6.4 %collective-permute-start.5 = (bf16[32,1024]{1,0:T(8,128)(2,1)S(1)}, bf16[32,1024]{1,0:T(8,128)(2,1)S(1)}, u32[]{:S(2)}, u32[]{:S(2)}) collective-permute-start(bf16[32,1024]{1,0:T(8,128)(2,1)S(1)} %get-tuple-element.42), channel_id=1, source_target_pairs={{0,12},{4,8},{8,4},{12,0},{1,13},{5,9},{9,5},{13,1},{2,14},{6,10},... | collective-permute-start | bytes 196616 | tf_op jit(solution)/shard_map/ppermute | solution.py:22
  13.5 5.8 %collective-permute-start.4 = (bf16[32,1024]{1,0:T(8,128)(2,1)S(1)}, bf16[32,1024]{1,0:T(8,128)(2,1)S(1)}, u32[]{:S(2)}, u32[]{:S(2)}) collective-permute-start(bf16[32,1024]{1,0:T(8,128)(2,1)S(1)} %get-tuple-element.43), channel_id=1, source_target_pairs={{0,8},{4,12},{8,0},{12,4},{1,9},{5,13},{9,1},{13,5},{2,10},{6,14},... | collective-permute-start | bytes 196616 | tf_op jit(solution)/shard_map/ppermute | solution.py:22
  13.5 5.8 %collective-permute-start.3 = (bf16[32,1024]{1,0:T(8,128)(2,1)S(1)}, bf16[32,1024]{1,0:T(8,128)(2,1)}, u32[]{:S(2)}, u32[]{:S(2)}) collective-permute-start(bf16[32,1024]{1,0:T(8,128)(2,1)S(1)} %get-tuple-element.44), channel_id=1, source_target_pairs={{0,4},{4,0},{8,12},{12,8},{1,5},{5,1},{9,13},{13,9},{2,6},{6,2},{1... | collective-permute-start | bytes 196616 | tf_op jit(solution)/shard_map/ppermute | solution.py:22
  14.2 7.5 %copy-start.2 = (bf16[1024,512]{1,0:T(8,128)(2,1)S(1)}, bf16[1024,512]{1,0:T(8,128)(2,1)}, u32[]{:S(2)}) copy-start(bf16[1024,512]{1,0:T(8,128)(2,1)} %param.15) | copy-start | bytes 3145732
  20.3 7.2 %collective-permute-start.6 = (bf16[128,1024]{1,0:T(8,128)(2,1)S(1)}, bf16[128,1024]{1,0:T(8,128)(2,1)}, u32[]{:S(2)}, u32[]{:S(2)}) collective-permute-start(bf16[128,1024]{1,0:T(8,128)(2,1)S(1)} %bitcast.100), channel_id=1, source_target_pairs={{0,1},{1,0},{2,3},{3,2},{4,5},{5,4},{6,7},{7,6},{8,9},{9,8},{10,11... | collective-permute-start | bytes 786440 | tf_op jit(solution)/shard_map/ppermute | solution.py:22
  22.7 12.8 %collective-permute-start.11 = (bf16[128,1024]{1,0:T(8,128)(2,1)S(1)}, bf16[128,1024]{1,0:T(8,128)(2,1)}, u32[]{:S(2)}, u32[]{:S(2)}) collective-permute-start(bf16[128,1024]{1,0:T(8,128)(2,1)S(1)} %bitcast.101), channel_id=1, source_target_pairs={{0,2},{1,3},{2,0},{3,1},{4,6},{5,7},{6,4},{7,5},{8,10},{9,11},{10,... | collective-permute-start | bytes 786440 | tf_op jit(solution)/shard_map/ppermute | solution.py:22
  28.8 15.1 %collective-permute-start.9 = (bf16[3,256,128]{2,1,0:T(8,128)(2,1)S(1)}, bf16[3,256,128]{2,1,0:T(8,128)(2,1)S(1)}, u32[]{:S(2)}, u32[]{:S(2)}) collective-permute-start(bf16[3,256,128]{2,1,0:T(8,128)(2,1)S(1)} %fusion.14), channel_id=1, source_target_pairs={{0,4},{12,8},{1,5},{13,9},{2,6},{14,10},{3,7},{15,11},{16,20},{28,... | collective-permute-start | bytes 589832 | tf_op jit(solution)/shard_map/ppermute | solution.py:72
  31.9 12.0 %collective-permute-start.8 = (bf16[3,256,128]{2,1,0:T(8,128)(2,1)S(1)}, bf16[3,256,128]{2,1,0:T(8,128)(2,1)S(1)}, u32[]{:S(2)}, u32[]{:S(2)}) collective-permute-start(bf16[3,256,128]{2,1,0:T(8,128)(2,1)S(1)} %fusion.14), channel_id=1, source_target_pairs={{4,8},{8,4},{5,9},{9,5},{6,10},{10,6},{7,11},{11,7},{20,24},{24,20... | collective-permute-start | bytes 589832 | tf_op jit(solution)/shard_map/ppermute | solution.py:71
  34.0 6.8 %collective-permute-start.7 = (bf16[3,256,128]{2,1,0:T(8,128)(2,1)S(1)}, bf16[3,256,128]{2,1,0:T(8,128)(2,1)S(1)}, u32[]{:S(2)}, u32[]{:S(2)}) collective-permute-start(bf16[3,256,128]{2,1,0:T(8,128)(2,1)S(1)} %fusion.13), channel_id=1, source_target_pairs={{0,4},{4,0},{8,12},{12,8},{1,5},{5,1},{9,13},{13,9},{2,6},{6,2},{1... | collective-permute-start | bytes 589832 | tf_op jit(solution)/shard_map/ppermute | solution.py:22
  35.5 9.6 %collective-permute-start.12 = (bf16[128,1024]{1,0:T(8,128)(2,1)}, bf16[128,1024]{1,0:T(8,128)(2,1)S(1)}, u32[]{:S(2)}, u32[]{:S(2)}) collective-permute-start(bf16[128,1024]{1,0:T(8,128)(2,1)} %collective-permute-done.11), channel_id=1, source_target_pairs={{0,1},{1,0},{2,3},{3,2},{4,5},{5,4},{6,7},{7,6},{8,9},{9,8},{10,11... | collective-permute-start | bytes 786440 | tf_op jit(solution)/shard_map/ppermute | solution.py:22
  41.2 17.6 %collective-permute-start.10 = (bf16[3,256,128]{2,1,0:T(8,128)(2,1)S(1)}, bf16[3,256,128]{2,1,0:T(8,128)(2,1)S(1)}, u32[]{:S(2)}, u32[]{:S(2)}) collective-permute-start(bf16[3,256,128]{2,1,0:T(8,128)(2,1)S(1)} %fusion.11), channel_id=1, source_target_pairs={{0,8},{4,12},{8,0},{12,4},{1,9},{5,13},{9,1},{13,5},{2,10},{6,14},... | collective-permute-start | bytes 589832 | tf_op jit(solution)/shard_map/ppermute | solution.py:22
  45.6 8.6 %collective-permute-start.13 = (bf16[3,256,128]{2,1,0:T(8,128)(2,1)S(1)}, bf16[3,256,128]{2,1,0:T(8,128)(2,1)S(1)}, u32[]{:S(2)}, u32[]{:S(2)}) collective-permute-start(bf16[3,256,128]{2,1,0:T(8,128)(2,1)S(1)} %fusion.15), channel_id=1, source_target_pairs={{0,4},{4,0},{8,12},{12,8},{1,5},{5,1},{9,13},{13,9},{2,6},{6,2},{1... | collective-permute-start | bytes 589832 | tf_op jit(solution)/shard_map/ppermute | solution.py:22
  46.1 11.5 %collective-permute-start.15 = (bf16[3,256,128]{2,1,0:T(8,128)(2,1)S(1)}, bf16[3,256,128]{2,1,0:T(8,128)(2,1)S(1)}, u32[]{:S(2)}, u32[]{:S(2)}) collective-permute-start(bf16[3,256,128]{2,1,0:T(8,128)(2,1)S(1)} %fusion.16), channel_id=1, source_target_pairs={{0,4},{12,8},{1,5},{13,9},{2,6},{14,10},{3,7},{15,11},{16,20},{28,... | collective-permute-start | bytes 589832 | tf_op jit(solution)/shard_map/ppermute | solution.py:72
  50.0 7.6 %collective-permute-start.14 = (bf16[3,256,128]{2,1,0:T(8,128)(2,1)S(1)}, bf16[3,256,128]{2,1,0:T(8,128)(2,1)S(1)}, u32[]{:S(2)}, u32[]{:S(2)}) collective-permute-start(bf16[3,256,128]{2,1,0:T(8,128)(2,1)S(1)} %fusion.16), channel_id=1, source_target_pairs={{4,8},{8,4},{5,9},{9,5},{6,10},{10,6},{7,11},{11,7},{20,24},{24,20... | collective-permute-start | bytes 589832 | tf_op jit(solution)/shard_map/ppermute | solution.py:71
  54.6 10.7 %collective-permute-start.16 = (bf16[3,256,128]{2,1,0:T(8,128)(2,1)S(1)}, bf16[3,256,128]{2,1,0:T(8,128)(2,1)S(1)}, u32[]{:S(2)}, u32[]{:S(2)}) collective-permute-start(bf16[3,256,128]{2,1,0:T(8,128)(2,1)S(1)} %fusion.12), channel_id=1, source_target_pairs={{0,8},{4,12},{8,0},{12,4},{1,9},{5,13},{9,1},{13,5},{2,10},{6,14},... | collective-permute-start | bytes 589832 | tf_op jit(solution)/shard_map/ppermute | solution.py:22
  58.8 6.5 %copy-start.7 = (bf16[3,256,128]{2,1,0:T(8,128)(2,1)}, bf16[3,256,128]{2,1,0:T(8,128)(2,1)S(1)}, u32[]{:S(2)}) copy-start(bf16[3,256,128]{2,1,0:T(8,128)(2,1)S(1)} %collective-permute-done.10.refs_1_) | copy-start | bytes 589828
  65.4 0.7 copy-start.8
  66.0 14.9 %copy-start.3 = (bf16[1024,128]{1,0:T(8,128)(2,1)S(1)}, bf16[1024,128]{1,0:T(8,128)(2,1)}, u32[]{:S(2)}) copy-start(bf16[1024,128]{1,0:T(8,128)(2,1)} %get-tuple-element.17) | copy-start | bytes 786436
  71.0 7.8 %collective-permute-start.21 = (bf16[256,128]{1,0:T(8,128)(2,1)}, bf16[256,128]{1,0:T(8,128)(2,1)S(1)}, u32[]{:S(2)}, u32[]{:S(2)}) collective-permute-start(bf16[256,128]{1,0:T(8,128)(2,1)} %get-tuple-element.16), channel_id=1, source_target_pairs={{0,4},{4,0},{8,12},{12,8},{1,5},{5,1},{9,13},{13,9},{2,6},{6,2},{1... | collective-permute-start | bytes 196616 | tf_op jit(solution)/shard_map/ppermute | solution.py:22
  71.1 9.8 %collective-permute-start.22 = (bf16[256,128]{1,0:T(8,128)(2,1)}, bf16[256,128]{1,0:T(8,128)(2,1)S(1)}, u32[]{:S(2)}, u32[]{:S(2)}) collective-permute-start(bf16[256,128]{1,0:T(8,128)(2,1)} %get-tuple-element.16), channel_id=1, source_target_pairs={{0,8},{4,12},{8,0},{12,4},{1,9},{5,13},{9,1},{13,5},{2,10},{6,14},... | collective-permute-start | bytes 196616 | tf_op jit(solution)/shard_map/ppermute | solution.py:22
  73.6 7.3 %collective-permute-start.23 = (bf16[256,128]{1,0:T(8,128)(2,1)}, bf16[256,128]{1,0:T(8,128)(2,1)S(1)}, u32[]{:S(2)}, u32[]{:S(2)}) collective-permute-start(bf16[256,128]{1,0:T(8,128)(2,1)} %get-tuple-element.16), channel_id=1, source_target_pairs={{0,12},{4,8},{8,4},{12,0},{1,13},{5,9},{9,5},{13,1},{2,14},{6,10},... | collective-permute-start | bytes 196616 | tf_op jit(solution)/shard_map/ppermute | solution.py:22
  75.5 7.2 %collective-permute-start.17 = (bf16[256,128]{1,0:T(8,128)(2,1)}, bf16[256,128]{1,0:T(8,128)(2,1)S(1)}, u32[]{:S(2)}, u32[]{:S(2)}) collective-permute-start(bf16[256,128]{1,0:T(8,128)(2,1)} %get-tuple-element.15), channel_id=1, source_target_pairs={{0,4},{4,0},{8,12},{12,8},{1,5},{5,1},{9,13},{13,9},{2,6},{6,2},{1... | collective-permute-start | bytes 196616 | tf_op jit(solution)/shard_map/ppermute | solution.py:22
  75.5 8.3 %collective-permute-start.18 = (bf16[256,128]{1,0:T(8,128)(2,1)}, bf16[256,128]{1,0:T(8,128)(2,1)S(1)}, u32[]{:S(2)}, u32[]{:S(2)}) collective-permute-start(bf16[256,128]{1,0:T(8,128)(2,1)} %get-tuple-element.15), channel_id=1, source_target_pairs={{0,8},{4,12},{8,0},{12,4},{1,9},{5,13},{9,1},{13,5},{2,10},{6,14},... | collective-permute-start | bytes 196616 | tf_op jit(solution)/shard_map/ppermute | solution.py:22
  78.9 6.4 %collective-permute-start.19 = (bf16[256,128]{1,0:T(8,128)(2,1)}, bf16[256,128]{1,0:T(8,128)(2,1)S(1)}, u32[]{:S(2)}, u32[]{:S(2)}) collective-permute-start(bf16[256,128]{1,0:T(8,128)(2,1)} %get-tuple-element.15), channel_id=1, source_target_pairs={{0,12},{4,8},{8,4},{12,0},{1,13},{5,9},{9,5},{13,1},{2,14},{6,10},... | collective-permute-start | bytes 196616 | tf_op jit(solution)/shard_map/ppermute | solution.py:22
  81.0 4.3 %copy-start.4 = (bf16[1024,128]{1,0:T(8,128)(2,1)S(1)}, bf16[1024,128]{1,0:T(8,128)(2,1)}, u32[]{:S(2)}) copy-start(bf16[1024,128]{1,0:T(8,128)(2,1)} %get-tuple-element.18) | copy-start | bytes 786436
  81.0 4.3 %copy-start.5 = (bf16[1024,128]{1,0:T(8,128)(2,1)S(1)}, bf16[1024,128]{1,0:T(8,128)(2,1)}, u32[]{:S(2)}) copy-start(bf16[1024,128]{1,0:T(8,128)(2,1)} %get-tuple-element.19) | copy-start | bytes 786436
  81.0 4.3 %copy-start.6 = (bf16[1024,128]{1,0:T(8,128)(2,1)S(1)}, bf16[1024,128]{1,0:T(8,128)(2,1)}, u32[]{:S(2)}) copy-start(bf16[1024,128]{1,0:T(8,128)(2,1)} %get-tuple-element.20) | copy-start | bytes 786436
  82.6 3.2 %collective-permute-start.24 = (bf16[128,1024]{1,0:T(8,128)(2,1)S(1)}, bf16[128,1024]{1,0:T(8,128)(2,1)S(1)}, u32[]{:S(2)}, u32[]{:S(2)}) collective-permute-start(bf16[128,1024]{1,0:T(8,128)(2,1)S(1)} %convolution_convert_fusion), channel_id=1, source_target_pairs={{0,1},{1,0},{2,3},{3,2},{4,5},{5,4},{6,7},{7,6},{8,9},{9,8},{10,11... | collective-permute-start | bytes 786440 | tf_op jit(solution)/shard_map/ppermute | solution.py:22
  85.8 1.6 %collective-permute-start.20 = (bf16[128,1024]{1,0:T(8,128)(2,1)S(1)}, bf16[128,1024]{1,0:T(8,128)(2,1)S(1)}, u32[]{:S(2)}, u32[]{:S(2)}) collective-permute-start(bf16[128,1024]{1,0:T(8,128)(2,1)S(1)} %convolution_convert_fusion.1), channel_id=1, source_target_pairs={{0,1},{1,0},{2,3},{3,2},{4,5},{5,4},{6,7},{7,6},{8,9},{9,8},{10,11... | collective-permute-start | bytes 786440 | tf_op jit(solution)/shard_map/ppermute | solution.py:22
  86.3 8.8 %collective-permute-start.25 = (bf16[128,1024]{1,0:T(8,128)(2,1)S(1)}, bf16[128,1024]{1,0:T(8,128)(2,1)S(1)}, u32[]{:S(2)}, u32[]{:S(2)}) collective-permute-start(bf16[128,1024]{1,0:T(8,128)(2,1)S(1)} %fusion.2), channel_id=1, source_target_pairs={{0,2},{1,3},{2,0},{3,1},{4,6},{5,7},{6,4},{7,5},{8,10},{9,11},{10,... | collective-permute-start | bytes 786440 | tf_op jit(solution)/shard_map/ppermute | solution.py:22
  95.6 14.5 %copy-start.1 = (f32[128,1024]{1,0:T(8,128)S(1)}, f32[128,1024]{1,0:T(8,128)}, u32[]{:S(2)}) copy-start(f32[128,1024]{1,0:T(8,128)} %param.10) | copy-start | bytes 1572868
  95.6 6.4 %collective-permute-start.28 = (bf16[32,1024]{1,0:T(8,128)(2,1)S(1)}, bf16[32,1024]{1,0:T(8,128)(2,1)S(1)}, u32[]{:S(2)}, u32[]{:S(2)}) collective-permute-start(bf16[32,1024]{1,0:T(8,128)(2,1)S(1)} %get-tuple-element.34), channel_id=1, source_target_pairs={{0,12},{4,8},{8,4},{12,0},{1,13},{5,9},{9,5},{13,1},{2,14},{6,10},... | collective-permute-start | bytes 196616 | tf_op jit(solution)/shard_map/ppermute | solution.py:22
  97.6 6.3 %collective-permute-start.27 = (bf16[32,1024]{1,0:T(8,128)(2,1)S(1)}, bf16[32,1024]{1,0:T(8,128)(2,1)S(1)}, u32[]{:S(2)}, u32[]{:S(2)}) collective-permute-start(bf16[32,1024]{1,0:T(8,128)(2,1)S(1)} %get-tuple-element.35), channel_id=1, source_target_pairs={{0,8},{4,12},{8,0},{12,4},{1,9},{5,13},{9,1},{13,5},{2,10},{6,14},... | collective-permute-start | bytes 196616 | tf_op jit(solution)/shard_map/ppermute | solution.py:22
  97.6 6.3 %collective-permute-start.26 = (bf16[32,1024]{1,0:T(8,128)(2,1)S(1)}, bf16[32,1024]{1,0:T(8,128)(2,1)S(1)}, u32[]{:S(2)}, u32[]{:S(2)}) collective-permute-start(bf16[32,1024]{1,0:T(8,128)(2,1)S(1)} %get-tuple-element.36), channel_id=1, source_target_pairs={{0,4},{4,0},{8,12},{12,8},{1,5},{5,1},{9,13},{13,9},{2,6},{6,2},{1... | collective-permute-start | bytes 196616 | tf_op jit(solution)/shard_map/ppermute | solution.py:22
  104.1 4.4 %collective-permute-start.31 = (bf16[32,1024]{1,0:T(8,128)(2,1)S(1)}, bf16[32,1024]{1,0:T(8,128)(2,1)S(1)}, u32[]{:S(2)}, u32[]{:S(2)}) collective-permute-start(bf16[32,1024]{1,0:T(8,128)(2,1)S(1)} %get-tuple-element.26), channel_id=1, source_target_pairs={{0,3},{1,2},{2,1},{3,0},{4,7},{5,6},{6,5},{7,4},{8,11},{9,10},{10,... | collective-permute-start | bytes 196616 | tf_op jit(solution)/shard_map/ppermute | solution.py:22
  104.2 5.8 %collective-permute-start.30 = (bf16[32,1024]{1,0:T(8,128)(2,1)S(1)}, bf16[32,1024]{1,0:T(8,128)(2,1)S(1)}, u32[]{:S(2)}, u32[]{:S(2)}) collective-permute-start(bf16[32,1024]{1,0:T(8,128)(2,1)S(1)} %get-tuple-element.27), channel_id=1, source_target_pairs={{0,2},{1,3},{2,0},{3,1},{4,6},{5,7},{6,4},{7,5},{8,10},{9,11},{10,... | collective-permute-start | bytes 196616 | tf_op jit(solution)/shard_map/ppermute | solution.py:22
  105.7 4.3 %collective-permute-start.29 = (bf16[32,1024]{1,0:T(8,128)(2,1)S(1)}, bf16[32,1024]{1,0:T(8,128)(2,1)S(1)}, u32[]{:S(2)}, u32[]{:S(2)}) collective-permute-start(bf16[32,1024]{1,0:T(8,128)(2,1)S(1)} %get-tuple-element.28), channel_id=1, source_target_pairs={{0,1},{1,0},{2,3},{3,2},{4,5},{5,4},{6,7},{7,6},{8,9},{9,8},{10,11... | collective-permute-start | bytes 196616 | tf_op jit(solution)/shard_map/ppermute | solution.py:22

commit v3 on v0

--- a/solution.py
+++ b/solution.py
@@ -35,7 +35,8 @@
     parts = {0: value}
     mask = lax.axis_size(axis) // 2
     while mask:
-        parts.update({slot ^ mask: hop(part, axis, mask) for slot, part in parts.items()})
+        for slot, part in list(parts.items()):
+            parts[slot ^ mask] = hop(part, axis, mask)
         mask //= 2
     return parts
 
@@ -59,10 +60,109 @@
         return jnp.einsum(form, rows, weight_of(mask), preferred_element_type=jnp.float32)
 
     sent = {mask: product(mask).astype(jnp.bfloat16) for mask in range(1, count)}
-    came = [hop(sent[mask], "seq", mask) for mask in sent]
-    if narrow:
-        return [term.transpose(0, 2, 1) for term in [product(0)] + came]
-    return [product(0)] + came
+    terms = [product(0)] + [hop(sent[mask], "seq", mask) for mask in sent]
+    return [term.transpose(0, 2, 1) for term in terms] if narrow else terms
+
+
+def project_kernel(pieces, chunks, ready, finish, index_ref, *refs):
+    rows_refs, weight_ref, refs = refs[:pieces], refs[pieces], refs[pieces + 1 :]
+    refs, (held, sems) = refs[:-2], refs[-2:]
+    own = held.shape[3]
+    z = index_ref[0]
+    end = (z == 0) | (z == 3)
+    copies = []
+    for place, chunk in enumerate(chunks(z, end)):
+        lanes = pl.ds(pl.multiple_of(chunk * own, own), own)
+        copies.append(pltpu.make_async_copy(weight_ref.at[:, :, lanes], held.at[place], sems.at[place]))
+        copies[-1].start()
+    for place, copy in enumerate(copies):
+        copy.wait()
+        for stream in range(held.shape[1]):
+            for piece, rows_ref in enumerate(rows_refs):
+                size = rows_ref.shape[0]
+                product = jnp.dot(rows_ref[...], held[place, stream], preferred_element_type=jnp.float32)
+                rows = pl.ds(piece * size, size)
+                finish(refs, place, stream, rows, product, ready(refs, stream, rows, end))
+
+
+def no_terms(refs, stream, rows, end):
+    return None
+
+
+def finish_first(refs, place, stream, rows, product, added):
+    low = product.astype(jnp.bfloat16)
+    refs[0][place, stream, rows] = low
+    if place:
+        refs[1][stream, rows] = low
+
+
+def relayed_terms(refs, stream, rows, end):
+    return jnp.where(end, 0.0, refs[0][0, stream, rows].astype(jnp.float32))
+
+
+def own_terms(refs, stream, rows, end):
+    came = refs[0]
+    first = came[0, stream, rows].astype(jnp.float32)
+    second = came[1, stream, rows].astype(jnp.float32)
+    return jnp.where(end, first, second) + refs[1][stream, rows].astype(jnp.float32)
+
+
+def finish_sum(refs, place, stream, rows, product, added):
+    refs[-1][stream, rows] = (product + added).astype(refs[-1].dtype)
+
+
+def first_chunks(z, end):
+    return [z ^ jnp.where(end, 3, 1), z ^ jnp.where(end, 1, 3)]
+
+
+def third_chunk(z, end):
+    return [z ^ 2]
+
+
+def own_chunk(z, end):
+    return [z]
+
+
+def project(pieces, weight, z, chunks, count, terms, outs, ready, finish):
+    vmem = pl.BlockSpec(memory_space=pltpu.VMEM)
+    streams, depth, channels = weight.shape
+    own = channels // lax.axis_size("seq")
+    rows = sum(piece.shape[0] for piece in pieces)
+    return pl.pallas_call(
+        functools.partial(project_kernel, len(pieces), chunks, ready, finish),
+        out_shape=outs,
+        in_specs=[pl.BlockSpec(memory_space=pltpu.SMEM)]
+        + [vmem] * len(pieces)
+        + [pl.BlockSpec(memory_space=pl.ANY)]
+        + [vmem] * len(terms),
+        out_specs=[vmem] * len(outs),
+        scratch_shapes=[
+            pltpu.VMEM((count, streams, depth, own), weight.dtype),
+            pltpu.SemaphoreType.DMA((count,)),
+        ],
+        cost_estimate=pl.CostEstimate(
+            flops=2 * rows * depth * streams * own * count,
+            bytes_accessed=2 * depth * streams * own * count,
+            transcendentals=0,
+        ),
+    )(z.reshape(1).astype(jnp.int32), *pieces, weight, *terms)
+
+
+def relay_sum(pieces, weight):
+    z = lax.axis_index("seq")
+    streams, _, channels = weight.shape
+    rows = sum(piece.shape[0] for piece in pieces)
+    shape = (streams, rows, channels // 4)
+    low = jax.ShapeDtypeStruct(shape, jnp.bfloat16)
+    outs = [jax.ShapeDtypeStruct((2, *shape), jnp.bfloat16), low]
+    both, second = project(pieces, weight, z, first_chunks, 2, [], outs, no_terms, finish_first)
+    came = hop(both, "seq", 1)
+    middle = lax.ppermute(second, "seq", [(1, 2), (2, 1)])
+    (merged,) = project(pieces, weight, z, third_chunk, 1, [came], [low], relayed_terms, finish_sum)
+    last = hop(merged, "seq", 2)
+    outs = [jax.ShapeDtypeStruct(shape, jnp.float32)]
+    (total,) = project(pieces, weight, z, own_chunk, 1, [came, middle], outs, own_terms, finish_sum)
+    return [total, last]
 
 
 def tables(block):
@@ -130,8 +230,8 @@
     out_ref[...] = wide_dot(high_ref[...], low_ref[...], taps_ref[...], ((1,), (1,)))
 
 
-def local_kernel(groups, seq, sub, t_ref, taps_ref, *refs):
-    count = seq * len(groups)
+def local_kernel(groups, each, seq, sub, t_ref, taps_ref, *refs):
+    count = each * len(groups)
     moved = count + 5
     sources, outs = refs[:moved], refs[moved : moved + 2]
     proj, gated, sems = refs[moved + 2 : moved + 5]
@@ -151,8 +251,8 @@
 
     proj[:, :8] = jnp.zeros((proj.shape[0], 8, proj.shape[2]), jnp.float32)
     for group, slots in enumerate(groups):
-        mine = terms[group * seq : (group + 1) * seq]
-        for copy in copies[group * seq : (group + 1) * seq]:
+        mine = terms[group * each : (group + 1) * each]
+        for copy in copies[group * each : (group + 1) * each]:
             copy.wait()
         for position, slot in enumerate(slots):
             for source in range(seq):
@@ -202,7 +302,7 @@
     lines = length // 2
     moved = [*flat, *wide[:2], spectrum, *wide[2:]]
     return pl.pallas_call(
-        functools.partial(local_kernel, groups, seq, sub),
+        functools.partial(local_kernel, groups, len(terms[0]), seq, sub),
         out_shape=[jax.ShapeDtypeStruct((lines, own), jnp.bfloat16)] * 2,
         in_specs=[pl.BlockSpec(memory_space=pltpu.SMEM), vmem] + [pl.BlockSpec(memory_space=pl.ANY)] * len(moved),
         out_specs=[vmem] * 2,
@@ -267,12 +367,17 @@
     normed = (whole * lax.rsqrt(mean_sq + EPSILON) * norm_gain).astype(jnp.bfloat16)
     normed = exchange(normed.reshape(sub, seq, depth).transpose(1, 0, 2), "seq")
     parts = spread(normed.reshape(seq * sub, depth), "tensor")
-    groups = (tuple(slots[:1]), tuple(slots[1:]))
+    groups = (tuple(slots[:2]), tuple(slots[2:]))
     terms = []
+    aligned = own % 128 == 0 and length <= BLOCK and sub % 16 == 0
     for group in groups:
-        terms.append(sum_over_seq(jnp.concatenate([parts[slot] for slot in group]), in_part))
+        pieces = [parts[slot] for slot in group]
+        if seq == 4 and aligned:
+            terms.append(relay_sum(pieces, in_weight))
+        else:
+            terms.append(sum_over_seq(jnp.concatenate(pieces), in_part))
     half = tensor // 2
-    if own % 128 == 0 and length <= BLOCK and sub % 16 == 0:
+    if aligned:
         lower_gated, upper_gated = local_stage(groups, terms, taps, long_filter, t, seq, sub)
     else:
         gated = plain_stage(terms, taps, long_filter, t, seq, sub)

time: 119 us -> 117 us (0.983)
  Pallas kernels: 8.42 us -> 30.7 us
  waiting for transfers between devices: 50.8 us -> 40.2 us
  matrix products: 11.9 us -> 1.91 us
  starting transfers between devices: 38 us -> 32.5 us
  local copies, waits for them, and re-layouts: 6.09 us -> 7.81 us
    pallas_call x1 -> x7, Pallas kernels: 5.32 us -> 27.6 us  [the longest x6 22.6 us: project(): pl.pallas_call(functools.partial(project_kernel, len(pieces), chunks, rea...]
    ppermute x30 -> x28, waiting for transfers between devices: 50.8 us -> 40.2 us  [hop(): return lax.ppermute(value, axis, [(a, a ^ mask) for a in range(count)])]
    dot_general x8 -> x0, matrix products: 8.83 us -> none  [product(): jnp.einsum(form, rows, weight_of(mask), preferred_element_type=jnp.float32)]
    ppermute x30 -> x28, starting transfers between devices: 38 us -> 31.2 us  [hop(): return lax.ppermute(value, axis, [(a, a ^ mask) for a in range(count)])]
    unnamed x25 -> x33, local copies, waits for them, and re-layouts: 1.65 us -> 6.04 us
    dynamic_slice x1, local copies, waits for them, and re-layouts: 2.22 us -> 0.18 us  [shards(): lax.dynamic_slice_in_dim(out_weight, (z ^ mask) * own, own, 1)]
    ppermute x0 -> x2, starting transfers between devices: none -> 1.33 us  [relay_sum(): middle = lax.ppermute(second, 'seq', [(1, 2), (2, 1)])]
  transfers between devices with their start and end apart: 30 -> 30, of which waited for: 16 -> 14; matrix products, arithmetic and copies ran while one was open for 13% -> 3% of each run, Pallas kernels for 3% -> 22%
where the time goes in v3:
time: 117 us; the launch traced here: 116 us
  waiting for transfers between devices  40.2 us (34%)
  starting transfers between devices  32.5 us (28%)
  Pallas kernels  30.7 us (26%)
  local copies, waits for them, and re-layouts  7.81 us (7%)
  other arithmetic  2.52 us (2%)
  matrix products  1.91 us (2%)
    ppermute x28, waiting for transfers between devices, hop(): return lax.ppermute(value, axis, [(a, a ^ mask) for a in range(count)])  40.2 us
    ppermute x28, starting transfers between devices, hop(): return lax.ppermute(value, axis, [(a, a ^ mask) for a in range(count)])  31.2 us
    pallas_call x6, Pallas kernels, project(): pl.pallas_call(functools.partial(project_kernel, len(pieces), chunks, rea...  22.6 us
    unnamed x33, local copies, waits for them, and re-layouts  6.04 us
    pallas_call x1, Pallas kernels, local_stage(): pl.pallas_call(functools.partial(local_kernel, groups, len(terms[0]), seq...  4.95 us
    pallas_call x1, Pallas kernels, local_stage(): spectrum = make_spectrum(*wide[:2], long_filter)  3.14 us
  transfers between devices with their start and end apart: 30, of which 14 were waited for; matrix products, arithmetic and copies ran while one was open for 3% of the time, Pallas kernels for 22%

profile of v3, /device:TPU:0, one launch (start us, length us, event | category | flops | bytes accessed | tf_op | source)
XLA Modules:
  0.0 116.1 jit_solution(17861563153847082385)
XLA Ops:
  0.0 1.1 convert_element_type.41
  1.1 2.5 %collective-permute-start.2 = (bf16[32,1024]{1,0:T(8,128)(2,1)S(1)}, bf16[32,1024]{1,0:T(8,128)(2,1)S(1)}, u32[]{:S(2)}, u32[]{:S(2)}) collective-permute-start(bf16[32,1024]{1,0:T(8,128)(2,1)S(1)} %get-tuple-element.50), channel_id=1, source_target_pairs={{0,3},{1,2},{2,1},{3,0},{4,7},{5,6},{6,5},{7,4},{8,11},{9,10},{10,... | collective-permute-start | bytes 196616 | tf_op jit(solution)/shard_map/ppermute | solution.py:22
  3.6 0.6 collective-permute-start.1
  4.3 0.7 mul.44
  5.0 1.1 collective-permute-done.2
  6.1 2.2 %collective-permute-done.1 = bf16[32,1024]{1,0:T(8,128)(2,1)S(1)} collective-permute-done((bf16[32,1024]{1,0:T(8,128)(2,1)S(1)}, bf16[32,1024]{1,0:T(8,128)(2,1)S(1)}, u32[]{:S(2)}, u32[]{:S(2)}) %collective-permute-start.1) | collective-permute-done | bytes 65568 | tf_op jit(solution)/shard_map/ppermute | solution.py:22
  8.4 0.2 fusion.3
  8.7 3.9 %collective-permute-start.5 = (bf16[32,1024]{1,0:T(8,128)(2,1)S(1)}, bf16[32,1024]{1,0:T(8,128)(2,1)S(1)}, u32[]{:S(2)}, u32[]{:S(2)}) collective-permute-start(bf16[32,1024]{1,0:T(8,128)(2,1)S(1)} %get-tuple-element.42), channel_id=1, source_target_pairs={{0,12},{4,8},{8,4},{12,0},{1,13},{5,9},{9,5},{13,1},{2,14},{6,10},... | collective-permute-start | bytes 196616 | tf_op jit(solution)/shard_map/ppermute | solution.py:22
  12.6 0.6 collective-permute-start.3
  13.2 1.9 %collective-permute-done.5 = bf16[32,1024]{1,0:T(8,128)(2,1)S(1)} collective-permute-done((bf16[32,1024]{1,0:T(8,128)(2,1)S(1)}, bf16[32,1024]{1,0:T(8,128)(2,1)S(1)}, u32[]{:S(2)}, u32[]{:S(2)}) %collective-permute-start.5) | collective-permute-done | bytes 65568 | tf_op jit(solution)/shard_map/ppermute | solution.py:22
  15.1 3.3 %collective-permute-done.4 = bf16[32,1024]{1,0:T(8,128)(2,1)S(1)} collective-permute-done((bf16[32,1024]{1,0:T(8,128)(2,1)S(1)}, bf16[32,1024]{1,0:T(8,128)(2,1)S(1)}, u32[]{:S(2)}, u32[]{:S(2)}) %collective-permute-start.4) | collective-permute-done | bytes 65568 | tf_op jit(solution)/shard_map/ppermute | solution.py:22
  18.5 1.6 %collective-permute-start.10 = (bf16[128,1024]{1,0:T(8,128)(2,1)S(1)}, bf16[128,1024]{1,0:T(8,128)(2,1)S(1)}, u32[]{:S(2)}, u32[]{:S(2)}) collective-permute-start(bf16[128,1024]{1,0:T(8,128)(2,1)S(1)} %bitcast.44), channel_id=1, source_target_pairs={{0,2},{1,3},{2,0},{3,1},{4,6},{5,7},{6,4},{7,5},{8,10},{9,11},{10,... | collective-permute-start | bytes 786440 | tf_op jit(solution)/shard_map/ppermute | solution.py:22
  20.2 6.3 %collective-permute-done.10.refs_0_ = bf16[128,1024]{1,0:T(8,128)(2,1)S(1)} collective-permute-done((bf16[128,1024]{1,0:T(8,128)(2,1)S(1)}, bf16[128,1024]{1,0:T(8,128)(2,1)S(1)}, u32[]{:S(2)}, u32[]{:S(2)}) %collective-permute-start.10) | collective-permute-done | bytes 262176 | tf_op jit(solution)/shard_map/ppermute | solution.py:22
  26.5 0.7 copy-done.4
  27.2 4.1 %shard_map.100 = (bf16[2,3,256,128]{3,2,1,0:T(8,128)(2,1)}, bf16[3,256,128]{2,1,0:T(8,128)(2,1)}) custom-call(s32[1]{0:T(128)} %bitcast.1.index_ref, bf16[128,1024]{1,0:T(8,128)(2,1)} %bitcast.46, bf16[128,1024]{1,0:T(8,128)(2,1)} %copy-done.4, bf16[3,1024,512]{2,1,0:T(8,128)(2,1)} %refs_2_.11), custom_call_target="tpu_custom_call" | custom-call | flops 402653184 | bytes 1572864 | tf_op jit(solution)/shard_map/pallas_call | solution.py:131
  31.3 0.3 collective-permute-start.7
  31.7 0.7 copy-done.3
  32.4 4.1 %shard_map.103 = (bf16[2,3,256,128]{3,2,1,0:T(8,128)(2,1)}, bf16[3,256,128]{2,1,0:T(8,128)(2,1)}) custom-call(s32[1]{0:T(128)} %bitcast.1.index_ref, bf16[128,1024]{1,0:T(8,128)(2,1)} %copy-done.2, bf16[128,1024]{1,0:T(8,128)(2,1)} %copy-done.3, bf16[3,1024,512]{2,1,0:T(8,128)(2,1)} %refs_2_.11), custom_call_target="tpu_custom_call" | custom-call | flops 402653184 | bytes 1572864 | tf_op jit(solution)/shard_map/pallas_call | solution.py:131
  36.5 1.8 %collective-permute-start.12 = (bf16[2,3,256,128]{3,2,1,0:T(8,128)(2,1)}, bf16[2,3,256,128]{3,2,1,0:T(8,128)(2,1)S(1)}, u32[]{:S(2)}, u32[]{:S(2)}) collective-permute-start(bf16[2,3,256,128]{3,2,1,0:T(8,128)(2,1)} %get-tuple-element.13), channel_id=1, source_target_pairs={{0,4},{4,0},{8,12},{12,8},{1,5},{5,1},{9,13},{13,9},{2,6},{6,2},{1... | collective-permute-start | bytes 1179656 | tf_op jit(solution)/shard_map/ppermute | solution.py:22
  38.4 0.6 constant_dynamic-slice_fusion.24.taps_ref
  39.0 0.7 collective-permute-start.8
  39.6 0.7 collective-permute-start.13
  40.3 3.3 %collective-permute-done.7.refs_3_ = bf16[2,3,256,128]{3,2,1,0:T(8,128)(2,1)S(1)} collective-permute-done((bf16[2,3,256,128]{3,2,1,0:T(8,128)(2,1)}, bf16[2,3,256,128]{3,2,1,0:T(8,128)(2,1)S(1)}, u32[]{:S(2)}, u32[]{:S(2)}) %collective-permute-start.7) | collective-permute-done | bytes 393248 | tf_op jit(solution)/shard_map/ppermute | solution.py:22
  43.6 0.8 copy-done.6
  44.4 3.5 %shard_map.102 = bf16[3,256,128]{2,1,0:T(8,128)(2,1)} custom-call(s32[1]{0:T(128)} %bitcast.1.index_ref, bf16[128,1024]{1,0:T(8,128)(2,1)} %bitcast.47, bf16[128,1024]{1,0:T(8,128)(2,1)} %copy-done.4, bf16[3,1024,512]{2,1,0:T(8,128)(2,1)} %refs_2_.11, bf16[2,3,256,128]{3,2,1,0:T(8,128)(2,1)} %copy-done.6), custom_call_target="tpu_custom_call" | custom-call | flops 201326592 | bytes 786432 | tf_op jit(solution)/shard_map/pallas_call | solution.py:131
  47.9 1.9 %collective-permute-start.9 = (bf16[3,256,128]{2,1,0:T(8,128)(2,1)}, bf16[3,256,128]{2,1,0:T(8,128)(2,1)S(1)}, u32[]{:S(2)}, u32[]{:S(2)}) collective-permute-start(bf16[3,256,128]{2,1,0:T(8,128)(2,1)} %shard_map.102), channel_id=1, source_target_pairs={{0,8},{4,12},{8,0},{12,4},{1,9},{5,13},{9,1},{13,5},{2,10},{6,14},... | collective-permute-start | bytes 589832 | tf_op jit(solution)/shard_map/ppermute | solution.py:22
  49.8 2.4 %collective-permute-done.12.refs_3_ = bf16[2,3,256,128]{3,2,1,0:T(8,128)(2,1)S(1)} collective-permute-done((bf16[2,3,256,128]{3,2,1,0:T(8,128)(2,1)}, bf16[2,3,256,128]{3,2,1,0:T(8,128)(2,1)S(1)}, u32[]{:S(2)}, u32[]{:S(2)}) %collective-permute-start.12) | collective-permute-done | bytes 393248 | tf_op jit(solution)/shard_map/ppermute | solution.py:22
  52.2 0.8 copy-done.7
  52.9 3.5 %shard_map.105 = bf16[3,256,128]{2,1,0:T(8,128)(2,1)} custom-call(s32[1]{0:T(128)} %bitcast.1.index_ref, bf16[128,1024]{1,0:T(8,128)(2,1)} %copy-done.2, bf16[128,1024]{1,0:T(8,128)(2,1)} %copy-done.3, bf16[3,1024,512]{2,1,0:T(8,128)(2,1)} %refs_2_.11, bf16[2,3,256,128]{3,2,1,0:T(8,128)(2,1)} %copy-done.7), custom_call_target="tpu_custom_call" | custom-call | flops 201326592 | bytes 786432 | tf_op jit(solution)/shard_map/pallas_call | solution.py:131
  56.5 0.3 collective-permute-start.14
  56.8 3.1 %filter_spectrum.1.refs_6_ = f32[1024,128]{1,0:T(8,128)} custom-call(bf16[1024,512]{1,0:T(8,128)(2,1)} %constant.101.clone.high_ref.refs_4_, bf16[1024,512]{1,0:T(8,128)(2,1)} %constant.102.clone.low_ref.refs_5_, f32[128,512]{1,0:T(8,128)} %taps_ref.1), custom_call_target="tpu_custom_call" | custom-call | flops 402653184 | bytes 1048576 | tf_op jit(solution)/shard_map/filter_spectrum/pallas_call | solution.py:300
  59.9 0.2 constant_dynamic-slice_fusion.13
  60.1 0.7 copy-done.12
  60.8 3.7 %shard_map.101.refs_0_ = f32[3,256,128]{2,1,0:T(8,128)} custom-call(s32[1]{0:T(128)} %bitcast.1.index_ref, bf16[128,1024]{1,0:T(8,128)(2,1)} %bitcast.48, bf16[128,1024]{1,0:T(8,128)(2,1)} %copy-done.4, bf16[3,1024,512]{2,1,0:T(8,128)(2,1)} %refs_2_.11, bf16[2,3,256,128]{3,2,1,0:T(8,128)(2,1)} %copy-done.6, bf16[3,256,128]{2,1,0:T(8,128)(2,1)} %copy-done.12), custom_call_target="tpu_custom_call" | custom-call | flops 201326592 | bytes 786432 | tf_op jit(solution)/shard_map/pallas_call | solution.py:131
  64.5 0.7 copy-done.11
  65.2 3.7 %shard_map.104.refs_2_ = f32[3,256,128]{2,1,0:T(8,128)} custom-call(s32[1]{0:T(128)} %bitcast.1.index_ref, bf16[128,1024]{1,0:T(8,128)(2,1)} %copy-done.2, bf16[128,1024]{1,0:T(8,128)(2,1)} %copy-done.3, bf16[3,1024,512]{2,1,0:T(8,128)(2,1)} %refs_2_.11, bf16[2,3,256,128]{3,2,1,0:T(8,128)(2,1)} %copy-done.7, bf16[3,256,128]{2,1,0:T(8,128)(2,1)} %copy-done.11), custom_call_target="tpu_custom_call" | custom-call | flops 201326592 | bytes 786432 | tf_op jit(solution)/shard_map/pallas_call | solution.py:131
  68.9 0.7 copy-done.9
  69.6 5.0 %filters.1 = (bf16[256,128]{1,0:T(8,128)(2,1)}, bf16[256,128]{1,0:T(8,128)(2,1)}) custom-call(s32[1]{0:T(128)} %bitcast.t_ref, f32[3,3,128]{2,1,0:T(4,128)} %constant_dynamic-slice_fusion.24.taps_ref, f32[3,256,128]{2,1,0:T(8,128)} %shard_map.101.refs_0_, bf16[3,256,128]{2,1,0:T(8,128)(2,1)} %copy-done.9, f32[3,256,128]{2,1,0:T(8,128)} %shard_map.104.refs_2_, ...), custom_call_target="tpu_custom_call" | custom-call | flops 805306368 | bytes 2097152 | tf_op jit(solution)/shard_map/filters/pallas_call | solution.py:304
  74.6 2.4 %collective-permute-start.19 = (bf16[256,128]{1,0:T(8,128)(2,1)}, bf16[256,128]{1,0:T(8,128)(2,1)S(1)}, u32[]{:S(2)}, u32[]{:S(2)}) collective-permute-start(bf16[256,128]{1,0:T(8,128)(2,1)} %get-tuple-element.16), channel_id=1, source_target_pairs={{0,4},{4,0},{8,12},{12,8},{1,5},{5,1},{9,13},{13,9},{2,6},{6,2},{1... | collective-permute-start | bytes 196616 | tf_op jit(solution)/shard_map/ppermute | solution.py:22
  77.0 0.4 collective-permute-start.20
  77.4 2.0 %collective-permute-start.21 = (bf16[256,128]{1,0:T(8,128)(2,1)}, bf16[256,128]{1,0:T(8,128)(2,1)S(1)}, u32[]{:S(2)}, u32[]{:S(2)}) collective-permute-start(bf16[256,128]{1,0:T(8,128)(2,1)} %get-tuple-element.16), channel_id=1, source_target_pairs={{0,12},{4,8},{8,4},{12,0},{1,13},{5,9},{9,5},{13,1},{2,14},{6,10},... | collective-permute-start | bytes 196616 | tf_op jit(solution)/shard_map/ppermute | solution.py:22
  79.4 1.0 collective-permute-start.15
  80.5 1.3 %collective-permute-start.16 = (bf16[256,128]{1,0:T(8,128)(2,1)}, bf16[256,128]{1,0:T(8,128)(2,1)S(1)}, u32[]{:S(2)}, u32[]{:S(2)}) collective-permute-start(bf16[256,128]{1,0:T(8,128)(2,1)} %get-tuple-element.15), channel_id=1, source_target_pairs={{0,8},{4,12},{8,0},{12,4},{1,9},{5,13},{9,1},{13,5},{2,10},{6,14},... | collective-permute-start | bytes 196616 | tf_op jit(solution)/shard_map/ppermute | solution.py:22
  81.8 0.9 constant_dynamic-update-slice_fusion.3
  82.7 2.1 %collective-permute-start.17 = (bf16[256,128]{1,0:T(8,128)(2,1)}, bf16[256,128]{1,0:T(8,128)(2,1)S(1)}, u32[]{:S(2)}, u32[]{:S(2)}) collective-permute-start(bf16[256,128]{1,0:T(8,128)(2,1)} %get-tuple-element.15), channel_id=1, source_target_pairs={{0,12},{4,8},{8,4},{12,0},{1,13},{5,9},{9,5},{13,1},{2,14},{6,10},... | collective-permute-start | bytes 196616 | tf_op jit(solution)/shard_map/ppermute | solution.py:22
  84.8 0.7 collective-permute-done.20
  85.6 0.5 convolution_convert_fusion
  86.2 3.5 %collective-permute-done.16 = bf16[256,128]{1,0:T(8,128)(2,1)S(1)} collective-permute-done((bf16[256,128]{1,0:T(8,128)(2,1)}, bf16[256,128]{1,0:T(8,128)(2,1)S(1)}, u32[]{:S(2)}, u32[]{:S(2)}) %collective-permute-start.16) | collective-permute-done | bytes 65568 | tf_op jit(solution)/shard_map/ppermute | solution.py:22
  89.7 0.5 convolution_convert_fusion.1
  90.3 0.5 fusion.2
  90.8 1.7 %collective-permute-start.23 = (bf16[128,1024]{1,0:T(8,128)(2,1)S(1)}, bf16[128,1024]{1,0:T(8,128)(2,1)S(1)}, u32[]{:S(2)}, u32[]{:S(2)}) collective-permute-start(bf16[128,1024]{1,0:T(8,128)(2,1)S(1)} %fusion.2), channel_id=1, source_target_pairs={{0,2},{1,3},{2,0},{3,1},{4,6},{5,7},{6,4},{7,5},{8,10},{9,11},{10,... | collective-permute-start | bytes 786440 | tf_op jit(solution)/shard_map/ppermute | solution.py:22
  92.5 7.1 %collective-permute-done.23 = bf16[128,1024]{1,0:T(8,128)(2,1)S(1)} collective-permute-done((bf16[128,1024]{1,0:T(8,128)(2,1)S(1)}, bf16[128,1024]{1,0:T(8,128)(2,1)S(1)}, u32[]{:S(2)}, u32[]{:S(2)}) %collective-permute-start.23) | collective-permute-done | bytes 262176 | tf_op jit(solution)/shard_map/ppermute | solution.py:22
  99.6 0.5 fusion.1
  100.1 2.0 %collective-permute-start.26 = (bf16[32,1024]{1,0:T(8,128)(2,1)S(1)}, bf16[32,1024]{1,0:T(8,128)(2,1)S(1)}, u32[]{:S(2)}, u32[]{:S(2)}) collective-permute-start(bf16[32,1024]{1,0:T(8,128)(2,1)S(1)} %get-tuple-element.34), channel_id=1, source_target_pairs={{0,12},{4,8},{8,4},{12,0},{1,13},{5,9},{9,5},{13,1},{2,14},{6,10},... | collective-permute-start | bytes 196616 | tf_op jit(solution)/shard_map/ppermute | solution.py:22
  102.1 0.7 collective-permute-start.25
  102.9 1.7 %collective-permute-start.24 = (bf16[32,1024]{1,0:T(8,128)(2,1)S(1)}, bf16[32,1024]{1,0:T(8,128)(2,1)S(1)}, u32[]{:S(2)}, u32[]{:S(2)}) collective-permute-start(bf16[32,1024]{1,0:T(8,128)(2,1)S(1)} %get-tuple-element.36), channel_id=1, source_target_pairs={{0,4},{4,0},{8,12},{12,8},{1,5},{5,1},{9,13},{13,9},{2,6},{6,2},{1... | collective-permute-start | bytes 196616 | tf_op jit(solution)/shard_map/ppermute | solution.py:22
  104.6 1.9 %collective-permute-done.26 = bf16[32,1024]{1,0:T(8,128)(2,1)S(1)} collective-permute-done((bf16[32,1024]{1,0:T(8,128)(2,1)S(1)}, bf16[32,1024]{1,0:T(8,128)(2,1)S(1)}, u32[]{:S(2)}, u32[]{:S(2)}) %collective-permute-start.26) | collective-permute-done | bytes 65568 | tf_op jit(solution)/shard_map/ppermute | solution.py:22
  106.5 2.6 %collective-permute-done.25 = bf16[32,1024]{1,0:T(8,128)(2,1)S(1)} collective-permute-done((bf16[32,1024]{1,0:T(8,128)(2,1)S(1)}, bf16[32,1024]{1,0:T(8,128)(2,1)S(1)}, u32[]{:S(2)}, u32[]{:S(2)}) %collective-permute-start.25) | collective-permute-done | bytes 65568 | tf_op jit(solution)/shard_map/ppermute | solution.py:22
  109.3 0.8 collective-permute-start.29
  110.0 1.0 collective-permute-start.28
  111.0 0.2 collective-permute-start.27
  111.2 2.3 %collective-permute-done.29 = bf16[32,1024]{1,0:T(8,128)(2,1)S(1)} collective-permute-done((bf16[32,1024]{1,0:T(8,128)(2,1)S(1)}, bf16[32,1024]{1,0:T(8,128)(2,1)S(1)}, u32[]{:S(2)}, u32[]{:S(2)}) %collective-permute-start.29) | collective-permute-done | bytes 65568 | tf_op jit(solution)/shard_map/ppermute | solution.py:22
  113.5 1.6 %collective-permute-done.28 = bf16[32,1024]{1,0:T(8,128)(2,1)S(1)} collective-permute-done((bf16[32,1024]{1,0:T(8,128)(2,1)S(1)}, bf16[32,1024]{1,0:T(8,128)(2,1)S(1)}, u32[]{:S(2)}, u32[]{:S(2)}) %collective-permute-start.28) | collective-permute-done | bytes 65568 | tf_op jit(solution)/shard_map/ppermute | solution.py:22
  115.3 0.9 convert_add_fusion
  (66 shorter events, 1.1 us)
Async XLA Ops:
  0.0 38.4 %copy-start = (f32[3,3,512]{2,1,0:T(4,128)S(1)}, f32[3,3,512]{2,1,0:T(4,128)}, u32[]{:S(2)}) copy-start(f32[3,3,512]{2,1,0:T(4,128)} %param.13) | copy-start | bytes 55300
  1.1 5.0 %collective-permute-start.2 = (bf16[32,1024]{1,0:T(8,128)(2,1)S(1)}, bf16[32,1024]{1,0:T(8,128)(2,1)S(1)}, u32[]{:S(2)}, u32[]{:S(2)}) collective-permute-start(bf16[32,1024]{1,0:T(8,128)(2,1)S(1)} %get-tuple-element.50), channel_id=1, source_target_pairs={{0,3},{1,2},{2,1},{3,0},{4,7},{5,6},{6,5},{7,4},{8,11},{9,10},{10,... | collective-permute-start | bytes 196616 | tf_op jit(solution)/shard_map/ppermute | solution.py:22
  3.6 4.7 %collective-permute-start.1 = (bf16[32,1024]{1,0:T(8,128)(2,1)S(1)}, bf16[32,1024]{1,0:T(8,128)(2,1)S(1)}, u32[]{:S(2)}, u32[]{:S(2)}) collective-permute-start(bf16[32,1024]{1,0:T(8,128)(2,1)S(1)} %get-tuple-element.51), channel_id=1, source_target_pairs={{0,2},{1,3},{2,0},{3,1},{4,6},{5,7},{6,4},{7,5},{8,10},{9,11},{10,... | collective-permute-start | bytes 196616 | tf_op jit(solution)/shard_map/ppermute | solution.py:22
  4.3 4.0 %collective-permute-start = (bf16[32,1024]{1,0:T(8,128)(2,1)S(1)}, bf16[32,1024]{1,0:T(8,128)(2,1)S(1)}, u32[]{:S(2)}, u32[]{:S(2)}) collective-permute-start(bf16[32,1024]{1,0:T(8,128)(2,1)S(1)} %get-tuple-element.52), channel_id=1, source_target_pairs={{0,1},{1,0},{2,3},{3,2},{4,5},{5,4},{6,7},{7,6},{8,9},{9,8},{10,11... | collective-permute-start | bytes 196616 | tf_op jit(solution)/shard_map/ppermute | solution.py:22
  8.7 6.4 %collective-permute-start.5 = (bf16[32,1024]{1,0:T(8,128)(2,1)S(1)}, bf16[32,1024]{1,0:T(8,128)(2,1)S(1)}, u32[]{:S(2)}, u32[]{:S(2)}) collective-permute-start(bf16[32,1024]{1,0:T(8,128)(2,1)S(1)} %get-tuple-element.42), channel_id=1, source_target_pairs={{0,12},{4,8},{8,4},{12,0},{1,13},{5,9},{9,5},{13,1},{2,14},{6,10},... | collective-permute-start | bytes 196616 | tf_op jit(solution)/shard_map/ppermute | solution.py:22
  12.6 5.8 %collective-permute-start.4 = (bf16[32,1024]{1,0:T(8,128)(2,1)S(1)}, bf16[32,1024]{1,0:T(8,128)(2,1)S(1)}, u32[]{:S(2)}, u32[]{:S(2)}) collective-permute-start(bf16[32,1024]{1,0:T(8,128)(2,1)S(1)} %get-tuple-element.43), channel_id=1, source_target_pairs={{0,8},{4,12},{8,0},{12,4},{1,9},{5,13},{9,1},{13,5},{2,10},{6,14},... | collective-permute-start | bytes 196616 | tf_op jit(solution)/shard_map/ppermute | solution.py:22
  12.6 5.8 %collective-permute-start.3 = (bf16[32,1024]{1,0:T(8,128)(2,1)S(1)}, bf16[32,1024]{1,0:T(8,128)(2,1)S(1)}, u32[]{:S(2)}, u32[]{:S(2)}) collective-permute-start(bf16[32,1024]{1,0:T(8,128)(2,1)S(1)} %get-tuple-element.44), channel_id=1, source_target_pairs={{0,4},{4,0},{8,12},{12,8},{1,5},{5,1},{9,13},{13,9},{2,6},{6,2},{1... | collective-permute-start | bytes 196616 | tf_op jit(solution)/shard_map/ppermute | solution.py:22
  18.5 8.0 %copy-start.1 = (bf16[4,32,1024]{2,1,0:T(8,128)(2,1)}, bf16[4,32,1024]{2,1,0:T(8,128)(2,1)S(1)}, u32[]{:S(2)}) copy-start(bf16[4,32,1024]{2,1,0:T(8,128)(2,1)S(1)} %pad_maximum_fusion.4) | copy-start | bytes 786436
  18.5 7.9 %collective-permute-start.10 = (bf16[128,1024]{1,0:T(8,128)(2,1)S(1)}, bf16[128,1024]{1,0:T(8,128)(2,1)S(1)}, u32[]{:S(2)}, u32[]{:S(2)}) collective-permute-start(bf16[128,1024]{1,0:T(8,128)(2,1)S(1)} %bitcast.44), channel_id=1, source_target_pairs={{0,2},{1,3},{2,0},{3,1},{4,6},{5,7},{6,4},{7,5},{8,10},{9,11},{10,... | collective-permute-start | bytes 786440 | tf_op jit(solution)/shard_map/ppermute | solution.py:22
  20.2 6.3 %collective-permute-start.6 = (bf16[128,1024]{1,0:T(8,128)(2,1)S(1)}, bf16[128,1024]{1,0:T(8,128)(2,1)S(1)}, u32[]{:S(2)}, u32[]{:S(2)}) collective-permute-start(bf16[128,1024]{1,0:T(8,128)(2,1)S(1)} %bitcast.45), channel_id=1, source_target_pairs={{0,1},{1,0},{2,3},{3,2},{4,5},{5,4},{6,7},{7,6},{8,9},{9,8},{10,11... | collective-permute-start | bytes 786440 | tf_op jit(solution)/shard_map/ppermute | solution.py:22
  26.5 5.2 %copy-start.2 = (bf16[128,1024]{1,0:T(8,128)(2,1)}, bf16[128,1024]{1,0:T(8,128)(2,1)S(1)}, u32[]{:S(2)}) copy-start(bf16[128,1024]{1,0:T(8,128)(2,1)S(1)} %collective-permute-done.10.refs_0_) | copy-start | bytes 786436
  26.5 5.2 %collective-permute-start.11 = (bf16[128,1024]{1,0:T(8,128)(2,1)S(1)}, bf16[128,1024]{1,0:T(8,128)(2,1)S(1)}, u32[]{:S(2)}, u32[]{:S(2)}) collective-permute-start(bf16[128,1024]{1,0:T(8,128)(2,1)S(1)} %collective-permute-done.10.refs_0_), channel_id=1, source_target_pairs={{0,1},{1,0},{2,3},{3,2},{4,5},{5,4},{6,7},{7,6},{8,9},{9,8},{10,11... | collective-permute-start | bytes 786440 | tf_op jit(solution)/shard_map/ppermute | solution.py:22
  26.5 0.7 copy-start.4
  31.3 7.6 %copy-start.13 = (bf16[3,256,128]{2,1,0:T(8,128)(2,1)S(1)}, bf16[3,256,128]{2,1,0:T(8,128)(2,1)}, u32[]{:S(2)}) copy-start(bf16[3,256,128]{2,1,0:T(8,128)(2,1)} %get-tuple-element.12) | copy-start | bytes 589828
  31.3 12.3 %collective-permute-start.7 = (bf16[2,3,256,128]{3,2,1,0:T(8,128)(2,1)}, bf16[2,3,256,128]{3,2,1,0:T(8,128)(2,1)S(1)}, u32[]{:S(2)}, u32[]{:S(2)}) collective-permute-start(bf16[2,3,256,128]{3,2,1,0:T(8,128)(2,1)} %get-tuple-element.11), channel_id=1, source_target_pairs={{0,4},{4,0},{8,12},{12,8},{1,5},{5,1},{9,13},{13,9},{2,6},{6,2},{1... | collective-permute-start | bytes 1179656 | tf_op jit(solution)/shard_map/ppermute | solution.py:22
  31.7 0.7 copy-start.3
  36.5 15.6 %collective-permute-start.12 = (bf16[2,3,256,128]{3,2,1,0:T(8,128)(2,1)}, bf16[2,3,256,128]{3,2,1,0:T(8,128)(2,1)S(1)}, u32[]{:S(2)}, u32[]{:S(2)}) collective-permute-start(bf16[2,3,256,128]{3,2,1,0:T(8,128)(2,1)} %get-tuple-element.13), channel_id=1, source_target_pairs={{0,4},{4,0},{8,12},{12,8},{1,5},{5,1},{9,13},{13,9},{2,6},{6,2},{1... | collective-permute-start | bytes 1179656 | tf_op jit(solution)/shard_map/ppermute | solution.py:22
  39.0 21.2 %collective-permute-start.8 = (bf16[3,256,128]{2,1,0:T(8,128)(2,1)S(1)}, bf16[3,256,128]{2,1,0:T(8,128)(2,1)S(1)}, u32[]{:S(2)}, u32[]{:S(2)}) collective-permute-start(bf16[3,256,128]{2,1,0:T(8,128)(2,1)S(1)} %copy-done.13), channel_id=1, source_target_pairs={{4,8},{8,4},{5,9},{9,5},{6,10},{10,6},{7,11},{11,7},{20,24},{24,20... | collective-permute-start | bytes 589832 | tf_op jit(solution)/shard_map/ppermute | solution.py:160
  39.6 24.9 %collective-permute-start.13 = (bf16[3,256,128]{2,1,0:T(8,128)(2,1)}, bf16[3,256,128]{2,1,0:T(8,128)(2,1)S(1)}, u32[]{:S(2)}, u32[]{:S(2)}) collective-permute-start(bf16[3,256,128]{2,1,0:T(8,128)(2,1)} %get-tuple-element.14), channel_id=1, source_target_pairs={{4,8},{8,4},{5,9},{9,5},{6,10},{10,6},{7,11},{11,7},{20,24},{24,20... | collective-permute-start | bytes 589832 | tf_op jit(solution)/shard_map/ppermute | solution.py:160
  43.6 0.8 copy-start.6
  47.9 20.9 %collective-permute-start.9 = (bf16[3,256,128]{2,1,0:T(8,128)(2,1)}, bf16[3,256,128]{2,1,0:T(8,128)(2,1)S(1)}, u32[]{:S(2)}, u32[]{:S(2)}) collective-permute-start(bf16[3,256,128]{2,1,0:T(8,128)(2,1)} %shard_map.102), channel_id=1, source_target_pairs={{0,8},{4,12},{8,0},{12,4},{1,9},{5,13},{9,1},{13,5},{2,10},{6,14},... | collective-permute-start | bytes 589832 | tf_op jit(solution)/shard_map/ppermute | solution.py:22
  52.2 0.8 copy-start.7
  56.5 3.4 %copy-start.8 = (bf16[1024,512]{1,0:T(8,128)(2,1)S(1)}, bf16[1024,512]{1,0:T(8,128)(2,1)}, u32[]{:S(2)}) copy-start(bf16[1024,512]{1,0:T(8,128)(2,1)} %param.15) | copy-start | bytes 3145732
  56.5 12.4 %collective-permute-start.14 = (bf16[3,256,128]{2,1,0:T(8,128)(2,1)}, bf16[3,256,128]{2,1,0:T(8,128)(2,1)S(1)}, u32[]{:S(2)}, u32[]{:S(2)}) collective-permute-start(bf16[3,256,128]{2,1,0:T(8,128)(2,1)} %shard_map.105), channel_id=1, source_target_pairs={{0,8},{4,12},{8,0},{12,4},{1,9},{5,13},{9,1},{13,5},{2,10},{6,14},... | collective-permute-start | bytes 589832 | tf_op jit(solution)/shard_map/ppermute | solution.py:22
  60.1 0.7 copy-start.12
  64.5 0.7 copy-start.11
  68.8 0.7 copy-start.9
  68.9 0.7 copy-start.10
  74.6 8.1 %collective-permute-start.19 = (bf16[256,128]{1,0:T(8,128)(2,1)}, bf16[256,128]{1,0:T(8,128)(2,1)S(1)}, u32[]{:S(2)}, u32[]{:S(2)}) collective-permute-start(bf16[256,128]{1,0:T(8,128)(2,1)} %get-tuple-element.16), channel_id=1, source_target_pairs={{0,4},{4,0},{8,12},{12,8},{1,5},{5,1},{9,13},{13,9},{2,6},{6,2},{1... | collective-permute-start | bytes 196616 | tf_op jit(solution)/shard_map/ppermute | solution.py:22
  77.0 8.6 %collective-permute-start.20 = (bf16[256,128]{1,0:T(8,128)(2,1)}, bf16[256,128]{1,0:T(8,128)(2,1)S(1)}, u32[]{:S(2)}, u32[]{:S(2)}) collective-permute-start(bf16[256,128]{1,0:T(8,128)(2,1)} %get-tuple-element.16), channel_id=1, source_target_pairs={{0,8},{4,12},{8,0},{12,4},{1,9},{5,13},{9,1},{13,5},{2,10},{6,14},... | collective-permute-start | bytes 196616 | tf_op jit(solution)/shard_map/ppermute | solution.py:22
  77.4 8.2 %collective-permute-start.21 = (bf16[256,128]{1,0:T(8,128)(2,1)}, bf16[256,128]{1,0:T(8,128)(2,1)S(1)}, u32[]{:S(2)}, u32[]{:S(2)}) collective-permute-start(bf16[256,128]{1,0:T(8,128)(2,1)} %get-tuple-element.16), channel_id=1, source_target_pairs={{0,12},{4,8},{8,4},{12,0},{1,13},{5,9},{9,5},{13,1},{2,14},{6,10},... | collective-permute-start | bytes 196616 | tf_op jit(solution)/shard_map/ppermute | solution.py:22
  79.4 6.7 %collective-permute-start.15 = (bf16[256,128]{1,0:T(8,128)(2,1)}, bf16[256,128]{1,0:T(8,128)(2,1)S(1)}, u32[]{:S(2)}, u32[]{:S(2)}) collective-permute-start(bf16[256,128]{1,0:T(8,128)(2,1)} %get-tuple-element.15), channel_id=1, source_target_pairs={{0,4},{4,0},{8,12},{12,8},{1,5},{5,1},{9,13},{13,9},{2,6},{6,2},{1... | collective-permute-start | bytes 196616 | tf_op jit(solution)/shard_map/ppermute | solution.py:22
  80.5 9.2 %collective-permute-start.16 = (bf16[256,128]{1,0:T(8,128)(2,1)}, bf16[256,128]{1,0:T(8,128)(2,1)S(1)}, u32[]{:S(2)}, u32[]{:S(2)}) collective-permute-start(bf16[256,128]{1,0:T(8,128)(2,1)} %get-tuple-element.15), channel_id=1, source_target_pairs={{0,8},{4,12},{8,0},{12,4},{1,9},{5,13},{9,1},{13,5},{2,10},{6,14},... | collective-permute-start | bytes 196616 | tf_op jit(solution)/shard_map/ppermute | solution.py:22
  82.7 7.0 %collective-permute-start.17 = (bf16[256,128]{1,0:T(8,128)(2,1)}, bf16[256,128]{1,0:T(8,128)(2,1)S(1)}, u32[]{:S(2)}, u32[]{:S(2)}) collective-permute-start(bf16[256,128]{1,0:T(8,128)(2,1)} %get-tuple-element.15), channel_id=1, source_target_pairs={{0,12},{4,8},{8,4},{12,0},{1,13},{5,9},{9,5},{13,1},{2,14},{6,10},... | collective-permute-start | bytes 196616 | tf_op jit(solution)/shard_map/ppermute | solution.py:22
  86.1 4.2 %collective-permute-start.22 = (bf16[128,1024]{1,0:T(8,128)(2,1)S(1)}, bf16[128,1024]{1,0:T(8,128)(2,1)S(1)}, u32[]{:S(2)}, u32[]{:S(2)}) collective-permute-start(bf16[128,1024]{1,0:T(8,128)(2,1)S(1)} %convolution_convert_fusion), channel_id=1, source_target_pairs={{0,1},{1,0},{2,3},{3,2},{4,5},{5,4},{6,7},{7,6},{8,9},{9,8},{10,11... | collective-permute-start | bytes 786440 | tf_op jit(solution)/shard_map/ppermute | solution.py:22
  90.2 2.3 %collective-permute-start.18 = (bf16[128,1024]{1,0:T(8,128)(2,1)S(1)}, bf16[128,1024]{1,0:T(8,128)(2,1)S(1)}, u32[]{:S(2)}, u32[]{:S(2)}) collective-permute-start(bf16[128,1024]{1,0:T(8,128)(2,1)S(1)} %convolution_convert_fusion.1), channel_id=1, source_target_pairs={{0,1},{1,0},{2,3},{3,2},{4,5},{5,4},{6,7},{7,6},{8,9},{9,8},{10,11... | collective-permute-start | bytes 786440 | tf_op jit(solution)/shard_map/ppermute | solution.py:22
  90.8 8.8 %collective-permute-start.23 = (bf16[128,1024]{1,0:T(8,128)(2,1)S(1)}, bf16[128,1024]{1,0:T(8,128)(2,1)S(1)}, u32[]{:S(2)}, u32[]{:S(2)}) collective-permute-start(bf16[128,1024]{1,0:T(8,128)(2,1)S(1)} %fusion.2), channel_id=1, source_target_pairs={{0,2},{1,3},{2,0},{3,1},{4,6},{5,7},{6,4},{7,5},{8,10},{9,11},{10,... | collective-permute-start | bytes 786440 | tf_op jit(solution)/shard_map/ppermute | solution.py:22
  100.1 15.2 %copy-start.5 = (f32[128,1024]{1,0:T(8,128)S(1)}, f32[128,1024]{1,0:T(8,128)}, u32[]{:S(2)}) copy-start(f32[128,1024]{1,0:T(8,128)} %param.10) | copy-start | bytes 1572868
  100.1 6.4 %collective-permute-start.26 = (bf16[32,1024]{1,0:T(8,128)(2,1)S(1)}, bf16[32,1024]{1,0:T(8,128)(2,1)S(1)}, u32[]{:S(2)}, u32[]{:S(2)}) collective-permute-start(bf16[32,1024]{1,0:T(8,128)(2,1)S(1)} %get-tuple-element.34), channel_id=1, source_target_pairs={{0,12},{4,8},{8,4},{12,0},{1,13},{5,9},{9,5},{13,1},{2,14},{6,10},... | collective-permute-start | bytes 196616 | tf_op jit(solution)/shard_map/ppermute | solution.py:22
  102.1 7.0 %collective-permute-start.25 = (bf16[32,1024]{1,0:T(8,128)(2,1)S(1)}, bf16[32,1024]{1,0:T(8,128)(2,1)S(1)}, u32[]{:S(2)}, u32[]{:S(2)}) collective-permute-start(bf16[32,1024]{1,0:T(8,128)(2,1)S(1)} %get-tuple-element.35), channel_id=1, source_target_pairs={{0,8},{4,12},{8,0},{12,4},{1,9},{5,13},{9,1},{13,5},{2,10},{6,14},... | collective-permute-start | bytes 196616 | tf_op jit(solution)/shard_map/ppermute | solution.py:22
  102.9 6.2 %collective-permute-start.24 = (bf16[32,1024]{1,0:T(8,128)(2,1)S(1)}, bf16[32,1024]{1,0:T(8,128)(2,1)S(1)}, u32[]{:S(2)}, u32[]{:S(2)}) collective-permute-start(bf16[32,1024]{1,0:T(8,128)(2,1)S(1)} %get-tuple-element.36), channel_id=1, source_target_pairs={{0,4},{4,0},{8,12},{12,8},{1,5},{5,1},{9,13},{13,9},{2,6},{6,2},{1... | collective-permute-start | bytes 196616 | tf_op jit(solution)/shard_map/ppermute | solution.py:22
  109.3 4.3 %collective-permute-start.29 = (bf16[32,1024]{1,0:T(8,128)(2,1)S(1)}, bf16[32,1024]{1,0:T(8,128)(2,1)S(1)}, u32[]{:S(2)}, u32[]{:S(2)}) collective-permute-start(bf16[32,1024]{1,0:T(8,128)(2,1)S(1)} %get-tuple-element.26), channel_id=1, source_target_pairs={{0,3},{1,2},{2,1},{3,0},{4,7},{5,6},{6,5},{7,4},{8,11},{9,10},{10,... | collective-permute-start | bytes 196616 | tf_op jit(solution)/shard_map/ppermute | solution.py:22
  110.0 5.1 %collective-permute-start.28 = (bf16[32,1024]{1,0:T(8,128)(2,1)S(1)}, bf16[32,1024]{1,0:T(8,128)(2,1)S(1)}, u32[]{:S(2)}, u32[]{:S(2)}) collective-permute-start(bf16[32,1024]{1,0:T(8,128)(2,1)S(1)} %get-tuple-element.27), channel_id=1, source_target_pairs={{0,2},{1,3},{2,0},{3,1},{4,6},{5,7},{6,4},{7,5},{8,10},{9,11},{10,... | collective-permute-start | bytes 196616 | tf_op jit(solution)/shard_map/ppermute | solution.py:22
  111.0 4.1 %collective-permute-start.27 = (bf16[32,1024]{1,0:T(8,128)(2,1)S(1)}, bf16[32,1024]{1,0:T(8,128)(2,1)S(1)}, u32[]{:S(2)}, u32[]{:S(2)}) collective-permute-start(bf16[32,1024]{1,0:T(8,128)(2,1)S(1)} %get-tuple-element.28), channel_id=1, source_target_pairs={{0,1},{1,0},{2,3},{3,2},{4,5},{5,4},{6,7},{7,6},{8,9},{9,8},{10,11... | collective-permute-start | bytes 196616 | tf_op jit(solution)/shard_map/ppermute | solution.py:22

commit v4 on v2

--- a/solution.py
+++ b/solution.py
@@ -69,12 +69,11 @@
         first = hop(product(jnp.where(end, 3, 1)).astype(low), "seq", 1)
         second = product(jnp.where(end, 1, 3)).astype(low)
         middle = lax.ppermute(second, "seq", [(1, 2), (2, 1)])
-        near = lax.ppermute(second, "seq", [(0, 1), (3, 2)])
+        near = hop(second, "seq", 1)
         rows, first = lax.optimization_barrier((rows, first))
         relayed = jnp.where(end, 0.0, first.astype(jnp.float32))
         last = hop((product(2) + relayed).astype(low), "seq", 2)
-        total = product(0) + jnp.where(end, first.astype(jnp.float32), 0.0)
-        total = total + middle.astype(jnp.float32) + near.astype(jnp.float32)
+        total = product(0) + jnp.where(end, first, near).astype(jnp.float32) + middle.astype(jnp.float32)
         return [total, last]
     if narrow:
         return [term.transpose(0, 2, 1) for term in [product(0)] + came]
@@ -286,7 +285,8 @@
     groups = (tuple(slots[:2]), tuple(slots[2:]))
     terms = []
     for group in groups:
-        terms.append(sum_over_seq(jnp.concatenate([parts[slot] for slot in group]), in_part))
+        rows_of = lax.optimization_barrier(jnp.concatenate([parts[slot] for slot in group]))
+        terms.append(sum_over_seq(rows_of, in_part))
     half = tensor // 2
     if own % 128 == 0 and length <= BLOCK and sub % 16 == 0:
         lower_gated, upper_gated = local_stage(groups, terms, taps, long_filter, t, seq, sub)

time: 112 us -> 109 us (0.973)
  waiting for transfers between devices: 41 us -> 43.7 us
  starting transfers between devices: 40.2 us -> 37.9 us
  matrix products: 10 us -> 8.11 us
    ppermute x2 -> x0, starting transfers between devices: 7.02 us -> none  [sum_over_seq(): near = lax.ppermute(second, 'seq', [(0, 1), (3, 2)])]
    ppermute x28 -> x30, starting transfers between devices: 31.8 us -> 36.5 us  [hop(): return lax.ppermute(value, axis, [(a, a ^ mask) for a in range(count)])]
    ppermute x28 -> x30, waiting for transfers between devices: 40.5 us -> 43.7 us  [hop(): return lax.ppermute(value, axis, [(a, a ^ mask) for a in range(count)])]
    dot_general x8, matrix products: 6.95 us -> 5.03 us  [product(): jnp.einsum(form, rows, weight_of(mask), preferred_element_type=jnp.float32)]
    dynamic_slice x1, local copies, waits for them, and re-layouts: 1.08 us -> 2.21 us  [shards(): lax.dynamic_slice_in_dim(out_weight, (z ^ mask) * own, own, 1)]
    unnamed x24 -> x21, local copies, waits for them, and re-layouts: 2.65 us -> 1.69 us
  transfers between devices with their start and end apart: 32 -> 32, of which waited for: 16 -> 17; matrix products, arithmetic and copies ran while one was open for 14% -> 13% of each run, Pallas kernels for 3% -> 3%
where the time goes in v4:
time: 109 us
  waiting for transfers between devices  43.7 us (40%)
  starting transfers between devices  37.9 us (35%)
  Pallas kernels  8.11 us (7%)
  matrix products  8.11 us (7%)
  local copies, waits for them, and re-layouts  6.83 us (6%)
  other arithmetic  3.69 us (3%)
    ppermute x30, waiting for transfers between devices, hop(): return lax.ppermute(value, axis, [(a, a ^ mask) for a in range(count)])  43.7 us
    ppermute x30, starting transfers between devices, hop(): return lax.ppermute(value, axis, [(a, a ^ mask) for a in range(count)])  36.5 us
    dot_general x8, matrix products, product(): jnp.einsum(form, rows, weight_of(mask), preferred_element_type=jnp.float32)  5.03 us
    pallas_call x1, Pallas kernels, local_stage(): pl.pallas_call(functools.partial(local_kernel, groups, len(terms[0]), seq...  5 us
    pallas_call x1, Pallas kernels, local_stage(): spectrum = make_spectrum(*wide[:2], long_filter)  3.12 us
    dot_general x4, matrix products, shards(): jnp.einsum('rc,nc->rn', got[place * seq * sub:(place + 1) * seq * sub], o...  3.08 us
    dynamic_slice x1, local copies, waits for them, and re-layouts, shards(): lax.dynamic_slice_in_dim(out_weight, (z ^ mask) * own, own, 1)  2.21 us
  transfers between devices with their start and end apart: 32, of which 17 were waited for; matrix products, arithmetic and copies ran while one was open for 13% of the time, Pallas kernels for 3%

profile of v4, /device:TPU:0, one launch (start us, length us, event | category | flops | bytes accessed | tf_op | source)
XLA Modules:
  0.0 108.8 jit_solution(6066999544587654503)
XLA Ops:
  0.0 1.2 %convert_element_type.89 = bf16[128,1024]{1,0:T(8,128)(2,1)S(1)} convert(f32[128,1024]{1,0:T(8,128)} %param.10) | non-fusion elementwise | flops 131072 | bytes 786432 | tf_op jit(solution)/shard_map/convert_element_type | solution.py:272
  1.2 0.7 constant_dynamic-slice_fusion.23
  1.9 2.4 %collective-permute-start.2 = (bf16[32,1024]{1,0:T(8,128)(2,1)}, bf16[32,1024]{1,0:T(8,128)(2,1)S(1)}, u32[]{:S(2)}, u32[]{:S(2)}) collective-permute-start(bf16[32,1024]{1,0:T(8,128)(2,1)} %get-tuple-element.50), channel_id=1, source_target_pairs={{0,3},{1,2},{2,1},{3,0},{4,7},{5,6},{6,5},{7,4},{8,11},{9,10},{10,... | collective-permute-start | bytes 196616 | tf_op jit(solution)/shard_map/ppermute | solution.py:22
  4.3 0.6 collective-permute-start.1
  5.0 0.7 mul.56
  5.7 1.4 %collective-permute-done.2 = bf16[32,1024]{1,0:T(8,128)(2,1)S(1)} collective-permute-done((bf16[32,1024]{1,0:T(8,128)(2,1)}, bf16[32,1024]{1,0:T(8,128)(2,1)S(1)}, u32[]{:S(2)}, u32[]{:S(2)}) %collective-permute-start.2) | collective-permute-done | bytes 65568 | tf_op jit(solution)/shard_map/ppermute | solution.py:22
  7.1 2.1 %collective-permute-done.1 = bf16[32,1024]{1,0:T(8,128)(2,1)S(1)} collective-permute-done((bf16[32,1024]{1,0:T(8,128)(2,1)}, bf16[32,1024]{1,0:T(8,128)(2,1)S(1)}, u32[]{:S(2)}, u32[]{:S(2)}) %collective-permute-start.1) | collective-permute-done | bytes 65568 | tf_op jit(solution)/shard_map/ppermute | solution.py:22
  9.3 0.2 fusion.23
  9.7 3.9 %collective-permute-start.5 = (bf16[32,1024]{1,0:T(8,128)(2,1)S(1)}, bf16[32,1024]{1,0:T(8,128)(2,1)S(1)}, u32[]{:S(2)}, u32[]{:S(2)}) collective-permute-start(bf16[32,1024]{1,0:T(8,128)(2,1)S(1)} %get-tuple-element.42), channel_id=1, source_target_pairs={{0,12},{4,8},{8,4},{12,0},{1,13},{5,9},{9,5},{13,1},{2,14},{6,10},... | collective-permute-start | bytes 196616 | tf_op jit(solution)/shard_map/ppermute | solution.py:22
  13.5 0.6 collective-permute-start.3
  14.2 1.9 %collective-permute-done.5 = bf16[32,1024]{1,0:T(8,128)(2,1)S(1)} collective-permute-done((bf16[32,1024]{1,0:T(8,128)(2,1)S(1)}, bf16[32,1024]{1,0:T(8,128)(2,1)S(1)}, u32[]{:S(2)}, u32[]{:S(2)}) %collective-permute-start.5) | collective-permute-done | bytes 65568 | tf_op jit(solution)/shard_map/ppermute | solution.py:22
  16.1 3.3 %collective-permute-done.4 = bf16[32,1024]{1,0:T(8,128)(2,1)S(1)} collective-permute-done((bf16[32,1024]{1,0:T(8,128)(2,1)S(1)}, bf16[32,1024]{1,0:T(8,128)(2,1)S(1)}, u32[]{:S(2)}, u32[]{:S(2)}) %collective-permute-start.4) | collective-permute-done | bytes 65568 | tf_op jit(solution)/shard_map/ppermute | solution.py:22
  19.5 3.1 %filter_spectrum.1.refs_6_ = f32[1024,128]{1,0:T(8,128)} custom-call(bf16[1024,512]{1,0:T(8,128)(2,1)} %constant.101.clone.high_ref.refs_4_, bf16[1024,512]{1,0:T(8,128)(2,1)} %constant.102.clone.low_ref.refs_5_, f32[128,512]{1,0:T(8,128)} %taps_ref.1), custom_call_target="tpu_custom_call" | custom-call | flops 402653184 | bytes 1048576 | tf_op jit(solution)/shard_map/filter_spectrum/pallas_call | solution.py:215
  22.6 1.3 %constant_dynamic-slice_fusion.24.taps_ref = f32[3,3,128]{2,1,0:T(4,128)} fusion(f32[3,3,512]{2,1,0:T(4,128)} %param.13, s32[]{:T(128)S(6)} %select_n.105), kind=kLoop, calls=%fused_computation.116 | loop fusion | bytes 9220 | tf_op jit(solution)/shard_map/dynamic_slice | solution.py:279
  23.9 2.2 %constant_dynamic-slice_fusion.13 = (bf16[1024,128]{1,0:T(8,128)(2,1)}, bf16[1024,128]{1,0:T(8,128)(2,1)}, bf16[1024,128]{1,0:T(8,128)(2,1)}, bf16[1024,128]{1,0:T(8,128)(2,1)}) fusion(bf16[1024,512]{1,0:T(8,128)(2,1)} %param.15, s32[]{:T(128)S(6)} %select_n.105, s32[]{:T(128)S(6)} %select_n.124, s32[]{:T(128)S(6)} %select_n.125, s32[]{:T(128)S(6)} %select_n.120), kind=kLoop, calls=%fused_computation.101 | loop fusion | bytes 2097168 | tf_op jit(solution)/shard_map/dynamic_slice | solution.py:277
  26.1 1.6 %collective-permute-start.11 = (bf16[128,1024]{1,0:T(8,128)(2,1)S(1)}, bf16[128,1024]{1,0:T(8,128)(2,1)S(1)}, u32[]{:S(2)}, u32[]{:S(2)}) collective-permute-start(bf16[128,1024]{1,0:T(8,128)(2,1)S(1)} %bitcast.97), channel_id=1, source_target_pairs={{0,2},{1,3},{2,0},{3,1},{4,6},{5,7},{6,4},{7,5},{8,10},{9,11},{10,... | collective-permute-start | bytes 786440 | tf_op jit(solution)/shard_map/ppermute | solution.py:22
  27.7 1.0 pad_maximum_fusion.1
  28.7 0.4 fusion.11
  29.1 1.1 %collective-permute-start.7 = (bf16[3,256,128]{2,1,0:T(8,128)(2,1)S(1)}, bf16[3,256,128]{2,1,0:T(8,128)(2,1)S(1)}, u32[]{:S(2)}, u32[]{:S(2)}) collective-permute-start(bf16[3,256,128]{2,1,0:T(8,128)(2,1)S(1)} %fusion.11), channel_id=1, source_target_pairs={{0,4},{4,0},{8,12},{12,8},{1,5},{5,1},{9,13},{13,9},{2,6},{6,2},{1... | collective-permute-start | bytes 589832 | tf_op jit(solution)/shard_map/ppermute | solution.py:22
  30.3 0.4 fusion.12
  30.7 0.7 collective-permute-start.9
  31.4 3.9 %collective-permute-start.8 = (bf16[3,256,128]{2,1,0:T(8,128)(2,1)S(1)}, bf16[3,256,128]{2,1,0:T(8,128)(2,1)S(1)}, u32[]{:S(2)}, u32[]{:S(2)}) collective-permute-start(bf16[3,256,128]{2,1,0:T(8,128)(2,1)S(1)} %fusion.12), channel_id=1, source_target_pairs={{0,4},{4,0},{8,12},{12,8},{1,5},{5,1},{9,13},{13,9},{2,6},{6,2},{1... | collective-permute-start | bytes 589832 | tf_op jit(solution)/shard_map/ppermute | solution.py:22
  35.3 1.4 %collective-permute-done.7 = bf16[3,256,128]{2,1,0:T(8,128)(2,1)S(1)} collective-permute-done((bf16[3,256,128]{2,1,0:T(8,128)(2,1)S(1)}, bf16[3,256,128]{2,1,0:T(8,128)(2,1)S(1)}, u32[]{:S(2)}, u32[]{:S(2)}) %collective-permute-start.7) | collective-permute-done | bytes 196640 | tf_op jit(solution)/shard_map/ppermute | solution.py:22
  36.7 0.4 fusion.9
  37.1 1.1 %collective-permute-start.10 = (bf16[3,256,128]{2,1,0:T(8,128)(2,1)S(1)}, bf16[3,256,128]{2,1,0:T(8,128)(2,1)S(1)}, u32[]{:S(2)}, u32[]{:S(2)}) collective-permute-start(bf16[3,256,128]{2,1,0:T(8,128)(2,1)S(1)} %fusion.9), channel_id=1, source_target_pairs={{0,8},{4,12},{8,0},{12,4},{1,9},{5,13},{9,1},{13,5},{2,10},{6,14},... | collective-permute-start | bytes 589832 | tf_op jit(solution)/shard_map/ppermute | solution.py:22
  38.3 3.2 %collective-permute-done.8 = bf16[3,256,128]{2,1,0:T(8,128)(2,1)S(1)} collective-permute-done((bf16[3,256,128]{2,1,0:T(8,128)(2,1)S(1)}, bf16[3,256,128]{2,1,0:T(8,128)(2,1)S(1)}, u32[]{:S(2)}, u32[]{:S(2)}) %collective-permute-start.8) | collective-permute-done | bytes 196640 | tf_op jit(solution)/shard_map/ppermute | solution.py:22
  41.4 1.2 %fusion.7.refs_0_ = f32[3,256,128]{2,1,0:T(8,128)} fusion(bf16[3,1024,512]{2,1,0:T(8,128)(2,1)S(1)} %copy-done, s32[]{:T(128)S(6)} %select_n.105, bf16[256,1024]{1,0:T(8,128)(2,1)S(1)} %pad_maximum_fusion.1, bf16[3,256,128]{2,1,0:T(8,128)(2,1)S(1)} %collective-permute-done.9, bf16[3,256,128]{2,1,0:T(8,128)(2,1)S(1)} %collective-permute-done.7, ...), kind=kOutput, calls=%fused_computation.15 | convolution fusion | flops 201818112 | bytes 2293765 | tf_op jit(solution)/shard_map/rd,sdc->src/dot_general | solution.py:60
  42.6 0.4 fusion.13
  43.1 1.7 %collective-permute-start.13 = (bf16[3,256,128]{2,1,0:T(8,128)(2,1)S(1)}, bf16[3,256,128]{2,1,0:T(8,128)(2,1)S(1)}, u32[]{:S(2)}, u32[]{:S(2)}) collective-permute-start(bf16[3,256,128]{2,1,0:T(8,128)(2,1)S(1)} %fusion.13), channel_id=1, source_target_pairs={{0,4},{4,0},{8,12},{12,8},{1,5},{5,1},{9,13},{13,9},{2,6},{6,2},{1... | collective-permute-start | bytes 589832 | tf_op jit(solution)/shard_map/ppermute | solution.py:22
  44.8 0.4 fusion.14
  45.2 0.7 collective-permute-start.15
  45.9 3.0 %collective-permute-start.14 = (bf16[3,256,128]{2,1,0:T(8,128)(2,1)S(1)}, bf16[3,256,128]{2,1,0:T(8,128)(2,1)S(1)}, u32[]{:S(2)}, u32[]{:S(2)}) collective-permute-start(bf16[3,256,128]{2,1,0:T(8,128)(2,1)S(1)} %fusion.14), channel_id=1, source_target_pairs={{0,4},{4,0},{8,12},{12,8},{1,5},{5,1},{9,13},{13,9},{2,6},{6,2},{1... | collective-permute-start | bytes 589832 | tf_op jit(solution)/shard_map/ppermute | solution.py:22
  48.9 3.6 %collective-permute-done.13 = bf16[3,256,128]{2,1,0:T(8,128)(2,1)S(1)} collective-permute-done((bf16[3,256,128]{2,1,0:T(8,128)(2,1)S(1)}, bf16[3,256,128]{2,1,0:T(8,128)(2,1)S(1)}, u32[]{:S(2)}, u32[]{:S(2)}) %collective-permute-start.13) | collective-permute-done | bytes 196640 | tf_op jit(solution)/shard_map/ppermute | solution.py:22
  52.5 0.4 fusion.10
  53.0 0.5 collective-permute-start.16
  53.5 2.2 %collective-permute-done.14 = bf16[3,256,128]{2,1,0:T(8,128)(2,1)S(1)} collective-permute-done((bf16[3,256,128]{2,1,0:T(8,128)(2,1)S(1)}, bf16[3,256,128]{2,1,0:T(8,128)(2,1)S(1)}, u32[]{:S(2)}, u32[]{:S(2)}) %collective-permute-start.14) | collective-permute-done | bytes 196640 | tf_op jit(solution)/shard_map/ppermute | solution.py:22
  55.7 1.2 %fusion.8.refs_2_ = f32[3,256,128]{2,1,0:T(8,128)} fusion(bf16[3,1024,512]{2,1,0:T(8,128)(2,1)S(1)} %copy-done, s32[]{:T(128)S(6)} %select_n.105, bf16[256,1024]{1,0:T(8,128)(2,1)S(1)} %pad_maximum_fusion.2, bf16[3,256,128]{2,1,0:T(8,128)(2,1)S(1)} %collective-permute-done.15, bf16[3,256,128]{2,1,0:T(8,128)(2,1)S(1)} %collective-permute-done.13, ...), kind=kOutput, calls=%fused_computation.16 | convolution fusion | flops 201818112 | bytes 2293765 | tf_op jit(solution)/shard_map/rd,sdc->src/dot_general | solution.py:60
  56.9 5.6 %collective-permute-done.16.refs_3_ = bf16[3,256,128]{2,1,0:T(8,128)(2,1)S(1)} collective-permute-done((bf16[3,256,128]{2,1,0:T(8,128)(2,1)S(1)}, bf16[3,256,128]{2,1,0:T(8,128)(2,1)S(1)}, u32[]{:S(2)}, u32[]{:S(2)}) %collective-permute-start.16) | collective-permute-done | bytes 196640 | tf_op jit(solution)/shard_map/ppermute | solution.py:22
  62.5 0.7 copy-done.7
  63.1 5.0 %filters.1 = (bf16[256,128]{1,0:T(8,128)(2,1)}, bf16[256,128]{1,0:T(8,128)(2,1)}) custom-call(s32[1]{0:T(128)} %bitcast.t_ref, f32[3,3,128]{2,1,0:T(4,128)} %constant_dynamic-slice_fusion.24.taps_ref, f32[3,256,128]{2,1,0:T(8,128)} %fusion.7.refs_0_, bf16[3,256,128]{2,1,0:T(8,128)(2,1)} %copy-done.6, f32[3,256,128]{2,1,0:T(8,128)} %fusion.8.refs_2_, ...), custom_call_target="tpu_custom_call" | custom-call | flops 805306368 | bytes 2097152 | tf_op jit(solution)/shard_map/filters/pallas_call | solution.py:219
  68.2 2.8 %collective-permute-start.22 = (bf16[256,128]{1,0:T(8,128)(2,1)}, bf16[256,128]{1,0:T(8,128)(2,1)S(1)}, u32[]{:S(2)}, u32[]{:S(2)}) collective-permute-start(bf16[256,128]{1,0:T(8,128)(2,1)} %get-tuple-element.16), channel_id=1, source_target_pairs={{0,8},{4,12},{8,0},{12,4},{1,9},{5,13},{9,1},{13,5},{2,10},{6,14},... | collective-permute-start | bytes 196616 | tf_op jit(solution)/shard_map/ppermute | solution.py:22
  71.0 1.6 %collective-permute-start.23 = (bf16[256,128]{1,0:T(8,128)(2,1)}, bf16[256,128]{1,0:T(8,128)(2,1)S(1)}, u32[]{:S(2)}, u32[]{:S(2)}) collective-permute-start(bf16[256,128]{1,0:T(8,128)(2,1)} %get-tuple-element.16), channel_id=1, source_target_pairs={{0,12},{4,8},{8,4},{12,0},{1,13},{5,9},{9,5},{13,1},{2,14},{6,10},... | collective-permute-start | bytes 196616 | tf_op jit(solution)/shard_map/ppermute | solution.py:22
  72.6 2.8 %collective-permute-start.18 = (bf16[256,128]{1,0:T(8,128)(2,1)}, bf16[256,128]{1,0:T(8,128)(2,1)S(1)}, u32[]{:S(2)}, u32[]{:S(2)}) collective-permute-start(bf16[256,128]{1,0:T(8,128)(2,1)} %get-tuple-element.15), channel_id=1, source_target_pairs={{0,8},{4,12},{8,0},{12,4},{1,9},{5,13},{9,1},{13,5},{2,10},{6,14},... | collective-permute-start | bytes 196616 | tf_op jit(solution)/shard_map/ppermute | solution.py:22
  75.4 0.9 constant_dynamic-update-slice_fusion.3
  76.3 1.7 %collective-permute-start.19 = (bf16[256,128]{1,0:T(8,128)(2,1)}, bf16[256,128]{1,0:T(8,128)(2,1)S(1)}, u32[]{:S(2)}, u32[]{:S(2)}) collective-permute-start(bf16[256,128]{1,0:T(8,128)(2,1)} %get-tuple-element.15), channel_id=1, source_target_pairs={{0,12},{4,8},{8,4},{12,0},{1,13},{5,9},{9,5},{13,1},{2,14},{6,10},... | collective-permute-start | bytes 196616 | tf_op jit(solution)/shard_map/ppermute | solution.py:22
  78.1 1.6 %convolution_convert_fusion = bf16[128,1024]{1,0:T(8,128)(2,1)S(1)} fusion(bf16[256,512]{1,0:T(8,128)(2,1)S(1)} %constant_dynamic-update-slice_fusion.4, bf16[1024,128]{1,0:T(8,128)(2,1)} %get-tuple-element.19, bf16[1024,128]{1,0:T(8,128)(2,1)} %get-tuple-element.20, bf16[1024,128]{1,0:T(8,128)(2,1)} %get-tuple-element.18, bf16[1024,128]{1,0:T(8,128)(2,1)S(1)} %copy-done.2), kind=kOutput, calls=%fused_computation.13 | convolution fusion | flops 138543104 | bytes 1441792 | tf_op jit(solution)/shard_map/rc,nc->rn/dot_general | solution.py:305
  79.9 1.7 %collective-permute-done.18 = bf16[256,128]{1,0:T(8,128)(2,1)S(1)} collective-permute-done((bf16[256,128]{1,0:T(8,128)(2,1)}, bf16[256,128]{1,0:T(8,128)(2,1)S(1)}, u32[]{:S(2)}, u32[]{:S(2)}) %collective-permute-start.18) | collective-permute-done | bytes 65568 | tf_op jit(solution)/shard_map/ppermute | solution.py:22
  81.6 1.1 %collective-permute-done.19 = bf16[256,128]{1,0:T(8,128)(2,1)S(1)} collective-permute-done((bf16[256,128]{1,0:T(8,128)(2,1)}, bf16[256,128]{1,0:T(8,128)(2,1)S(1)}, u32[]{:S(2)}, u32[]{:S(2)}) %collective-permute-start.19) | collective-permute-done | bytes 65568 | tf_op jit(solution)/shard_map/ppermute | solution.py:22
  82.8 0.5 convolution_convert_fusion.1
  83.4 0.5 fusion.2
  83.8 0.6 collective-permute-start.25
  84.5 0.4 collective-permute-done.20
  84.9 7.7 %collective-permute-done.25 = bf16[128,1024]{1,0:T(8,128)(2,1)S(1)} collective-permute-done((bf16[128,1024]{1,0:T(8,128)(2,1)S(1)}, bf16[128,1024]{1,0:T(8,128)(2,1)S(1)}, u32[]{:S(2)}, u32[]{:S(2)}) %collective-permute-start.25) | collective-permute-done | bytes 262176 | tf_op jit(solution)/shard_map/ppermute | solution.py:22
  92.6 0.5 fusion.1
  93.2 1.7 %collective-permute-start.28 = (bf16[32,1024]{1,0:T(8,128)(2,1)S(1)}, bf16[32,1024]{1,0:T(8,128)(2,1)S(1)}, u32[]{:S(2)}, u32[]{:S(2)}) collective-permute-start(bf16[32,1024]{1,0:T(8,128)(2,1)S(1)} %get-tuple-element.34), channel_id=1, source_target_pairs={{0,12},{4,8},{8,4},{12,0},{1,13},{5,9},{9,5},{13,1},{2,14},{6,10},... | collective-permute-start | bytes 196616 | tf_op jit(solution)/shard_map/ppermute | solution.py:22
  94.9 0.6 collective-permute-start.27
  95.5 2.1 %collective-permute-start.26 = (bf16[32,1024]{1,0:T(8,128)(2,1)S(1)}, bf16[32,1024]{1,0:T(8,128)(2,1)S(1)}, u32[]{:S(2)}, u32[]{:S(2)}) collective-permute-start(bf16[32,1024]{1,0:T(8,128)(2,1)S(1)} %get-tuple-element.36), channel_id=1, source_target_pairs={{0,4},{4,0},{8,12},{12,8},{1,5},{5,1},{9,13},{13,9},{2,6},{6,2},{1... | collective-permute-start | bytes 196616 | tf_op jit(solution)/shard_map/ppermute | solution.py:22
  97.6 2.3 %collective-permute-done.28 = bf16[32,1024]{1,0:T(8,128)(2,1)S(1)} collective-permute-done((bf16[32,1024]{1,0:T(8,128)(2,1)S(1)}, bf16[32,1024]{1,0:T(8,128)(2,1)S(1)}, u32[]{:S(2)}, u32[]{:S(2)}) %collective-permute-start.28) | collective-permute-done | bytes 65568 | tf_op jit(solution)/shard_map/ppermute | solution.py:22
  99.9 2.1 %collective-permute-done.27 = bf16[32,1024]{1,0:T(8,128)(2,1)S(1)} collective-permute-done((bf16[32,1024]{1,0:T(8,128)(2,1)S(1)}, bf16[32,1024]{1,0:T(8,128)(2,1)S(1)}, u32[]{:S(2)}, u32[]{:S(2)}) %collective-permute-start.27) | collective-permute-done | bytes 65568 | tf_op jit(solution)/shard_map/ppermute | solution.py:22
  102.2 1.3 %collective-permute-start.30 = (bf16[32,1024]{1,0:T(8,128)(2,1)S(1)}, bf16[32,1024]{1,0:T(8,128)(2,1)S(1)}, u32[]{:S(2)}, u32[]{:S(2)}) collective-permute-start(bf16[32,1024]{1,0:T(8,128)(2,1)S(1)} %get-tuple-element.27), channel_id=1, source_target_pairs={{0,2},{1,3},{2,0},{3,1},{4,6},{5,7},{6,4},{7,5},{8,10},{9,11},{10,... | collective-permute-start | bytes 196616 | tf_op jit(solution)/shard_map/ppermute | solution.py:22
  103.5 0.5 collective-permute-start.29
  104.1 2.5 %collective-permute-done.31 = bf16[32,1024]{1,0:T(8,128)(2,1)S(1)} collective-permute-done((bf16[32,1024]{1,0:T(8,128)(2,1)S(1)}, bf16[32,1024]{1,0:T(8,128)(2,1)S(1)}, u32[]{:S(2)}, u32[]{:S(2)}) %collective-permute-start.31) | collective-permute-done | bytes 65568 | tf_op jit(solution)/shard_map/ppermute | solution.py:22
  106.6 1.2 %collective-permute-done.30 = bf16[32,1024]{1,0:T(8,128)(2,1)S(1)} collective-permute-done((bf16[32,1024]{1,0:T(8,128)(2,1)S(1)}, bf16[32,1024]{1,0:T(8,128)(2,1)S(1)}, u32[]{:S(2)}, u32[]{:S(2)}) %collective-permute-start.30) | collective-permute-done | bytes 65568 | tf_op jit(solution)/shard_map/ppermute | solution.py:22
  107.9 0.9 convert_add_fusion
  (62 shorter events, 1.3 us)
Async XLA Ops:
  0.0 28.7 %copy-start = (bf16[3,1024,512]{2,1,0:T(8,128)(2,1)S(1)}, bf16[3,1024,512]{2,1,0:T(8,128)(2,1)}, u32[]{:S(2)}) copy-start(bf16[3,1024,512]{2,1,0:T(8,128)(2,1)} %param.12) | copy-start | bytes 9437188
  1.9 5.2 %collective-permute-start.2 = (bf16[32,1024]{1,0:T(8,128)(2,1)}, bf16[32,1024]{1,0:T(8,128)(2,1)S(1)}, u32[]{:S(2)}, u32[]{:S(2)}) collective-permute-start(bf16[32,1024]{1,0:T(8,128)(2,1)} %get-tuple-element.50), channel_id=1, source_target_pairs={{0,3},{1,2},{2,1},{3,0},{4,7},{5,6},{6,5},{7,4},{8,11},{9,10},{10,... | collective-permute-start | bytes 196616 | tf_op jit(solution)/shard_map/ppermute | solution.py:22
  4.3 4.9 %collective-permute-start.1 = (bf16[32,1024]{1,0:T(8,128)(2,1)}, bf16[32,1024]{1,0:T(8,128)(2,1)S(1)}, u32[]{:S(2)}, u32[]{:S(2)}) collective-permute-start(bf16[32,1024]{1,0:T(8,128)(2,1)} %get-tuple-element.51), channel_id=1, source_target_pairs={{0,2},{1,3},{2,0},{3,1},{4,6},{5,7},{6,4},{7,5},{8,10},{9,11},{10,... | collective-permute-start | bytes 196616 | tf_op jit(solution)/shard_map/ppermute | solution.py:22
  4.9 4.3 %collective-permute-start = (bf16[32,1024]{1,0:T(8,128)(2,1)S(1)}, bf16[32,1024]{1,0:T(8,128)(2,1)S(1)}, u32[]{:S(2)}, u32[]{:S(2)}) collective-permute-start(bf16[32,1024]{1,0:T(8,128)(2,1)S(1)} %get-tuple-element.52), channel_id=1, source_target_pairs={{0,1},{1,0},{2,3},{3,2},{4,5},{5,4},{6,7},{7,6},{8,9},{9,8},{10,11... | collective-permute-start | bytes 196616 | tf_op jit(solution)/shard_map/ppermute | solution.py:22
  9.7 6.4 %collective-permute-start.5 = (bf16[32,1024]{1,0:T(8,128)(2,1)S(1)}, bf16[32,1024]{1,0:T(8,128)(2,1)S(1)}, u32[]{:S(2)}, u32[]{:S(2)}) collective-permute-start(bf16[32,1024]{1,0:T(8,128)(2,1)S(1)} %get-tuple-element.42), channel_id=1, source_target_pairs={{0,12},{4,8},{8,4},{12,0},{1,13},{5,9},{9,5},{13,1},{2,14},{6,10},... | collective-permute-start | bytes 196616 | tf_op jit(solution)/shard_map/ppermute | solution.py:22
  13.5 5.8 %collective-permute-start.4 = (bf16[32,1024]{1,0:T(8,128)(2,1)S(1)}, bf16[32,1024]{1,0:T(8,128)(2,1)S(1)}, u32[]{:S(2)}, u32[]{:S(2)}) collective-permute-start(bf16[32,1024]{1,0:T(8,128)(2,1)S(1)} %get-tuple-element.43), channel_id=1, source_target_pairs={{0,8},{4,12},{8,0},{12,4},{1,9},{5,13},{9,1},{13,5},{2,10},{6,14},... | collective-permute-start | bytes 196616 | tf_op jit(solution)/shard_map/ppermute | solution.py:22
  13.5 5.8 %collective-permute-start.3 = (bf16[32,1024]{1,0:T(8,128)(2,1)S(1)}, bf16[32,1024]{1,0:T(8,128)(2,1)S(1)}, u32[]{:S(2)}, u32[]{:S(2)}) collective-permute-start(bf16[32,1024]{1,0:T(8,128)(2,1)S(1)} %get-tuple-element.44), channel_id=1, source_target_pairs={{0,4},{4,0},{8,12},{12,8},{1,5},{5,1},{9,13},{13,9},{2,6},{6,2},{1... | collective-permute-start | bytes 196616 | tf_op jit(solution)/shard_map/ppermute | solution.py:22
  19.4 8.3 %collective-permute-start.6 = (bf16[128,1024]{1,0:T(8,128)(2,1)S(1)}, bf16[128,1024]{1,0:T(8,128)(2,1)}, u32[]{:S(2)}, u32[]{:S(2)}) collective-permute-start(bf16[128,1024]{1,0:T(8,128)(2,1)S(1)} %bitcast.96), channel_id=1, source_target_pairs={{0,1},{1,0},{2,3},{3,2},{4,5},{5,4},{6,7},{7,6},{8,9},{9,8},{10,11... | collective-permute-start | bytes 786440 | tf_op jit(solution)/shard_map/ppermute | solution.py:22
  26.1 9.1 %collective-permute-start.11 = (bf16[128,1024]{1,0:T(8,128)(2,1)S(1)}, bf16[128,1024]{1,0:T(8,128)(2,1)S(1)}, u32[]{:S(2)}, u32[]{:S(2)}) collective-permute-start(bf16[128,1024]{1,0:T(8,128)(2,1)S(1)} %bitcast.97), channel_id=1, source_target_pairs={{0,2},{1,3},{2,0},{3,1},{4,6},{5,7},{6,4},{7,5},{8,10},{9,11},{10,... | collective-permute-start | bytes 786440 | tf_op jit(solution)/shard_map/ppermute | solution.py:22
  29.1 7.5 %collective-permute-start.7 = (bf16[3,256,128]{2,1,0:T(8,128)(2,1)S(1)}, bf16[3,256,128]{2,1,0:T(8,128)(2,1)S(1)}, u32[]{:S(2)}, u32[]{:S(2)}) collective-permute-start(bf16[3,256,128]{2,1,0:T(8,128)(2,1)S(1)} %fusion.11), channel_id=1, source_target_pairs={{0,4},{4,0},{8,12},{12,8},{1,5},{5,1},{9,13},{13,9},{2,6},{6,2},{1... | collective-permute-start | bytes 589832 | tf_op jit(solution)/shard_map/ppermute | solution.py:22
  30.7 7.5 %collective-permute-start.9 = (bf16[3,256,128]{2,1,0:T(8,128)(2,1)S(1)}, bf16[3,256,128]{2,1,0:T(8,128)(2,1)S(1)}, u32[]{:S(2)}, u32[]{:S(2)}) collective-permute-start(bf16[3,256,128]{2,1,0:T(8,128)(2,1)S(1)} %fusion.12), channel_id=1, source_target_pairs={{4,8},{8,4},{5,9},{9,5},{6,10},{10,6},{7,11},{11,7},{20,24},{24,20... | collective-permute-start | bytes 589832 | tf_op jit(solution)/shard_map/ppermute | solution.py:71
  31.4 10.0 %collective-permute-start.8 = (bf16[3,256,128]{2,1,0:T(8,128)(2,1)S(1)}, bf16[3,256,128]{2,1,0:T(8,128)(2,1)S(1)}, u32[]{:S(2)}, u32[]{:S(2)}) collective-permute-start(bf16[3,256,128]{2,1,0:T(8,128)(2,1)S(1)} %fusion.12), channel_id=1, source_target_pairs={{0,4},{4,0},{8,12},{12,8},{1,5},{5,1},{9,13},{13,9},{2,6},{6,2},{1... | collective-permute-start | bytes 589832 | tf_op jit(solution)/shard_map/ppermute | solution.py:22
  35.3 7.3 %collective-permute-start.12 = (bf16[128,1024]{1,0:T(8,128)(2,1)S(1)}, bf16[128,1024]{1,0:T(8,128)(2,1)S(1)}, u32[]{:S(2)}, u32[]{:S(2)}) collective-permute-start(bf16[128,1024]{1,0:T(8,128)(2,1)S(1)} %collective-permute-done.11), channel_id=1, source_target_pairs={{0,1},{1,0},{2,3},{3,2},{4,5},{5,4},{6,7},{7,6},{8,9},{9,8},{10,11... | collective-permute-start | bytes 786440 | tf_op jit(solution)/shard_map/ppermute | solution.py:22
  37.1 19.8 %collective-permute-start.10 = (bf16[3,256,128]{2,1,0:T(8,128)(2,1)S(1)}, bf16[3,256,128]{2,1,0:T(8,128)(2,1)S(1)}, u32[]{:S(2)}, u32[]{:S(2)}) collective-permute-start(bf16[3,256,128]{2,1,0:T(8,128)(2,1)S(1)} %fusion.9), channel_id=1, source_target_pairs={{0,8},{4,12},{8,0},{12,4},{1,9},{5,13},{9,1},{13,5},{2,10},{6,14},... | collective-permute-start | bytes 589832 | tf_op jit(solution)/shard_map/ppermute | solution.py:22
  43.1 9.4 %collective-permute-start.13 = (bf16[3,256,128]{2,1,0:T(8,128)(2,1)S(1)}, bf16[3,256,128]{2,1,0:T(8,128)(2,1)S(1)}, u32[]{:S(2)}, u32[]{:S(2)}) collective-permute-start(bf16[3,256,128]{2,1,0:T(8,128)(2,1)S(1)} %fusion.13), channel_id=1, source_target_pairs={{0,4},{4,0},{8,12},{12,8},{1,5},{5,1},{9,13},{13,9},{2,6},{6,2},{1... | collective-permute-start | bytes 589832 | tf_op jit(solution)/shard_map/ppermute | solution.py:22
  45.2 8.2 %collective-permute-start.15 = (bf16[3,256,128]{2,1,0:T(8,128)(2,1)S(1)}, bf16[3,256,128]{2,1,0:T(8,128)(2,1)S(1)}, u32[]{:S(2)}, u32[]{:S(2)}) collective-permute-start(bf16[3,256,128]{2,1,0:T(8,128)(2,1)S(1)} %fusion.14), channel_id=1, source_target_pairs={{4,8},{8,4},{5,9},{9,5},{6,10},{10,6},{7,11},{11,7},{20,24},{24,20... | collective-permute-start | bytes 589832 | tf_op jit(solution)/shard_map/ppermute | solution.py:71
  45.9 9.8 %collective-permute-start.14 = (bf16[3,256,128]{2,1,0:T(8,128)(2,1)S(1)}, bf16[3,256,128]{2,1,0:T(8,128)(2,1)S(1)}, u32[]{:S(2)}, u32[]{:S(2)}) collective-permute-start(bf16[3,256,128]{2,1,0:T(8,128)(2,1)S(1)} %fusion.14), channel_id=1, source_target_pairs={{0,4},{4,0},{8,12},{12,8},{1,5},{5,1},{9,13},{13,9},{2,6},{6,2},{1... | collective-permute-start | bytes 589832 | tf_op jit(solution)/shard_map/ppermute | solution.py:22
  53.0 9.5 %collective-permute-start.16 = (bf16[3,256,128]{2,1,0:T(8,128)(2,1)S(1)}, bf16[3,256,128]{2,1,0:T(8,128)(2,1)S(1)}, u32[]{:S(2)}, u32[]{:S(2)}) collective-permute-start(bf16[3,256,128]{2,1,0:T(8,128)(2,1)S(1)} %fusion.10), channel_id=1, source_target_pairs={{0,8},{4,12},{8,0},{12,4},{1,9},{5,13},{9,1},{13,5},{2,10},{6,14},... | collective-permute-start | bytes 589832 | tf_op jit(solution)/shard_map/ppermute | solution.py:22
  56.9 5.6 %copy-start.6 = (bf16[3,256,128]{2,1,0:T(8,128)(2,1)}, bf16[3,256,128]{2,1,0:T(8,128)(2,1)S(1)}, u32[]{:S(2)}) copy-start(bf16[3,256,128]{2,1,0:T(8,128)(2,1)S(1)} %collective-permute-done.10.refs_1_) | copy-start | bytes 589828
  62.5 0.7 copy-start.7
  63.1 14.9 %copy-start.2 = (bf16[1024,128]{1,0:T(8,128)(2,1)S(1)}, bf16[1024,128]{1,0:T(8,128)(2,1)}, u32[]{:S(2)}) copy-start(bf16[1024,128]{1,0:T(8,128)(2,1)} %get-tuple-element.17) | copy-start | bytes 786436
  68.1 8.1 %collective-permute-start.21 = (bf16[256,128]{1,0:T(8,128)(2,1)}, bf16[256,128]{1,0:T(8,128)(2,1)S(1)}, u32[]{:S(2)}, u32[]{:S(2)}) collective-permute-start(bf16[256,128]{1,0:T(8,128)(2,1)} %get-tuple-element.16), channel_id=1, source_target_pairs={{0,4},{4,0},{8,12},{12,8},{1,5},{5,1},{9,13},{13,9},{2,6},{6,2},{1... | collective-permute-start | bytes 196616 | tf_op jit(solution)/shard_map/ppermute | solution.py:22
  68.2 9.8 %collective-permute-start.22 = (bf16[256,128]{1,0:T(8,128)(2,1)}, bf16[256,128]{1,0:T(8,128)(2,1)S(1)}, u32[]{:S(2)}, u32[]{:S(2)}) collective-permute-start(bf16[256,128]{1,0:T(8,128)(2,1)} %get-tuple-element.16), channel_id=1, source_target_pairs={{0,8},{4,12},{8,0},{12,4},{1,9},{5,13},{9,1},{13,5},{2,10},{6,14},... | collective-permute-start | bytes 196616 | tf_op jit(solution)/shard_map/ppermute | solution.py:22
  71.0 7.0 %collective-permute-start.23 = (bf16[256,128]{1,0:T(8,128)(2,1)}, bf16[256,128]{1,0:T(8,128)(2,1)S(1)}, u32[]{:S(2)}, u32[]{:S(2)}) collective-permute-start(bf16[256,128]{1,0:T(8,128)(2,1)} %get-tuple-element.16), channel_id=1, source_target_pairs={{0,12},{4,8},{8,4},{12,0},{1,13},{5,9},{9,5},{13,1},{2,14},{6,10},... | collective-permute-start | bytes 196616 | tf_op jit(solution)/shard_map/ppermute | solution.py:22
  72.6 7.2 %collective-permute-start.17 = (bf16[256,128]{1,0:T(8,128)(2,1)}, bf16[256,128]{1,0:T(8,128)(2,1)S(1)}, u32[]{:S(2)}, u32[]{:S(2)}) collective-permute-start(bf16[256,128]{1,0:T(8,128)(2,1)} %get-tuple-element.15), channel_id=1, source_target_pairs={{0,4},{4,0},{8,12},{12,8},{1,5},{5,1},{9,13},{13,9},{2,6},{6,2},{1... | collective-permute-start | bytes 196616 | tf_op jit(solution)/shard_map/ppermute | solution.py:22
  72.6 9.0 %collective-permute-start.18 = (bf16[256,128]{1,0:T(8,128)(2,1)}, bf16[256,128]{1,0:T(8,128)(2,1)S(1)}, u32[]{:S(2)}, u32[]{:S(2)}) collective-permute-start(bf16[256,128]{1,0:T(8,128)(2,1)} %get-tuple-element.15), channel_id=1, source_target_pairs={{0,8},{4,12},{8,0},{12,4},{1,9},{5,13},{9,1},{13,5},{2,10},{6,14},... | collective-permute-start | bytes 196616 | tf_op jit(solution)/shard_map/ppermute | solution.py:22
  76.3 6.4 %collective-permute-start.19 = (bf16[256,128]{1,0:T(8,128)(2,1)}, bf16[256,128]{1,0:T(8,128)(2,1)S(1)}, u32[]{:S(2)}, u32[]{:S(2)}) collective-permute-start(bf16[256,128]{1,0:T(8,128)(2,1)} %get-tuple-element.15), channel_id=1, source_target_pairs={{0,12},{4,8},{8,4},{12,0},{1,13},{5,9},{9,5},{13,1},{2,14},{6,10},... | collective-permute-start | bytes 196616 | tf_op jit(solution)/shard_map/ppermute | solution.py:22
  78.1 4.7 %copy-start.3 = (bf16[1024,128]{1,0:T(8,128)(2,1)S(1)}, bf16[1024,128]{1,0:T(8,128)(2,1)}, u32[]{:S(2)}) copy-start(bf16[1024,128]{1,0:T(8,128)(2,1)} %get-tuple-element.18) | copy-start | bytes 786436
  78.1 4.7 %copy-start.4 = (bf16[1024,128]{1,0:T(8,128)(2,1)S(1)}, bf16[1024,128]{1,0:T(8,128)(2,1)}, u32[]{:S(2)}) copy-start(bf16[1024,128]{1,0:T(8,128)(2,1)} %get-tuple-element.19) | copy-start | bytes 786436
  78.1 4.7 %copy-start.5 = (bf16[1024,128]{1,0:T(8,128)(2,1)S(1)}, bf16[1024,128]{1,0:T(8,128)(2,1)}, u32[]{:S(2)}) copy-start(bf16[1024,128]{1,0:T(8,128)(2,1)} %get-tuple-element.20) | copy-start | bytes 786436
  79.8 3.6 %collective-permute-start.24 = (bf16[128,1024]{1,0:T(8,128)(2,1)S(1)}, bf16[128,1024]{1,0:T(8,128)(2,1)S(1)}, u32[]{:S(2)}, u32[]{:S(2)}) collective-permute-start(bf16[128,1024]{1,0:T(8,128)(2,1)S(1)} %convolution_convert_fusion), channel_id=1, source_target_pairs={{0,1},{1,0},{2,3},{3,2},{4,5},{5,4},{6,7},{7,6},{8,9},{9,8},{10,11... | collective-permute-start | bytes 786440 | tf_op jit(solution)/shard_map/ppermute | solution.py:22
  83.3 1.6 %collective-permute-start.20 = (bf16[128,1024]{1,0:T(8,128)(2,1)S(1)}, bf16[128,1024]{1,0:T(8,128)(2,1)S(1)}, u32[]{:S(2)}, u32[]{:S(2)}) collective-permute-start(bf16[128,1024]{1,0:T(8,128)(2,1)S(1)} %convolution_convert_fusion.1), channel_id=1, source_target_pairs={{0,1},{1,0},{2,3},{3,2},{4,5},{5,4},{6,7},{7,6},{8,9},{9,8},{10,11... | collective-permute-start | bytes 786440 | tf_op jit(solution)/shard_map/ppermute | solution.py:22
  83.8 8.8 %collective-permute-start.25 = (bf16[128,1024]{1,0:T(8,128)(2,1)S(1)}, bf16[128,1024]{1,0:T(8,128)(2,1)S(1)}, u32[]{:S(2)}, u32[]{:S(2)}) collective-permute-start(bf16[128,1024]{1,0:T(8,128)(2,1)S(1)} %fusion.2), channel_id=1, source_target_pairs={{0,2},{1,3},{2,0},{3,1},{4,6},{5,7},{6,4},{7,5},{8,10},{9,11},{10,... | collective-permute-start | bytes 786440 | tf_op jit(solution)/shard_map/ppermute | solution.py:22
  93.1 14.8 %copy-start.1 = (f32[128,1024]{1,0:T(8,128)S(1)}, f32[128,1024]{1,0:T(8,128)}, u32[]{:S(2)}) copy-start(f32[128,1024]{1,0:T(8,128)} %param.10) | copy-start | bytes 1572868
  93.2 6.7 %collective-permute-start.28 = (bf16[32,1024]{1,0:T(8,128)(2,1)S(1)}, bf16[32,1024]{1,0:T(8,128)(2,1)S(1)}, u32[]{:S(2)}, u32[]{:S(2)}) collective-permute-start(bf16[32,1024]{1,0:T(8,128)(2,1)S(1)} %get-tuple-element.34), channel_id=1, source_target_pairs={{0,12},{4,8},{8,4},{12,0},{1,13},{5,9},{9,5},{13,1},{2,14},{6,10},... | collective-permute-start | bytes 196616 | tf_op jit(solution)/shard_map/ppermute | solution.py:22
  94.9 7.1 %collective-permute-start.27 = (bf16[32,1024]{1,0:T(8,128)(2,1)S(1)}, bf16[32,1024]{1,0:T(8,128)(2,1)S(1)}, u32[]{:S(2)}, u32[]{:S(2)}) collective-permute-start(bf16[32,1024]{1,0:T(8,128)(2,1)S(1)} %get-tuple-element.35), channel_id=1, source_target_pairs={{0,8},{4,12},{8,0},{12,4},{1,9},{5,13},{9,1},{13,5},{2,10},{6,14},... | collective-permute-start | bytes 196616 | tf_op jit(solution)/shard_map/ppermute | solution.py:22
  95.5 6.5 %collective-permute-start.26 = (bf16[32,1024]{1,0:T(8,128)(2,1)S(1)}, bf16[32,1024]{1,0:T(8,128)(2,1)S(1)}, u32[]{:S(2)}, u32[]{:S(2)}) collective-permute-start(bf16[32,1024]{1,0:T(8,128)(2,1)S(1)} %get-tuple-element.36), channel_id=1, source_target_pairs={{0,4},{4,0},{8,12},{12,8},{1,5},{5,1},{9,13},{13,9},{2,6},{6,2},{1... | collective-permute-start | bytes 196616 | tf_op jit(solution)/shard_map/ppermute | solution.py:22
  102.1 4.5 %collective-permute-start.31 = (bf16[32,1024]{1,0:T(8,128)(2,1)S(1)}, bf16[32,1024]{1,0:T(8,128)(2,1)S(1)}, u32[]{:S(2)}, u32[]{:S(2)}) collective-permute-start(bf16[32,1024]{1,0:T(8,128)(2,1)S(1)} %get-tuple-element.26), channel_id=1, source_target_pairs={{0,3},{1,2},{2,1},{3,0},{4,7},{5,6},{6,5},{7,4},{8,11},{9,10},{10,... | collective-permute-start | bytes 196616 | tf_op jit(solution)/shard_map/ppermute | solution.py:22
  102.2 5.5 %collective-permute-start.30 = (bf16[32,1024]{1,0:T(8,128)(2,1)S(1)}, bf16[32,1024]{1,0:T(8,128)(2,1)S(1)}, u32[]{:S(2)}, u32[]{:S(2)}) collective-permute-start(bf16[32,1024]{1,0:T(8,128)(2,1)S(1)} %get-tuple-element.27), channel_id=1, source_target_pairs={{0,2},{1,3},{2,0},{3,1},{4,6},{5,7},{6,4},{7,5},{8,10},{9,11},{10,... | collective-permute-start | bytes 196616 | tf_op jit(solution)/shard_map/ppermute | solution.py:22
  103.5 4.2 %collective-permute-start.29 = (bf16[32,1024]{1,0:T(8,128)(2,1)S(1)}, bf16[32,1024]{1,0:T(8,128)(2,1)S(1)}, u32[]{:S(2)}, u32[]{:S(2)}) collective-permute-start(bf16[32,1024]{1,0:T(8,128)(2,1)S(1)} %get-tuple-element.28), channel_id=1, source_target_pairs={{0,1},{1,0},{2,3},{3,2},{4,5},{5,4},{6,7},{7,6},{8,9},{9,8},{10,11... | collective-permute-start | bytes 196616 | tf_op jit(solution)/shard_map/ppermute | solution.py:22

commit v5 on v4

--- a/solution.py
+++ b/solution.py
@@ -69,12 +69,12 @@
         first = hop(product(jnp.where(end, 3, 1)).astype(low), "seq", 1)
         second = product(jnp.where(end, 1, 3)).astype(low)
         middle = lax.ppermute(second, "seq", [(1, 2), (2, 1)])
-        near = hop(second, "seq", 1)
+        near = lax.ppermute(second, "seq", [(0, 1), (3, 2)])
         rows, first = lax.optimization_barrier((rows, first))
         relayed = jnp.where(end, 0.0, first.astype(jnp.float32))
         last = hop((product(2) + relayed).astype(low), "seq", 2)
-        total = product(0) + jnp.where(end, first, near).astype(jnp.float32) + middle.astype(jnp.float32)
-        return [total, last]
+        total = product(0) + jnp.where(end, first, 0.0).astype(jnp.float32) + middle.astype(jnp.float32)
+        return [total, last, near]
     if narrow:
         return [term.transpose(0, 2, 1) for term in [product(0)] + came]
     return [product(0)] + came

time: 109 us -> 109 us (level)
  waiting for transfers between devices: 43.7 us -> 37.5 us
  starting transfers between devices: 37.9 us -> 43.3 us
    ppermute x0 -> x2, starting transfers between devices: none -> 10.5 us  [sum_over_seq(): near = lax.ppermute(second, 'seq', [(0, 1), (3, 2)])]
    ppermute x30 -> x28, waiting for transfers between devices: 43.7 us -> 37.3 us  [hop(): return lax.ppermute(value, axis, [(a, a ^ mask) for a in range(count)])]
    ppermute x30 -> x28, starting transfers between devices: 36.5 us -> 31.5 us  [hop(): return lax.ppermute(value, axis, [(a, a ^ mask) for a in range(count)])]
  transfers between devices with their start and end apart: 32 -> 32, of which waited for: 17 -> 14; matrix products, arithmetic and copies ran while one was open for 13% -> 13% of each run, Pallas kernels for 3% -> 3%
where the time goes in v5:
time: 109 us; the launch traced here: 108 us
  starting transfers between devices  43.3 us (40%)
  waiting for transfers between devices  37.5 us (34%)
  Pallas kernels  8.24 us (8%)
  matrix products  8.1 us (7%)
  local copies, waits for them, and re-layouts  6.84 us (6%)
  other arithmetic  3.69 us (3%)
    ppermute x28, waiting for transfers between devices, hop(): return lax.ppermute(value, axis, [(a, a ^ mask) for a in range(count)])  37.3 us
    ppermute x28, starting transfers between devices, hop(): return lax.ppermute(value, axis, [(a, a ^ mask) for a in range(count)])  31.5 us
    ppermute x2, starting transfers between devices, sum_over_seq(): near = lax.ppermute(second, 'seq', [(0, 1), (3, 2)])  10.5 us
    pallas_call x1, Pallas kernels, local_stage(): pl.pallas_call(functools.partial(local_kernel, groups, len(terms[0]), seq...  5.13 us
    dot_general x8, matrix products, product(): jnp.einsum(form, rows, weight_of(mask), preferred_element_type=jnp.float32)  5.02 us
    pallas_call x1, Pallas kernels, local_stage(): spectrum = make_spectrum(*wide[:2], long_filter)  3.11 us
    dot_general x4, matrix products, shards(): jnp.einsum('rc,nc->rn', got[place * seq * sub:(place + 1) * seq * sub], o...  3.08 us
    dynamic_slice x1, local copies, waits for them, and re-layouts, shards(): lax.dynamic_slice_in_dim(out_weight, (z ^ mask) * own, own, 1)  2.2 us
  transfers between devices with their start and end apart: 32, of which 14 were waited for; matrix products, arithmetic and copies ran while one was open for 13% of the time, Pallas kernels for 3%

profile of v5, /device:TPU:0, one launch (start us, length us, event | category | flops | bytes accessed | tf_op | source)
XLA Modules:
  0.0 108.2 jit_solution(6915666948539265928)
XLA Ops:
  0.0 1.2 %convert_element_type.92 = bf16[128,1024]{1,0:T(8,128)(2,1)S(1)} convert(f32[128,1024]{1,0:T(8,128)} %param.10) | non-fusion elementwise | flops 131072 | bytes 786432 | tf_op jit(solution)/shard_map/convert_element_type | solution.py:272
  1.2 0.7 constant_dynamic-slice_fusion.23
  1.9 2.4 %collective-permute-start.2 = (bf16[32,1024]{1,0:T(8,128)(2,1)}, bf16[32,1024]{1,0:T(8,128)(2,1)S(1)}, u32[]{:S(2)}, u32[]{:S(2)}) collective-permute-start(bf16[32,1024]{1,0:T(8,128)(2,1)} %get-tuple-element.50), channel_id=1, source_target_pairs={{0,3},{1,2},{2,1},{3,0},{4,7},{5,6},{6,5},{7,4},{8,11},{9,10},{10,... | collective-permute-start | bytes 196616 | tf_op jit(solution)/shard_map/ppermute | solution.py:22
  4.3 0.6 collective-permute-start.1
  4.9 0.1 collective-permute-start
  5.0 0.7 mul.56
  5.8 1.4 %collective-permute-done.2 = bf16[32,1024]{1,0:T(8,128)(2,1)S(1)} collective-permute-done((bf16[32,1024]{1,0:T(8,128)(2,1)}, bf16[32,1024]{1,0:T(8,128)(2,1)S(1)}, u32[]{:S(2)}, u32[]{:S(2)}) %collective-permute-start.2) | collective-permute-done | bytes 65568 | tf_op jit(solution)/shard_map/ppermute | solution.py:22
  7.1 2.1 %collective-permute-done.1 = bf16[32,1024]{1,0:T(8,128)(2,1)S(1)} collective-permute-done((bf16[32,1024]{1,0:T(8,128)(2,1)}, bf16[32,1024]{1,0:T(8,128)(2,1)S(1)}, u32[]{:S(2)}, u32[]{:S(2)}) %collective-permute-start.1) | collective-permute-done | bytes 65568 | tf_op jit(solution)/shard_map/ppermute | solution.py:22
  9.3 0.2 fusion.23
  9.5 0.1 fusion.25
  9.7 3.9 %collective-permute-start.5 = (bf16[32,1024]{1,0:T(8,128)(2,1)S(1)}, bf16[32,1024]{1,0:T(8,128)(2,1)S(1)}, u32[]{:S(2)}, u32[]{:S(2)}) collective-permute-start(bf16[32,1024]{1,0:T(8,128)(2,1)S(1)} %get-tuple-element.42), channel_id=1, source_target_pairs={{0,12},{4,8},{8,4},{12,0},{1,13},{5,9},{9,5},{13,1},{2,14},{6,10},... | collective-permute-start | bytes 196616 | tf_op jit(solution)/shard_map/ppermute | solution.py:22
  13.5 0.6 collective-permute-start.3
  14.2 1.9 %collective-permute-done.5 = bf16[32,1024]{1,0:T(8,128)(2,1)S(1)} collective-permute-done((bf16[32,1024]{1,0:T(8,128)(2,1)S(1)}, bf16[32,1024]{1,0:T(8,128)(2,1)S(1)}, u32[]{:S(2)}, u32[]{:S(2)}) %collective-permute-start.5) | collective-permute-done | bytes 65568 | tf_op jit(solution)/shard_map/ppermute | solution.py:22
  16.1 3.3 %collective-permute-done.4 = bf16[32,1024]{1,0:T(8,128)(2,1)S(1)} collective-permute-done((bf16[32,1024]{1,0:T(8,128)(2,1)S(1)}, bf16[32,1024]{1,0:T(8,128)(2,1)S(1)}, u32[]{:S(2)}, u32[]{:S(2)}) %collective-permute-start.4) | collective-permute-done | bytes 65568 | tf_op jit(solution)/shard_map/ppermute | solution.py:22
  19.4 0.1 collective-permute-start.6
  19.5 3.1 %filter_spectrum.1.refs_8_ = f32[1024,128]{1,0:T(8,128)} custom-call(bf16[1024,512]{1,0:T(8,128)(2,1)} %constant.103.clone.high_ref.refs_6_, bf16[1024,512]{1,0:T(8,128)(2,1)} %constant.104.clone.low_ref.refs_7_, f32[128,512]{1,0:T(8,128)} %taps_ref.1), custom_call_target="tpu_custom_call" | custom-call | flops 402653184 | bytes 1048576 | tf_op jit(solution)/shard_map/filter_spectrum/pallas_call | solution.py:215
  22.6 1.3 %constant_dynamic-slice_fusion.24.taps_ref = f32[3,3,128]{2,1,0:T(4,128)} fusion(f32[3,3,512]{2,1,0:T(4,128)} %param.13, s32[]{:T(128)S(6)} %select_n.105), kind=kLoop, calls=%fused_computation.116 | loop fusion | bytes 9220 | tf_op jit(solution)/shard_map/dynamic_slice | solution.py:279
  23.9 2.2 %constant_dynamic-slice_fusion.13 = (bf16[1024,128]{1,0:T(8,128)(2,1)}, bf16[1024,128]{1,0:T(8,128)(2,1)}, bf16[1024,128]{1,0:T(8,128)(2,1)}, bf16[1024,128]{1,0:T(8,128)(2,1)}) fusion(bf16[1024,512]{1,0:T(8,128)(2,1)} %param.15, s32[]{:T(128)S(6)} %select_n.105, s32[]{:T(128)S(6)} %select_n.124, s32[]{:T(128)S(6)} %select_n.125, s32[]{:T(128)S(6)} %select_n.120), kind=kLoop, calls=%fused_computation.101 | loop fusion | bytes 2097168 | tf_op jit(solution)/shard_map/dynamic_slice | solution.py:277
  26.1 1.6 %collective-permute-start.11 = (bf16[128,1024]{1,0:T(8,128)(2,1)S(1)}, bf16[128,1024]{1,0:T(8,128)(2,1)S(1)}, u32[]{:S(2)}, u32[]{:S(2)}) collective-permute-start(bf16[128,1024]{1,0:T(8,128)(2,1)S(1)} %bitcast.97), channel_id=1, source_target_pairs={{0,2},{1,3},{2,0},{3,1},{4,6},{5,7},{6,4},{7,5},{8,10},{9,11},{10,... | collective-permute-start | bytes 786440 | tf_op jit(solution)/shard_map/ppermute | solution.py:22
  27.7 1.0 pad_maximum_fusion.1
  28.7 0.4 fusion.11
  29.1 1.1 %collective-permute-start.7 = (bf16[3,256,128]{2,1,0:T(8,128)(2,1)S(1)}, bf16[3,256,128]{2,1,0:T(8,128)(2,1)S(1)}, u32[]{:S(2)}, u32[]{:S(2)}) collective-permute-start(bf16[3,256,128]{2,1,0:T(8,128)(2,1)S(1)} %fusion.11), channel_id=1, source_target_pairs={{0,4},{4,0},{8,12},{12,8},{1,5},{5,1},{9,13},{13,9},{2,6},{6,2},{1... | collective-permute-start | bytes 589832 | tf_op jit(solution)/shard_map/ppermute | solution.py:22
  30.3 0.4 fusion.12
  30.7 0.7 collective-permute-start.8
  31.4 5.7 %collective-permute-start.10 = (bf16[3,256,128]{2,1,0:T(8,128)(2,1)S(1)}, bf16[3,256,128]{2,1,0:T(8,128)(2,1)S(1)}, u32[]{:S(2)}, u32[]{:S(2)}) collective-permute-start(bf16[3,256,128]{2,1,0:T(8,128)(2,1)S(1)} %fusion.12), channel_id=1, source_target_pairs={{0,4},{12,8},{1,5},{13,9},{2,6},{14,10},{3,7},{15,11},{16,20},{28,... | collective-permute-start | bytes 589832 | tf_op jit(solution)/shard_map/ppermute | solution.py:72
  37.2 0.4 fusion.9
  37.7 0.4 collective-permute-start.9
  38.1 1.2 %fusion.7.refs_0_ = f32[3,256,128]{2,1,0:T(8,128)} fusion(bf16[3,1024,512]{2,1,0:T(8,128)(2,1)S(1)} %copy-done, s32[]{:T(128)S(6)} %select_n.105, bf16[256,1024]{1,0:T(8,128)(2,1)S(1)} %pad_maximum_fusion.1, bf16[3,256,128]{2,1,0:T(8,128)(2,1)S(1)} %collective-permute-done.8, bf16[3,256,128]{2,1,0:T(8,128)(2,1)S(1)} %collective-permute-done.7, pred[]{:T(512)S(6)} %or.4), kind=kOutput, calls=%fused_computation.15 | convolution fusion | flops 201818112 | bytes 2097157 | tf_op jit(solution)/shard_map/rd,sdc->src/dot_general | solution.py:60
  39.3 0.4 fusion.13
  39.7 2.3 %collective-permute-start.13 = (bf16[3,256,128]{2,1,0:T(8,128)(2,1)S(1)}, bf16[3,256,128]{2,1,0:T(8,128)(2,1)S(1)}, u32[]{:S(2)}, u32[]{:S(2)}) collective-permute-start(bf16[3,256,128]{2,1,0:T(8,128)(2,1)S(1)} %fusion.13), channel_id=1, source_target_pairs={{0,4},{4,0},{8,12},{12,8},{1,5},{5,1},{9,13},{13,9},{2,6},{6,2},{1... | collective-permute-start | bytes 589832 | tf_op jit(solution)/shard_map/ppermute | solution.py:22
  42.1 0.4 fusion.14
  42.5 0.7 collective-permute-start.14
  43.2 4.8 %collective-permute-start.16 = (bf16[3,256,128]{2,1,0:T(8,128)(2,1)S(1)}, bf16[3,256,128]{2,1,0:T(8,128)(2,1)S(1)}, u32[]{:S(2)}, u32[]{:S(2)}) collective-permute-start(bf16[3,256,128]{2,1,0:T(8,128)(2,1)S(1)} %fusion.14), channel_id=1, source_target_pairs={{0,4},{12,8},{1,5},{13,9},{2,6},{14,10},{3,7},{15,11},{16,20},{28,... | collective-permute-start | bytes 589832 | tf_op jit(solution)/shard_map/ppermute | solution.py:72
  48.0 2.9 %collective-permute-done.13 = bf16[3,256,128]{2,1,0:T(8,128)(2,1)S(1)} collective-permute-done((bf16[3,256,128]{2,1,0:T(8,128)(2,1)S(1)}, bf16[3,256,128]{2,1,0:T(8,128)(2,1)S(1)}, u32[]{:S(2)}, u32[]{:S(2)}) %collective-permute-start.13) | collective-permute-done | bytes 196640 | tf_op jit(solution)/shard_map/ppermute | solution.py:22
  50.9 0.4 fusion.10
  51.3 2.4 %collective-permute-start.15 = (bf16[3,256,128]{2,1,0:T(8,128)(2,1)S(1)}, bf16[3,256,128]{2,1,0:T(8,128)(2,1)S(1)}, u32[]{:S(2)}, u32[]{:S(2)}) collective-permute-start(bf16[3,256,128]{2,1,0:T(8,128)(2,1)S(1)} %fusion.10), channel_id=1, source_target_pairs={{0,8},{4,12},{8,0},{12,4},{1,9},{5,13},{9,1},{13,5},{2,10},{6,14},... | collective-permute-start | bytes 589832 | tf_op jit(solution)/shard_map/ppermute | solution.py:22
  53.7 1.2 %fusion.8.refs_3_ = f32[3,256,128]{2,1,0:T(8,128)} fusion(bf16[3,1024,512]{2,1,0:T(8,128)(2,1)S(1)} %copy-done, s32[]{:T(128)S(6)} %select_n.105, bf16[256,1024]{1,0:T(8,128)(2,1)S(1)} %pad_maximum_fusion.2, bf16[3,256,128]{2,1,0:T(8,128)(2,1)S(1)} %collective-permute-done.14, bf16[3,256,128]{2,1,0:T(8,128)(2,1)S(1)} %collective-permute-done.13, pred[]{:T(512)S(6)} %or.4), kind=kOutput, calls=%fused_computation.16 | convolution fusion | flops 201818112 | bytes 2097157 | tf_op jit(solution)/shard_map/rd,sdc->src/dot_general | solution.py:60
  54.9 0.1 collective-permute-done.16.refs_5_
  55.1 7.7 %collective-permute-done.15.refs_4_ = bf16[3,256,128]{2,1,0:T(8,128)(2,1)S(1)} collective-permute-done((bf16[3,256,128]{2,1,0:T(8,128)(2,1)S(1)}, bf16[3,256,128]{2,1,0:T(8,128)(2,1)S(1)}, u32[]{:S(2)}, u32[]{:S(2)}) %collective-permute-start.15) | collective-permute-done | bytes 196640 | tf_op jit(solution)/shard_map/ppermute | solution.py:22
  62.8 0.7 copy-done.9
  63.4 5.1 %filters.1 = (bf16[256,128]{1,0:T(8,128)(2,1)}, bf16[256,128]{1,0:T(8,128)(2,1)}) custom-call(s32[1]{0:T(128)} %bitcast.t_ref, f32[3,3,128]{2,1,0:T(4,128)} %constant_dynamic-slice_fusion.24.taps_ref, f32[3,256,128]{2,1,0:T(8,128)} %fusion.7.refs_0_, bf16[3,256,128]{2,1,0:T(8,128)(2,1)} %copy-done.7, bf16[3,256,128]{2,1,0:T(8,128)(2,1)} %copy-done.6, ...), custom_call_target="tpu_custom_call" | custom-call | flops 805306368 | bytes 2097152 | tf_op jit(solution)/shard_map/filters/pallas_call | solution.py:219
  68.7 1.9 %collective-permute-start.22 = (bf16[256,128]{1,0:T(8,128)(2,1)}, bf16[256,128]{1,0:T(8,128)(2,1)S(1)}, u32[]{:S(2)}, u32[]{:S(2)}) collective-permute-start(bf16[256,128]{1,0:T(8,128)(2,1)} %get-tuple-element.16), channel_id=1, source_target_pairs={{0,8},{4,12},{8,0},{12,4},{1,9},{5,13},{9,1},{13,5},{2,10},{6,14},... | collective-permute-start | bytes 196616 | tf_op jit(solution)/shard_map/ppermute | solution.py:22
  70.6 2.5 %collective-permute-start.23 = (bf16[256,128]{1,0:T(8,128)(2,1)}, bf16[256,128]{1,0:T(8,128)(2,1)S(1)}, u32[]{:S(2)}, u32[]{:S(2)}) collective-permute-start(bf16[256,128]{1,0:T(8,128)(2,1)} %get-tuple-element.16), channel_id=1, source_target_pairs={{0,12},{4,8},{8,4},{12,0},{1,13},{5,9},{9,5},{13,1},{2,14},{6,10},... | collective-permute-start | bytes 196616 | tf_op jit(solution)/shard_map/ppermute | solution.py:22
  73.0 1.9 %collective-permute-start.18 = (bf16[256,128]{1,0:T(8,128)(2,1)}, bf16[256,128]{1,0:T(8,128)(2,1)S(1)}, u32[]{:S(2)}, u32[]{:S(2)}) collective-permute-start(bf16[256,128]{1,0:T(8,128)(2,1)} %get-tuple-element.15), channel_id=1, source_target_pairs={{0,8},{4,12},{8,0},{12,4},{1,9},{5,13},{9,1},{13,5},{2,10},{6,14},... | collective-permute-start | bytes 196616 | tf_op jit(solution)/shard_map/ppermute | solution.py:22
  75.0 0.9 constant_dynamic-update-slice_fusion.3
  75.9 2.5 %collective-permute-start.19 = (bf16[256,128]{1,0:T(8,128)(2,1)}, bf16[256,128]{1,0:T(8,128)(2,1)S(1)}, u32[]{:S(2)}, u32[]{:S(2)}) collective-permute-start(bf16[256,128]{1,0:T(8,128)(2,1)} %get-tuple-element.15), channel_id=1, source_target_pairs={{0,12},{4,8},{8,4},{12,0},{1,13},{5,9},{9,5},{13,1},{2,14},{6,10},... | collective-permute-start | bytes 196616 | tf_op jit(solution)/shard_map/ppermute | solution.py:22
  78.5 1.6 %convolution_convert_fusion = bf16[128,1024]{1,0:T(8,128)(2,1)S(1)} fusion(bf16[256,512]{1,0:T(8,128)(2,1)S(1)} %constant_dynamic-update-slice_fusion.4, bf16[1024,128]{1,0:T(8,128)(2,1)} %get-tuple-element.19, bf16[1024,128]{1,0:T(8,128)(2,1)} %get-tuple-element.20, bf16[1024,128]{1,0:T(8,128)(2,1)} %get-tuple-element.18, bf16[1024,128]{1,0:T(8,128)(2,1)S(1)} %copy-done.2), kind=kOutput, calls=%fused_computation.13 | convolution fusion | flops 138543104 | bytes 1441792 | tf_op jit(solution)/shard_map/rc,nc->rn/dot_general | solution.py:305
  80.3 2.0 %collective-permute-done.18 = bf16[256,128]{1,0:T(8,128)(2,1)S(1)} collective-permute-done((bf16[256,128]{1,0:T(8,128)(2,1)}, bf16[256,128]{1,0:T(8,128)(2,1)S(1)}, u32[]{:S(2)}, u32[]{:S(2)}) %collective-permute-start.18) | collective-permute-done | bytes 65568 | tf_op jit(solution)/shard_map/ppermute | solution.py:22
  82.4 0.5 convolution_convert_fusion.1
  83.0 0.5 fusion.2
  83.5 0.5 collective-permute-start.25
  84.0 0.5 collective-permute-done.20
  84.5 7.7 %collective-permute-done.25 = bf16[128,1024]{1,0:T(8,128)(2,1)S(1)} collective-permute-done((bf16[128,1024]{1,0:T(8,128)(2,1)S(1)}, bf16[128,1024]{1,0:T(8,128)(2,1)S(1)}, u32[]{:S(2)}, u32[]{:S(2)}) %collective-permute-start.25) | collective-permute-done | bytes 262176 | tf_op jit(solution)/shard_map/ppermute | solution.py:22
  92.2 0.5 fusion.1
  92.8 2.4 %collective-permute-start.28 = (bf16[32,1024]{1,0:T(8,128)(2,1)S(1)}, bf16[32,1024]{1,0:T(8,128)(2,1)S(1)}, u32[]{:S(2)}, u32[]{:S(2)}) collective-permute-start(bf16[32,1024]{1,0:T(8,128)(2,1)S(1)} %get-tuple-element.34), channel_id=1, source_target_pairs={{0,12},{4,8},{8,4},{12,0},{1,13},{5,9},{9,5},{13,1},{2,14},{6,10},... | collective-permute-start | bytes 196616 | tf_op jit(solution)/shard_map/ppermute | solution.py:22
  95.1 0.4 collective-permute-start.27
  95.5 1.7 %collective-permute-start.26 = (bf16[32,1024]{1,0:T(8,128)(2,1)S(1)}, bf16[32,1024]{1,0:T(8,128)(2,1)S(1)}, u32[]{:S(2)}, u32[]{:S(2)}) collective-permute-start(bf16[32,1024]{1,0:T(8,128)(2,1)S(1)} %get-tuple-element.36), channel_id=1, source_target_pairs={{0,4},{4,0},{8,12},{12,8},{1,5},{5,1},{9,13},{13,9},{2,6},{6,2},{1... | collective-permute-start | bytes 196616 | tf_op jit(solution)/shard_map/ppermute | solution.py:22
  97.2 1.8 %collective-permute-done.28 = bf16[32,1024]{1,0:T(8,128)(2,1)S(1)} collective-permute-done((bf16[32,1024]{1,0:T(8,128)(2,1)S(1)}, bf16[32,1024]{1,0:T(8,128)(2,1)S(1)}, u32[]{:S(2)}, u32[]{:S(2)}) %collective-permute-start.28) | collective-permute-done | bytes 65568 | tf_op jit(solution)/shard_map/ppermute | solution.py:22
  99.1 2.7 %collective-permute-done.27 = bf16[32,1024]{1,0:T(8,128)(2,1)S(1)} collective-permute-done((bf16[32,1024]{1,0:T(8,128)(2,1)S(1)}, bf16[32,1024]{1,0:T(8,128)(2,1)S(1)}, u32[]{:S(2)}, u32[]{:S(2)}) %collective-permute-start.27) | collective-permute-done | bytes 65568 | tf_op jit(solution)/shard_map/ppermute | solution.py:22
  102.0 1.1 %collective-permute-start.30 = (bf16[32,1024]{1,0:T(8,128)(2,1)S(1)}, bf16[32,1024]{1,0:T(8,128)(2,1)S(1)}, u32[]{:S(2)}, u32[]{:S(2)}) collective-permute-start(bf16[32,1024]{1,0:T(8,128)(2,1)S(1)} %get-tuple-element.27), channel_id=1, source_target_pairs={{0,2},{1,3},{2,0},{3,1},{4,6},{5,7},{6,4},{7,5},{8,10},{9,11},{10,... | collective-permute-start | bytes 196616 | tf_op jit(solution)/shard_map/ppermute | solution.py:22
  103.1 0.7 collective-permute-start.29
  103.9 2.5 %collective-permute-done.31 = bf16[32,1024]{1,0:T(8,128)(2,1)S(1)} collective-permute-done((bf16[32,1024]{1,0:T(8,128)(2,1)S(1)}, bf16[32,1024]{1,0:T(8,128)(2,1)S(1)}, u32[]{:S(2)}, u32[]{:S(2)}) %collective-permute-start.31) | collective-permute-done | bytes 65568 | tf_op jit(solution)/shard_map/ppermute | solution.py:22
  106.4 0.8 collective-permute-done.30
  107.3 0.9 convert_add_fusion
  (66 shorter events, 1.1 us)
Async XLA Ops:
  0.0 28.7 %copy-start = (bf16[3,1024,512]{2,1,0:T(8,128)(2,1)S(1)}, bf16[3,1024,512]{2,1,0:T(8,128)(2,1)}, u32[]{:S(2)}) copy-start(bf16[3,1024,512]{2,1,0:T(8,128)(2,1)} %param.12) | copy-start | bytes 9437188
  1.9 5.2 %collective-permute-start.2 = (bf16[32,1024]{1,0:T(8,128)(2,1)}, bf16[32,1024]{1,0:T(8,128)(2,1)S(1)}, u32[]{:S(2)}, u32[]{:S(2)}) collective-permute-start(bf16[32,1024]{1,0:T(8,128)(2,1)} %get-tuple-element.50), channel_id=1, source_target_pairs={{0,3},{1,2},{2,1},{3,0},{4,7},{5,6},{6,5},{7,4},{8,11},{9,10},{10,... | collective-permute-start | bytes 196616 | tf_op jit(solution)/shard_map/ppermute | solution.py:22
  4.3 4.9 %collective-permute-start.1 = (bf16[32,1024]{1,0:T(8,128)(2,1)}, bf16[32,1024]{1,0:T(8,128)(2,1)S(1)}, u32[]{:S(2)}, u32[]{:S(2)}) collective-permute-start(bf16[32,1024]{1,0:T(8,128)(2,1)} %get-tuple-element.51), channel_id=1, source_target_pairs={{0,2},{1,3},{2,0},{3,1},{4,6},{5,7},{6,4},{7,5},{8,10},{9,11},{10,... | collective-permute-start | bytes 196616 | tf_op jit(solution)/shard_map/ppermute | solution.py:22
  4.9 4.3 %collective-permute-start = (bf16[32,1024]{1,0:T(8,128)(2,1)S(1)}, bf16[32,1024]{1,0:T(8,128)(2,1)S(1)}, u32[]{:S(2)}, u32[]{:S(2)}) collective-permute-start(bf16[32,1024]{1,0:T(8,128)(2,1)S(1)} %get-tuple-element.52), channel_id=1, source_target_pairs={{0,1},{1,0},{2,3},{3,2},{4,5},{5,4},{6,7},{7,6},{8,9},{9,8},{10,11... | collective-permute-start | bytes 196616 | tf_op jit(solution)/shard_map/ppermute | solution.py:22
  9.7 6.4 %collective-permute-start.5 = (bf16[32,1024]{1,0:T(8,128)(2,1)S(1)}, bf16[32,1024]{1,0:T(8,128)(2,1)S(1)}, u32[]{:S(2)}, u32[]{:S(2)}) collective-permute-start(bf16[32,1024]{1,0:T(8,128)(2,1)S(1)} %get-tuple-element.42), channel_id=1, source_target_pairs={{0,12},{4,8},{8,4},{12,0},{1,13},{5,9},{9,5},{13,1},{2,14},{6,10},... | collective-permute-start | bytes 196616 | tf_op jit(solution)/shard_map/ppermute | solution.py:22
  13.5 5.8 %collective-permute-start.4 = (bf16[32,1024]{1,0:T(8,128)(2,1)S(1)}, bf16[32,1024]{1,0:T(8,128)(2,1)S(1)}, u32[]{:S(2)}, u32[]{:S(2)}) collective-permute-start(bf16[32,1024]{1,0:T(8,128)(2,1)S(1)} %get-tuple-element.43), channel_id=1, source_target_pairs={{0,8},{4,12},{8,0},{12,4},{1,9},{5,13},{9,1},{13,5},{2,10},{6,14},... | collective-permute-start | bytes 196616 | tf_op jit(solution)/shard_map/ppermute | solution.py:22
  13.5 5.8 %collective-permute-start.3 = (bf16[32,1024]{1,0:T(8,128)(2,1)S(1)}, bf16[32,1024]{1,0:T(8,128)(2,1)S(1)}, u32[]{:S(2)}, u32[]{:S(2)}) collective-permute-start(bf16[32,1024]{1,0:T(8,128)(2,1)S(1)} %get-tuple-element.44), channel_id=1, source_target_pairs={{0,4},{4,0},{8,12},{12,8},{1,5},{5,1},{9,13},{13,9},{2,6},{6,2},{1... | collective-permute-start | bytes 196616 | tf_op jit(solution)/shard_map/ppermute | solution.py:22
  19.4 8.3 %collective-permute-start.6 = (bf16[128,1024]{1,0:T(8,128)(2,1)S(1)}, bf16[128,1024]{1,0:T(8,128)(2,1)}, u32[]{:S(2)}, u32[]{:S(2)}) collective-permute-start(bf16[128,1024]{1,0:T(8,128)(2,1)S(1)} %bitcast.96), channel_id=1, source_target_pairs={{0,1},{1,0},{2,3},{3,2},{4,5},{5,4},{6,7},{7,6},{8,9},{9,8},{10,11... | collective-permute-start | bytes 786440 | tf_op jit(solution)/shard_map/ppermute | solution.py:22
  26.1 11.0 %collective-permute-start.11 = (bf16[128,1024]{1,0:T(8,128)(2,1)S(1)}, bf16[128,1024]{1,0:T(8,128)(2,1)S(1)}, u32[]{:S(2)}, u32[]{:S(2)}) collective-permute-start(bf16[128,1024]{1,0:T(8,128)(2,1)S(1)} %bitcast.97), channel_id=1, source_target_pairs={{0,2},{1,3},{2,0},{3,1},{4,6},{5,7},{6,4},{7,5},{8,10},{9,11},{10,... | collective-permute-start | bytes 786440 | tf_op jit(solution)/shard_map/ppermute | solution.py:22
  29.1 8.1 %collective-permute-start.7 = (bf16[3,256,128]{2,1,0:T(8,128)(2,1)S(1)}, bf16[3,256,128]{2,1,0:T(8,128)(2,1)S(1)}, u32[]{:S(2)}, u32[]{:S(2)}) collective-permute-start(bf16[3,256,128]{2,1,0:T(8,128)(2,1)S(1)} %fusion.11), channel_id=1, source_target_pairs={{0,4},{4,0},{8,12},{12,8},{1,5},{5,1},{9,13},{13,9},{2,6},{6,2},{1... | collective-permute-start | bytes 589832 | tf_op jit(solution)/shard_map/ppermute | solution.py:22
  30.7 7.3 %collective-permute-start.8 = (bf16[3,256,128]{2,1,0:T(8,128)(2,1)S(1)}, bf16[3,256,128]{2,1,0:T(8,128)(2,1)S(1)}, u32[]{:S(2)}, u32[]{:S(2)}) collective-permute-start(bf16[3,256,128]{2,1,0:T(8,128)(2,1)S(1)} %fusion.12), channel_id=1, source_target_pairs={{4,8},{8,4},{5,9},{9,5},{6,10},{10,6},{7,11},{11,7},{20,24},{24,20... | collective-permute-start | bytes 589832 | tf_op jit(solution)/shard_map/ppermute | solution.py:71
  31.4 23.5 %collective-permute-start.10 = (bf16[3,256,128]{2,1,0:T(8,128)(2,1)S(1)}, bf16[3,256,128]{2,1,0:T(8,128)(2,1)S(1)}, u32[]{:S(2)}, u32[]{:S(2)}) collective-permute-start(bf16[3,256,128]{2,1,0:T(8,128)(2,1)S(1)} %fusion.12), channel_id=1, source_target_pairs={{0,4},{12,8},{1,5},{13,9},{2,6},{14,10},{3,7},{15,11},{16,20},{28,... | collective-permute-start | bytes 589832 | tf_op jit(solution)/shard_map/ppermute | solution.py:72
  37.1 2.1 %collective-permute-start.12 = (bf16[128,1024]{1,0:T(8,128)(2,1)S(1)}, bf16[128,1024]{1,0:T(8,128)(2,1)S(1)}, u32[]{:S(2)}, u32[]{:S(2)}) collective-permute-start(bf16[128,1024]{1,0:T(8,128)(2,1)S(1)} %collective-permute-done.11), channel_id=1, source_target_pairs={{0,1},{1,0},{2,3},{3,2},{4,5},{5,4},{6,7},{7,6},{8,9},{9,8},{10,11... | collective-permute-start | bytes 786440 | tf_op jit(solution)/shard_map/ppermute | solution.py:22
  37.7 17.3 %collective-permute-start.9 = (bf16[3,256,128]{2,1,0:T(8,128)(2,1)S(1)}, bf16[3,256,128]{2,1,0:T(8,128)(2,1)S(1)}, u32[]{:S(2)}, u32[]{:S(2)}) collective-permute-start(bf16[3,256,128]{2,1,0:T(8,128)(2,1)S(1)} %fusion.9), channel_id=1, source_target_pairs={{0,8},{4,12},{8,0},{12,4},{1,9},{5,13},{9,1},{13,5},{2,10},{6,14},... | collective-permute-start | bytes 589832 | tf_op jit(solution)/shard_map/ppermute | solution.py:22
  39.7 11.1 %collective-permute-start.13 = (bf16[3,256,128]{2,1,0:T(8,128)(2,1)S(1)}, bf16[3,256,128]{2,1,0:T(8,128)(2,1)S(1)}, u32[]{:S(2)}, u32[]{:S(2)}) collective-permute-start(bf16[3,256,128]{2,1,0:T(8,128)(2,1)S(1)} %fusion.13), channel_id=1, source_target_pairs={{0,4},{4,0},{8,12},{12,8},{1,5},{5,1},{9,13},{13,9},{2,6},{6,2},{1... | collective-permute-start | bytes 589832 | tf_op jit(solution)/shard_map/ppermute | solution.py:22
  42.5 11.2 %collective-permute-start.14 = (bf16[3,256,128]{2,1,0:T(8,128)(2,1)S(1)}, bf16[3,256,128]{2,1,0:T(8,128)(2,1)S(1)}, u32[]{:S(2)}, u32[]{:S(2)}) collective-permute-start(bf16[3,256,128]{2,1,0:T(8,128)(2,1)S(1)} %fusion.14), channel_id=1, source_target_pairs={{4,8},{8,4},{5,9},{9,5},{6,10},{10,6},{7,11},{11,7},{20,24},{24,20... | collective-permute-start | bytes 589832 | tf_op jit(solution)/shard_map/ppermute | solution.py:71
  43.2 11.9 %collective-permute-start.16 = (bf16[3,256,128]{2,1,0:T(8,128)(2,1)S(1)}, bf16[3,256,128]{2,1,0:T(8,128)(2,1)S(1)}, u32[]{:S(2)}, u32[]{:S(2)}) collective-permute-start(bf16[3,256,128]{2,1,0:T(8,128)(2,1)S(1)} %fusion.14), channel_id=1, source_target_pairs={{0,4},{12,8},{1,5},{13,9},{2,6},{14,10},{3,7},{15,11},{16,20},{28,... | collective-permute-start | bytes 589832 | tf_op jit(solution)/shard_map/ppermute | solution.py:72
  51.3 11.4 %collective-permute-start.15 = (bf16[3,256,128]{2,1,0:T(8,128)(2,1)S(1)}, bf16[3,256,128]{2,1,0:T(8,128)(2,1)S(1)}, u32[]{:S(2)}, u32[]{:S(2)}) collective-permute-start(bf16[3,256,128]{2,1,0:T(8,128)(2,1)S(1)} %fusion.10), channel_id=1, source_target_pairs={{0,8},{4,12},{8,0},{12,4},{1,9},{5,13},{9,1},{13,5},{2,10},{6,14},... | collective-permute-start | bytes 589832 | tf_op jit(solution)/shard_map/ppermute | solution.py:22
  54.9 7.8 %copy-start.6 = (bf16[3,256,128]{2,1,0:T(8,128)(2,1)}, bf16[3,256,128]{2,1,0:T(8,128)(2,1)S(1)}, u32[]{:S(2)}) copy-start(bf16[3,256,128]{2,1,0:T(8,128)(2,1)S(1)} %collective-permute-done.10.refs_2_) | copy-start | bytes 589828
  54.9 7.8 %copy-start.7 = (bf16[3,256,128]{2,1,0:T(8,128)(2,1)}, bf16[3,256,128]{2,1,0:T(8,128)(2,1)S(1)}, u32[]{:S(2)}) copy-start(bf16[3,256,128]{2,1,0:T(8,128)(2,1)S(1)} %collective-permute-done.9.refs_1_) | copy-start | bytes 589828
  55.1 7.7 %copy-start.8 = (bf16[3,256,128]{2,1,0:T(8,128)(2,1)}, bf16[3,256,128]{2,1,0:T(8,128)(2,1)S(1)}, u32[]{:S(2)}) copy-start(bf16[3,256,128]{2,1,0:T(8,128)(2,1)S(1)} %collective-permute-done.16.refs_5_) | copy-start | bytes 589828
  62.8 0.7 copy-start.9
  63.4 15.1 %copy-start.2 = (bf16[1024,128]{1,0:T(8,128)(2,1)S(1)}, bf16[1024,128]{1,0:T(8,128)(2,1)}, u32[]{:S(2)}) copy-start(bf16[1024,128]{1,0:T(8,128)(2,1)} %get-tuple-element.17) | copy-start | bytes 786436
  68.6 7.3 %collective-permute-start.21 = (bf16[256,128]{1,0:T(8,128)(2,1)}, bf16[256,128]{1,0:T(8,128)(2,1)S(1)}, u32[]{:S(2)}, u32[]{:S(2)}) collective-permute-start(bf16[256,128]{1,0:T(8,128)(2,1)} %get-tuple-element.16), channel_id=1, source_target_pairs={{0,4},{4,0},{8,12},{12,8},{1,5},{5,1},{9,13},{13,9},{2,6},{6,2},{1... | collective-permute-start | bytes 196616 | tf_op jit(solution)/shard_map/ppermute | solution.py:22
  68.7 9.8 %collective-permute-start.22 = (bf16[256,128]{1,0:T(8,128)(2,1)}, bf16[256,128]{1,0:T(8,128)(2,1)S(1)}, u32[]{:S(2)}, u32[]{:S(2)}) collective-permute-start(bf16[256,128]{1,0:T(8,128)(2,1)} %get-tuple-element.16), channel_id=1, source_target_pairs={{0,8},{4,12},{8,0},{12,4},{1,9},{5,13},{9,1},{13,5},{2,10},{6,14},... | collective-permute-start | bytes 196616 | tf_op jit(solution)/shard_map/ppermute | solution.py:22
  70.6 7.9 %collective-permute-start.23 = (bf16[256,128]{1,0:T(8,128)(2,1)}, bf16[256,128]{1,0:T(8,128)(2,1)S(1)}, u32[]{:S(2)}, u32[]{:S(2)}) collective-permute-start(bf16[256,128]{1,0:T(8,128)(2,1)} %get-tuple-element.16), channel_id=1, source_target_pairs={{0,12},{4,8},{8,4},{12,0},{1,13},{5,9},{9,5},{13,1},{2,14},{6,10},... | collective-permute-start | bytes 196616 | tf_op jit(solution)/shard_map/ppermute | solution.py:22
  73.0 7.2 %collective-permute-start.17 = (bf16[256,128]{1,0:T(8,128)(2,1)}, bf16[256,128]{1,0:T(8,128)(2,1)S(1)}, u32[]{:S(2)}, u32[]{:S(2)}) collective-permute-start(bf16[256,128]{1,0:T(8,128)(2,1)} %get-tuple-element.15), channel_id=1, source_target_pairs={{0,4},{4,0},{8,12},{12,8},{1,5},{5,1},{9,13},{13,9},{2,6},{6,2},{1... | collective-permute-start | bytes 196616 | tf_op jit(solution)/shard_map/ppermute | solution.py:22
  73.0 9.3 %collective-permute-start.18 = (bf16[256,128]{1,0:T(8,128)(2,1)}, bf16[256,128]{1,0:T(8,128)(2,1)S(1)}, u32[]{:S(2)}, u32[]{:S(2)}) collective-permute-start(bf16[256,128]{1,0:T(8,128)(2,1)} %get-tuple-element.15), channel_id=1, source_target_pairs={{0,8},{4,12},{8,0},{12,4},{1,9},{5,13},{9,1},{13,5},{2,10},{6,14},... | collective-permute-start | bytes 196616 | tf_op jit(solution)/shard_map/ppermute | solution.py:22
  75.9 6.5 %collective-permute-start.19 = (bf16[256,128]{1,0:T(8,128)(2,1)}, bf16[256,128]{1,0:T(8,128)(2,1)S(1)}, u32[]{:S(2)}, u32[]{:S(2)}) collective-permute-start(bf16[256,128]{1,0:T(8,128)(2,1)} %get-tuple-element.15), channel_id=1, source_target_pairs={{0,12},{4,8},{8,4},{12,0},{1,13},{5,9},{9,5},{13,1},{2,14},{6,10},... | collective-permute-start | bytes 196616 | tf_op jit(solution)/shard_map/ppermute | solution.py:22
  78.5 3.9 %copy-start.3 = (bf16[1024,128]{1,0:T(8,128)(2,1)S(1)}, bf16[1024,128]{1,0:T(8,128)(2,1)}, u32[]{:S(2)}) copy-start(bf16[1024,128]{1,0:T(8,128)(2,1)} %get-tuple-element.18) | copy-start | bytes 786436
  78.5 3.9 %copy-start.4 = (bf16[1024,128]{1,0:T(8,128)(2,1)S(1)}, bf16[1024,128]{1,0:T(8,128)(2,1)}, u32[]{:S(2)}) copy-start(bf16[1024,128]{1,0:T(8,128)(2,1)} %get-tuple-element.19) | copy-start | bytes 786436
  78.5 3.9 %copy-start.5 = (bf16[1024,128]{1,0:T(8,128)(2,1)S(1)}, bf16[1024,128]{1,0:T(8,128)(2,1)}, u32[]{:S(2)}) copy-start(bf16[1024,128]{1,0:T(8,128)(2,1)} %get-tuple-element.20) | copy-start | bytes 786436
  80.2 2.8 %collective-permute-start.24 = (bf16[128,1024]{1,0:T(8,128)(2,1)S(1)}, bf16[128,1024]{1,0:T(8,128)(2,1)S(1)}, u32[]{:S(2)}, u32[]{:S(2)}) collective-permute-start(bf16[128,1024]{1,0:T(8,128)(2,1)S(1)} %convolution_convert_fusion), channel_id=1, source_target_pairs={{0,1},{1,0},{2,3},{3,2},{4,5},{5,4},{6,7},{7,6},{8,9},{9,8},{10,11... | collective-permute-start | bytes 786440 | tf_op jit(solution)/shard_map/ppermute | solution.py:22
  82.9 1.6 %collective-permute-start.20 = (bf16[128,1024]{1,0:T(8,128)(2,1)S(1)}, bf16[128,1024]{1,0:T(8,128)(2,1)S(1)}, u32[]{:S(2)}, u32[]{:S(2)}) collective-permute-start(bf16[128,1024]{1,0:T(8,128)(2,1)S(1)} %convolution_convert_fusion.1), channel_id=1, source_target_pairs={{0,1},{1,0},{2,3},{3,2},{4,5},{5,4},{6,7},{7,6},{8,9},{9,8},{10,11... | collective-permute-start | bytes 786440 | tf_op jit(solution)/shard_map/ppermute | solution.py:22
  83.5 8.8 %collective-permute-start.25 = (bf16[128,1024]{1,0:T(8,128)(2,1)S(1)}, bf16[128,1024]{1,0:T(8,128)(2,1)S(1)}, u32[]{:S(2)}, u32[]{:S(2)}) collective-permute-start(bf16[128,1024]{1,0:T(8,128)(2,1)S(1)} %fusion.2), channel_id=1, source_target_pairs={{0,2},{1,3},{2,0},{3,1},{4,6},{5,7},{6,4},{7,5},{8,10},{9,11},{10,... | collective-permute-start | bytes 786440 | tf_op jit(solution)/shard_map/ppermute | solution.py:22
  92.7 14.6 %copy-start.1 = (f32[128,1024]{1,0:T(8,128)S(1)}, f32[128,1024]{1,0:T(8,128)}, u32[]{:S(2)}) copy-start(f32[128,1024]{1,0:T(8,128)} %param.10) | copy-start | bytes 1572868
  92.8 6.3 %collective-permute-start.28 = (bf16[32,1024]{1,0:T(8,128)(2,1)S(1)}, bf16[32,1024]{1,0:T(8,128)(2,1)S(1)}, u32[]{:S(2)}, u32[]{:S(2)}) collective-permute-start(bf16[32,1024]{1,0:T(8,128)(2,1)S(1)} %get-tuple-element.34), channel_id=1, source_target_pairs={{0,12},{4,8},{8,4},{12,0},{1,13},{5,9},{9,5},{13,1},{2,14},{6,10},... | collective-permute-start | bytes 196616 | tf_op jit(solution)/shard_map/ppermute | solution.py:22
  95.1 6.6 %collective-permute-start.27 = (bf16[32,1024]{1,0:T(8,128)(2,1)S(1)}, bf16[32,1024]{1,0:T(8,128)(2,1)S(1)}, u32[]{:S(2)}, u32[]{:S(2)}) collective-permute-start(bf16[32,1024]{1,0:T(8,128)(2,1)S(1)} %get-tuple-element.35), channel_id=1, source_target_pairs={{0,8},{4,12},{8,0},{12,4},{1,9},{5,13},{9,1},{13,5},{2,10},{6,14},... | collective-permute-start | bytes 196616 | tf_op jit(solution)/shard_map/ppermute | solution.py:22
  95.5 6.3 %collective-permute-start.26 = (bf16[32,1024]{1,0:T(8,128)(2,1)S(1)}, bf16[32,1024]{1,0:T(8,128)(2,1)S(1)}, u32[]{:S(2)}, u32[]{:S(2)}) collective-permute-start(bf16[32,1024]{1,0:T(8,128)(2,1)S(1)} %get-tuple-element.36), channel_id=1, source_target_pairs={{0,4},{4,0},{8,12},{12,8},{1,5},{5,1},{9,13},{13,9},{2,6},{6,2},{1... | collective-permute-start | bytes 196616 | tf_op jit(solution)/shard_map/ppermute | solution.py:22
  102.0 4.5 %collective-permute-start.31 = (bf16[32,1024]{1,0:T(8,128)(2,1)S(1)}, bf16[32,1024]{1,0:T(8,128)(2,1)S(1)}, u32[]{:S(2)}, u32[]{:S(2)}) collective-permute-start(bf16[32,1024]{1,0:T(8,128)(2,1)S(1)} %get-tuple-element.26), channel_id=1, source_target_pairs={{0,3},{1,2},{2,1},{3,0},{4,7},{5,6},{6,5},{7,4},{8,11},{9,10},{10,... | collective-permute-start | bytes 196616 | tf_op jit(solution)/shard_map/ppermute | solution.py:22
  102.0 5.1 %collective-permute-start.30 = (bf16[32,1024]{1,0:T(8,128)(2,1)S(1)}, bf16[32,1024]{1,0:T(8,128)(2,1)S(1)}, u32[]{:S(2)}, u32[]{:S(2)}) collective-permute-start(bf16[32,1024]{1,0:T(8,128)(2,1)S(1)} %get-tuple-element.27), channel_id=1, source_target_pairs={{0,2},{1,3},{2,0},{3,1},{4,6},{5,7},{6,4},{7,5},{8,10},{9,11},{10,... | collective-permute-start | bytes 196616 | tf_op jit(solution)/shard_map/ppermute | solution.py:22
  103.1 4.0 %collective-permute-start.29 = (bf16[32,1024]{1,0:T(8,128)(2,1)S(1)}, bf16[32,1024]{1,0:T(8,128)(2,1)S(1)}, u32[]{:S(2)}, u32[]{:S(2)}) collective-permute-start(bf16[32,1024]{1,0:T(8,128)(2,1)S(1)} %get-tuple-element.28), channel_id=1, source_target_pairs={{0,1},{1,0},{2,3},{3,2},{4,5},{5,4},{6,7},{7,6},{8,9},{9,8},{10,11... | collective-permute-start | bytes 196616 | tf_op jit(solution)/shard_map/ppermute | solution.py:22

commit v6 on v5

--- a/solution.py
+++ b/solution.py
@@ -24,11 +24,16 @@
 
 def exchange(blocks, axis):
     me = lax.axis_index(axis)
-    count = lax.axis_size(axis)
-    got = [pick(blocks, me)]
-    got += [hop(pick(blocks, me ^ mask), axis, mask) for mask in range(1, count)]
-    got = jnp.stack(got)
-    return jnp.stack([pick(got, me ^ source) for source in range(count)])
+    masks = range(1, lax.axis_size(axis))
+    came = [hop(pick(blocks, me ^ mask).astype(jnp.bfloat16), axis, mask) for mask in masks]
+    own = pick(blocks, me).astype(jnp.bfloat16)
+    return arrange(jnp.broadcast_to(own, blocks.shape), came, me)
+
+
+def arrange(held, came, me):
+    for mask, part in enumerate(came, 1):
+        held = lax.dynamic_update_index_in_dim(held, part, me ^ mask, 0)
+    return held
 
 
 def spread(value, axis):
@@ -145,9 +150,9 @@
     out_ref[...] = wide_dot(high_ref[...], low_ref[...], taps_ref[...], ((1,), (1,)))
 
 
-def local_kernel(groups, each, seq, sub, t_ref, taps_ref, *refs):
+def local_kernel(groups, each, seq, sub, t_ref, *refs):
     count = each * len(groups)
-    moved = count + 5
+    moved = count + 6
     sources, outs = refs[:moved], refs[moved : moved + 2]
     proj, gated, sems = refs[moved + 2 : moved + 5]
     held = refs[moved + 5 :]
@@ -155,7 +160,7 @@
     for copy in copies:
         copy.start()
     terms = held[:count]
-    fore_high, fore_low, spectrum_ref, back_high, back_low = held[count:]
+    fore_high, fore_low, spectrum_ref, back_high, back_low, taps_ref = held[count:]
     t = t_ref[0]
     length = gated.shape[0]
     shard = length // seq
@@ -183,6 +188,7 @@
             total = total + taps_ref[stream, offset : offset + 1] * proj[stream, pl.ds(8 - offset, length)]
         return total
 
+    copies[count + 5].wait()
     signal = mixed(1) * mixed(2)
     for copy in copies[count : count + 3]:
         copy.wait()
@@ -190,7 +196,7 @@
     cos, sin = both[:length], both[length:]
     taps_cos, taps_sin = spectrum_ref[:length], spectrum_ref[length:]
     both = jnp.concatenate([cos * taps_cos - sin * taps_sin, cos * taps_sin + sin * taps_cos])
-    for copy in copies[count + 3 :]:
+    for copy in copies[count + 3 : count + 5]:
         copy.wait()
     gated[...] = mixed(0) * wide_dot(back_high[...], back_low[...], both, ((1,), (0,)))
     for slot in range(tensor):
@@ -215,11 +221,11 @@
     spectrum = make_spectrum(*wide[:2], long_filter)
     flat = [term for group in terms for term in group]
     lines = length // 2
-    moved = [*flat, *wide[:2], spectrum, *wide[2:]]
+    moved = [*flat, *wide[:2], spectrum, *wide[2:], taps]
     return pl.pallas_call(
         functools.partial(local_kernel, groups, len(terms[0]), seq, sub),
         out_shape=[jax.ShapeDtypeStruct((lines, own), jnp.bfloat16)] * 2,
-        in_specs=[pl.BlockSpec(memory_space=pltpu.SMEM), vmem] + [pl.BlockSpec(memory_space=pl.ANY)] * len(moved),
+        in_specs=[pl.BlockSpec(memory_space=pltpu.SMEM)] + [pl.BlockSpec(memory_space=pl.ANY)] * len(moved),
         out_specs=[vmem] * 2,
         scratch_shapes=[
             pltpu.VMEM((3, length + 8, own), jnp.float32),
@@ -229,7 +235,7 @@
         ],
         name="filters",
         cost_estimate=pl.CostEstimate(flops=24 * length * length * own, bytes_accessed=8 * length * length, transcendentals=0),
-    )(t.reshape(1).astype(jnp.int32), taps, *moved)
+    )(t.reshape(1).astype(jnp.int32), *moved)
 
 
 def plain_stage(terms, taps, long_filter, t, seq, sub):
@@ -269,7 +275,7 @@
     length = rows * seq
     slots = range(tensor)
 
-    whole = exchange(residual_in.astype(jnp.bfloat16).reshape(tensor, sub, width), "tensor")
+    whole = exchange(residual_in.reshape(tensor, sub, width), "tensor")
 
     def in_part(mask):
         return lax.dynamic_slice_in_dim(in_weight, (z ^ mask) * own, own, 2)
@@ -296,9 +302,11 @@
         upper_gated = jnp.concatenate(gated[half:])
 
     lower = [1 << bit for bit in range(half.bit_length() - 1)]
-    held = None
+    totals = []
     for chosen, piece in ((slots[half:], upper_gated), (slots[:half], lower_gated)):
         got = [piece] + [hop(piece, "seq", mask) for mask in range(1, seq)]
+        if totals:
+            got, totals[0] = lax.optimization_barrier((got, totals[0]))
         got = jnp.concatenate(got, axis=1)
         terms = {}
         for place, slot in enumerate(chosen):
@@ -308,12 +316,22 @@
                 out_turned,
                 preferred_element_type=jnp.float32,
             )
-        terms = fold(terms, "tensor", lower)
-        if held is None:
-            held = hop(terms[half].astype(jnp.bfloat16), "tensor", half)
-        else:
-            held = (terms[0] + held.astype(jnp.float32)).astype(jnp.bfloat16)
-    back = exchange(held.reshape(seq, sub, depth), "seq")
+        totals.append(fold(terms, "tensor", lower)[chosen[0]])
+    pairs = seq // 2
+    side = z // pairs
+    crossing = totals[0].astype(jnp.bfloat16).reshape(2, pairs, sub, depth)
+    kept = totals[1].reshape(2, pairs, sub, depth)
+    sums = []
+    for which in (1 - side, side):
+        came = hop(pick(crossing, which), "tensor", half)
+        if sums:
+            kept, sums[0] = lax.optimization_barrier((kept, sums[0]))
+        sums.append((pick(kept, which) + came.astype(jnp.float32)).astype(jnp.bfloat16))
+    came = []
+    for mask in range(1, seq):
+        block = pick(sums[0] if mask >= pairs else sums[1], (z ^ mask) % pairs)
+        came.append(hop(block, "seq", mask))
+    back = arrange(jnp.concatenate([sums[1], sums[1]]), came, z)
     back = back.transpose(1, 0, 2).reshape(sub, tensor, width).transpose(1, 0, 2)
     summed = exchange(back, "tensor").reshape(rows, width)
     return residual_in + summed.astype(jnp.float32)

time: 109 us -> 115 us (1.055)
  matrix products: 8.1 us -> 10.7 us
  local copies, waits for them, and re-layouts: 6.84 us -> 9.1 us
  waiting for transfers between devices: 37.5 us -> 39.5 us
  other arithmetic: 3.69 us -> 2.29 us
  starting transfers between devices: 43.3 us -> 44.6 us
    dot_general x4, matrix products: 3.08 us -> 5.66 us  [shards(): jnp.einsum('rc,nc->rn', got[place * seq * sub:(place + 1) * seq * sub], o...]
    ppermute x28 -> x29, waiting for transfers between devices: 37.3 us -> 39.5 us  [hop(): return lax.ppermute(value, axis, [(a, a ^ mask) for a in range(count)])]
    convert_element_type x0 -> x1, local copies, waits for them, and re-layouts: none -> 1.91 us  [exchange(): pick(blocks, me ^ mask).astype(jnp.bfloat16)]
    ppermute x28 -> x29, starting transfers between devices: 31.5 us -> 33.2 us  [hop(): return lax.ppermute(value, axis, [(a, a ^ mask) for a in range(count)])]
    convert_element_type x1 -> x2, other arithmetic: 1.22 us -> 0.06 us  [shards(): (pick(kept, which) + came.astype(jnp.float32)).astype(jnp.bfloat16)]
  transfers between devices with their start and end apart: 32 -> 33, of which waited for: 14 -> 13; matrix products, arithmetic and copies ran while one was open for 13% -> 13% of each run, Pallas kernels for 3% -> 3%
where the time goes in v6:
time: 115 us
  starting transfers between devices  44.6 us (39%)
  waiting for transfers between devices  39.5 us (34%)
  matrix products  10.7 us (9%)
  local copies, waits for them, and re-layouts  9.1 us (8%)
  Pallas kernels  8.17 us (7%)
  other arithmetic  2.29 us (2%)
    ppermute x29, waiting for transfers between devices, hop(): return lax.ppermute(value, axis, [(a, a ^ mask) for a in range(count)])  39.5 us
    ppermute x29, starting transfers between devices, hop(): return lax.ppermute(value, axis, [(a, a ^ mask) for a in range(count)])  33.2 us
    ppermute x2, starting transfers between devices, sum_over_seq(): near = lax.ppermute(second, 'seq', [(0, 1), (3, 2)])  10 us
    dot_general x4, matrix products, shards(): jnp.einsum('rc,nc->rn', got[place * seq * sub:(place + 1) * seq * sub], o...  5.66 us
    pallas_call x1, Pallas kernels, local_stage(): pl.pallas_call(functools.partial(local_kernel, groups, len(terms[0]), seq...  5.06 us
    dot_general x8, matrix products, product(): jnp.einsum(form, rows, weight_of(mask), preferred_element_type=jnp.float32)  5.02 us
    pallas_call x1, Pallas kernels, local_stage(): spectrum = make_spectrum(*wide[:2], long_filter)  3.11 us
  transfers between devices with their start and end apart: 33, of which 13 were waited for; matrix products, arithmetic and copies ran while one was open for 13% of the time, Pallas kernels for 3%

profile of v6, /device:TPU:0, one launch (start us, length us, event | category | flops | bytes accessed | tf_op | source)
XLA Modules:
  0.0 114.9 jit_solution(3893536501693020087)
XLA Ops:
  0.0 1.9 %fusion.43 = (bf16[32,1024]{1,0:T(8,128)(2,1)S(1)}, bf16[32,1024]{1,0:T(8,128)(2,1)S(1)}, bf16[32,1024]{1,0:T(8,128)(2,1)}, bf16[32,1024]{1,0:T(8,128)(2,1)S(1)}) fusion(f32[4,32,1024]{2,1,0:T(8,128)} %bitcast.126, s32[]{:T(128)S(6)} %select_n.142, s32[]{:T(128)S(6)} %select_n.141, s32[]{:T(128)S(6)} %select_n.140, s32[]{:T(128)S(6)} %select_n.139), kind=kLoop, calls=%fused_computation.68 | loop fusion | bytes 524304 | tf_op jit(solution)/shard_map/convert_element_type | solution.py:28
  1.9 0.5 collective-permute-start
  2.4 2.5 %collective-permute-start.1 = (bf16[32,1024]{1,0:T(8,128)(2,1)S(1)}, bf16[32,1024]{1,0:T(8,128)(2,1)S(1)}, u32[]{:S(2)}, u32[]{:S(2)}) collective-permute-start(bf16[32,1024]{1,0:T(8,128)(2,1)S(1)} %get-tuple-element.36), channel_id=1, source_target_pairs={{0,2},{1,3},{2,0},{3,1},{4,6},{5,7},{6,4},{7,5},{8,10},{9,11},{10,... | collective-permute-start | bytes 196616 | tf_op jit(solution)/shard_map/ppermute | solution.py:22
  4.9 0.1 collective-permute-start.2
  5.0 0.7 mul.56
  5.8 1.9 %collective-permute-done.1 = bf16[32,1024]{1,0:T(8,128)(2,1)S(1)} collective-permute-done((bf16[32,1024]{1,0:T(8,128)(2,1)S(1)}, bf16[32,1024]{1,0:T(8,128)(2,1)S(1)}, u32[]{:S(2)}, u32[]{:S(2)}) %collective-permute-start.1) | collective-permute-done | bytes 65568 | tf_op jit(solution)/shard_map/ppermute | solution.py:22
  7.7 1.2 %collective-permute-done.2 = bf16[32,1024]{1,0:T(8,128)(2,1)S(1)} collective-permute-done((bf16[32,1024]{1,0:T(8,128)(2,1)S(1)}, bf16[32,1024]{1,0:T(8,128)(2,1)S(1)}, u32[]{:S(2)}, u32[]{:S(2)}) %collective-permute-start.2) | collective-permute-done | bytes 65568 | tf_op jit(solution)/shard_map/ppermute | solution.py:22
  8.9 0.2 fusion.20
  9.1 0.1 fusion.22
  9.2 1.7 %collective-permute-start.3 = (bf16[32,1024]{1,0:T(8,128)(2,1)S(1)}, bf16[32,1024]{1,0:T(8,128)(2,1)S(1)}, u32[]{:S(2)}, u32[]{:S(2)}) collective-permute-start(bf16[32,1024]{1,0:T(8,128)(2,1)S(1)} %get-tuple-element.47), channel_id=1, source_target_pairs={{0,4},{4,0},{8,12},{12,8},{1,5},{5,1},{9,13},{13,9},{2,6},{6,2},{1... | collective-permute-start | bytes 196616 | tf_op jit(solution)/shard_map/ppermute | solution.py:22
  10.9 2.6 %collective-permute-start.4 = (bf16[32,1024]{1,0:T(8,128)(2,1)S(1)}, bf16[32,1024]{1,0:T(8,128)(2,1)S(1)}, u32[]{:S(2)}, u32[]{:S(2)}) collective-permute-start(bf16[32,1024]{1,0:T(8,128)(2,1)S(1)} %get-tuple-element.46), channel_id=1, source_target_pairs={{0,8},{4,12},{8,0},{12,4},{1,9},{5,13},{9,1},{13,5},{2,10},{6,14},... | collective-permute-start | bytes 196616 | tf_op jit(solution)/shard_map/ppermute | solution.py:22
  13.5 0.2 collective-permute-start.5
  13.7 4.8 %collective-permute-done.4 = bf16[32,1024]{1,0:T(8,128)(2,1)S(1)} collective-permute-done((bf16[32,1024]{1,0:T(8,128)(2,1)S(1)}, bf16[32,1024]{1,0:T(8,128)(2,1)S(1)}, u32[]{:S(2)}, u32[]{:S(2)}) %collective-permute-start.4) | collective-permute-done | bytes 65568 | tf_op jit(solution)/shard_map/ppermute | solution.py:22
  18.5 1.2 %collective-permute-done.5 = bf16[32,1024]{1,0:T(8,128)(2,1)S(1)} collective-permute-done((bf16[32,1024]{1,0:T(8,128)(2,1)S(1)}, bf16[32,1024]{1,0:T(8,128)(2,1)S(1)}, u32[]{:S(2)}, u32[]{:S(2)}) %collective-permute-start.5) | collective-permute-done | bytes 65568 | tf_op jit(solution)/shard_map/ppermute | solution.py:22
  19.8 3.1 %filter_spectrum.1.refs_8_ = f32[1024,128]{1,0:T(8,128)} custom-call(bf16[1024,512]{1,0:T(8,128)(2,1)} %constant.140.clone.high_ref.refs_6_, bf16[1024,512]{1,0:T(8,128)(2,1)} %constant.141.clone.low_ref.refs_7_, f32[128,512]{1,0:T(8,128)} %taps_ref.1), custom_call_target="tpu_custom_call" | custom-call | flops 402653184 | bytes 1048576 | tf_op jit(solution)/shard_map/filter_spectrum/pallas_call | solution.py:221
  22.9 1.3 %constant_dynamic-slice_fusion.4.refs_11_ = f32[3,3,128]{2,1,0:T(4,128)} fusion(f32[3,3,512]{2,1,0:T(4,128)} %param.13, s32[]{:T(128)S(6)} %select_n.138), kind=kLoop, calls=%fused_computation.108 | loop fusion | bytes 9220 | tf_op jit(solution)/shard_map/dynamic_slice | solution.py:285
  24.2 2.2 %constant_dynamic-slice_fusion.3 = (bf16[1024,128]{1,0:T(8,128)(2,1)}, bf16[1024,128]{1,0:T(8,128)(2,1)}, bf16[1024,128]{1,0:T(8,128)(2,1)}, bf16[1024,128]{1,0:T(8,128)(2,1)}) fusion(bf16[1024,512]{1,0:T(8,128)(2,1)} %param.15, s32[]{:T(128)S(6)} %select_n.138, s32[]{:T(128)S(6)} %select_n.157, s32[]{:T(128)S(6)} %select_n.158, s32[]{:T(128)S(6)} %select_n.153), kind=kLoop, calls=%fused_computation.107 | loop fusion | bytes 2097168 | tf_op jit(solution)/shard_map/dynamic_slice | solution.py:283
  26.4 1.3 %collective-permute-start.11 = (bf16[128,1024]{1,0:T(8,128)(2,1)S(1)}, bf16[128,1024]{1,0:T(8,128)(2,1)S(1)}, u32[]{:S(2)}, u32[]{:S(2)}) collective-permute-start(bf16[128,1024]{1,0:T(8,128)(2,1)S(1)} %bitcast.128), channel_id=1, source_target_pairs={{0,2},{1,3},{2,0},{3,1},{4,6},{5,7},{6,4},{7,5},{8,10},{9,11},{10,... | collective-permute-start | bytes 786440 | tf_op jit(solution)/shard_map/ppermute | solution.py:22
  27.7 1.0 pad_maximum_fusion.1
  28.7 0.4 fusion.8
  29.2 1.1 collective-permute-start.7
  30.3 0.4 fusion.9
  30.7 0.7 collective-permute-start.8
  31.4 5.5 %collective-permute-start.10 = (bf16[3,256,128]{2,1,0:T(8,128)(2,1)S(1)}, bf16[3,256,128]{2,1,0:T(8,128)(2,1)S(1)}, u32[]{:S(2)}, u32[]{:S(2)}) collective-permute-start(bf16[3,256,128]{2,1,0:T(8,128)(2,1)S(1)} %fusion.9), channel_id=1, source_target_pairs={{0,4},{12,8},{1,5},{13,9},{2,6},{14,10},{3,7},{15,11},{16,20},{28,... | collective-permute-start | bytes 589832 | tf_op jit(solution)/shard_map/ppermute | solution.py:77
  37.0 0.4 fusion.6
  37.4 1.3 %collective-permute-start.9 = (bf16[3,256,128]{2,1,0:T(8,128)(2,1)S(1)}, bf16[3,256,128]{2,1,0:T(8,128)(2,1)S(1)}, u32[]{:S(2)}, u32[]{:S(2)}) collective-permute-start(bf16[3,256,128]{2,1,0:T(8,128)(2,1)S(1)} %fusion.6), channel_id=1, source_target_pairs={{0,8},{4,12},{8,0},{12,4},{1,9},{5,13},{9,1},{13,5},{2,10},{6,14},... | collective-permute-start | bytes 589832 | tf_op jit(solution)/shard_map/ppermute | solution.py:22
  38.8 1.2 %fusion.4.refs_0_ = f32[3,256,128]{2,1,0:T(8,128)} fusion(bf16[3,1024,512]{2,1,0:T(8,128)(2,1)S(1)} %copy-done, s32[]{:T(128)S(6)} %select_n.138, bf16[256,1024]{1,0:T(8,128)(2,1)S(1)} %pad_maximum_fusion.1, bf16[3,256,128]{2,1,0:T(8,128)(2,1)S(1)} %collective-permute-done.8, bf16[3,256,128]{2,1,0:T(8,128)(2,1)S(1)} %collective-permute-done.7, pred[]{:T(512)S(6)} %or.4), kind=kOutput, calls=%fused_computation.11 | convolution fusion | flops 201818112 | bytes 2097157 | tf_op jit(solution)/shard_map/rd,sdc->src/dot_general | solution.py:65
  40.0 0.4 fusion.10
  40.5 1.6 %collective-permute-start.13 = (bf16[3,256,128]{2,1,0:T(8,128)(2,1)S(1)}, bf16[3,256,128]{2,1,0:T(8,128)(2,1)S(1)}, u32[]{:S(2)}, u32[]{:S(2)}) collective-permute-start(bf16[3,256,128]{2,1,0:T(8,128)(2,1)S(1)} %fusion.10), channel_id=1, source_target_pairs={{0,4},{4,0},{8,12},{12,8},{1,5},{5,1},{9,13},{13,9},{2,6},{6,2},{1... | collective-permute-start | bytes 589832 | tf_op jit(solution)/shard_map/ppermute | solution.py:22
  42.0 0.4 fusion.11
  42.5 0.7 collective-permute-start.14
  43.2 4.5 %collective-permute-start.16 = (bf16[3,256,128]{2,1,0:T(8,128)(2,1)S(1)}, bf16[3,256,128]{2,1,0:T(8,128)(2,1)S(1)}, u32[]{:S(2)}, u32[]{:S(2)}) collective-permute-start(bf16[3,256,128]{2,1,0:T(8,128)(2,1)S(1)} %fusion.11), channel_id=1, source_target_pairs={{0,4},{12,8},{1,5},{13,9},{2,6},{14,10},{3,7},{15,11},{16,20},{28,... | collective-permute-start | bytes 589832 | tf_op jit(solution)/shard_map/ppermute | solution.py:77
  47.7 2.9 %collective-permute-done.13 = bf16[3,256,128]{2,1,0:T(8,128)(2,1)S(1)} collective-permute-done((bf16[3,256,128]{2,1,0:T(8,128)(2,1)S(1)}, bf16[3,256,128]{2,1,0:T(8,128)(2,1)S(1)}, u32[]{:S(2)}, u32[]{:S(2)}) %collective-permute-start.13) | collective-permute-done | bytes 196640 | tf_op jit(solution)/shard_map/ppermute | solution.py:22
  50.6 0.4 fusion.7
  51.1 2.6 %collective-permute-start.15 = (bf16[3,256,128]{2,1,0:T(8,128)(2,1)S(1)}, bf16[3,256,128]{2,1,0:T(8,128)(2,1)S(1)}, u32[]{:S(2)}, u32[]{:S(2)}) collective-permute-start(bf16[3,256,128]{2,1,0:T(8,128)(2,1)S(1)} %fusion.7), channel_id=1, source_target_pairs={{0,8},{4,12},{8,0},{12,4},{1,9},{5,13},{9,1},{13,5},{2,10},{6,14},... | collective-permute-start | bytes 589832 | tf_op jit(solution)/shard_map/ppermute | solution.py:22
  53.7 1.2 %fusion.5.refs_3_ = f32[3,256,128]{2,1,0:T(8,128)} fusion(bf16[3,1024,512]{2,1,0:T(8,128)(2,1)S(1)} %copy-done, s32[]{:T(128)S(6)} %select_n.138, bf16[256,1024]{1,0:T(8,128)(2,1)S(1)} %pad_maximum_fusion.2, bf16[3,256,128]{2,1,0:T(8,128)(2,1)S(1)} %collective-permute-done.14, bf16[3,256,128]{2,1,0:T(8,128)(2,1)S(1)} %collective-permute-done.13, pred[]{:T(512)S(6)} %or.4), kind=kOutput, calls=%fused_computation.12 | convolution fusion | flops 201818112 | bytes 2097157 | tf_op jit(solution)/shard_map/rd,sdc->src/dot_general | solution.py:65
  55.0 7.6 %collective-permute-done.15.refs_4_ = bf16[3,256,128]{2,1,0:T(8,128)(2,1)S(1)} collective-permute-done((bf16[3,256,128]{2,1,0:T(8,128)(2,1)S(1)}, bf16[3,256,128]{2,1,0:T(8,128)(2,1)S(1)}, u32[]{:S(2)}, u32[]{:S(2)}) %collective-permute-start.15) | collective-permute-done | bytes 196640 | tf_op jit(solution)/shard_map/ppermute | solution.py:22
  62.6 0.7 copy-done.9
  63.3 5.1 %filters.1 = (bf16[256,128]{1,0:T(8,128)(2,1)}, bf16[256,128]{1,0:T(8,128)(2,1)}) custom-call(s32[1]{0:T(128)} %bitcast.t_ref, f32[3,256,128]{2,1,0:T(8,128)} %fusion.4.refs_0_, bf16[3,256,128]{2,1,0:T(8,128)(2,1)} %copy-done.7, bf16[3,256,128]{2,1,0:T(8,128)(2,1)} %copy-done.6, f32[3,256,128]{2,1,0:T(8,128)} %fusion.5.refs_3_, ...), custom_call_target="tpu_custom_call" | custom-call | flops 805306368 | bytes 2097152 | tf_op jit(solution)/shard_map/filters/pallas_call | solution.py:225
  68.4 2.1 %collective-permute-start.21 = (bf16[256,128]{1,0:T(8,128)(2,1)}, bf16[256,128]{1,0:T(8,128)(2,1)S(1)}, u32[]{:S(2)}, u32[]{:S(2)}) collective-permute-start(bf16[256,128]{1,0:T(8,128)(2,1)} %get-tuple-element.23), channel_id=1, source_target_pairs={{0,8},{4,12},{8,0},{12,4},{1,9},{5,13},{9,1},{13,5},{2,10},{6,14},... | collective-permute-start | bytes 196616 | tf_op jit(solution)/shard_map/ppermute | solution.py:22
  70.5 2.3 %collective-permute-start.22 = (bf16[256,128]{1,0:T(8,128)(2,1)}, bf16[256,128]{1,0:T(8,128)(2,1)S(1)}, u32[]{:S(2)}, u32[]{:S(2)}) collective-permute-start(bf16[256,128]{1,0:T(8,128)(2,1)} %get-tuple-element.23), channel_id=1, source_target_pairs={{0,12},{4,8},{8,4},{12,0},{1,13},{5,9},{9,5},{13,1},{2,14},{6,10},... | collective-permute-start | bytes 196616 | tf_op jit(solution)/shard_map/ppermute | solution.py:22
  72.8 0.9 constant_dynamic-update-slice_fusion.3
  73.7 2.1 %collective-permute-done.21 = bf16[256,128]{1,0:T(8,128)(2,1)S(1)} collective-permute-done((bf16[256,128]{1,0:T(8,128)(2,1)}, bf16[256,128]{1,0:T(8,128)(2,1)S(1)}, u32[]{:S(2)}, u32[]{:S(2)}) %collective-permute-start.21) | collective-permute-done | bytes 65568 | tf_op jit(solution)/shard_map/ppermute | solution.py:22
  75.9 1.0 collective-permute-done.22
  76.9 1.6 %convolution_convert_fusion.1 = bf16[128,1024]{1,0:T(8,128)(2,1)S(1)} fusion(bf16[256,512]{1,0:T(8,128)(2,1)S(1)} %constant_dynamic-update-slice_fusion, bf16[1024,128]{1,0:T(8,128)(2,1)} %get-tuple-element.33, bf16[1024,128]{1,0:T(8,128)(2,1)} %get-tuple-element.34, bf16[1024,128]{1,0:T(8,128)(2,1)} %get-tuple-element.32, bf16[1024,128]{1,0:T(8,128)(2,1)S(1)} %copy-done.2), kind=kOutput, calls=%fused_computation.10 | convolution fusion | flops 138543104 | bytes 1441792 | tf_op jit(solution)/shard_map/rc,nc->rn/dot_general | solution.py:313
  78.6 1.0 collective-permute-start.17
  79.5 1.9 %collective-permute-start.18 = (bf16[256,128]{1,0:T(8,128)(2,1)S(1)}, bf16[256,128]{1,0:T(8,128)(2,1)S(1)}, u32[]{:S(2)}, u32[]{:S(2)}) collective-permute-start(bf16[256,128]{1,0:T(8,128)(2,1)S(1)} %copy-done.10), channel_id=1, source_target_pairs={{0,8},{4,12},{8,0},{12,4},{1,9},{5,13},{9,1},{13,5},{2,10},{6,14},... | collective-permute-start | bytes 196616 | tf_op jit(solution)/shard_map/ppermute | solution.py:22
  81.4 1.6 %collective-permute-start.19 = (bf16[256,128]{1,0:T(8,128)(2,1)S(1)}, bf16[256,128]{1,0:T(8,128)(2,1)S(1)}, u32[]{:S(2)}, u32[]{:S(2)}) collective-permute-start(bf16[256,128]{1,0:T(8,128)(2,1)S(1)} %copy-done.10), channel_id=1, source_target_pairs={{0,12},{4,8},{8,4},{12,0},{1,13},{5,9},{9,5},{13,1},{2,14},{6,10},... | collective-permute-start | bytes 196616 | tf_op jit(solution)/shard_map/ppermute | solution.py:22
  83.1 1.2 %convolution_add_fusion = bf16[128,1024]{1,0:T(8,128)(2,1)} fusion(bf16[128,1024]{1,0:T(8,128)(2,1)S(1)} %collective-permute-done.23, bf16[256,512]{1,0:T(8,128)(2,1)S(1)} %constant_dynamic-update-slice_fusion, bf16[1024,128]{1,0:T(8,128)(2,1)S(1)} %copy-done.4, bf16[1024,128]{1,0:T(8,128)(2,1)S(1)} %copy-done.5, bf16[1024,128]{1,0:T(8,128)(2,1)S(1)} %copy-done.3, ...), kind=kOutput, calls=%fused_computation | convolution fusion | flops 138805248 | bytes 1703936 | tf_op jit(solution)/shard_map/rc,nc->rn/dot_general | solution.py:313
  84.2 3.8 %collective-permute-done.18 = bf16[256,128]{1,0:T(8,128)(2,1)S(1)} collective-permute-done((bf16[256,128]{1,0:T(8,128)(2,1)S(1)}, bf16[256,128]{1,0:T(8,128)(2,1)S(1)}, u32[]{:S(2)}, u32[]{:S(2)}) %collective-permute-start.18) | collective-permute-done | bytes 65568 | tf_op jit(solution)/shard_map/ppermute | solution.py:22
  88.2 1.2 %convolution_convert_fusion = bf16[128,1024]{1,0:T(8,128)(2,1)} fusion(bf16[256,512]{1,0:T(8,128)(2,1)S(1)} %constant_dynamic-update-slice_fusion.4, bf16[1024,128]{1,0:T(8,128)(2,1)S(1)} %copy-done.4, bf16[1024,128]{1,0:T(8,128)(2,1)S(1)} %copy-done.5, bf16[1024,128]{1,0:T(8,128)(2,1)S(1)} %copy-done.3, bf16[1024,128]{1,0:T(8,128)(2,1)S(1)} %copy-done.2), kind=kOutput, calls=%fused_computation.9 | convolution fusion | flops 138543104 | bytes 1441792 | tf_op jit(solution)/shard_map/rc,nc->rn/dot_general | solution.py:313
  89.4 1.0 dynamic-slice_bitcast_fusion.1
  90.4 2.0 %collective-permute-start.25 = (bf16[2,32,1024]{2,1,0:T(8,128)(2,1)S(1)}, bf16[2,32,1024]{2,1,0:T(8,128)(2,1)S(1)}, u32[]{:S(2)}, u32[]{:S(2)}) collective-permute-start(bf16[2,32,1024]{2,1,0:T(8,128)(2,1)S(1)} %get-tuple-element.43), channel_id=1, source_target_pairs={{0,2},{1,3},{2,0},{3,1},{4,6},{5,7},{6,4},{7,5},{8,10},{9,11},{10,... | collective-permute-start | bytes 393224 | tf_op jit(solution)/shard_map/ppermute | solution.py:22
  92.4 1.7 %convert_add_fusion.1 = f32[128,1024]{1,0:T(8,128)S(1)} fusion(bf16[128,1024]{1,0:T(8,128)(2,1)} %collective-permute-done.24, bf16[256,512]{1,0:T(8,128)(2,1)} %copy-done.11, bf16[1024,128]{1,0:T(8,128)(2,1)} %get-tuple-element.33, bf16[1024,128]{1,0:T(8,128)(2,1)} %get-tuple-element.34, bf16[1024,128]{1,0:T(8,128)(2,1)} %get-tuple-element.32, ...), kind=kOutput, calls=%fused_computation.48 | convolution fusion | flops 138674176 | bytes 1966080 | tf_op jit(solution)/shard_map/rc,nc->rn/dot_general | solution.py:313
  94.2 5.0 %collective-permute-done.25 = bf16[2,32,1024]{2,1,0:T(8,128)(2,1)S(1)} collective-permute-done((bf16[2,32,1024]{2,1,0:T(8,128)(2,1)S(1)}, bf16[2,32,1024]{2,1,0:T(8,128)(2,1)S(1)}, u32[]{:S(2)}, u32[]{:S(2)}) %collective-permute-start.25) | collective-permute-done | bytes 131104 | tf_op jit(solution)/shard_map/ppermute | solution.py:22
  99.2 1.4 %collective-permute-start.27 = (bf16[32,1024]{1,0:T(8,128)(2,1)S(1)}, bf16[32,1024]{1,0:T(8,128)(2,1)S(1)}, u32[]{:S(2)}, u32[]{:S(2)}) collective-permute-start(bf16[32,1024]{1,0:T(8,128)(2,1)S(1)} %dynamic-slice_bitcast_fusion.8), channel_id=1, source_target_pairs={{0,4},{4,0},{8,12},{12,8},{1,5},{5,1},{9,13},{13,9},{2,6},{6,2},{1... | collective-permute-start | bytes 196616 | tf_op jit(solution)/shard_map/ppermute | solution.py:22
  100.6 0.7 collective-permute-start.28
  101.3 2.4 %collective-permute-start.29 = (bf16[32,1024]{1,0:T(8,128)(2,1)S(1)}, bf16[32,1024]{1,0:T(8,128)(2,1)S(1)}, u32[]{:S(2)}, u32[]{:S(2)}) collective-permute-start(bf16[32,1024]{1,0:T(8,128)(2,1)S(1)} %get-tuple-element.49), channel_id=1, source_target_pairs={{0,12},{4,8},{8,4},{12,0},{1,13},{5,9},{9,5},{13,1},{2,14},{6,10},... | collective-permute-start | bytes 196616 | tf_op jit(solution)/shard_map/ppermute | solution.py:22
  103.8 4.6 %collective-permute-done.28 = bf16[32,1024]{1,0:T(8,128)(2,1)S(1)} collective-permute-done((bf16[32,1024]{1,0:T(8,128)(2,1)S(1)}, bf16[32,1024]{1,0:T(8,128)(2,1)S(1)}, u32[]{:S(2)}, u32[]{:S(2)}) %collective-permute-start.28) | collective-permute-done | bytes 65568 | tf_op jit(solution)/shard_map/ppermute | solution.py:22
  108.6 0.6 collective-permute-start.31
  109.2 1.3 %collective-permute-start.32 = (bf16[32,1024]{1,0:T(8,128)(2,1)S(1)}, bf16[32,1024]{1,0:T(8,128)(2,1)S(1)}, u32[]{:S(2)}, u32[]{:S(2)}) collective-permute-start(bf16[32,1024]{1,0:T(8,128)(2,1)S(1)} %get-tuple-element.39), channel_id=1, source_target_pairs={{0,3},{1,2},{2,1},{3,0},{4,7},{5,6},{6,5},{7,4},{8,11},{9,10},{10,... | collective-permute-start | bytes 196616 | tf_op jit(solution)/shard_map/ppermute | solution.py:22
  110.5 3.1 %collective-permute-done.31 = bf16[32,1024]{1,0:T(8,128)(2,1)S(1)} collective-permute-done((bf16[32,1024]{1,0:T(8,128)(2,1)S(1)}, bf16[32,1024]{1,0:T(8,128)(2,1)S(1)}, u32[]{:S(2)}, u32[]{:S(2)}) %collective-permute-start.31) | collective-permute-done | bytes 65568 | tf_op jit(solution)/shard_map/ppermute | solution.py:22
  113.7 0.3 collective-permute-done.32
  114.0 0.9 convert_add_fusion
  (81 shorter events, 1.0 us)
Async XLA Ops:
  0.0 28.7 %copy-start = (bf16[3,1024,512]{2,1,0:T(8,128)(2,1)S(1)}, bf16[3,1024,512]{2,1,0:T(8,128)(2,1)}, u32[]{:S(2)}) copy-start(bf16[3,1024,512]{2,1,0:T(8,128)(2,1)} %param.12) | copy-start | bytes 9437188
  1.9 3.8 %collective-permute-start = (bf16[32,1024]{1,0:T(8,128)(2,1)}, bf16[32,1024]{1,0:T(8,128)(2,1)S(1)}, u32[]{:S(2)}, u32[]{:S(2)}) collective-permute-start(bf16[32,1024]{1,0:T(8,128)(2,1)} %get-tuple-element.37), channel_id=1, source_target_pairs={{0,1},{1,0},{2,3},{3,2},{4,5},{5,4},{6,7},{7,6},{8,9},{9,8},{10,11... | collective-permute-start | bytes 196616 | tf_op jit(solution)/shard_map/ppermute | solution.py:22
  2.4 5.2 %collective-permute-start.1 = (bf16[32,1024]{1,0:T(8,128)(2,1)S(1)}, bf16[32,1024]{1,0:T(8,128)(2,1)S(1)}, u32[]{:S(2)}, u32[]{:S(2)}) collective-permute-start(bf16[32,1024]{1,0:T(8,128)(2,1)S(1)} %get-tuple-element.36), channel_id=1, source_target_pairs={{0,2},{1,3},{2,0},{3,1},{4,6},{5,7},{6,4},{7,5},{8,10},{9,11},{10,... | collective-permute-start | bytes 196616 | tf_op jit(solution)/shard_map/ppermute | solution.py:22
  4.9 4.0 %collective-permute-start.2 = (bf16[32,1024]{1,0:T(8,128)(2,1)S(1)}, bf16[32,1024]{1,0:T(8,128)(2,1)S(1)}, u32[]{:S(2)}, u32[]{:S(2)}) collective-permute-start(bf16[32,1024]{1,0:T(8,128)(2,1)S(1)} %get-tuple-element.35), channel_id=1, source_target_pairs={{0,3},{1,2},{2,1},{3,0},{4,7},{5,6},{6,5},{7,4},{8,11},{9,10},{10,... | collective-permute-start | bytes 196616 | tf_op jit(solution)/shard_map/ppermute | solution.py:22
  9.2 4.5 %collective-permute-start.3 = (bf16[32,1024]{1,0:T(8,128)(2,1)S(1)}, bf16[32,1024]{1,0:T(8,128)(2,1)S(1)}, u32[]{:S(2)}, u32[]{:S(2)}) collective-permute-start(bf16[32,1024]{1,0:T(8,128)(2,1)S(1)} %get-tuple-element.47), channel_id=1, source_target_pairs={{0,4},{4,0},{8,12},{12,8},{1,5},{5,1},{9,13},{13,9},{2,6},{6,2},{1... | collective-permute-start | bytes 196616 | tf_op jit(solution)/shard_map/ppermute | solution.py:22
  10.9 7.6 %collective-permute-start.4 = (bf16[32,1024]{1,0:T(8,128)(2,1)S(1)}, bf16[32,1024]{1,0:T(8,128)(2,1)S(1)}, u32[]{:S(2)}, u32[]{:S(2)}) collective-permute-start(bf16[32,1024]{1,0:T(8,128)(2,1)S(1)} %get-tuple-element.46), channel_id=1, source_target_pairs={{0,8},{4,12},{8,0},{12,4},{1,9},{5,13},{9,1},{13,5},{2,10},{6,14},... | collective-permute-start | bytes 196616 | tf_op jit(solution)/shard_map/ppermute | solution.py:22
  13.5 6.2 %collective-permute-start.5 = (bf16[32,1024]{1,0:T(8,128)(2,1)S(1)}, bf16[32,1024]{1,0:T(8,128)(2,1)S(1)}, u32[]{:S(2)}, u32[]{:S(2)}) collective-permute-start(bf16[32,1024]{1,0:T(8,128)(2,1)S(1)} %get-tuple-element.45), channel_id=1, source_target_pairs={{0,12},{4,8},{8,4},{12,0},{1,13},{5,9},{9,5},{13,1},{2,14},{6,10},... | collective-permute-start | bytes 196616 | tf_op jit(solution)/shard_map/ppermute | solution.py:22
  19.7 8.0 %collective-permute-start.6 = (bf16[128,1024]{1,0:T(8,128)(2,1)S(1)}, bf16[128,1024]{1,0:T(8,128)(2,1)}, u32[]{:S(2)}, u32[]{:S(2)}) collective-permute-start(bf16[128,1024]{1,0:T(8,128)(2,1)S(1)} %bitcast.127), channel_id=1, source_target_pairs={{0,1},{1,0},{2,3},{3,2},{4,5},{5,4},{6,7},{7,6},{8,9},{9,8},{10,11... | collective-permute-start | bytes 786440 | tf_op jit(solution)/shard_map/ppermute | solution.py:22
  26.4 10.5 %collective-permute-start.11 = (bf16[128,1024]{1,0:T(8,128)(2,1)S(1)}, bf16[128,1024]{1,0:T(8,128)(2,1)S(1)}, u32[]{:S(2)}, u32[]{:S(2)}) collective-permute-start(bf16[128,1024]{1,0:T(8,128)(2,1)S(1)} %bitcast.128), channel_id=1, source_target_pairs={{0,2},{1,3},{2,0},{3,1},{4,6},{5,7},{6,4},{7,5},{8,10},{9,11},{10,... | collective-permute-start | bytes 786440 | tf_op jit(solution)/shard_map/ppermute | solution.py:22
  29.2 7.8 %collective-permute-start.7 = (bf16[3,256,128]{2,1,0:T(8,128)(2,1)S(1)}, bf16[3,256,128]{2,1,0:T(8,128)(2,1)S(1)}, u32[]{:S(2)}, u32[]{:S(2)}) collective-permute-start(bf16[3,256,128]{2,1,0:T(8,128)(2,1)S(1)} %fusion.8), channel_id=1, source_target_pairs={{0,4},{4,0},{8,12},{12,8},{1,5},{5,1},{9,13},{13,9},{2,6},{6,2},{1... | collective-permute-start | bytes 589832 | tf_op jit(solution)/shard_map/ppermute | solution.py:22
  30.7 8.0 %collective-permute-start.8 = (bf16[3,256,128]{2,1,0:T(8,128)(2,1)S(1)}, bf16[3,256,128]{2,1,0:T(8,128)(2,1)S(1)}, u32[]{:S(2)}, u32[]{:S(2)}) collective-permute-start(bf16[3,256,128]{2,1,0:T(8,128)(2,1)S(1)} %fusion.9), channel_id=1, source_target_pairs={{4,8},{8,4},{5,9},{9,5},{6,10},{10,6},{7,11},{11,7},{20,24},{24,20... | collective-permute-start | bytes 589832 | tf_op jit(solution)/shard_map/ppermute | solution.py:76
  31.4 23.5 %collective-permute-start.10 = (bf16[3,256,128]{2,1,0:T(8,128)(2,1)S(1)}, bf16[3,256,128]{2,1,0:T(8,128)(2,1)S(1)}, u32[]{:S(2)}, u32[]{:S(2)}) collective-permute-start(bf16[3,256,128]{2,1,0:T(8,128)(2,1)S(1)} %fusion.9), channel_id=1, source_target_pairs={{0,4},{12,8},{1,5},{13,9},{2,6},{14,10},{3,7},{15,11},{16,20},{28,... | collective-permute-start | bytes 589832 | tf_op jit(solution)/shard_map/ppermute | solution.py:77
  36.9 3.1 %collective-permute-start.12 = (bf16[128,1024]{1,0:T(8,128)(2,1)S(1)}, bf16[128,1024]{1,0:T(8,128)(2,1)S(1)}, u32[]{:S(2)}, u32[]{:S(2)}) collective-permute-start(bf16[128,1024]{1,0:T(8,128)(2,1)S(1)} %collective-permute-done.11), channel_id=1, source_target_pairs={{0,1},{1,0},{2,3},{3,2},{4,5},{5,4},{6,7},{7,6},{8,9},{9,8},{10,11... | collective-permute-start | bytes 786440 | tf_op jit(solution)/shard_map/ppermute | solution.py:22
  37.4 17.5 %collective-permute-start.9 = (bf16[3,256,128]{2,1,0:T(8,128)(2,1)S(1)}, bf16[3,256,128]{2,1,0:T(8,128)(2,1)S(1)}, u32[]{:S(2)}, u32[]{:S(2)}) collective-permute-start(bf16[3,256,128]{2,1,0:T(8,128)(2,1)S(1)} %fusion.6), channel_id=1, source_target_pairs={{0,8},{4,12},{8,0},{12,4},{1,9},{5,13},{9,1},{13,5},{2,10},{6,14},... | collective-permute-start | bytes 589832 | tf_op jit(solution)/shard_map/ppermute | solution.py:22
  40.5 10.2 %collective-permute-start.13 = (bf16[3,256,128]{2,1,0:T(8,128)(2,1)S(1)}, bf16[3,256,128]{2,1,0:T(8,128)(2,1)S(1)}, u32[]{:S(2)}, u32[]{:S(2)}) collective-permute-start(bf16[3,256,128]{2,1,0:T(8,128)(2,1)S(1)} %fusion.10), channel_id=1, source_target_pairs={{0,4},{4,0},{8,12},{12,8},{1,5},{5,1},{9,13},{13,9},{2,6},{6,2},{1... | collective-permute-start | bytes 589832 | tf_op jit(solution)/shard_map/ppermute | solution.py:22
  42.5 11.2 %collective-permute-start.14 = (bf16[3,256,128]{2,1,0:T(8,128)(2,1)S(1)}, bf16[3,256,128]{2,1,0:T(8,128)(2,1)S(1)}, u32[]{:S(2)}, u32[]{:S(2)}) collective-permute-start(bf16[3,256,128]{2,1,0:T(8,128)(2,1)S(1)} %fusion.11), channel_id=1, source_target_pairs={{4,8},{8,4},{5,9},{9,5},{6,10},{10,6},{7,11},{11,7},{20,24},{24,20... | collective-permute-start | bytes 589832 | tf_op jit(solution)/shard_map/ppermute | solution.py:76
  43.2 11.8 %collective-permute-start.16 = (bf16[3,256,128]{2,1,0:T(8,128)(2,1)S(1)}, bf16[3,256,128]{2,1,0:T(8,128)(2,1)S(1)}, u32[]{:S(2)}, u32[]{:S(2)}) collective-permute-start(bf16[3,256,128]{2,1,0:T(8,128)(2,1)S(1)} %fusion.11), channel_id=1, source_target_pairs={{0,4},{12,8},{1,5},{13,9},{2,6},{14,10},{3,7},{15,11},{16,20},{28,... | collective-permute-start | bytes 589832 | tf_op jit(solution)/shard_map/ppermute | solution.py:77
  51.1 11.5 %collective-permute-start.15 = (bf16[3,256,128]{2,1,0:T(8,128)(2,1)S(1)}, bf16[3,256,128]{2,1,0:T(8,128)(2,1)S(1)}, u32[]{:S(2)}, u32[]{:S(2)}) collective-permute-start(bf16[3,256,128]{2,1,0:T(8,128)(2,1)S(1)} %fusion.7), channel_id=1, source_target_pairs={{0,8},{4,12},{8,0},{12,4},{1,9},{5,13},{9,1},{13,5},{2,10},{6,14},... | collective-permute-start | bytes 589832 | tf_op jit(solution)/shard_map/ppermute | solution.py:22
  54.9 7.7 %copy-start.6 = (bf16[3,256,128]{2,1,0:T(8,128)(2,1)}, bf16[3,256,128]{2,1,0:T(8,128)(2,1)S(1)}, u32[]{:S(2)}) copy-start(bf16[3,256,128]{2,1,0:T(8,128)(2,1)S(1)} %collective-permute-done.10.refs_2_) | copy-start | bytes 589828
  54.9 7.7 %copy-start.7 = (bf16[3,256,128]{2,1,0:T(8,128)(2,1)}, bf16[3,256,128]{2,1,0:T(8,128)(2,1)S(1)}, u32[]{:S(2)}) copy-start(bf16[3,256,128]{2,1,0:T(8,128)(2,1)S(1)} %collective-permute-done.9.refs_1_) | copy-start | bytes 589828
  55.0 7.6 %copy-start.8 = (bf16[3,256,128]{2,1,0:T(8,128)(2,1)}, bf16[3,256,128]{2,1,0:T(8,128)(2,1)S(1)}, u32[]{:S(2)}) copy-start(bf16[3,256,128]{2,1,0:T(8,128)(2,1)S(1)} %collective-permute-done.16.refs_5_) | copy-start | bytes 589828
  62.6 0.7 copy-start.9
  63.3 13.6 %copy-start.2 = (bf16[1024,128]{1,0:T(8,128)(2,1)S(1)}, bf16[1024,128]{1,0:T(8,128)(2,1)}, u32[]{:S(2)}) copy-start(bf16[1024,128]{1,0:T(8,128)(2,1)} %get-tuple-element.31) | copy-start | bytes 786436
  68.4 5.3 %collective-permute-start.20 = (bf16[256,128]{1,0:T(8,128)(2,1)}, bf16[256,128]{1,0:T(8,128)(2,1)S(1)}, u32[]{:S(2)}, u32[]{:S(2)}) collective-permute-start(bf16[256,128]{1,0:T(8,128)(2,1)} %get-tuple-element.23), channel_id=1, source_target_pairs={{0,4},{4,0},{8,12},{12,8},{1,5},{5,1},{9,13},{13,9},{2,6},{6,2},{1... | collective-permute-start | bytes 196616 | tf_op jit(solution)/shard_map/ppermute | solution.py:22
  68.4 7.4 %collective-permute-start.21 = (bf16[256,128]{1,0:T(8,128)(2,1)}, bf16[256,128]{1,0:T(8,128)(2,1)S(1)}, u32[]{:S(2)}, u32[]{:S(2)}) collective-permute-start(bf16[256,128]{1,0:T(8,128)(2,1)} %get-tuple-element.23), channel_id=1, source_target_pairs={{0,8},{4,12},{8,0},{12,4},{1,9},{5,13},{9,1},{13,5},{2,10},{6,14},... | collective-permute-start | bytes 196616 | tf_op jit(solution)/shard_map/ppermute | solution.py:22
  70.5 6.4 %collective-permute-start.22 = (bf16[256,128]{1,0:T(8,128)(2,1)}, bf16[256,128]{1,0:T(8,128)(2,1)S(1)}, u32[]{:S(2)}, u32[]{:S(2)}) collective-permute-start(bf16[256,128]{1,0:T(8,128)(2,1)} %get-tuple-element.23), channel_id=1, source_target_pairs={{0,12},{4,8},{8,4},{12,0},{1,13},{5,9},{9,5},{13,1},{2,14},{6,10},... | collective-permute-start | bytes 196616 | tf_op jit(solution)/shard_map/ppermute | solution.py:22
  75.8 2.8 %copy-start.10 = (bf16[256,128]{1,0:T(8,128)(2,1)S(1)}, bf16[256,128]{1,0:T(8,128)(2,1)}, u32[]{:S(2)}) copy-start(bf16[256,128]{1,0:T(8,128)(2,1)} %get-tuple-element.24) | copy-start | bytes 196612
  75.8 7.2 %copy-start.3 = (bf16[1024,128]{1,0:T(8,128)(2,1)S(1)}, bf16[1024,128]{1,0:T(8,128)(2,1)}, u32[]{:S(2)}) copy-start(bf16[1024,128]{1,0:T(8,128)(2,1)} %get-tuple-element.32) | copy-start | bytes 786436
  75.8 7.2 %copy-start.4 = (bf16[1024,128]{1,0:T(8,128)(2,1)S(1)}, bf16[1024,128]{1,0:T(8,128)(2,1)}, u32[]{:S(2)}) copy-start(bf16[1024,128]{1,0:T(8,128)(2,1)} %get-tuple-element.33) | copy-start | bytes 786436
  75.8 7.2 %copy-start.5 = (bf16[1024,128]{1,0:T(8,128)(2,1)S(1)}, bf16[1024,128]{1,0:T(8,128)(2,1)}, u32[]{:S(2)}) copy-start(bf16[1024,128]{1,0:T(8,128)(2,1)} %get-tuple-element.34) | copy-start | bytes 786436
  78.5 4.5 %collective-permute-start.23 = (bf16[128,1024]{1,0:T(8,128)(2,1)S(1)}, bf16[128,1024]{1,0:T(8,128)(2,1)S(1)}, u32[]{:S(2)}, u32[]{:S(2)}) collective-permute-start(bf16[128,1024]{1,0:T(8,128)(2,1)S(1)} %convolution_convert_fusion.1), channel_id=1, source_target_pairs={{0,1},{1,0},{2,3},{3,2},{4,5},{5,4},{6,7},{7,6},{8,9},{9,8},{10,11... | collective-permute-start | bytes 786440 | tf_op jit(solution)/shard_map/ppermute | solution.py:22
  78.6 5.7 %collective-permute-start.17 = (bf16[256,128]{1,0:T(8,128)(2,1)S(1)}, bf16[256,128]{1,0:T(8,128)(2,1)S(1)}, u32[]{:S(2)}, u32[]{:S(2)}) collective-permute-start(bf16[256,128]{1,0:T(8,128)(2,1)S(1)} %copy-done.10), channel_id=1, source_target_pairs={{0,4},{4,0},{8,12},{12,8},{1,5},{5,1},{9,13},{13,9},{2,6},{6,2},{1... | collective-permute-start | bytes 196616 | tf_op jit(solution)/shard_map/ppermute | solution.py:22
  79.5 8.5 %collective-permute-start.18 = (bf16[256,128]{1,0:T(8,128)(2,1)S(1)}, bf16[256,128]{1,0:T(8,128)(2,1)S(1)}, u32[]{:S(2)}, u32[]{:S(2)}) collective-permute-start(bf16[256,128]{1,0:T(8,128)(2,1)S(1)} %copy-done.10), channel_id=1, source_target_pairs={{0,8},{4,12},{8,0},{12,4},{1,9},{5,13},{9,1},{13,5},{2,10},{6,14},... | collective-permute-start | bytes 196616 | tf_op jit(solution)/shard_map/ppermute | solution.py:22
  81.4 6.6 %collective-permute-start.19 = (bf16[256,128]{1,0:T(8,128)(2,1)S(1)}, bf16[256,128]{1,0:T(8,128)(2,1)S(1)}, u32[]{:S(2)}, u32[]{:S(2)}) collective-permute-start(bf16[256,128]{1,0:T(8,128)(2,1)S(1)} %copy-done.10), channel_id=1, source_target_pairs={{0,12},{4,8},{8,4},{12,0},{1,13},{5,9},{9,5},{13,1},{2,14},{6,10},... | collective-permute-start | bytes 196616 | tf_op jit(solution)/shard_map/ppermute | solution.py:22
  88.2 1.2 %copy-start.11 = (bf16[256,512]{1,0:T(8,128)(2,1)}, bf16[256,512]{1,0:T(8,128)(2,1)S(1)}, u32[]{:S(2)}) copy-start(bf16[256,512]{1,0:T(8,128)(2,1)S(1)} %constant_dynamic-update-slice_fusion.4) | copy-start | bytes 786436
  89.4 3.1 %collective-permute-start.24 = (bf16[128,1024]{1,0:T(8,128)(2,1)}, bf16[128,1024]{1,0:T(8,128)(2,1)}, u32[]{:S(2)}, u32[]{:S(2)}) collective-permute-start(bf16[128,1024]{1,0:T(8,128)(2,1)} %convolution_convert_fusion), channel_id=1, source_target_pairs={{0,1},{1,0},{2,3},{3,2},{4,5},{5,4},{6,7},{7,6},{8,9},{9,8},{10,11... | collective-permute-start | bytes 786440 | tf_op jit(solution)/shard_map/ppermute | solution.py:22
  90.4 8.8 %collective-permute-start.26 = (bf16[2,32,1024]{2,1,0:T(8,128)(2,1)S(1)}, bf16[2,32,1024]{2,1,0:T(8,128)(2,1)S(1)}, u32[]{:S(2)}, u32[]{:S(2)}) collective-permute-start(bf16[2,32,1024]{2,1,0:T(8,128)(2,1)S(1)} %get-tuple-element.44), channel_id=1, source_target_pairs={{0,2},{1,3},{2,0},{3,1},{4,6},{5,7},{6,4},{7,5},{8,10},{9,11},{10,... | collective-permute-start | bytes 393224 | tf_op jit(solution)/shard_map/ppermute | solution.py:22
  90.4 8.7 %collective-permute-start.25 = (bf16[2,32,1024]{2,1,0:T(8,128)(2,1)S(1)}, bf16[2,32,1024]{2,1,0:T(8,128)(2,1)S(1)}, u32[]{:S(2)}, u32[]{:S(2)}) collective-permute-start(bf16[2,32,1024]{2,1,0:T(8,128)(2,1)S(1)} %get-tuple-element.43), channel_id=1, source_target_pairs={{0,2},{1,3},{2,0},{3,1},{4,6},{5,7},{6,4},{7,5},{8,10},{9,11},{10,... | collective-permute-start | bytes 393224 | tf_op jit(solution)/shard_map/ppermute | solution.py:22
  94.2 19.8 %copy-start.1 = (f32[128,1024]{1,0:T(8,128)S(1)}, f32[128,1024]{1,0:T(8,128)}, u32[]{:S(2)}) copy-start(f32[128,1024]{1,0:T(8,128)} %param.10) | copy-start | bytes 1572868
  99.2 4.6 %collective-permute-start.27 = (bf16[32,1024]{1,0:T(8,128)(2,1)S(1)}, bf16[32,1024]{1,0:T(8,128)(2,1)S(1)}, u32[]{:S(2)}, u32[]{:S(2)}) collective-permute-start(bf16[32,1024]{1,0:T(8,128)(2,1)S(1)} %dynamic-slice_bitcast_fusion.8), channel_id=1, source_target_pairs={{0,4},{4,0},{8,12},{12,8},{1,5},{5,1},{9,13},{13,9},{2,6},{6,2},{1... | collective-permute-start | bytes 196616 | tf_op jit(solution)/shard_map/ppermute | solution.py:22
  100.6 7.8 %collective-permute-start.28 = (bf16[32,1024]{1,0:T(8,128)(2,1)S(1)}, bf16[32,1024]{1,0:T(8,128)(2,1)S(1)}, u32[]{:S(2)}, u32[]{:S(2)}) collective-permute-start(bf16[32,1024]{1,0:T(8,128)(2,1)S(1)} %get-tuple-element.50), channel_id=1, source_target_pairs={{0,8},{4,12},{8,0},{12,4},{1,9},{5,13},{9,1},{13,5},{2,10},{6,14},... | collective-permute-start | bytes 196616 | tf_op jit(solution)/shard_map/ppermute | solution.py:22
  101.3 7.1 %collective-permute-start.29 = (bf16[32,1024]{1,0:T(8,128)(2,1)S(1)}, bf16[32,1024]{1,0:T(8,128)(2,1)S(1)}, u32[]{:S(2)}, u32[]{:S(2)}) collective-permute-start(bf16[32,1024]{1,0:T(8,128)(2,1)S(1)} %get-tuple-element.49), channel_id=1, source_target_pairs={{0,12},{4,8},{8,4},{12,0},{1,13},{5,9},{9,5},{13,1},{2,14},{6,10},... | collective-permute-start | bytes 196616 | tf_op jit(solution)/shard_map/ppermute | solution.py:22
  108.5 1.9 %collective-permute-start.30 = (bf16[32,1024]{1,0:T(8,128)(2,1)S(1)}, bf16[32,1024]{1,0:T(8,128)(2,1)S(1)}, u32[]{:S(2)}, u32[]{:S(2)}) collective-permute-start(bf16[32,1024]{1,0:T(8,128)(2,1)S(1)} %get-tuple-element.41), channel_id=1, source_target_pairs={{0,1},{1,0},{2,3},{3,2},{4,5},{5,4},{6,7},{7,6},{8,9},{9,8},{10,11... | collective-permute-start | bytes 196616 | tf_op jit(solution)/shard_map/ppermute | solution.py:22
  108.6 5.0 %collective-permute-start.31 = (bf16[32,1024]{1,0:T(8,128)(2,1)S(1)}, bf16[32,1024]{1,0:T(8,128)(2,1)S(1)}, u32[]{:S(2)}, u32[]{:S(2)}) collective-permute-start(bf16[32,1024]{1,0:T(8,128)(2,1)S(1)} %get-tuple-element.40), channel_id=1, source_target_pairs={{0,2},{1,3},{2,0},{3,1},{4,6},{5,7},{6,4},{7,5},{8,10},{9,11},{10,... | collective-permute-start | bytes 196616 | tf_op jit(solution)/shard_map/ppermute | solution.py:22
  109.2 4.8 %collective-permute-start.32 = (bf16[32,1024]{1,0:T(8,128)(2,1)S(1)}, bf16[32,1024]{1,0:T(8,128)(2,1)S(1)}, u32[]{:S(2)}, u32[]{:S(2)}) collective-permute-start(bf16[32,1024]{1,0:T(8,128)(2,1)S(1)} %get-tuple-element.39), channel_id=1, source_target_pairs={{0,3},{1,2},{2,1},{3,0},{4,7},{5,6},{6,5},{7,4},{8,11},{9,10},{10,... | collective-permute-start | bytes 196616 | tf_op jit(solution)/shard_map/ppermute | solution.py:22

commit v7 on v5

--- a/solution.py
+++ b/solution.py
@@ -123,13 +123,10 @@
     return high, (value - high.astype(jnp.float32)).astype(jnp.bfloat16)
 
 
-def split_tables(block):
+def split_table(block):
     table = tables(block)[:, :block]
-    out = []
-    for part in (table, table.T / np.float32(block)):
-        high = part.astype(jnp.bfloat16)
-        out += [high, (part - high.astype(np.float32)).astype(jnp.bfloat16)]
-    return out
+    high = table.astype(jnp.bfloat16)
+    return [high, (table - high.astype(np.float32)).astype(jnp.bfloat16)]
 
 
 def wide_dot(high, low, value, dims):
@@ -147,7 +144,7 @@
 
 def local_kernel(groups, each, seq, sub, t_ref, taps_ref, *refs):
     count = each * len(groups)
-    moved = count + 5
+    moved = count + 3
     sources, outs = refs[:moved], refs[moved : moved + 2]
     proj, gated, sems = refs[moved + 2 : moved + 5]
     held = refs[moved + 5 :]
@@ -155,7 +152,7 @@
     for copy in copies:
         copy.start()
     terms = held[:count]
-    fore_high, fore_low, spectrum_ref, back_high, back_low = held[count:]
+    high_ref, low_ref, spectrum_ref = held[count:]
     t = t_ref[0]
     length = gated.shape[0]
     shard = length // seq
@@ -186,13 +183,15 @@
     signal = mixed(1) * mixed(2)
     for copy in copies[count : count + 3]:
         copy.wait()
-    both = wide_dot(fore_high[...], fore_low[...], signal, ((1,), (0,)))
+    both = wide_dot(high_ref[...], low_ref[...], signal, ((1,), (0,)))
     cos, sin = both[:length], both[length:]
     taps_cos, taps_sin = spectrum_ref[:length], spectrum_ref[length:]
     both = jnp.concatenate([cos * taps_cos - sin * taps_sin, cos * taps_sin + sin * taps_cos])
-    for copy in copies[count + 3 :]:
-        copy.wait()
-    gated[...] = mixed(0) * wide_dot(back_high[...], back_low[...], both, ((1,), (0,)))
+    upper, lower = halves(both.T)
+    dot = functools.partial(jnp.dot, preferred_element_type=jnp.float32)
+    back = dot(jnp.concatenate([upper, lower]), high_ref[...])
+    back = back[: upper.shape[0]] + back[upper.shape[0] :] + dot(upper, low_ref[...])
+    gated[...] = mixed(0) * back.T * (1.0 / length)
     for slot in range(tensor):
         out = outs[slot // (tensor // 2)]
         for source in range(seq):
@@ -202,7 +201,7 @@
 
 def local_stage(groups, terms, taps, long_filter, t, seq, sub):
     own, length = long_filter.shape
-    wide = split_tables(length)
+    wide = split_table(length)
     vmem = pl.BlockSpec(memory_space=pltpu.VMEM)
     make_spectrum = pl.pallas_call(
         filter_kernel,
@@ -210,12 +209,13 @@
         in_specs=[vmem] * 3,
         out_specs=vmem,
         name="filter_spectrum",
+        compiler_params=pltpu.CompilerParams(vmem_limit_bytes=32 * 2**20),
         cost_estimate=pl.CostEstimate(flops=12 * length * length * own, bytes_accessed=4 * length * length, transcendentals=0),
     )
-    spectrum = make_spectrum(*wide[:2], long_filter)
+    spectrum = make_spectrum(*wide, long_filter)
     flat = [term for group in terms for term in group]
     lines = length // 2
-    moved = [*flat, *wide[:2], spectrum, *wide[2:]]
+    moved = [*flat, *wide, spectrum]
     return pl.pallas_call(
         functools.partial(local_kernel, groups, len(terms[0]), seq, sub),
         out_shape=[jax.ShapeDtypeStruct((lines, own), jnp.bfloat16)] * 2,
@@ -228,6 +228,7 @@
             *(pltpu.VMEM(part.shape, part.dtype) for part in moved),
         ],
         name="filters",
+        compiler_params=pltpu.CompilerParams(vmem_limit_bytes=32 * 2**20),
         cost_estimate=pl.CostEstimate(flops=24 * length * length * own, bytes_accessed=8 * length * length, transcendentals=0),
     )(t.reshape(1).astype(jnp.int32), taps, *moved)
 

time: 109 us -> 104 us (0.954)
  Pallas kernels: 8.24 us -> 4.02 us
  waiting for transfers between devices: 37.5 us -> 40.9 us
  matrix products: 8.1 us -> 5.44 us
  local copies, waits for them, and re-layouts: 6.84 us -> 4.55 us
  other arithmetic: 3.69 us -> 5.37 us
    ppermute x28, waiting for transfers between devices: 37.3 us -> 40 us  [hop(): return lax.ppermute(value, axis, [(a, a ^ mask) for a in range(count)])]
    pallas_call x1, Pallas kernels: 3.11 us -> 0.74 us  [local_stage(): spectrum = make_spectrum(*wide, long_filter)]
    pallas_call x1, Pallas kernels: 5.13 us -> 3.29 us  [local_stage(): pl.pallas_call(functools.partial(local_kernel, groups, len(terms[0]), seq...]
    dot_general x8, matrix products: 5.02 us -> 3.52 us  [product(): jnp.einsum(form, rows, weight_of(mask), preferred_element_type=jnp.float32)]
    dot_general x4, matrix products: 3.08 us -> 1.91 us  [shards(): jnp.einsum('rc,nc->rn', got[place * seq * sub:(place + 1) * seq * sub], o...]
  transfers between devices with their start and end apart: 32 -> 32, of which waited for: 14 -> 15; matrix products, arithmetic and copies ran while one was open for 13% -> 9% of each run, Pallas kernels for 3% -> 1%
where the time goes in v7:
time: 104 us
  starting transfers between devices  43.2 us (42%)
  waiting for transfers between devices  40.9 us (39%)
  matrix products  5.44 us (5%)
  other arithmetic  5.37 us (5%)
  local copies, waits for them, and re-layouts  4.55 us (4%)
  Pallas kernels  4.02 us (4%)
    ppermute x28, waiting for transfers between devices, hop(): return lax.ppermute(value, axis, [(a, a ^ mask) for a in range(count)])  40 us
    ppermute x28, starting transfers between devices, hop(): return lax.ppermute(value, axis, [(a, a ^ mask) for a in range(count)])  31.3 us
    ppermute x2, starting transfers between devices, sum_over_seq(): near = lax.ppermute(second, 'seq', [(0, 1), (3, 2)])  10.5 us
    dot_general x8, matrix products, product(): jnp.einsum(form, rows, weight_of(mask), preferred_element_type=jnp.float32)  3.52 us
    pallas_call x1, Pallas kernels, local_stage(): pl.pallas_call(functools.partial(local_kernel, groups, len(terms[0]), seq...  3.29 us
  transfers between devices with their start and end apart: 32, of which 15 were waited for; matrix products, arithmetic and copies ran while one was open for 9% of the time, Pallas kernels for 1%

profile of v7, /device:TPU:0, one launch (start us, length us, event | category | flops | bytes accessed | tf_op | source)
XLA Modules:
  0.0 104.0 jit_solution(3211076087646346523)
XLA Ops:
  0.0 1.2 %convert_element_type.92 = bf16[128,1024]{1,0:T(8,128)(2,1)S(1)} convert(f32[128,1024]{1,0:T(8,128)} %param.8) | non-fusion elementwise | flops 131072 | bytes 786432 | tf_op jit(solution)/shard_map/convert_element_type | solution.py:273
  1.2 0.7 constant_dynamic-slice_fusion.23
  1.9 2.4 %collective-permute-start.2 = (bf16[32,1024]{1,0:T(8,128)(2,1)}, bf16[32,1024]{1,0:T(8,128)(2,1)}, u32[]{:S(2)}, u32[]{:S(2)}) collective-permute-start(bf16[32,1024]{1,0:T(8,128)(2,1)} %get-tuple-element.50), channel_id=1, source_target_pairs={{0,3},{1,2},{2,1},{3,0},{4,7},{5,6},{6,5},{7,4},{8,11},{9,10},{10,... | collective-permute-start | bytes 196616 | tf_op jit(solution)/shard_map/ppermute | solution.py:22
  4.3 0.6 collective-permute-start.1
  5.0 0.7 mul.56
  5.7 1.4 %collective-permute-done.2 = bf16[32,1024]{1,0:T(8,128)(2,1)} collective-permute-done((bf16[32,1024]{1,0:T(8,128)(2,1)}, bf16[32,1024]{1,0:T(8,128)(2,1)}, u32[]{:S(2)}, u32[]{:S(2)}) %collective-permute-start.2) | collective-permute-done | bytes 65568 | tf_op jit(solution)/shard_map/ppermute | solution.py:22
  7.1 2.2 %collective-permute-done.1 = bf16[32,1024]{1,0:T(8,128)(2,1)} collective-permute-done((bf16[32,1024]{1,0:T(8,128)(2,1)}, bf16[32,1024]{1,0:T(8,128)(2,1)}, u32[]{:S(2)}, u32[]{:S(2)}) %collective-permute-start.1) | collective-permute-done | bytes 65568 | tf_op jit(solution)/shard_map/ppermute | solution.py:22
  9.3 0.9 pad_maximum_fusion.3
  10.3 0.2 fusion.23
  10.5 0.1 fusion.25
  10.7 3.9 %collective-permute-start.5 = (bf16[32,1024]{1,0:T(8,128)(2,1)S(1)}, bf16[32,1024]{1,0:T(8,128)(2,1)S(1)}, u32[]{:S(2)}, u32[]{:S(2)}) collective-permute-start(bf16[32,1024]{1,0:T(8,128)(2,1)S(1)} %get-tuple-element.42), channel_id=1, source_target_pairs={{0,12},{4,8},{8,4},{12,0},{1,13},{5,9},{9,5},{13,1},{2,14},{6,10},... | collective-permute-start | bytes 196616 | tf_op jit(solution)/shard_map/ppermute | solution.py:22
  14.5 0.6 collective-permute-start.3
  15.2 1.9 %collective-permute-done.5 = bf16[32,1024]{1,0:T(8,128)(2,1)S(1)} collective-permute-done((bf16[32,1024]{1,0:T(8,128)(2,1)S(1)}, bf16[32,1024]{1,0:T(8,128)(2,1)S(1)}, u32[]{:S(2)}, u32[]{:S(2)}) %collective-permute-start.5) | collective-permute-done | bytes 65568 | tf_op jit(solution)/shard_map/ppermute | solution.py:22
  17.1 3.3 %collective-permute-done.4 = bf16[32,1024]{1,0:T(8,128)(2,1)S(1)} collective-permute-done((bf16[32,1024]{1,0:T(8,128)(2,1)S(1)}, bf16[32,1024]{1,0:T(8,128)(2,1)S(1)}, u32[]{:S(2)}, u32[]{:S(2)}) %collective-permute-start.4) | collective-permute-done | bytes 65568 | tf_op jit(solution)/shard_map/ppermute | solution.py:22
  20.4 0.7 pad_maximum_fusion.6
  21.1 0.7 filter_spectrum.1.refs_8_
  21.9 0.8 copy-done.5
  22.7 0.7 constant_dynamic-slice_fusion.24.taps_ref
  23.4 1.3 %constant_dynamic-slice_fusion.13 = (bf16[1024,128]{1,0:T(8,128)(2,1)S(1)}, bf16[1024,128]{1,0:T(8,128)(2,1)S(1)}, bf16[1024,128]{1,0:T(8,128)(2,1)S(1)}, bf16[1024,128]{1,0:T(8,128)(2,1)S(1)}) fusion(bf16[1024,512]{1,0:T(8,128)(2,1)} %param.13, s32[]{:T(128)S(6)} %select_n.105, s32[]{:T(128)S(6)} %select_n.124, s32[]{:T(128)S(6)} %select_n.125, ...), kind=kLoop, calls=%fused_computation.101 | loop fusion | bytes 2097168 | tf_op jit(solution)/shard_map/dynamic_slice | solution.py:278
  24.7 1.6 %collective-permute-start.11 = (bf16[128,1024]{1,0:T(8,128)(2,1)}, bf16[128,1024]{1,0:T(8,128)(2,1)S(1)}, u32[]{:S(2)}, u32[]{:S(2)}) collective-permute-start(bf16[128,1024]{1,0:T(8,128)(2,1)} %bitcast.14), channel_id=1, source_target_pairs={{0,2},{1,3},{2,0},{3,1},{4,6},{5,7},{6,4},{7,5},{8,10},{9,11},{10,... | collective-permute-start | bytes 786440 | tf_op jit(solution)/shard_map/ppermute | solution.py:22
  26.3 1.1 %pad_maximum_fusion.1 = bf16[256,1024]{1,0:T(8,128)(2,1)S(1)} fusion(bf16[128,1024]{1,0:T(8,128)(2,1)} %collective-permute-done.6, bf16[128,1024]{1,0:T(8,128)(2,1)} %bitcast.14), kind=kLoop, calls=%fused_computation.41 | loop fusion | flops 1048576 | bytes 1048576 | tf_op jit(solution)/shard_map/concatenate | solution.py:289
  27.4 0.4 fusion.11
  27.8 1.1 %collective-permute-start.7 = (bf16[3,256,128]{2,1,0:T(8,128)(2,1)S(1)}, bf16[3,256,128]{2,1,0:T(8,128)(2,1)S(1)}, u32[]{:S(2)}, u32[]{:S(2)}) collective-permute-start(bf16[3,256,128]{2,1,0:T(8,128)(2,1)S(1)} %fusion.11), channel_id=1, source_target_pairs={{0,4},{4,0},{8,12},{12,8},{1,5},{5,1},{9,13},{13,9},{2,6},{6,2},{1... | collective-permute-start | bytes 589832 | tf_op jit(solution)/shard_map/ppermute | solution.py:22
  29.0 0.4 fusion.12
  29.4 0.7 collective-permute-start.8
  30.1 5.7 %collective-permute-start.10 = (bf16[3,256,128]{2,1,0:T(8,128)(2,1)S(1)}, bf16[3,256,128]{2,1,0:T(8,128)(2,1)S(1)}, u32[]{:S(2)}, u32[]{:S(2)}) collective-permute-start(bf16[3,256,128]{2,1,0:T(8,128)(2,1)S(1)} %fusion.12), channel_id=1, source_target_pairs={{0,4},{12,8},{1,5},{13,9},{2,6},{14,10},{3,7},{15,11},{16,20},{28,... | collective-permute-start | bytes 589832 | tf_op jit(solution)/shard_map/ppermute | solution.py:72
  35.9 0.4 fusion.9
  36.4 0.4 collective-permute-start.9
  36.8 0.4 fusion.7.refs_0_
  37.2 0.2 collective-permute-done.12
  37.5 0.4 fusion.13
  37.9 2.1 %collective-permute-start.13 = (bf16[3,256,128]{2,1,0:T(8,128)(2,1)S(1)}, bf16[3,256,128]{2,1,0:T(8,128)(2,1)S(1)}, u32[]{:S(2)}, u32[]{:S(2)}) collective-permute-start(bf16[3,256,128]{2,1,0:T(8,128)(2,1)S(1)} %fusion.13), channel_id=1, source_target_pairs={{0,4},{4,0},{8,12},{12,8},{1,5},{5,1},{9,13},{13,9},{2,6},{6,2},{1... | collective-permute-start | bytes 589832 | tf_op jit(solution)/shard_map/ppermute | solution.py:22
  40.0 0.4 fusion.14
  40.5 0.8 collective-permute-start.14
  41.3 4.8 %collective-permute-start.16 = (bf16[3,256,128]{2,1,0:T(8,128)(2,1)S(1)}, bf16[3,256,128]{2,1,0:T(8,128)(2,1)S(1)}, u32[]{:S(2)}, u32[]{:S(2)}) collective-permute-start(bf16[3,256,128]{2,1,0:T(8,128)(2,1)S(1)} %fusion.14), channel_id=1, source_target_pairs={{0,4},{12,8},{1,5},{13,9},{2,6},{14,10},{3,7},{15,11},{16,20},{28,... | collective-permute-start | bytes 589832 | tf_op jit(solution)/shard_map/ppermute | solution.py:72
  46.1 3.5 %collective-permute-done.13 = bf16[3,256,128]{2,1,0:T(8,128)(2,1)S(1)} collective-permute-done((bf16[3,256,128]{2,1,0:T(8,128)(2,1)S(1)}, bf16[3,256,128]{2,1,0:T(8,128)(2,1)S(1)}, u32[]{:S(2)}, u32[]{:S(2)}) %collective-permute-start.13) | collective-permute-done | bytes 196640 | tf_op jit(solution)/shard_map/ppermute | solution.py:22
  49.5 0.4 fusion.10
  50.0 2.4 %collective-permute-start.15 = (bf16[3,256,128]{2,1,0:T(8,128)(2,1)S(1)}, bf16[3,256,128]{2,1,0:T(8,128)(2,1)S(1)}, u32[]{:S(2)}, u32[]{:S(2)}) collective-permute-start(bf16[3,256,128]{2,1,0:T(8,128)(2,1)S(1)} %fusion.10), channel_id=1, source_target_pairs={{0,8},{4,12},{8,0},{12,4},{1,9},{5,13},{9,1},{13,5},{2,10},{6,14},... | collective-permute-start | bytes 589832 | tf_op jit(solution)/shard_map/ppermute | solution.py:22
  52.4 0.4 fusion.8.refs_3_
  52.9 0.9 collective-permute-done.16.refs_5_
  53.8 7.7 %collective-permute-done.15.refs_4_ = bf16[3,256,128]{2,1,0:T(8,128)(2,1)S(1)} collective-permute-done((bf16[3,256,128]{2,1,0:T(8,128)(2,1)S(1)}, bf16[3,256,128]{2,1,0:T(8,128)(2,1)S(1)}, u32[]{:S(2)}, u32[]{:S(2)}) %collective-permute-start.15) | collective-permute-done | bytes 196640 | tf_op jit(solution)/shard_map/ppermute | solution.py:22
  61.4 3.3 %filters.1 = (bf16[256,128]{1,0:T(8,128)(2,1)S(1)}, bf16[256,128]{1,0:T(8,128)(2,1)S(1)}) custom-call(s32[1]{0:T(128)} %bitcast.t_ref, f32[3,3,128]{2,1,0:T(4,128)S(1)} %constant_dynamic-slice_fusion.24.taps_ref, f32[3,256,128]{2,1,0:T(8,128)S(1)} %fusion.7.refs_0_, bf16[3,256,128]{2,1,0:T(8,128)(2,1)S(1)} %collective-permute-done.9.refs_1_, ...), custom_call_target="tpu_custom_call" | custom-call | flops 805306368 | bytes 2097152 | tf_op jit(solution)/shard_map/filters/pallas_call | solution.py:219
  64.8 1.9 %collective-permute-start.22 = (bf16[256,128]{1,0:T(8,128)(2,1)S(1)}, bf16[256,128]{1,0:T(8,128)(2,1)S(1)}, u32[]{:S(2)}, u32[]{:S(2)}) collective-permute-start(bf16[256,128]{1,0:T(8,128)(2,1)S(1)} %get-tuple-element.16), channel_id=1, source_target_pairs={{0,8},{4,12},{8,0},{12,4},{1,9},{5,13},{9,1},{13,5},{2,10},{6,14},... | collective-permute-start | bytes 196616 | tf_op jit(solution)/shard_map/ppermute | solution.py:22
  66.7 2.5 %collective-permute-start.23 = (bf16[256,128]{1,0:T(8,128)(2,1)S(1)}, bf16[256,128]{1,0:T(8,128)(2,1)S(1)}, u32[]{:S(2)}, u32[]{:S(2)}) collective-permute-start(bf16[256,128]{1,0:T(8,128)(2,1)S(1)} %get-tuple-element.16), channel_id=1, source_target_pairs={{0,12},{4,8},{8,4},{12,0},{1,13},{5,9},{9,5},{13,1},{2,14},{6,10},... | collective-permute-start | bytes 196616 | tf_op jit(solution)/shard_map/ppermute | solution.py:22
  69.2 1.9 %collective-permute-start.18 = (bf16[256,128]{1,0:T(8,128)(2,1)S(1)}, bf16[256,128]{1,0:T(8,128)(2,1)S(1)}, u32[]{:S(2)}, u32[]{:S(2)}) collective-permute-start(bf16[256,128]{1,0:T(8,128)(2,1)S(1)} %get-tuple-element.15), channel_id=1, source_target_pairs={{0,8},{4,12},{8,0},{12,4},{1,9},{5,13},{9,1},{13,5},{2,10},{6,14},... | collective-permute-start | bytes 196616 | tf_op jit(solution)/shard_map/ppermute | solution.py:22
  71.2 2.5 %collective-permute-start.19 = (bf16[256,128]{1,0:T(8,128)(2,1)S(1)}, bf16[256,128]{1,0:T(8,128)(2,1)S(1)}, u32[]{:S(2)}, u32[]{:S(2)}) collective-permute-start(bf16[256,128]{1,0:T(8,128)(2,1)S(1)} %get-tuple-element.15), channel_id=1, source_target_pairs={{0,12},{4,8},{8,4},{12,0},{1,13},{5,9},{9,5},{13,1},{2,14},{6,10},... | collective-permute-start | bytes 196616 | tf_op jit(solution)/shard_map/ppermute | solution.py:22
  73.8 0.5 convolution_convert_fusion
  74.4 3.9 %collective-permute-done.18 = bf16[256,128]{1,0:T(8,128)(2,1)S(1)} collective-permute-done((bf16[256,128]{1,0:T(8,128)(2,1)S(1)}, bf16[256,128]{1,0:T(8,128)(2,1)S(1)}, u32[]{:S(2)}, u32[]{:S(2)}) %collective-permute-start.18) | collective-permute-done | bytes 65568 | tf_op jit(solution)/shard_map/ppermute | solution.py:22
  78.3 0.5 convolution_convert_fusion.1
  78.9 0.5 fusion.2
  79.4 0.5 collective-permute-start.25
  79.9 0.5 collective-permute-done.20
  80.4 7.7 %collective-permute-done.25 = bf16[128,1024]{1,0:T(8,128)(2,1)S(1)} collective-permute-done((bf16[128,1024]{1,0:T(8,128)(2,1)S(1)}, bf16[128,1024]{1,0:T(8,128)(2,1)S(1)}, u32[]{:S(2)}, u32[]{:S(2)}) %collective-permute-start.25) | collective-permute-done | bytes 262176 | tf_op jit(solution)/shard_map/ppermute | solution.py:22
  88.2 0.5 fusion.1
  88.7 1.6 %collective-permute-start.28 = (bf16[32,1024]{1,0:T(8,128)(2,1)S(1)}, bf16[32,1024]{1,0:T(8,128)(2,1)S(1)}, u32[]{:S(2)}, u32[]{:S(2)}) collective-permute-start(bf16[32,1024]{1,0:T(8,128)(2,1)S(1)} %get-tuple-element.34), channel_id=1, source_target_pairs={{0,12},{4,8},{8,4},{12,0},{1,13},{5,9},{9,5},{13,1},{2,14},{6,10},... | collective-permute-start | bytes 196616 | tf_op jit(solution)/shard_map/ppermute | solution.py:22
  90.3 1.2 %collective-permute-start.27 = (bf16[32,1024]{1,0:T(8,128)(2,1)S(1)}, bf16[32,1024]{1,0:T(8,128)(2,1)S(1)}, u32[]{:S(2)}, u32[]{:S(2)}) collective-permute-start(bf16[32,1024]{1,0:T(8,128)(2,1)S(1)} %get-tuple-element.35), channel_id=1, source_target_pairs={{0,8},{4,12},{8,0},{12,4},{1,9},{5,13},{9,1},{13,5},{2,10},{6,14},... | collective-permute-start | bytes 196616 | tf_op jit(solution)/shard_map/ppermute | solution.py:22
  91.4 1.7 %collective-permute-start.26 = (bf16[32,1024]{1,0:T(8,128)(2,1)S(1)}, bf16[32,1024]{1,0:T(8,128)(2,1)S(1)}, u32[]{:S(2)}, u32[]{:S(2)}) collective-permute-start(bf16[32,1024]{1,0:T(8,128)(2,1)S(1)} %get-tuple-element.36), channel_id=1, source_target_pairs={{0,4},{4,0},{8,12},{12,8},{1,5},{5,1},{9,13},{13,9},{2,6},{6,2},{1... | collective-permute-start | bytes 196616 | tf_op jit(solution)/shard_map/ppermute | solution.py:22
  93.1 2.3 %collective-permute-done.28 = bf16[32,1024]{1,0:T(8,128)(2,1)S(1)} collective-permute-done((bf16[32,1024]{1,0:T(8,128)(2,1)S(1)}, bf16[32,1024]{1,0:T(8,128)(2,1)S(1)}, u32[]{:S(2)}, u32[]{:S(2)}) %collective-permute-start.28) | collective-permute-done | bytes 65568 | tf_op jit(solution)/shard_map/ppermute | solution.py:22
  95.5 2.2 %collective-permute-done.27 = bf16[32,1024]{1,0:T(8,128)(2,1)S(1)} collective-permute-done((bf16[32,1024]{1,0:T(8,128)(2,1)S(1)}, bf16[32,1024]{1,0:T(8,128)(2,1)S(1)}, u32[]{:S(2)}, u32[]{:S(2)}) %collective-permute-start.27) | collective-permute-done | bytes 65568 | tf_op jit(solution)/shard_map/ppermute | solution.py:22
  97.9 1.0 collective-permute-start.30
  99.0 0.8 collective-permute-start.29
  99.8 2.5 %collective-permute-done.31 = bf16[32,1024]{1,0:T(8,128)(2,1)S(1)} collective-permute-done((bf16[32,1024]{1,0:T(8,128)(2,1)S(1)}, bf16[32,1024]{1,0:T(8,128)(2,1)S(1)}, u32[]{:S(2)}, u32[]{:S(2)}) %collective-permute-start.31) | collective-permute-done | bytes 65568 | tf_op jit(solution)/shard_map/ppermute | solution.py:22
  102.3 0.7 collective-permute-done.30
  103.1 0.9 convert_add_fusion
  (64 shorter events, 1.1 us)
Async XLA Ops:
  0.0 27.4 %copy-start = (bf16[3,1024,512]{2,1,0:T(8,128)(2,1)S(1)}, bf16[3,1024,512]{2,1,0:T(8,128)(2,1)}, u32[]{:S(2)}) copy-start(bf16[3,1024,512]{2,1,0:T(8,128)(2,1)} %param.10) | copy-start | bytes 9437188
  1.9 19.2 %copy-start.7 = (f32[128,512]{1,0:T(8,128)S(1)}, f32[128,512]{1,0:T(8,128)}, u32[]{:S(2)}) copy-start(f32[128,512]{1,0:T(8,128)} %taps_ref.1) | copy-start | bytes 786436
  1.9 5.2 %collective-permute-start.2 = (bf16[32,1024]{1,0:T(8,128)(2,1)}, bf16[32,1024]{1,0:T(8,128)(2,1)}, u32[]{:S(2)}, u32[]{:S(2)}) collective-permute-start(bf16[32,1024]{1,0:T(8,128)(2,1)} %get-tuple-element.50), channel_id=1, source_target_pairs={{0,3},{1,2},{2,1},{3,0},{4,7},{5,6},{6,5},{7,4},{8,11},{9,10},{10,... | collective-permute-start | bytes 196616 | tf_op jit(solution)/shard_map/ppermute | solution.py:22
  4.3 5.0 %collective-permute-start.1 = (bf16[32,1024]{1,0:T(8,128)(2,1)}, bf16[32,1024]{1,0:T(8,128)(2,1)}, u32[]{:S(2)}, u32[]{:S(2)}) collective-permute-start(bf16[32,1024]{1,0:T(8,128)(2,1)} %get-tuple-element.51), channel_id=1, source_target_pairs={{0,2},{1,3},{2,0},{3,1},{4,6},{5,7},{6,4},{7,5},{8,10},{9,11},{10,... | collective-permute-start | bytes 196616 | tf_op jit(solution)/shard_map/ppermute | solution.py:22
  4.9 4.4 %collective-permute-start = (bf16[32,1024]{1,0:T(8,128)(2,1)S(1)}, bf16[32,1024]{1,0:T(8,128)(2,1)}, u32[]{:S(2)}, u32[]{:S(2)}) collective-permute-start(bf16[32,1024]{1,0:T(8,128)(2,1)S(1)} %get-tuple-element.52), channel_id=1, source_target_pairs={{0,1},{1,0},{2,3},{3,2},{4,5},{5,4},{6,7},{7,6},{8,9},{9,8},{10,11... | collective-permute-start | bytes 196616 | tf_op jit(solution)/shard_map/ppermute | solution.py:22
  5.7 15.4 %copy-start.1 = (bf16[1024,512]{1,0:T(8,128)(2,1)S(1)}, bf16[1024,512]{1,0:T(8,128)(2,1)}, u32[]{:S(2)}) copy-start(bf16[1024,512]{1,0:T(8,128)(2,1)} %constant.99.clone.high_ref.refs_6_) | copy-start | bytes 3145732
  5.7 15.4 %copy-start.3 = (bf16[1024,512]{1,0:T(8,128)(2,1)S(1)}, bf16[1024,512]{1,0:T(8,128)(2,1)}, u32[]{:S(2)}) copy-start(bf16[1024,512]{1,0:T(8,128)(2,1)} %constant.100.clone.low_ref.refs_7_) | copy-start | bytes 3145732
  10.7 6.4 %collective-permute-start.5 = (bf16[32,1024]{1,0:T(8,128)(2,1)S(1)}, bf16[32,1024]{1,0:T(8,128)(2,1)S(1)}, u32[]{:S(2)}, u32[]{:S(2)}) collective-permute-start(bf16[32,1024]{1,0:T(8,128)(2,1)S(1)} %get-tuple-element.42), channel_id=1, source_target_pairs={{0,12},{4,8},{8,4},{12,0},{1,13},{5,9},{9,5},{13,1},{2,14},{6,10},... | collective-permute-start | bytes 196616 | tf_op jit(solution)/shard_map/ppermute | solution.py:22
  14.5 5.8 %collective-permute-start.4 = (bf16[32,1024]{1,0:T(8,128)(2,1)S(1)}, bf16[32,1024]{1,0:T(8,128)(2,1)S(1)}, u32[]{:S(2)}, u32[]{:S(2)}) collective-permute-start(bf16[32,1024]{1,0:T(8,128)(2,1)S(1)} %get-tuple-element.43), channel_id=1, source_target_pairs={{0,8},{4,12},{8,0},{12,4},{1,9},{5,13},{9,1},{13,5},{2,10},{6,14},... | collective-permute-start | bytes 196616 | tf_op jit(solution)/shard_map/ppermute | solution.py:22
  14.5 5.8 %collective-permute-start.3 = (bf16[32,1024]{1,0:T(8,128)(2,1)S(1)}, bf16[32,1024]{1,0:T(8,128)(2,1)S(1)}, u32[]{:S(2)}, u32[]{:S(2)}) collective-permute-start(bf16[32,1024]{1,0:T(8,128)(2,1)S(1)} %get-tuple-element.44), channel_id=1, source_target_pairs={{0,4},{4,0},{8,12},{12,8},{1,5},{5,1},{9,13},{13,9},{2,6},{6,2},{1... | collective-permute-start | bytes 196616 | tf_op jit(solution)/shard_map/ppermute | solution.py:22
  21.1 5.2 %collective-permute-start.6 = (bf16[128,1024]{1,0:T(8,128)(2,1)}, bf16[128,1024]{1,0:T(8,128)(2,1)}, u32[]{:S(2)}, u32[]{:S(2)}) collective-permute-start(bf16[128,1024]{1,0:T(8,128)(2,1)} %bitcast.14), channel_id=1, source_target_pairs={{0,1},{1,0},{2,3},{3,2},{4,5},{5,4},{6,7},{7,6},{8,9},{9,8},{10,11... | collective-permute-start | bytes 786440 | tf_op jit(solution)/shard_map/ppermute | solution.py:22
  21.9 0.8 copy-start.5
  24.7 11.1 %collective-permute-start.11 = (bf16[128,1024]{1,0:T(8,128)(2,1)}, bf16[128,1024]{1,0:T(8,128)(2,1)S(1)}, u32[]{:S(2)}, u32[]{:S(2)}) collective-permute-start(bf16[128,1024]{1,0:T(8,128)(2,1)} %bitcast.14), channel_id=1, source_target_pairs={{0,2},{1,3},{2,0},{3,1},{4,6},{5,7},{6,4},{7,5},{8,10},{9,11},{10,... | collective-permute-start | bytes 786440 | tf_op jit(solution)/shard_map/ppermute | solution.py:22
  27.8 8.1 %collective-permute-start.7 = (bf16[3,256,128]{2,1,0:T(8,128)(2,1)S(1)}, bf16[3,256,128]{2,1,0:T(8,128)(2,1)S(1)}, u32[]{:S(2)}, u32[]{:S(2)}) collective-permute-start(bf16[3,256,128]{2,1,0:T(8,128)(2,1)S(1)} %fusion.11), channel_id=1, source_target_pairs={{0,4},{4,0},{8,12},{12,8},{1,5},{5,1},{9,13},{13,9},{2,6},{6,2},{1... | collective-permute-start | bytes 589832 | tf_op jit(solution)/shard_map/ppermute | solution.py:22
  29.4 7.3 %collective-permute-start.8 = (bf16[3,256,128]{2,1,0:T(8,128)(2,1)S(1)}, bf16[3,256,128]{2,1,0:T(8,128)(2,1)S(1)}, u32[]{:S(2)}, u32[]{:S(2)}) collective-permute-start(bf16[3,256,128]{2,1,0:T(8,128)(2,1)S(1)} %fusion.12), channel_id=1, source_target_pairs={{4,8},{8,4},{5,9},{9,5},{6,10},{10,6},{7,11},{11,7},{20,24},{24,20... | collective-permute-start | bytes 589832 | tf_op jit(solution)/shard_map/ppermute | solution.py:71
  30.1 22.8 %collective-permute-start.10 = (bf16[3,256,128]{2,1,0:T(8,128)(2,1)S(1)}, bf16[3,256,128]{2,1,0:T(8,128)(2,1)S(1)}, u32[]{:S(2)}, u32[]{:S(2)}) collective-permute-start(bf16[3,256,128]{2,1,0:T(8,128)(2,1)S(1)} %fusion.12), channel_id=1, source_target_pairs={{0,4},{12,8},{1,5},{13,9},{2,6},{14,10},{3,7},{15,11},{16,20},{28,... | collective-permute-start | bytes 589832 | tf_op jit(solution)/shard_map/ppermute | solution.py:72
  35.8 1.6 %collective-permute-start.12 = (bf16[128,1024]{1,0:T(8,128)(2,1)S(1)}, bf16[128,1024]{1,0:T(8,128)(2,1)S(1)}, u32[]{:S(2)}, u32[]{:S(2)}) collective-permute-start(bf16[128,1024]{1,0:T(8,128)(2,1)S(1)} %collective-permute-done.11), channel_id=1, source_target_pairs={{0,1},{1,0},{2,3},{3,2},{4,5},{5,4},{6,7},{7,6},{8,9},{9,8},{10,11... | collective-permute-start | bytes 786440 | tf_op jit(solution)/shard_map/ppermute | solution.py:22
  36.4 16.5 %collective-permute-start.9 = (bf16[3,256,128]{2,1,0:T(8,128)(2,1)S(1)}, bf16[3,256,128]{2,1,0:T(8,128)(2,1)S(1)}, u32[]{:S(2)}, u32[]{:S(2)}) collective-permute-start(bf16[3,256,128]{2,1,0:T(8,128)(2,1)S(1)} %fusion.9), channel_id=1, source_target_pairs={{0,8},{4,12},{8,0},{12,4},{1,9},{5,13},{9,1},{13,5},{2,10},{6,14},... | collective-permute-start | bytes 589832 | tf_op jit(solution)/shard_map/ppermute | solution.py:22
  37.9 11.6 %collective-permute-start.13 = (bf16[3,256,128]{2,1,0:T(8,128)(2,1)S(1)}, bf16[3,256,128]{2,1,0:T(8,128)(2,1)S(1)}, u32[]{:S(2)}, u32[]{:S(2)}) collective-permute-start(bf16[3,256,128]{2,1,0:T(8,128)(2,1)S(1)} %fusion.13), channel_id=1, source_target_pairs={{0,4},{4,0},{8,12},{12,8},{1,5},{5,1},{9,13},{13,9},{2,6},{6,2},{1... | collective-permute-start | bytes 589832 | tf_op jit(solution)/shard_map/ppermute | solution.py:22
  40.5 21.0 %copy-start.2 = (bf16[1024,512]{1,0:T(8,128)(2,1)S(1)}, bf16[1024,512]{1,0:T(8,128)(2,1)}, u32[]{:S(2)}) copy-start(bf16[1024,512]{1,0:T(8,128)(2,1)} %constant.99.clone.high_ref.refs_6_) | copy-start | bytes 3145732
  40.5 20.9 %copy-start.4 = (bf16[1024,512]{1,0:T(8,128)(2,1)S(1)}, bf16[1024,512]{1,0:T(8,128)(2,1)}, u32[]{:S(2)}) copy-start(bf16[1024,512]{1,0:T(8,128)(2,1)} %constant.100.clone.low_ref.refs_7_) | copy-start | bytes 3145732
  40.5 20.9 %copy-start.6 = (f32[1024,128]{1,0:T(8,128)S(1)}, f32[1024,128]{1,0:T(8,128)}, u32[]{:S(2)}) copy-start(f32[1024,128]{1,0:T(8,128)} %copy-done.5) | copy-start | bytes 1572868
  40.5 11.9 %collective-permute-start.14 = (bf16[3,256,128]{2,1,0:T(8,128)(2,1)S(1)}, bf16[3,256,128]{2,1,0:T(8,128)(2,1)S(1)}, u32[]{:S(2)}, u32[]{:S(2)}) collective-permute-start(bf16[3,256,128]{2,1,0:T(8,128)(2,1)S(1)} %fusion.14), channel_id=1, source_target_pairs={{4,8},{8,4},{5,9},{9,5},{6,10},{10,6},{7,11},{11,7},{20,24},{24,20... | collective-permute-start | bytes 589832 | tf_op jit(solution)/shard_map/ppermute | solution.py:71
  41.3 12.4 %collective-permute-start.16 = (bf16[3,256,128]{2,1,0:T(8,128)(2,1)S(1)}, bf16[3,256,128]{2,1,0:T(8,128)(2,1)S(1)}, u32[]{:S(2)}, u32[]{:S(2)}) collective-permute-start(bf16[3,256,128]{2,1,0:T(8,128)(2,1)S(1)} %fusion.14), channel_id=1, source_target_pairs={{0,4},{12,8},{1,5},{13,9},{2,6},{14,10},{3,7},{15,11},{16,20},{28,... | collective-permute-start | bytes 589832 | tf_op jit(solution)/shard_map/ppermute | solution.py:72
  50.0 11.4 %collective-permute-start.15 = (bf16[3,256,128]{2,1,0:T(8,128)(2,1)S(1)}, bf16[3,256,128]{2,1,0:T(8,128)(2,1)S(1)}, u32[]{:S(2)}, u32[]{:S(2)}) collective-permute-start(bf16[3,256,128]{2,1,0:T(8,128)(2,1)S(1)} %fusion.10), channel_id=1, source_target_pairs={{0,8},{4,12},{8,0},{12,4},{1,9},{5,13},{9,1},{13,5},{2,10},{6,14},... | collective-permute-start | bytes 589832 | tf_op jit(solution)/shard_map/ppermute | solution.py:22
  64.7 6.4 %collective-permute-start.21 = (bf16[256,128]{1,0:T(8,128)(2,1)S(1)}, bf16[256,128]{1,0:T(8,128)(2,1)S(1)}, u32[]{:S(2)}, u32[]{:S(2)}) collective-permute-start(bf16[256,128]{1,0:T(8,128)(2,1)S(1)} %get-tuple-element.16), channel_id=1, source_target_pairs={{0,4},{4,0},{8,12},{12,8},{1,5},{5,1},{9,13},{13,9},{2,6},{6,2},{1... | collective-permute-start | bytes 196616 | tf_op jit(solution)/shard_map/ppermute | solution.py:22
  64.8 8.9 %collective-permute-start.22 = (bf16[256,128]{1,0:T(8,128)(2,1)S(1)}, bf16[256,128]{1,0:T(8,128)(2,1)S(1)}, u32[]{:S(2)}, u32[]{:S(2)}) collective-permute-start(bf16[256,128]{1,0:T(8,128)(2,1)S(1)} %get-tuple-element.16), channel_id=1, source_target_pairs={{0,8},{4,12},{8,0},{12,4},{1,9},{5,13},{9,1},{13,5},{2,10},{6,14},... | collective-permute-start | bytes 196616 | tf_op jit(solution)/shard_map/ppermute | solution.py:22
  66.7 7.0 %collective-permute-start.23 = (bf16[256,128]{1,0:T(8,128)(2,1)S(1)}, bf16[256,128]{1,0:T(8,128)(2,1)S(1)}, u32[]{:S(2)}, u32[]{:S(2)}) collective-permute-start(bf16[256,128]{1,0:T(8,128)(2,1)S(1)} %get-tuple-element.16), channel_id=1, source_target_pairs={{0,12},{4,8},{8,4},{12,0},{1,13},{5,9},{9,5},{13,1},{2,14},{6,10},... | collective-permute-start | bytes 196616 | tf_op jit(solution)/shard_map/ppermute | solution.py:22
  69.2 5.2 %collective-permute-start.17 = (bf16[256,128]{1,0:T(8,128)(2,1)S(1)}, bf16[256,128]{1,0:T(8,128)(2,1)S(1)}, u32[]{:S(2)}, u32[]{:S(2)}) collective-permute-start(bf16[256,128]{1,0:T(8,128)(2,1)S(1)} %get-tuple-element.15), channel_id=1, source_target_pairs={{0,4},{4,0},{8,12},{12,8},{1,5},{5,1},{9,13},{13,9},{2,6},{6,2},{1... | collective-permute-start | bytes 196616 | tf_op jit(solution)/shard_map/ppermute | solution.py:22
  69.2 9.1 %collective-permute-start.18 = (bf16[256,128]{1,0:T(8,128)(2,1)S(1)}, bf16[256,128]{1,0:T(8,128)(2,1)S(1)}, u32[]{:S(2)}, u32[]{:S(2)}) collective-permute-start(bf16[256,128]{1,0:T(8,128)(2,1)S(1)} %get-tuple-element.15), channel_id=1, source_target_pairs={{0,8},{4,12},{8,0},{12,4},{1,9},{5,13},{9,1},{13,5},{2,10},{6,14},... | collective-permute-start | bytes 196616 | tf_op jit(solution)/shard_map/ppermute | solution.py:22
  71.2 7.1 %collective-permute-start.19 = (bf16[256,128]{1,0:T(8,128)(2,1)S(1)}, bf16[256,128]{1,0:T(8,128)(2,1)S(1)}, u32[]{:S(2)}, u32[]{:S(2)}) collective-permute-start(bf16[256,128]{1,0:T(8,128)(2,1)S(1)} %get-tuple-element.15), channel_id=1, source_target_pairs={{0,12},{4,8},{8,4},{12,0},{1,13},{5,9},{9,5},{13,1},{2,14},{6,10},... | collective-permute-start | bytes 196616 | tf_op jit(solution)/shard_map/ppermute | solution.py:22
  74.2 4.6 %collective-permute-start.24 = (bf16[128,1024]{1,0:T(8,128)(2,1)S(1)}, bf16[128,1024]{1,0:T(8,128)(2,1)S(1)}, u32[]{:S(2)}, u32[]{:S(2)}) collective-permute-start(bf16[128,1024]{1,0:T(8,128)(2,1)S(1)} %convolution_convert_fusion), channel_id=1, source_target_pairs={{0,1},{1,0},{2,3},{3,2},{4,5},{5,4},{6,7},{7,6},{8,9},{9,8},{10,11... | collective-permute-start | bytes 786440 | tf_op jit(solution)/shard_map/ppermute | solution.py:22
  78.8 1.6 %collective-permute-start.20 = (bf16[128,1024]{1,0:T(8,128)(2,1)S(1)}, bf16[128,1024]{1,0:T(8,128)(2,1)S(1)}, u32[]{:S(2)}, u32[]{:S(2)}) collective-permute-start(bf16[128,1024]{1,0:T(8,128)(2,1)S(1)} %convolution_convert_fusion.1), channel_id=1, source_target_pairs={{0,1},{1,0},{2,3},{3,2},{4,5},{5,4},{6,7},{7,6},{8,9},{9,8},{10,11... | collective-permute-start | bytes 786440 | tf_op jit(solution)/shard_map/ppermute | solution.py:22
  79.4 8.8 %collective-permute-start.25 = (bf16[128,1024]{1,0:T(8,128)(2,1)S(1)}, bf16[128,1024]{1,0:T(8,128)(2,1)S(1)}, u32[]{:S(2)}, u32[]{:S(2)}) collective-permute-start(bf16[128,1024]{1,0:T(8,128)(2,1)S(1)} %fusion.2), channel_id=1, source_target_pairs={{0,2},{1,3},{2,0},{3,1},{4,6},{5,7},{6,4},{7,5},{8,10},{9,11},{10,... | collective-permute-start | bytes 786440 | tf_op jit(solution)/shard_map/ppermute | solution.py:22
  88.6 14.5 %copy-start.8 = (f32[128,1024]{1,0:T(8,128)S(1)}, f32[128,1024]{1,0:T(8,128)}, u32[]{:S(2)}) copy-start(f32[128,1024]{1,0:T(8,128)} %param.8) | copy-start | bytes 1572868
  88.7 6.8 %collective-permute-start.28 = (bf16[32,1024]{1,0:T(8,128)(2,1)S(1)}, bf16[32,1024]{1,0:T(8,128)(2,1)S(1)}, u32[]{:S(2)}, u32[]{:S(2)}) collective-permute-start(bf16[32,1024]{1,0:T(8,128)(2,1)S(1)} %get-tuple-element.34), channel_id=1, source_target_pairs={{0,12},{4,8},{8,4},{12,0},{1,13},{5,9},{9,5},{13,1},{2,14},{6,10},... | collective-permute-start | bytes 196616 | tf_op jit(solution)/shard_map/ppermute | solution.py:22
  90.3 7.4 %collective-permute-start.27 = (bf16[32,1024]{1,0:T(8,128)(2,1)S(1)}, bf16[32,1024]{1,0:T(8,128)(2,1)S(1)}, u32[]{:S(2)}, u32[]{:S(2)}) collective-permute-start(bf16[32,1024]{1,0:T(8,128)(2,1)S(1)} %get-tuple-element.35), channel_id=1, source_target_pairs={{0,8},{4,12},{8,0},{12,4},{1,9},{5,13},{9,1},{13,5},{2,10},{6,14},... | collective-permute-start | bytes 196616 | tf_op jit(solution)/shard_map/ppermute | solution.py:22
  91.4 6.3 %collective-permute-start.26 = (bf16[32,1024]{1,0:T(8,128)(2,1)S(1)}, bf16[32,1024]{1,0:T(8,128)(2,1)S(1)}, u32[]{:S(2)}, u32[]{:S(2)}) collective-permute-start(bf16[32,1024]{1,0:T(8,128)(2,1)S(1)} %get-tuple-element.36), channel_id=1, source_target_pairs={{0,4},{4,0},{8,12},{12,8},{1,5},{5,1},{9,13},{13,9},{2,6},{6,2},{1... | collective-permute-start | bytes 196616 | tf_op jit(solution)/shard_map/ppermute | solution.py:22
  97.9 4.4 %collective-permute-start.31 = (bf16[32,1024]{1,0:T(8,128)(2,1)S(1)}, bf16[32,1024]{1,0:T(8,128)(2,1)S(1)}, u32[]{:S(2)}, u32[]{:S(2)}) collective-permute-start(bf16[32,1024]{1,0:T(8,128)(2,1)S(1)} %get-tuple-element.26), channel_id=1, source_target_pairs={{0,3},{1,2},{2,1},{3,0},{4,7},{5,6},{6,5},{7,4},{8,11},{9,10},{10,... | collective-permute-start | bytes 196616 | tf_op jit(solution)/shard_map/ppermute | solution.py:22
  97.9 5.0 %collective-permute-start.30 = (bf16[32,1024]{1,0:T(8,128)(2,1)S(1)}, bf16[32,1024]{1,0:T(8,128)(2,1)S(1)}, u32[]{:S(2)}, u32[]{:S(2)}) collective-permute-start(bf16[32,1024]{1,0:T(8,128)(2,1)S(1)} %get-tuple-element.27), channel_id=1, source_target_pairs={{0,2},{1,3},{2,0},{3,1},{4,6},{5,7},{6,4},{7,5},{8,10},{9,11},{10,... | collective-permute-start | bytes 196616 | tf_op jit(solution)/shard_map/ppermute | solution.py:22
  99.0 4.0 %collective-permute-start.29 = (bf16[32,1024]{1,0:T(8,128)(2,1)S(1)}, bf16[32,1024]{1,0:T(8,128)(2,1)S(1)}, u32[]{:S(2)}, u32[]{:S(2)}) collective-permute-start(bf16[32,1024]{1,0:T(8,128)(2,1)S(1)} %get-tuple-element.28), channel_id=1, source_target_pairs={{0,1},{1,0},{2,3},{3,2},{4,5},{5,4},{6,7},{7,6},{8,9},{9,8},{10,11... | collective-permute-start | bytes 196616 | tf_op jit(solution)/shard_map/ppermute | solution.py:22

commit v8 on v7

--- a/solution.py
+++ b/solution.py
@@ -143,7 +143,7 @@
 
 
 def local_kernel(groups, each, seq, sub, t_ref, taps_ref, *refs):
-    count = each * len(groups)
+    count = sum(each)
     moved = count + 3
     sources, outs = refs[:moved], refs[moved : moved + 2]
     proj, gated, sems = refs[moved + 2 : moved + 5]
@@ -163,8 +163,9 @@
 
     proj[:, :8] = jnp.zeros((proj.shape[0], 8, proj.shape[2]), jnp.float32)
     for group, slots in enumerate(groups):
-        mine = terms[group * each : (group + 1) * each]
-        for copy in copies[group * each : (group + 1) * each]:
+        start = sum(each[:group])
+        mine = terms[start : start + each[group]]
+        for copy in copies[start : start + each[group]]:
             copy.wait()
         for position, slot in enumerate(slots):
             for source in range(seq):
@@ -217,7 +218,7 @@
     lines = length // 2
     moved = [*flat, *wide, spectrum]
     return pl.pallas_call(
-        functools.partial(local_kernel, groups, len(terms[0]), seq, sub),
+        functools.partial(local_kernel, groups, [len(group) for group in terms], seq, sub),
         out_shape=[jax.ShapeDtypeStruct((lines, own), jnp.bfloat16)] * 2,
         in_specs=[pl.BlockSpec(memory_space=pltpu.SMEM), vmem] + [pl.BlockSpec(memory_space=pl.ANY)] * len(moved),
         out_specs=[vmem] * 2,
@@ -275,8 +276,8 @@
     def in_part(mask):
         return lax.dynamic_slice_in_dim(in_weight, (z ^ mask) * own, own, 2)
 
-    out_parts = [lax.dynamic_slice_in_dim(out_weight, (z ^ mask) * own, own, 1) for mask in range(seq)]
-    out_turned = jnp.concatenate(out_parts, axis=1)
+    out_parts = [lax.dynamic_slice_in_dim(out_weight, (z ^ mask) * own, own, 1) for mask in (0, *reversed(range(1, seq)))]
+    out_turned = lax.optimization_barrier(jnp.concatenate(out_parts, axis=1))
     taps = lax.dynamic_slice_in_dim(short_taps, z * own, own, 2)
     whole = whole.transpose(1, 0, 2).reshape(sub, model).astype(jnp.float32)
     mean_sq = jnp.mean(whole * whole, axis=1, keepdims=True)
@@ -285,9 +286,14 @@
     parts = spread(normed.reshape(seq * sub, depth), "tensor")
     groups = (tuple(slots[:2]), tuple(slots[2:]))
     terms = []
-    for group in groups:
+    for group, name in zip(groups, ("sum_early", "sum_late")):
         rows_of = lax.optimization_barrier(jnp.concatenate([parts[slot] for slot in group]))
         terms.append(sum_over_seq(rows_of, in_part))
+        if name == "sum_early":
+            total = terms[0][0]
+            for term in terms[0][1:]:
+                total = total + term.astype(jnp.float32)
+            terms[0] = [total]
     half = tensor // 2
     if own % 128 == 0 and length <= BLOCK and sub % 16 == 0:
         lower_gated, upper_gated = local_stage(groups, terms, taps, long_filter, t, seq, sub)
@@ -299,7 +305,7 @@
     lower = [1 << bit for bit in range(half.bit_length() - 1)]
     held = None
     for chosen, piece in ((slots[half:], upper_gated), (slots[:half], lower_gated)):
-        got = [piece] + [hop(piece, "seq", mask) for mask in range(1, seq)]
+        got = [piece] + [hop(piece, "seq", mask) for mask in reversed(range(1, seq))]
         got = jnp.concatenate(got, axis=1)
         terms = {}
         for place, slot in enumerate(chosen):

time: 104 us -> 117 us (1.12)
  waiting for transfers between devices: 40.9 us -> 51.5 us
  starting transfers between devices: 43.2 us -> 39.9 us
  local copies, waits for them, and re-layouts: 4.55 us -> 7.77 us
  other arithmetic: 5.37 us -> 7.68 us
    ppermute x28, waiting for transfers between devices: 40 us -> 51.5 us  [hop(): return lax.ppermute(value, axis, [(a, a ^ mask) for a in range(count)])]
    ppermute x2, starting transfers between devices: 10.5 us -> 5.07 us  [sum_over_seq(): near = lax.ppermute(second, 'seq', [(0, 1), (3, 2)])]
    concatenate x0 -> x1, other arithmetic: none -> 2.31 us  [shards(): out_turned = lax.optimization_barrier(jnp.concatenate(out_parts, axis=1))]
    ppermute x28, starting transfers between devices: 31.3 us -> 33.5 us  [hop(): return lax.ppermute(value, axis, [(a, a ^ mask) for a in range(count)])]
    unnamed x23 -> x17, local copies, waits for them, and re-layouts: 0.93 us -> 2.57 us
  transfers between devices with their start and end apart: 32 -> 32, of which waited for: 15 -> 15; matrix products, arithmetic and copies ran while one was open for 9% -> 10% of each run, Pallas kernels for 1% -> 1%
where the time goes in v8:
time: 117 us; the launch traced here: 116 us
  waiting for transfers between devices  51.5 us (44%)
  starting transfers between devices  39.9 us (34%)
  local copies, waits for them, and re-layouts  7.77 us (7%)
  other arithmetic  7.68 us (7%)
  matrix products  5.45 us (5%)
  Pallas kernels  3.46 us (3%)
    ppermute x28, waiting for transfers between devices, hop(): return lax.ppermute(value, axis, [(a, a ^ mask) for a in range(count)])  51.5 us
    ppermute x28, starting transfers between devices, hop(): return lax.ppermute(value, axis, [(a, a ^ mask) for a in range(count)])  33.5 us
    ppermute x2, starting transfers between devices, sum_over_seq(): near = lax.ppermute(second, 'seq', [(0, 1), (3, 2)])  5.07 us
    dot_general x8, matrix products, product(): jnp.einsum(form, rows, weight_of(mask), preferred_element_type=jnp.float32)  3.56 us
    pallas_call x1, Pallas kernels, local_stage(): pl.pallas_call(functools.partial(local_kernel, groups, [len(group) for gr...  2.72 us
    unnamed x17, local copies, waits for them, and re-layouts  2.57 us
  transfers between devices with their start and end apart: 32, of which 15 were waited for; matrix products, arithmetic and copies ran while one was open for 10% of the time, Pallas kernels for 1%

profile of v8, /device:TPU:0, one launch (start us, length us, event | category | flops | bytes accessed | tf_op | source)
XLA Modules:
  0.0 116.2 jit_solution(7602634451669059191)
XLA Ops:
  0.0 1.2 %convert_element_type.98 = bf16[128,1024]{1,0:T(8,128)(2,1)S(1)} convert(f32[128,1024]{1,0:T(8,128)} %param.8) | non-fusion elementwise | flops 131072 | bytes 786432 | tf_op jit(solution)/shard_map/convert_element_type | solution.py:274
  1.2 0.7 constant_dynamic-slice_fusion.23
  1.9 2.4 %collective-permute-start.2 = (bf16[32,1024]{1,0:T(8,128)(2,1)}, bf16[32,1024]{1,0:T(8,128)(2,1)S(1)}, u32[]{:S(2)}, u32[]{:S(2)}) collective-permute-start(bf16[32,1024]{1,0:T(8,128)(2,1)} %get-tuple-element.50), channel_id=1, source_target_pairs={{0,3},{1,2},{2,1},{3,0},{4,7},{5,6},{6,5},{7,4},{8,11},{9,10},{10,... | collective-permute-start | bytes 196616 | tf_op jit(solution)/shard_map/ppermute | solution.py:22
  4.3 0.6 collective-permute-start.1
  5.0 0.7 mul.56
  5.7 1.4 %collective-permute-done.2 = bf16[32,1024]{1,0:T(8,128)(2,1)S(1)} collective-permute-done((bf16[32,1024]{1,0:T(8,128)(2,1)}, bf16[32,1024]{1,0:T(8,128)(2,1)S(1)}, u32[]{:S(2)}, u32[]{:S(2)}) %collective-permute-start.2) | collective-permute-done | bytes 65568 | tf_op jit(solution)/shard_map/ppermute | solution.py:22
  7.1 2.1 %collective-permute-done.1 = bf16[32,1024]{1,0:T(8,128)(2,1)S(1)} collective-permute-done((bf16[32,1024]{1,0:T(8,128)(2,1)}, bf16[32,1024]{1,0:T(8,128)(2,1)S(1)}, u32[]{:S(2)}, u32[]{:S(2)}) %collective-permute-start.1) | collective-permute-done | bytes 65568 | tf_op jit(solution)/shard_map/ppermute | solution.py:22
  9.6 0.7 constant_dynamic-slice_fusion.18
  10.3 3.8 %collective-permute-start.5 = (bf16[32,1024]{1,0:T(8,128)(2,1)}, bf16[32,1024]{1,0:T(8,128)(2,1)}, u32[]{:S(2)}, u32[]{:S(2)}) collective-permute-start(bf16[32,1024]{1,0:T(8,128)(2,1)} %get-tuple-element.42), channel_id=1, source_target_pairs={{0,12},{4,8},{8,4},{12,0},{1,13},{5,9},{9,5},{13,1},{2,14},{6,10},... | collective-permute-start | bytes 196616 | tf_op jit(solution)/shard_map/ppermute | solution.py:22
  14.1 0.6 collective-permute-start.3
  14.7 2.2 %constant_dynamic-slice_fusion.13 = (bf16[1024,128]{1,0:T(8,128)(2,1)}, bf16[1024,128]{1,0:T(8,128)(2,1)}, bf16[1024,128]{1,0:T(8,128)(2,1)}, bf16[1024,128]{1,0:T(8,128)(2,1)}) fusion(bf16[1024,512]{1,0:T(8,128)(2,1)} %param.13, s32[]{:T(128)S(6)} %select_n.105, s32[]{:T(128)S(6)} %select_n.124, s32[]{:T(128)S(6)} %select_n.125, s32[]{:T(128)S(6)} %select_n.120), kind=kLoop, calls=%fused_computation.103 | loop fusion | bytes 2097168 | tf_op jit(solution)/shard_map/dynamic_slice | solution.py:279
  17.0 3.2 %collective-permute-done.4 = bf16[32,1024]{1,0:T(8,128)(2,1)} collective-permute-done((bf16[32,1024]{1,0:T(8,128)(2,1)}, bf16[32,1024]{1,0:T(8,128)(2,1)}, u32[]{:S(2)}, u32[]{:S(2)}) %collective-permute-start.4) | collective-permute-done | bytes 65568 | tf_op jit(solution)/shard_map/ppermute | solution.py:22
  20.2 0.9 pad_maximum_fusion.5
  21.2 0.7 pad_maximum_fusion.6
  21.9 2.3 %pad_maximum_fusion = bf16[1024,512]{1,0:T(8,128)(2,1)} fusion(bf16[1024,128]{1,0:T(8,128)(2,1)} %get-tuple-element.19, bf16[1024,128]{1,0:T(8,128)(2,1)} %get-tuple-element.20, bf16[1024,128]{1,0:T(8,128)(2,1)} %get-tuple-element.18, bf16[1024,128]{1,0:T(8,128)(2,1)} %get-tuple-element.17), kind=kLoop, calls=%fused_computation.29 | loop fusion | flops 4194304 | bytes 2097152 | tf_op jit(solution)/shard_map/concatenate | solution.py:280
  24.3 1.2 %copy-done.1 = bf16[1024,512]{1,0:T(8,128)(2,1)S(1)} copy-done((bf16[1024,512]{1,0:T(8,128)(2,1)S(1)}, bf16[1024,512]{1,0:T(8,128)(2,1)}, u32[]{:S(2)}) %copy-start.1) | copy-done | bytes 1048600
  25.5 1.2 %copy-done.2 = bf16[1024,512]{1,0:T(8,128)(2,1)S(1)} copy-done((bf16[1024,512]{1,0:T(8,128)(2,1)S(1)}, bf16[1024,512]{1,0:T(8,128)(2,1)}, u32[]{:S(2)}) %copy-start.2) | copy-done | bytes 1048600
  26.7 0.7 filter_spectrum.1.refs_6_
  27.4 0.7 constant_dynamic-slice_fusion.24.taps_ref
  28.1 1.6 %collective-permute-start.11 = (bf16[128,1024]{1,0:T(8,128)(2,1)}, bf16[128,1024]{1,0:T(8,128)(2,1)S(1)}, u32[]{:S(2)}, u32[]{:S(2)}) collective-permute-start(bf16[128,1024]{1,0:T(8,128)(2,1)} %bitcast.14), channel_id=1, source_target_pairs={{0,2},{1,3},{2,0},{3,1},{4,6},{5,7},{6,4},{7,5},{8,10},{9,11},{10,... | collective-permute-start | bytes 786440 | tf_op jit(solution)/shard_map/ppermute | solution.py:22
  29.7 1.1 pad_maximum_fusion.1
  30.8 0.4 fusion.13
  31.2 1.1 collective-permute-start.7
  32.4 4.7 %collective-permute-done.11 = bf16[128,1024]{1,0:T(8,128)(2,1)S(1)} collective-permute-done((bf16[128,1024]{1,0:T(8,128)(2,1)}, bf16[128,1024]{1,0:T(8,128)(2,1)S(1)}, u32[]{:S(2)}, u32[]{:S(2)}) %collective-permute-start.11) | collective-permute-done | bytes 262176 | tf_op jit(solution)/shard_map/ppermute | solution.py:22
  37.1 0.4 fusion.14
  37.5 3.0 %collective-permute-start.10 = (bf16[3,256,128]{2,1,0:T(8,128)(2,1)S(1)}, bf16[3,256,128]{2,1,0:T(8,128)(2,1)S(1)}, u32[]{:S(2)}, u32[]{:S(2)}) collective-permute-start(bf16[3,256,128]{2,1,0:T(8,128)(2,1)S(1)} %fusion.14), channel_id=1, source_target_pairs={{0,4},{12,8},{1,5},{13,9},{2,6},{14,10},{3,7},{15,11},{16,20},{28,... | collective-permute-start | bytes 589832 | tf_op jit(solution)/shard_map/ppermute | solution.py:72
  40.5 0.7 collective-permute-start.8
  41.2 0.4 fusion.11
  41.7 2.1 %collective-permute-start.9 = (bf16[3,256,128]{2,1,0:T(8,128)(2,1)S(1)}, bf16[3,256,128]{2,1,0:T(8,128)(2,1)S(1)}, u32[]{:S(2)}, u32[]{:S(2)}) collective-permute-start(bf16[3,256,128]{2,1,0:T(8,128)(2,1)S(1)} %fusion.11), channel_id=1, source_target_pairs={{0,8},{4,12},{8,0},{12,4},{1,9},{5,13},{9,1},{13,5},{2,10},{6,14},... | collective-permute-start | bytes 589832 | tf_op jit(solution)/shard_map/ppermute | solution.py:22
  43.8 0.4 fusion.16
  44.3 2.1 %collective-permute-start.16 = (bf16[3,256,128]{2,1,0:T(8,128)(2,1)S(1)}, bf16[3,256,128]{2,1,0:T(8,128)(2,1)S(1)}, u32[]{:S(2)}, u32[]{:S(2)}) collective-permute-start(bf16[3,256,128]{2,1,0:T(8,128)(2,1)S(1)} %fusion.16), channel_id=1, source_target_pairs={{0,4},{12,8},{1,5},{13,9},{2,6},{14,10},{3,7},{15,11},{16,20},{28,... | collective-permute-start | bytes 589832 | tf_op jit(solution)/shard_map/ppermute | solution.py:72
  46.4 0.7 collective-permute-start.14
  47.1 0.4 fusion.15
  47.5 1.9 %collective-permute-start.13 = (bf16[3,256,128]{2,1,0:T(8,128)(2,1)S(1)}, bf16[3,256,128]{2,1,0:T(8,128)(2,1)S(1)}, u32[]{:S(2)}, u32[]{:S(2)}) collective-permute-start(bf16[3,256,128]{2,1,0:T(8,128)(2,1)S(1)} %fusion.15), channel_id=1, source_target_pairs={{0,4},{4,0},{8,12},{12,8},{1,5},{5,1},{9,13},{13,9},{2,6},{6,2},{1... | collective-permute-start | bytes 589832 | tf_op jit(solution)/shard_map/ppermute | solution.py:22
  49.4 8.0 %collective-permute-done.9 = bf16[3,256,128]{2,1,0:T(8,128)(2,1)S(1)} collective-permute-done((bf16[3,256,128]{2,1,0:T(8,128)(2,1)S(1)}, bf16[3,256,128]{2,1,0:T(8,128)(2,1)S(1)}, u32[]{:S(2)}, u32[]{:S(2)}) %collective-permute-start.9) | collective-permute-done | bytes 196640 | tf_op jit(solution)/shard_map/ppermute | solution.py:22
  57.5 0.5 fusion.9.refs_0_
  58.0 0.4 collective-permute-done.13
  58.4 0.4 fusion.12
  58.9 2.4 %collective-permute-start.15 = (bf16[3,256,128]{2,1,0:T(8,128)(2,1)S(1)}, bf16[3,256,128]{2,1,0:T(8,128)(2,1)S(1)}, u32[]{:S(2)}, u32[]{:S(2)}) collective-permute-start(bf16[3,256,128]{2,1,0:T(8,128)(2,1)S(1)} %fusion.12), channel_id=1, source_target_pairs={{0,8},{4,12},{8,0},{12,4},{1,9},{5,13},{9,1},{13,5},{2,10},{6,14},... | collective-permute-start | bytes 589832 | tf_op jit(solution)/shard_map/ppermute | solution.py:22
  61.2 0.4 fusion.10.refs_1_
  61.7 8.5 %collective-permute-done.15.refs_2_ = bf16[3,256,128]{2,1,0:T(8,128)(2,1)S(1)} collective-permute-done((bf16[3,256,128]{2,1,0:T(8,128)(2,1)S(1)}, bf16[3,256,128]{2,1,0:T(8,128)(2,1)S(1)}, u32[]{:S(2)}, u32[]{:S(2)}) %collective-permute-start.15) | collective-permute-done | bytes 196640 | tf_op jit(solution)/shard_map/ppermute | solution.py:22
  70.1 2.7 %filters.1 = (bf16[256,128]{1,0:T(8,128)(2,1)S(1)}, bf16[256,128]{1,0:T(8,128)(2,1)S(1)}) custom-call(s32[1]{0:T(128)} %bitcast.t_ref, f32[3,3,128]{2,1,0:T(4,128)S(1)} %constant_dynamic-slice_fusion.24.taps_ref, f32[3,256,128]{2,1,0:T(8,128)S(1)} %fusion.9.refs_0_, f32[3,256,128]{2,1,0:T(8,128)S(1)} %fusion.10.refs_1_, ...), custom_call_target="tpu_custom_call" | custom-call | flops 805306368 | bytes 2097152 | tf_op jit(solution)/shard_map/filters/pallas_call | solution.py:220
  73.0 2.7 %collective-permute-start.18 = (bf16[256,128]{1,0:T(8,128)(2,1)S(1)}, bf16[256,128]{1,0:T(8,128)(2,1)S(1)}, u32[]{:S(2)}, u32[]{:S(2)}) collective-permute-start(bf16[256,128]{1,0:T(8,128)(2,1)S(1)} %get-tuple-element.15), channel_id=1, source_target_pairs={{0,8},{4,12},{8,0},{12,4},{1,9},{5,13},{9,1},{13,5},{2,10},{6,14},... | collective-permute-start | bytes 196616 | tf_op jit(solution)/shard_map/ppermute | solution.py:22
  75.7 1.7 %collective-permute-start.17 = (bf16[256,128]{1,0:T(8,128)(2,1)S(1)}, bf16[256,128]{1,0:T(8,128)(2,1)S(1)}, u32[]{:S(2)}, u32[]{:S(2)}) collective-permute-start(bf16[256,128]{1,0:T(8,128)(2,1)S(1)} %get-tuple-element.15), channel_id=1, source_target_pairs={{0,12},{4,8},{8,4},{12,0},{1,13},{5,9},{9,5},{13,1},{2,14},{6,10},... | collective-permute-start | bytes 196616 | tf_op jit(solution)/shard_map/ppermute | solution.py:22
  77.3 2.2 %collective-permute-start.21 = (bf16[256,128]{1,0:T(8,128)(2,1)S(1)}, bf16[256,128]{1,0:T(8,128)(2,1)S(1)}, u32[]{:S(2)}, u32[]{:S(2)}) collective-permute-start(bf16[256,128]{1,0:T(8,128)(2,1)S(1)} %get-tuple-element.16), channel_id=1, source_target_pairs={{0,12},{4,8},{8,4},{12,0},{1,13},{5,9},{9,5},{13,1},{2,14},{6,10},... | collective-permute-start | bytes 196616 | tf_op jit(solution)/shard_map/ppermute | solution.py:22
  79.5 4.0 %collective-permute-done.21 = bf16[256,128]{1,0:T(8,128)(2,1)S(1)} collective-permute-done((bf16[256,128]{1,0:T(8,128)(2,1)S(1)}, bf16[256,128]{1,0:T(8,128)(2,1)S(1)}, u32[]{:S(2)}, u32[]{:S(2)}) %collective-permute-start.21) | collective-permute-done | bytes 65568 | tf_op jit(solution)/shard_map/ppermute | solution.py:22
  83.5 1.6 %collective-permute-start.22 = (bf16[256,128]{1,0:T(8,128)(2,1)S(1)}, bf16[256,128]{1,0:T(8,128)(2,1)S(1)}, u32[]{:S(2)}, u32[]{:S(2)}) collective-permute-start(bf16[256,128]{1,0:T(8,128)(2,1)S(1)} %get-tuple-element.16), channel_id=1, source_target_pairs={{0,8},{4,12},{8,0},{12,4},{1,9},{5,13},{9,1},{13,5},{2,10},{6,14},... | collective-permute-start | bytes 196616 | tf_op jit(solution)/shard_map/ppermute | solution.py:22
  85.2 4.2 %collective-permute-done.22 = bf16[256,128]{1,0:T(8,128)(2,1)S(1)} collective-permute-done((bf16[256,128]{1,0:T(8,128)(2,1)S(1)}, bf16[256,128]{1,0:T(8,128)(2,1)S(1)}, u32[]{:S(2)}, u32[]{:S(2)}) %collective-permute-start.22) | collective-permute-done | bytes 65568 | tf_op jit(solution)/shard_map/ppermute | solution.py:22
  89.4 0.5 convolution_convert_fusion
  90.1 0.5 convolution_convert_fusion.1
  90.6 0.6 collective-permute-start.20
  91.5 0.5 fusion.2
  92.0 1.6 %collective-permute-start.25 = (bf16[128,1024]{1,0:T(8,128)(2,1)S(1)}, bf16[128,1024]{1,0:T(8,128)(2,1)S(1)}, u32[]{:S(2)}, u32[]{:S(2)}) collective-permute-start(bf16[128,1024]{1,0:T(8,128)(2,1)S(1)} %fusion.2), channel_id=1, source_target_pairs={{0,2},{1,3},{2,0},{3,1},{4,6},{5,7},{6,4},{7,5},{8,10},{9,11},{10,... | collective-permute-start | bytes 786440 | tf_op jit(solution)/shard_map/ppermute | solution.py:22
  93.6 6.8 %collective-permute-done.25 = bf16[128,1024]{1,0:T(8,128)(2,1)S(1)} collective-permute-done((bf16[128,1024]{1,0:T(8,128)(2,1)S(1)}, bf16[128,1024]{1,0:T(8,128)(2,1)S(1)}, u32[]{:S(2)}, u32[]{:S(2)}) %collective-permute-start.25) | collective-permute-done | bytes 262176 | tf_op jit(solution)/shard_map/ppermute | solution.py:22
  100.4 0.5 fusion.1
  100.9 2.2 %collective-permute-start.28 = (bf16[32,1024]{1,0:T(8,128)(2,1)S(1)}, bf16[32,1024]{1,0:T(8,128)(2,1)S(1)}, u32[]{:S(2)}, u32[]{:S(2)}) collective-permute-start(bf16[32,1024]{1,0:T(8,128)(2,1)S(1)} %get-tuple-element.34), channel_id=1, source_target_pairs={{0,12},{4,8},{8,4},{12,0},{1,13},{5,9},{9,5},{13,1},{2,14},{6,10},... | collective-permute-start | bytes 196616 | tf_op jit(solution)/shard_map/ppermute | solution.py:22
  103.2 2.2 %collective-permute-start.26 = (bf16[32,1024]{1,0:T(8,128)(2,1)S(1)}, bf16[32,1024]{1,0:T(8,128)(2,1)S(1)}, u32[]{:S(2)}, u32[]{:S(2)}) collective-permute-start(bf16[32,1024]{1,0:T(8,128)(2,1)S(1)} %get-tuple-element.36), channel_id=1, source_target_pairs={{0,4},{4,0},{8,12},{12,8},{1,5},{5,1},{9,13},{13,9},{2,6},{6,2},{1... | collective-permute-start | bytes 196616 | tf_op jit(solution)/shard_map/ppermute | solution.py:22
  105.4 1.9 %collective-permute-done.28 = bf16[32,1024]{1,0:T(8,128)(2,1)S(1)} collective-permute-done((bf16[32,1024]{1,0:T(8,128)(2,1)S(1)}, bf16[32,1024]{1,0:T(8,128)(2,1)S(1)}, u32[]{:S(2)}, u32[]{:S(2)}) %collective-permute-start.28) | collective-permute-done | bytes 65568 | tf_op jit(solution)/shard_map/ppermute | solution.py:22
  107.3 1.9 %collective-permute-done.27 = bf16[32,1024]{1,0:T(8,128)(2,1)S(1)} collective-permute-done((bf16[32,1024]{1,0:T(8,128)(2,1)S(1)}, bf16[32,1024]{1,0:T(8,128)(2,1)S(1)}, u32[]{:S(2)}, u32[]{:S(2)}) %collective-permute-start.27) | collective-permute-done | bytes 65568 | tf_op jit(solution)/shard_map/ppermute | solution.py:22
  109.3 1.0 collective-permute-start.31
  110.3 0.7 collective-permute-start.30
  111.3 2.4 %collective-permute-done.31 = bf16[32,1024]{1,0:T(8,128)(2,1)S(1)} collective-permute-done((bf16[32,1024]{1,0:T(8,128)(2,1)S(1)}, bf16[32,1024]{1,0:T(8,128)(2,1)S(1)}, u32[]{:S(2)}, u32[]{:S(2)}) %collective-permute-start.31) | collective-permute-done | bytes 65568 | tf_op jit(solution)/shard_map/ppermute | solution.py:22
  113.7 1.5 %collective-permute-done.30 = bf16[32,1024]{1,0:T(8,128)(2,1)S(1)} collective-permute-done((bf16[32,1024]{1,0:T(8,128)(2,1)S(1)}, bf16[32,1024]{1,0:T(8,128)(2,1)S(1)}, u32[]{:S(2)}, u32[]{:S(2)}) %collective-permute-start.30) | collective-permute-done | bytes 65568 | tf_op jit(solution)/shard_map/ppermute | solution.py:22
  115.3 0.9 convert_add_fusion
  (59 shorter events, 1.8 us)
Async XLA Ops:
  0.0 30.8 %copy-start = (bf16[3,1024,512]{2,1,0:T(8,128)(2,1)S(1)}, bf16[3,1024,512]{2,1,0:T(8,128)(2,1)}, u32[]{:S(2)}) copy-start(bf16[3,1024,512]{2,1,0:T(8,128)(2,1)} %param.10) | copy-start | bytes 9437188
  1.9 5.2 %collective-permute-start.2 = (bf16[32,1024]{1,0:T(8,128)(2,1)}, bf16[32,1024]{1,0:T(8,128)(2,1)S(1)}, u32[]{:S(2)}, u32[]{:S(2)}) collective-permute-start(bf16[32,1024]{1,0:T(8,128)(2,1)} %get-tuple-element.50), channel_id=1, source_target_pairs={{0,3},{1,2},{2,1},{3,0},{4,7},{5,6},{6,5},{7,4},{8,11},{9,10},{10,... | collective-permute-start | bytes 196616 | tf_op jit(solution)/shard_map/ppermute | solution.py:22
  4.3 4.9 %collective-permute-start.1 = (bf16[32,1024]{1,0:T(8,128)(2,1)}, bf16[32,1024]{1,0:T(8,128)(2,1)S(1)}, u32[]{:S(2)}, u32[]{:S(2)}) collective-permute-start(bf16[32,1024]{1,0:T(8,128)(2,1)} %get-tuple-element.51), channel_id=1, source_target_pairs={{0,2},{1,3},{2,0},{3,1},{4,6},{5,7},{6,4},{7,5},{8,10},{9,11},{10,... | collective-permute-start | bytes 196616 | tf_op jit(solution)/shard_map/ppermute | solution.py:22
  4.9 4.3 %collective-permute-start = (bf16[32,1024]{1,0:T(8,128)(2,1)S(1)}, bf16[32,1024]{1,0:T(8,128)(2,1)S(1)}, u32[]{:S(2)}, u32[]{:S(2)}) collective-permute-start(bf16[32,1024]{1,0:T(8,128)(2,1)S(1)} %get-tuple-element.52), channel_id=1, source_target_pairs={{0,1},{1,0},{2,3},{3,2},{4,5},{5,4},{6,7},{7,6},{8,9},{9,8},{10,11... | collective-permute-start | bytes 196616 | tf_op jit(solution)/shard_map/ppermute | solution.py:22
  9.6 14.6 %copy-start.3 = (f32[128,512]{1,0:T(8,128)S(1)}, f32[128,512]{1,0:T(8,128)}, u32[]{:S(2)}) copy-start(f32[128,512]{1,0:T(8,128)} %taps_ref.1) | copy-start | bytes 786436
  10.3 6.6 %collective-permute-start.5 = (bf16[32,1024]{1,0:T(8,128)(2,1)}, bf16[32,1024]{1,0:T(8,128)(2,1)}, u32[]{:S(2)}, u32[]{:S(2)}) collective-permute-start(bf16[32,1024]{1,0:T(8,128)(2,1)} %get-tuple-element.42), channel_id=1, source_target_pairs={{0,12},{4,8},{8,4},{12,0},{1,13},{5,9},{9,5},{13,1},{2,14},{6,10},... | collective-permute-start | bytes 196616 | tf_op jit(solution)/shard_map/ppermute | solution.py:22
  14.1 6.1 %collective-permute-start.4 = (bf16[32,1024]{1,0:T(8,128)(2,1)}, bf16[32,1024]{1,0:T(8,128)(2,1)}, u32[]{:S(2)}, u32[]{:S(2)}) collective-permute-start(bf16[32,1024]{1,0:T(8,128)(2,1)} %get-tuple-element.43), channel_id=1, source_target_pairs={{0,8},{4,12},{8,0},{12,4},{1,9},{5,13},{9,1},{13,5},{2,10},{6,14},... | collective-permute-start | bytes 196616 | tf_op jit(solution)/shard_map/ppermute | solution.py:22
  14.1 6.1 %collective-permute-start.3 = (bf16[32,1024]{1,0:T(8,128)(2,1)S(1)}, bf16[32,1024]{1,0:T(8,128)(2,1)}, u32[]{:S(2)}, u32[]{:S(2)}) collective-permute-start(bf16[32,1024]{1,0:T(8,128)(2,1)S(1)} %get-tuple-element.44), channel_id=1, source_target_pairs={{0,4},{4,0},{8,12},{12,8},{1,5},{5,1},{9,13},{13,9},{2,6},{6,2},{1... | collective-permute-start | bytes 196616 | tf_op jit(solution)/shard_map/ppermute | solution.py:22
  21.9 7.8 %collective-permute-start.6 = (bf16[128,1024]{1,0:T(8,128)(2,1)}, bf16[128,1024]{1,0:T(8,128)(2,1)}, u32[]{:S(2)}, u32[]{:S(2)}) collective-permute-start(bf16[128,1024]{1,0:T(8,128)(2,1)} %bitcast.14), channel_id=1, source_target_pairs={{0,1},{1,0},{2,3},{3,2},{4,5},{5,4},{6,7},{7,6},{8,9},{9,8},{10,11... | collective-permute-start | bytes 786440 | tf_op jit(solution)/shard_map/ppermute | solution.py:22
  24.2 1.2 %copy-start.1 = (bf16[1024,512]{1,0:T(8,128)(2,1)S(1)}, bf16[1024,512]{1,0:T(8,128)(2,1)}, u32[]{:S(2)}) copy-start(bf16[1024,512]{1,0:T(8,128)(2,1)} %constant.100.clone.low_ref.refs_5_) | copy-start | bytes 3145732
  25.5 1.2 %copy-start.2 = (bf16[1024,512]{1,0:T(8,128)(2,1)S(1)}, bf16[1024,512]{1,0:T(8,128)(2,1)}, u32[]{:S(2)}) copy-start(bf16[1024,512]{1,0:T(8,128)(2,1)} %constant.99.clone.high_ref.refs_4_) | copy-start | bytes 3145732
  28.1 8.9 %collective-permute-start.11 = (bf16[128,1024]{1,0:T(8,128)(2,1)}, bf16[128,1024]{1,0:T(8,128)(2,1)S(1)}, u32[]{:S(2)}, u32[]{:S(2)}) collective-permute-start(bf16[128,1024]{1,0:T(8,128)(2,1)} %bitcast.14), channel_id=1, source_target_pairs={{0,2},{1,3},{2,0},{3,1},{4,6},{5,7},{6,4},{7,5},{8,10},{9,11},{10,... | collective-permute-start | bytes 786440 | tf_op jit(solution)/shard_map/ppermute | solution.py:22
  31.2 10.0 %collective-permute-start.7 = (bf16[3,256,128]{2,1,0:T(8,128)(2,1)S(1)}, bf16[3,256,128]{2,1,0:T(8,128)(2,1)S(1)}, u32[]{:S(2)}, u32[]{:S(2)}) collective-permute-start(bf16[3,256,128]{2,1,0:T(8,128)(2,1)S(1)} %fusion.13), channel_id=1, source_target_pairs={{0,4},{4,0},{8,12},{12,8},{1,5},{5,1},{9,13},{13,9},{2,6},{6,2},{1... | collective-permute-start | bytes 589832 | tf_op jit(solution)/shard_map/ppermute | solution.py:22
  37.1 6.7 %collective-permute-start.12 = (bf16[128,1024]{1,0:T(8,128)(2,1)S(1)}, bf16[128,1024]{1,0:T(8,128)(2,1)S(1)}, u32[]{:S(2)}, u32[]{:S(2)}) collective-permute-start(bf16[128,1024]{1,0:T(8,128)(2,1)S(1)} %collective-permute-done.11), channel_id=1, source_target_pairs={{0,1},{1,0},{2,3},{3,2},{4,5},{5,4},{6,7},{7,6},{8,9},{9,8},{10,11... | collective-permute-start | bytes 786440 | tf_op jit(solution)/shard_map/ppermute | solution.py:22
  37.5 10.0 %collective-permute-start.10 = (bf16[3,256,128]{2,1,0:T(8,128)(2,1)S(1)}, bf16[3,256,128]{2,1,0:T(8,128)(2,1)S(1)}, u32[]{:S(2)}, u32[]{:S(2)}) collective-permute-start(bf16[3,256,128]{2,1,0:T(8,128)(2,1)S(1)} %fusion.14), channel_id=1, source_target_pairs={{0,4},{12,8},{1,5},{13,9},{2,6},{14,10},{3,7},{15,11},{16,20},{28,... | collective-permute-start | bytes 589832 | tf_op jit(solution)/shard_map/ppermute | solution.py:72
  40.5 8.9 %collective-permute-start.8 = (bf16[3,256,128]{2,1,0:T(8,128)(2,1)S(1)}, bf16[3,256,128]{2,1,0:T(8,128)(2,1)S(1)}, u32[]{:S(2)}, u32[]{:S(2)}) collective-permute-start(bf16[3,256,128]{2,1,0:T(8,128)(2,1)S(1)} %fusion.14), channel_id=1, source_target_pairs={{4,8},{8,4},{5,9},{9,5},{6,10},{10,6},{7,11},{11,7},{20,24},{24,20... | collective-permute-start | bytes 589832 | tf_op jit(solution)/shard_map/ppermute | solution.py:71
  41.7 15.8 %collective-permute-start.9 = (bf16[3,256,128]{2,1,0:T(8,128)(2,1)S(1)}, bf16[3,256,128]{2,1,0:T(8,128)(2,1)S(1)}, u32[]{:S(2)}, u32[]{:S(2)}) collective-permute-start(bf16[3,256,128]{2,1,0:T(8,128)(2,1)S(1)} %fusion.11), channel_id=1, source_target_pairs={{0,8},{4,12},{8,0},{12,4},{1,9},{5,13},{9,1},{13,5},{2,10},{6,14},... | collective-permute-start | bytes 589832 | tf_op jit(solution)/shard_map/ppermute | solution.py:22
  44.3 17.4 %collective-permute-start.16 = (bf16[3,256,128]{2,1,0:T(8,128)(2,1)S(1)}, bf16[3,256,128]{2,1,0:T(8,128)(2,1)S(1)}, u32[]{:S(2)}, u32[]{:S(2)}) collective-permute-start(bf16[3,256,128]{2,1,0:T(8,128)(2,1)S(1)} %fusion.16), channel_id=1, source_target_pairs={{0,4},{12,8},{1,5},{13,9},{2,6},{14,10},{3,7},{15,11},{16,20},{28,... | collective-permute-start | bytes 589832 | tf_op jit(solution)/shard_map/ppermute | solution.py:72
  46.4 14.8 %collective-permute-start.14 = (bf16[3,256,128]{2,1,0:T(8,128)(2,1)S(1)}, bf16[3,256,128]{2,1,0:T(8,128)(2,1)S(1)}, u32[]{:S(2)}, u32[]{:S(2)}) collective-permute-start(bf16[3,256,128]{2,1,0:T(8,128)(2,1)S(1)} %fusion.16), channel_id=1, source_target_pairs={{4,8},{8,4},{5,9},{9,5},{6,10},{10,6},{7,11},{11,7},{20,24},{24,20... | collective-permute-start | bytes 589832 | tf_op jit(solution)/shard_map/ppermute | solution.py:71
  47.5 10.9 %collective-permute-start.13 = (bf16[3,256,128]{2,1,0:T(8,128)(2,1)S(1)}, bf16[3,256,128]{2,1,0:T(8,128)(2,1)S(1)}, u32[]{:S(2)}, u32[]{:S(2)}) collective-permute-start(bf16[3,256,128]{2,1,0:T(8,128)(2,1)S(1)} %fusion.15), channel_id=1, source_target_pairs={{0,4},{4,0},{8,12},{12,8},{1,5},{5,1},{9,13},{13,9},{2,6},{6,2},{1... | collective-permute-start | bytes 589832 | tf_op jit(solution)/shard_map/ppermute | solution.py:22
  58.8 30.6 %copy-start.4 = (bf16[1024,512]{1,0:T(8,128)(2,1)S(1)}, bf16[1024,512]{1,0:T(8,128)(2,1)}, u32[]{:S(2)}) copy-start(bf16[1024,512]{1,0:T(8,128)(2,1)} %pad_maximum_fusion) | copy-start | bytes 3145732
  58.9 11.3 %collective-permute-start.15 = (bf16[3,256,128]{2,1,0:T(8,128)(2,1)S(1)}, bf16[3,256,128]{2,1,0:T(8,128)(2,1)S(1)}, u32[]{:S(2)}, u32[]{:S(2)}) collective-permute-start(bf16[3,256,128]{2,1,0:T(8,128)(2,1)S(1)} %fusion.12), channel_id=1, source_target_pairs={{0,8},{4,12},{8,0},{12,4},{1,9},{5,13},{9,1},{13,5},{2,10},{6,14},... | collective-permute-start | bytes 589832 | tf_op jit(solution)/shard_map/ppermute | solution.py:22
  72.9 17.2 %collective-permute-start.19 = (bf16[256,128]{1,0:T(8,128)(2,1)S(1)}, bf16[256,128]{1,0:T(8,128)(2,1)S(1)}, u32[]{:S(2)}, u32[]{:S(2)}) collective-permute-start(bf16[256,128]{1,0:T(8,128)(2,1)S(1)} %get-tuple-element.15), channel_id=1, source_target_pairs={{0,4},{4,0},{8,12},{12,8},{1,5},{5,1},{9,13},{13,9},{2,6},{6,2},{1... | collective-permute-start | bytes 196616 | tf_op jit(solution)/shard_map/ppermute | solution.py:22
  73.0 17.1 %collective-permute-start.18 = (bf16[256,128]{1,0:T(8,128)(2,1)S(1)}, bf16[256,128]{1,0:T(8,128)(2,1)S(1)}, u32[]{:S(2)}, u32[]{:S(2)}) collective-permute-start(bf16[256,128]{1,0:T(8,128)(2,1)S(1)} %get-tuple-element.15), channel_id=1, source_target_pairs={{0,8},{4,12},{8,0},{12,4},{1,9},{5,13},{9,1},{13,5},{2,10},{6,14},... | collective-permute-start | bytes 196616 | tf_op jit(solution)/shard_map/ppermute | solution.py:22
  75.7 14.3 %collective-permute-start.17 = (bf16[256,128]{1,0:T(8,128)(2,1)S(1)}, bf16[256,128]{1,0:T(8,128)(2,1)S(1)}, u32[]{:S(2)}, u32[]{:S(2)}) collective-permute-start(bf16[256,128]{1,0:T(8,128)(2,1)S(1)} %get-tuple-element.15), channel_id=1, source_target_pairs={{0,12},{4,8},{8,4},{12,0},{1,13},{5,9},{9,5},{13,1},{2,14},{6,10},... | collective-permute-start | bytes 196616 | tf_op jit(solution)/shard_map/ppermute | solution.py:22
  77.3 12.1 %collective-permute-start.23 = (bf16[256,128]{1,0:T(8,128)(2,1)S(1)}, bf16[256,128]{1,0:T(8,128)(2,1)S(1)}, u32[]{:S(2)}, u32[]{:S(2)}) collective-permute-start(bf16[256,128]{1,0:T(8,128)(2,1)S(1)} %get-tuple-element.16), channel_id=1, source_target_pairs={{0,4},{4,0},{8,12},{12,8},{1,5},{5,1},{9,13},{13,9},{2,6},{6,2},{1... | collective-permute-start | bytes 196616 | tf_op jit(solution)/shard_map/ppermute | solution.py:22
  77.3 6.2 %collective-permute-start.21 = (bf16[256,128]{1,0:T(8,128)(2,1)S(1)}, bf16[256,128]{1,0:T(8,128)(2,1)S(1)}, u32[]{:S(2)}, u32[]{:S(2)}) collective-permute-start(bf16[256,128]{1,0:T(8,128)(2,1)S(1)} %get-tuple-element.16), channel_id=1, source_target_pairs={{0,12},{4,8},{8,4},{12,0},{1,13},{5,9},{9,5},{13,1},{2,14},{6,10},... | collective-permute-start | bytes 196616 | tf_op jit(solution)/shard_map/ppermute | solution.py:22
  83.5 5.9 %collective-permute-start.22 = (bf16[256,128]{1,0:T(8,128)(2,1)S(1)}, bf16[256,128]{1,0:T(8,128)(2,1)S(1)}, u32[]{:S(2)}, u32[]{:S(2)}) collective-permute-start(bf16[256,128]{1,0:T(8,128)(2,1)S(1)} %get-tuple-element.16), channel_id=1, source_target_pairs={{0,8},{4,12},{8,0},{12,4},{1,9},{5,13},{9,1},{13,5},{2,10},{6,14},... | collective-permute-start | bytes 196616 | tf_op jit(solution)/shard_map/ppermute | solution.py:22
  89.9 1.6 %collective-permute-start.24 = (bf16[128,1024]{1,0:T(8,128)(2,1)S(1)}, bf16[128,1024]{1,0:T(8,128)(2,1)S(1)}, u32[]{:S(2)}, u32[]{:S(2)}) collective-permute-start(bf16[128,1024]{1,0:T(8,128)(2,1)S(1)} %convolution_convert_fusion), channel_id=1, source_target_pairs={{0,1},{1,0},{2,3},{3,2},{4,5},{5,4},{6,7},{7,6},{8,9},{9,8},{10,11... | collective-permute-start | bytes 786440 | tf_op jit(solution)/shard_map/ppermute | solution.py:22
  90.6 3.1 %collective-permute-start.20 = (bf16[128,1024]{1,0:T(8,128)(2,1)S(1)}, bf16[128,1024]{1,0:T(8,128)(2,1)S(1)}, u32[]{:S(2)}, u32[]{:S(2)}) collective-permute-start(bf16[128,1024]{1,0:T(8,128)(2,1)S(1)} %convolution_convert_fusion.1), channel_id=1, source_target_pairs={{0,1},{1,0},{2,3},{3,2},{4,5},{5,4},{6,7},{7,6},{8,9},{9,8},{10,11... | collective-permute-start | bytes 786440 | tf_op jit(solution)/shard_map/ppermute | solution.py:22
  92.0 23.3 %copy-start.5 = (f32[128,1024]{1,0:T(8,128)S(1)}, f32[128,1024]{1,0:T(8,128)}, u32[]{:S(2)}) copy-start(f32[128,1024]{1,0:T(8,128)} %param.8) | copy-start | bytes 1572868
  92.0 8.4 %collective-permute-start.25 = (bf16[128,1024]{1,0:T(8,128)(2,1)S(1)}, bf16[128,1024]{1,0:T(8,128)(2,1)S(1)}, u32[]{:S(2)}, u32[]{:S(2)}) collective-permute-start(bf16[128,1024]{1,0:T(8,128)(2,1)S(1)} %fusion.2), channel_id=1, source_target_pairs={{0,2},{1,3},{2,0},{3,1},{4,6},{5,7},{6,4},{7,5},{8,10},{9,11},{10,... | collective-permute-start | bytes 786440 | tf_op jit(solution)/shard_map/ppermute | solution.py:22
  100.9 6.4 %collective-permute-start.28 = (bf16[32,1024]{1,0:T(8,128)(2,1)S(1)}, bf16[32,1024]{1,0:T(8,128)(2,1)S(1)}, u32[]{:S(2)}, u32[]{:S(2)}) collective-permute-start(bf16[32,1024]{1,0:T(8,128)(2,1)S(1)} %get-tuple-element.34), channel_id=1, source_target_pairs={{0,12},{4,8},{8,4},{12,0},{1,13},{5,9},{9,5},{13,1},{2,14},{6,10},... | collective-permute-start | bytes 196616 | tf_op jit(solution)/shard_map/ppermute | solution.py:22
  103.2 6.0 %collective-permute-start.27 = (bf16[32,1024]{1,0:T(8,128)(2,1)S(1)}, bf16[32,1024]{1,0:T(8,128)(2,1)S(1)}, u32[]{:S(2)}, u32[]{:S(2)}) collective-permute-start(bf16[32,1024]{1,0:T(8,128)(2,1)S(1)} %get-tuple-element.35), channel_id=1, source_target_pairs={{0,8},{4,12},{8,0},{12,4},{1,9},{5,13},{9,1},{13,5},{2,10},{6,14},... | collective-permute-start | bytes 196616 | tf_op jit(solution)/shard_map/ppermute | solution.py:22
  103.2 6.0 %collective-permute-start.26 = (bf16[32,1024]{1,0:T(8,128)(2,1)S(1)}, bf16[32,1024]{1,0:T(8,128)(2,1)S(1)}, u32[]{:S(2)}, u32[]{:S(2)}) collective-permute-start(bf16[32,1024]{1,0:T(8,128)(2,1)S(1)} %get-tuple-element.36), channel_id=1, source_target_pairs={{0,4},{4,0},{8,12},{12,8},{1,5},{5,1},{9,13},{13,9},{2,6},{6,2},{1... | collective-permute-start | bytes 196616 | tf_op jit(solution)/shard_map/ppermute | solution.py:22
  109.3 4.3 %collective-permute-start.31 = (bf16[32,1024]{1,0:T(8,128)(2,1)S(1)}, bf16[32,1024]{1,0:T(8,128)(2,1)S(1)}, u32[]{:S(2)}, u32[]{:S(2)}) collective-permute-start(bf16[32,1024]{1,0:T(8,128)(2,1)S(1)} %get-tuple-element.26), channel_id=1, source_target_pairs={{0,3},{1,2},{2,1},{3,0},{4,7},{5,6},{6,5},{7,4},{8,11},{9,10},{10,... | collective-permute-start | bytes 196616 | tf_op jit(solution)/shard_map/ppermute | solution.py:22
  110.3 4.9 %collective-permute-start.30 = (bf16[32,1024]{1,0:T(8,128)(2,1)S(1)}, bf16[32,1024]{1,0:T(8,128)(2,1)S(1)}, u32[]{:S(2)}, u32[]{:S(2)}) collective-permute-start(bf16[32,1024]{1,0:T(8,128)(2,1)S(1)} %get-tuple-element.27), channel_id=1, source_target_pairs={{0,2},{1,3},{2,0},{3,1},{4,6},{5,7},{6,4},{7,5},{8,10},{9,11},{10,... | collective-permute-start | bytes 196616 | tf_op jit(solution)/shard_map/ppermute | solution.py:22
  111.1 4.1 %collective-permute-start.29 = (bf16[32,1024]{1,0:T(8,128)(2,1)S(1)}, bf16[32,1024]{1,0:T(8,128)(2,1)S(1)}, u32[]{:S(2)}, u32[]{:S(2)}) collective-permute-start(bf16[32,1024]{1,0:T(8,128)(2,1)S(1)} %get-tuple-element.28), channel_id=1, source_target_pairs={{0,1},{1,0},{2,3},{3,2},{4,5},{5,4},{6,7},{7,6},{8,9},{9,8},{10,11... | collective-permute-start | bytes 196616 | tf_op jit(solution)/shard_map/ppermute | solution.py:22
